TPU v7x, 32 devices: a whole 2x2x4 slice. The times are simulated.
32 devices in a mesh: clip: 8 (over y, x, core), head: 4 (over z).
Axes of the slice: x: 2, y: 2, z: 4, core: 2. Of those that a mesh axis runs over, the one named last changes fastest.
Arguments:
- tokens: bfloat16 [40960, 1024], P(('clip', 'head')), may hold values from -6 to 6
- d_out: bfloat16 [40960, 1024], P(('clip', 'head')), may hold values from -6 to 6
- modulation: float32 [8, 12, 1024], P('clip'), may hold values from -1.5 to 1.5
- frame_counts: int32 [8], P('clip'), may hold values from 2 to 5, as said below
- w_qkv: bfloat16 [2, 3, 1024, 1024], P(None, None, None, 'head'), may hold values from -0.1875 to 0.1875
- w_out: bfloat16 [2, 1024, 1024], P(None, 'head'), may hold values from -0.75 to 0.75
- w_up: bfloat16 [2, 1024, 4096], P(None, None, 'head'), may hold values from -0.1875 to 0.1875
- w_down: bfloat16 [2, 4096, 1024], P(None, 'head'), may hold values from -0.09375 to 0.09375
- table_s: float32 [16, 961], P('head'), may hold values from -4 to 4
- table_t: float32 [16, 2025], P('head'), may hold values from -4 to 4
Outputs:
- output: bfloat16 [40960, 1024], P(('clip', 'head'))
- grad_tokens: float32 [40960, 1024], P(('clip', 'head'))
- grad_modulation: float32 [8, 12, 1024], P('clip')
- grad_qkv: float32 [2, 3, 1024, 1024], P(None, None, None, 'head')
- grad_out: float32 [2, 1024, 1024], P(None, 'head')
- grad_up: float32 [2, 1024, 4096], P(None, None, 'head')
- grad_down: float32 [2, 4096, 1024], P(None, 'head')
- grad_table_s: float32 [16, 961], P('head')
- grad_table_t: float32 [16, 2025], P('head')
Inputs may be any that keep to these rules, and one draw needn't show every extreme that they name: `frame_counts`: every clip has 2 to 5 live frames; in every draw some clip has 5 and some has 2.
All inputs are finite; a program needn't handle non-finite values.
Results may differ from a plain program's by a relative error of at most 0.04.
Values may be sent and summed in bfloat16 or wider, within the bound.
A program may use at most 512 MiB of HBM per device.

v0:
```python
import jax
import jax.numpy as jnp
from jax import lax
from jax.sharding import PartitionSpec as P

HD = 64
FH = 32
FW = 32
SWIN = 16
TWIN = 8
PADF = 5


EPS = 1e-06
HIGHEST_PRECISION = lax.Precision.HIGHEST
NEGATIVE = -1e30


def layer_norm(values, shift_row, scale_row):
    average = jnp.mean(values, axis=-1, keepdims=True)
    centred = values - average
    spread = jnp.mean(centred * centred, axis=-1, keepdims=True)
    return centred * lax.rsqrt(spread + EPS) * (1.0 + scale_row) + shift_row


def gelu_tanh(values):
    return jax.nn.gelu(values, approximate=True)


def window_index(side_t, side_len):
    window_size = side_t * side_len * side_len
    places = jnp.arange(window_size, dtype=jnp.int32)
    time_pos = places // (side_len * side_len)
    height_pos = places // side_len % side_len
    width_pos = places % side_len
    span_len = 2 * side_len - 1
    return (
        (time_pos[:, None] - time_pos[None, :] + side_t - 1) * span_len * span_len
        + (height_pos[:, None] - height_pos[None, :] + side_len - 1) * span_len
        + (width_pos[:, None] - width_pos[None, :] + side_len - 1)
    )


def to_windows(values, side_t, side_len):
    tail_shape = values.shape[1:]
    frames = values.shape[0] // (FH * FW)
    shaped = values.reshape(
        (frames // side_t, side_t, FH // side_len, side_len, FW // side_len, side_len) + tail_shape
    )
    axis_order = (0, 2, 4, 1, 3, 5) + tuple(range(6, 6 + len(tail_shape)))
    shaped = shaped.transpose(axis_order)
    return shaped.reshape((-1, side_t * side_len * side_len) + tail_shape)


def from_windows(values, side_t, side_len):
    tail_shape = values.shape[2:]
    blocks_high = FH // side_len
    blocks_wide = FW // side_len
    frame_groups = values.shape[0] // (blocks_high * blocks_wide)
    shaped = values.reshape(
        (frame_groups, blocks_high, blocks_wide, side_t, side_len, side_len) + tail_shape
    )
    axis_order = (0, 3, 1, 4, 2, 5) + tuple(range(6, 6 + len(tail_shape)))
    return shaped.transpose(axis_order).reshape((frame_groups * side_t * FH * FW,) + tail_shape)


def on_device(
    tokens, d_out, modulation, frame_counts, w_qkv, w_out, w_up, w_down, table_s, table_t
):
    local_rows = tokens.shape[0]
    clip_len = PADF * FH * FW
    group_clips = modulation.shape[0]
    group_rows = group_clips * clip_len
    scale_dot = HD ** (-0.5)
    my_index = lax.axis_index("head")
    first_row = my_index * local_rows
    row_ids = first_row + jnp.arange(local_rows, dtype=jnp.int32)
    clip_slots = jnp.arange(group_clips, dtype=jnp.int32)
    row_onehot = ((row_ids // clip_len)[:, None] == clip_slots[None, :]).astype(jnp.float32)
    count_float = frame_counts.astype(jnp.float32)
    row_frames = jnp.dot(row_onehot, count_float, precision=HIGHEST_PRECISION)
    row_keep = ((row_ids % clip_len // (FH * FW)).astype(jnp.float32) < row_frames).astype(
        jnp.float32
    )[:, None]
    group_ids = jnp.arange(group_rows, dtype=jnp.int32)
    group_onehot = ((group_ids // clip_len)[:, None] == clip_slots[None, :]).astype(jnp.float32)
    group_frames = jnp.dot(group_onehot, count_float, precision=HIGHEST_PRECISION)
    group_keep = (group_ids % clip_len // (FH * FW)).astype(jnp.float32) < group_frames

    def block_shape(block_id):
        if block_id == 0:
            return (1, SWIN)
        return (PADF, TWIN)

    def mod_row(slot):
        return jnp.dot(row_onehot, modulation[:, slot, :], precision=HIGHEST_PRECISION)

    def rows_in(values):
        return lax.all_gather(values, "head", axis=0, tiled=True)

    def grads_in(values):
        return lax.all_gather(values, "head", axis=0, tiled=True)

    def rows_out(full_rows, weight):
        return lax.psum_scatter(
            jnp.dot(full_rows, weight, preferred_element_type=jnp.float32).astype(jnp.bfloat16),
            "head",
            scatter_dimension=0,
            tiled=True,
        ).astype(jnp.float32)

    def grads_out(full_rows, weight, einsum_form):
        return lax.psum_scatter(
            jnp.einsum(einsum_form, full_rows, weight, preferred_element_type=jnp.float32).astype(
                jnp.bfloat16
            ),
            "head",
            scatter_dimension=0,
            tiled=True,
        ).astype(jnp.float32)

    def rows_keep(block_id):
        if block_id == 0:
            return None
        return to_windows(group_keep[:, None], PADF, TWIN)[:, :, 0]

    def shape_windows(projected, side_t, side_len):
        head_count = projected.shape[-1] // HD
        window_size = side_t * side_len * side_len
        windows = to_windows(projected, side_t, side_len)
        return windows.reshape(windows.shape[0], window_size, 3, head_count, HD)

    def shape_grad(grad_attended, side_t, side_len):
        head_count = grad_attended.shape[-1] // HD
        window_size = side_t * side_len * side_len
        windows = to_windows(grad_attended, side_t, side_len)
        return windows.reshape(windows.shape[0], window_size, head_count, HD)

    def flat_rows(windowed, side_t, side_len):
        return from_windows(windowed, side_t, side_len)

    def logits_of(queries, key_rows, table_arg, rel_index, keep_win):
        logits = (
            jnp.einsum("wqhe,wkhe->whqk", queries, key_rows, preferred_element_type=jnp.float32)
            * scale_dot
        )
        logits = logits + table_arg[:, rel_index][None]
        if keep_win is not None:
            logits = jnp.where(keep_win[:, None, None, :], logits, NEGATIVE)
        return logits

    def attend(windows, table_arg, rel_index, keep_win):
        logits = logits_of(windows[:, :, 0], windows[:, :, 1], table_arg, rel_index, keep_win)
        row_max = jnp.max(logits, axis=-1, keepdims=True)
        exponent = jnp.exp(logits - row_max)
        row_total = jnp.sum(exponent, axis=-1, keepdims=True)
        probs = exponent / row_total
        log_total = row_max + jnp.log(row_total)
        attended = jnp.einsum(
            "whqk,wkhe->wqhe",
            probs.astype(jnp.bfloat16),
            windows[:, :, 2],
            preferred_element_type=jnp.float32,
        )
        return (attended.reshape(attended.shape[0], attended.shape[1], -1), log_total)

    def attend_back(windows, grad_windows, log_total, table_arg, rel_index, keep_win):
        queries = windows[:, :, 0]
        key_rows = windows[:, :, 1]
        value_rows = windows[:, :, 2]
        logits = logits_of(queries, key_rows, table_arg, rel_index, keep_win)
        probs = jnp.exp(logits - log_total)
        grad_probs = jnp.einsum(
            "wqhe,wkhe->whqk", grad_windows, value_rows, preferred_element_type=jnp.float32
        )
        grad_values = jnp.einsum(
            "whqk,wqhe->wkhe",
            probs.astype(jnp.bfloat16),
            grad_windows,
            preferred_element_type=jnp.float32,
        )
        grad_logits = (
            probs * (grad_probs - jnp.sum(grad_probs * probs, axis=-1, keepdims=True))
        ).astype(jnp.bfloat16)
        head_count = queries.shape[2]
        table_terms = jnp.sum(grad_logits.astype(jnp.float32), axis=0).reshape(head_count, -1)
        grad_table = jax.ops.segment_sum(
            table_terms.T, rel_index.reshape(-1), num_segments=table_arg.shape[1]
        ).T
        grad_queries = (
            jnp.einsum("whqk,wkhe->wqhe", grad_logits, key_rows, preferred_element_type=jnp.float32)
            * scale_dot
        )
        grad_keys = (
            jnp.einsum("whqk,wqhe->wkhe", grad_logits, queries, preferred_element_type=jnp.float32)
            * scale_dot
        )
        grad_stack = jnp.stack([grad_queries, grad_keys, grad_values], axis=2)
        return (
            grad_stack.reshape(grad_stack.shape[0], grad_stack.shape[1], 3, head_count * HD),
            grad_table,
        )

    def forward_block(hidden, block_id):
        side_t, side_len = block_shape(block_id)
        table_local = table_s if block_id == 0 else table_t
        rel_index = window_index(side_t, side_len)
        normed = layer_norm(hidden, mod_row(6 * block_id), mod_row(6 * block_id + 1)).astype(
            jnp.bfloat16
        )
        plan = None
        normed_in = rows_in(normed)
        qkv_use, out_use, table_use = (w_qkv[block_id], w_out[block_id], table_local)
        keep_win = rows_keep(block_id)
        projected = jnp.einsum(
            "gd,cde->gce", normed_in, qkv_use, preferred_element_type=jnp.float32
        ).astype(jnp.bfloat16)
        windows = shape_windows(projected, side_t, side_len)
        attended_win, log_total = attend(windows, table_use, rel_index, keep_win)
        attended = flat_rows(attended_win, side_t, side_len).astype(jnp.bfloat16)
        branch = rows_out(attended, out_use)
        middle = hidden + mod_row(6 * block_id + 2) * branch
        shifted = layer_norm(middle, mod_row(6 * block_id + 3), mod_row(6 * block_id + 4)).astype(
            jnp.bfloat16
        )
        up_full, down_full = (
            lax.all_gather(w_up[block_id], "head", axis=1, tiled=True),
            lax.all_gather(w_down[block_id], "head", axis=0, tiled=True),
        )
        pre_gelu = jnp.dot(shifted, up_full, preferred_element_type=jnp.float32)
        activated = gelu_tanh(pre_gelu).astype(jnp.bfloat16)
        feed_out = jnp.dot(activated, down_full, preferred_element_type=jnp.float32)
        mlp_state = (shifted, pre_gelu, activated, up_full, down_full)
        result = middle + mod_row(6 * block_id + 5) * feed_out
        attn_state = (
            normed_in,
            projected,
            log_total,
            attended,
            qkv_use,
            out_use,
            table_use,
            keep_win,
            plan,
        )
        saved_state = (hidden, attn_state, branch, middle, feed_out, mlp_state)
        return (saved_state, result)

    def backward_block(saved_state, grad_result, block_id):
        hidden, attn_state, branch, middle, feed_out, mlp_state = saved_state
        normed_in, projected, log_total, attended, qkv_use, out_use, table_use, keep_win, plan = (
            attn_state
        )
        shifted_in, pre_gelu, activated, up_weight, down_weight = mlp_state
        side_t, side_len = block_shape(block_id)
        rel_index = window_index(side_t, side_len)
        grad_feed = (grad_result * mod_row(6 * block_id + 5)).astype(jnp.bfloat16)
        grad_gate_mlp = grad_result * feed_out
        grad_down = jnp.einsum(
            "gf,gd->fd", activated, grad_feed, preferred_element_type=jnp.float32
        )
        grad_activated = jnp.einsum(
            "gd,fd->gf", grad_feed, down_weight, preferred_element_type=jnp.float32
        )
        grad_pre = jax.vjp(gelu_tanh, pre_gelu)[1](grad_activated)[0].astype(jnp.bfloat16)
        grad_up = jnp.einsum("gd,gf->df", shifted_in, grad_pre, preferred_element_type=jnp.float32)
        grad_shifted = jnp.einsum(
            "gf,df->gd", grad_pre, up_weight, preferred_element_type=jnp.float32
        )
        grad_up, grad_down = (
            lax.psum_scatter(
                grad_up.astype(jnp.bfloat16), "head", scatter_dimension=1, tiled=True
            ).astype(jnp.float32),
            lax.psum_scatter(
                grad_down.astype(jnp.bfloat16), "head", scatter_dimension=0, tiled=True
            ).astype(jnp.float32),
        )
        unused_mid, pull_second = jax.vjp(
            layer_norm, middle, mod_row(6 * block_id + 3), mod_row(6 * block_id + 4)
        )
        grad_mid_norm, grad_shift_mlp, grad_scale_mlp = pull_second(grad_shifted)
        grad_middle = grad_result + grad_mid_norm
        grad_branch = (grad_middle * mod_row(6 * block_id + 2)).astype(jnp.bfloat16)
        grad_gate_att = grad_middle * branch
        branch_in = grads_in(grad_branch)
        grad_wout = jnp.einsum("ge,gd->ed", attended, branch_in, preferred_element_type=jnp.float32)
        grad_attended = jnp.einsum(
            "gd,ed->ge", branch_in, out_use, preferred_element_type=jnp.float32
        ).astype(jnp.bfloat16)
        windows = shape_windows(projected, side_t, side_len)
        grad_windows = shape_grad(grad_attended, side_t, side_len)
        grad_stack, grad_table = attend_back(
            windows, grad_windows, log_total, table_use, rel_index, keep_win
        )
        grad_projected = flat_rows(grad_stack, side_t, side_len).astype(jnp.bfloat16)
        grad_qkv = jnp.einsum(
            "gd,gce->cde", normed_in, grad_projected, preferred_element_type=jnp.float32
        )
        grad_normed = grads_out(grad_projected, qkv_use, "gce,cde->gd")
        unused_hid, pull_first = jax.vjp(
            layer_norm, hidden, mod_row(6 * block_id), mod_row(6 * block_id + 1)
        )
        grad_hid_norm, grad_shift_att, grad_scale_att = pull_first(grad_normed)
        grad_hidden = grad_middle + grad_hid_norm
        mod_terms = jnp.stack(
            [
                grad_shift_att,
                grad_scale_att,
                grad_gate_att,
                grad_shift_mlp,
                grad_scale_mlp,
                grad_gate_mlp,
            ],
            axis=1,
        )
        grad_mods = jnp.einsum("rc,rke->cke", row_onehot, mod_terms, precision=HIGHEST_PRECISION)
        return (grad_hidden, grad_mods, (grad_qkv, grad_wout, grad_up, grad_down, grad_table))

    hidden_first = tokens.astype(jnp.float32)
    saved_first, hidden_second = forward_block(hidden_first, 0)
    saved_second, hidden_last = forward_block(hidden_second, 1)
    output = (hidden_last * row_keep).astype(jnp.bfloat16)
    grad_second, mods_second, weights_second = backward_block(
        saved_second, d_out.astype(jnp.float32) * row_keep, 1
    )
    grad_first, mods_first, weights_first = backward_block(saved_first, grad_second, 0)
    grad_modulation = lax.psum(
        jnp.concatenate([mods_first, mods_second], axis=1).astype(jnp.bfloat16), "head"
    ).astype(jnp.float32)
    summed = (
        lax.psum(
            jnp.stack([weights_first[0], weights_second[0]]).astype(jnp.bfloat16), "clip"
        ).astype(jnp.float32),
        lax.psum(
            jnp.stack([weights_first[1], weights_second[1]]).astype(jnp.bfloat16), "clip"
        ).astype(jnp.float32),
        lax.psum(
            jnp.stack([weights_first[2], weights_second[2]]).astype(jnp.bfloat16), "clip"
        ).astype(jnp.float32),
        lax.psum(
            jnp.stack([weights_first[3], weights_second[3]]).astype(jnp.bfloat16), "clip"
        ).astype(jnp.float32),
        lax.psum(weights_first[4].astype(jnp.bfloat16), "clip").astype(jnp.float32),
        lax.psum(weights_second[4].astype(jnp.bfloat16), "clip").astype(jnp.float32),
    )
    return (
        output,
        grad_first,
        grad_modulation,
        summed[0],
        summed[1],
        summed[2],
        summed[3],
        summed[4],
        summed[5],
    )


def solution(mesh):
    return jax.shard_map(
        on_device,
        mesh=mesh,
        in_specs=(
            P(("clip", "head"), None),
            P(("clip", "head"), None),
            P("clip", None, None),
            P("clip"),
            P(None, None, None, "head"),
            P(None, "head", None),
            P(None, None, "head"),
            P(None, "head", None),
            P("head", None),
            P("head", None),
        ),
        out_specs=(
            P(("clip", "head"), None),
            P(("clip", "head"), None),
            P("clip", None, None),
            P(None, None, None, "head"),
            P(None, "head", None),
            P(None, None, "head"),
            P(None, "head", None),
            P("head", None),
            P("head", None),
        ),
        check_vma=False,
    )
```

profile of v0, /device:TPU:0, one launch (start us, length us, event | category | flops | bytes accessed | tf_op | source)
XLA Modules:
  0.0 4494.6 jit_solution(16337818062129815433)
XLA Ops:
  18.4 217.4 %gather_fusion = f32[65536,4]{1,0:T(8,128)} fusion(f32[4,961]{0,1:T(8,128)S(1)} %copy.209, s32[65536]{0:T(1024)S(1)} %broadcast_clamp_fusion.1), kind=kCustom, calls=%fused_computation | custom fusion | bytes 2359296 | tf_op jit(solution)/shard_map/gather | solution.py:147
  235.8 19.8 copy.210
  276.7 23.1 reshape_reshape.8
  406.0 171.0 %reduce-scatter.9.cloned.1.call-done = bf16[1280,1024]{1,0:T(8,128)(2,1)} async-done(((bf16[5120,1024]{1,0:T(8,128)(2,1)}), bf16[1280,1024]{1,0:T(8,128)(2,1)}) %reduce-scatter.9.cloned.1.call-update) | async-done | bytes 2621456 | tf_op jit(solution)/shard_map/reduce_scatter | solution.py:105
  582.8 147.1 %all-gather.21.cloned.1.call-done = bf16[1,1024,4096]{2,1,0:T(8,128)(2,1)} async-done(((bf16[1,1024,1024]{2,1,0:T(8,128)(2,1)}), bf16[1,1024,4096]{2,1,0:T(8,128)(2,1)}) %all-gather.21.cloned.1.call-update) | async-done | bytes 8388624 | tf_op jit(solution)/shard_map/all_gather | solution.py:227
  729.8 20.5 fusion.58
  750.3 129.3 %all-gather.23.cloned.1.call-done = bf16[1,4096,1024]{2,1,0:T(8,128)(2,1)} async-done(((bf16[1,1024,1024]{2,1,0:T(8,128)(2,1)}), bf16[1,4096,1024]{2,1,0:T(8,128)(2,1)}) %all-gather.23.cloned.1.call-update) | async-done | bytes 8388624 | tf_op jit(solution)/shard_map/all_gather | solution.py:228
  879.7 23.1 fusion.208
  912.8 339.0 %gather_fusion.1 = f32[102400,4]{1,0:T(8,128)} fusion(f32[4,2025]{0,1:T(8,128)S(1)} %copy.220, s32[102400]{0:T(1024)S(1)} %broadcast_clamp_fusion), kind=kCustom, calls=%fused_computation.1 | custom fusion | bytes 3686400 | tf_op jit(solution)/shard_map/gather | solution.py:147
  1251.7 33.2 copy.221
  1300.8 23.1 reshape_reshape.9
  1437.3 174.6 %reduce-scatter.11.cloned.1.call-done = bf16[1280,1024]{1,0:T(8,128)(2,1)} async-done(((bf16[5120,1024]{1,0:T(8,128)(2,1)}), bf16[1280,1024]{1,0:T(8,128)(2,1)}) %reduce-scatter.11.cloned.1.call-update) | async-done | bytes 2621456 | tf_op jit(solution)/shard_map/reduce_scatter | solution.py:105
  1619.4 144.8 %all-gather.25.cloned.1.call-done = bf16[1,1024,4096]{2,1,0:T(8,128)(2,1)} async-done(((bf16[1,1024,1024]{2,1,0:T(8,128)(2,1)}), bf16[1,1024,4096]{2,1,0:T(8,128)(2,1)}) %all-gather.25.cloned.1.call-update) | async-done | bytes 8388624 | tf_op jit(solution)/shard_map/all_gather | solution.py:227
  1764.2 20.0 fusion.48
  1784.3 129.9 %all-gather.27.cloned.1.call-done = bf16[1,4096,1024]{2,1,0:T(8,128)(2,1)} async-done(((bf16[1,1024,1024]{2,1,0:T(8,128)(2,1)}), bf16[1,4096,1024]{2,1,0:T(8,128)(2,1)}) %all-gather.27.cloned.1.call-update) | async-done | bytes 8388624 | tf_op jit(solution)/shard_map/all_gather | solution.py:228
  1914.2 29.8 fusion.15
  1962.3 25.5 fusion.205
  1992.6 182.2 %all-gather.17.cloned.1.call-done = bf16[5120,1024]{1,0:T(8,128)(2,1)} async-done(((bf16[1280,1024]{1,0:T(8,128)(2,1)}), bf16[5120,1024]{1,0:T(8,128)(2,1)}) %all-gather.17.cloned.1.call-update) | async-done | bytes 10485776 | tf_op jit(solution)/shard_map/all_gather | solution.py:102
  2208.4 26.3 multiply_reduce_fusion
  2234.8 27.6 convert_reduce_fusion
  2350.1 176.3 %reduce-scatter.13.cloned.1.call-done = bf16[1280,1024]{1,0:T(8,128)(2,1)} async-done(((bf16[5120,1024]{1,0:T(8,128)(2,1)}), bf16[1280,1024]{1,0:T(8,128)(2,1)}) %reduce-scatter.13.cloned.1.call-update) | async-done | bytes 2621456 | tf_op jit(solution)/shard_map/reduce_scatter | solution.py:113
  2538.8 30.2 fusion.8
  2638.5 23.0 convolution_convert_fusion.2
  2661.5 24.0 convolution_convert_fusion.3
  2709.0 73.8 %all-gather.19.cloned.1.call-done = bf16[5120,1024]{1,0:T(8,128)(2,1)} async-done(((bf16[1280,1024]{1,0:T(8,128)(2,1)}), bf16[5120,1024]{1,0:T(8,128)(2,1)}) %all-gather.19.cloned.1.call-update) | async-done | bytes 10485776 | tf_op jit(solution)/shard_map/all_gather | solution.py:102
  2941.5 134.9 %reduce-scatter.17.cloned.1.call-done = bf16[1024,1024]{1,0:T(8,128)(2,1)} async-done(((bf16[1024,4096]{1,0:T(8,128)(2,1)}), bf16[1024,1024]{1,0:T(8,128)(2,1)}) %reduce-scatter.17.cloned.1.call-update) | async-done | bytes 2097168 | tf_op jit(solution)/shard_map/reduce_scatter | solution.py:271
  3081.1 142.8 %reduce-scatter.23.cloned.1.call-done = bf16[1024,1024]{1,0:T(8,128)(2,1)} async-done(((bf16[4096,1024]{1,0:T(8,128)(2,1)}), bf16[1024,1024]{1,0:T(8,128)(2,1)}) %reduce-scatter.23.cloned.1.call-update) | async-done | bytes 2097168 | tf_op jit(solution)/shard_map/reduce_scatter | solution.py:274
  3223.9 147.4 %reduce-scatter.21.cloned.1.call-done = bf16[1024,1024]{1,0:T(8,128)(2,1)} async-done(((bf16[4096,1024]{1,0:T(8,128)(2,1)}), bf16[1024,1024]{1,0:T(8,128)(2,1)}) %reduce-scatter.21.cloned.1.call-update) | async-done | bytes 2097168 | tf_op jit(solution)/shard_map/reduce_scatter | solution.py:274
  3398.3 24.2 copy.257
  3422.4 542.8 %scatter_custom_fusion.1 = f32[2025,4]{1,0:T(8,128)S(1)} fusion(s32[102400]{0:T(1024)S(1)} %reshape.1031, f32[102400,4]{1,0:T(8,128)} %copy.257, f32[]{:T(128)} %constant.246.clone.1), kind=kCustom, calls=%fused_computation.223 | custom fusion | flops 409600 | bytes 32912 | tf_op jit(solution)/shard_map/scatter-add | solution.py:187
  4020.8 347.6 %scatter_custom_fusion = f32[961,4]{1,0:T(8,128)S(1)} fusion(s32[65536]{0:T(1024)S(1)} %bitcast.383, f32[65536,4]{1,0:T(8,128)} %copy.255, f32[]{:T(128)} %constant.246.clone.1), kind=kCustom, calls=%fused_computation.233 | custom fusion | flops 262144 | bytes 15888 | tf_op jit(solution)/shard_map/scatter-add | solution.py:187
  4368.4 31.3 all-reduce
  (499 shorter events, 872.2 us)
Async XLA Ops:
  7.2 248.4 %all-gather.13.cloned.1.call-start = ((), (), s32[]{:S(2)}) async-start(), calls=%async_computation.8 | async-start | bytes 13107200 | tf_op jit(solution)/shard_map/all_gather | solution.py:99
  7.3 899.5 %copy-start.36 = (f32[1280]{0:T(1024)}, f32[1280]{0:T(1024)S(1)}, u32[]{:S(2)}) copy-start(f32[1280]{0:T(1024)S(1)} %fusion.187) | copy-start | bytes 15364
  12.9 717.0 %copy-start.103 = (f32[1,1,1024]{2,0,1:T(1,128)}, f32[1,1,1024]{2,0,1:T(1,128)S(1)}, u32[]{:S(2)}) copy-start(f32[1,1,1024]{2,0,1:T(1,128)S(1)} %get-tuple-element.92) | copy-start | bytes 12292
  12.9 717.0 %copy-start.111 = (f32[1,1,1024]{2,0,1:T(1,128)}, f32[1,1,1024]{2,0,1:T(1,128)S(1)}, u32[]{:S(2)}) copy-start(f32[1,1,1024]{2,0,1:T(1,128)S(1)} %get-tuple-element.91) | copy-start | bytes 12292
  12.9 866.8 %copy-start.57 = (f32[1,1,1024]{2,0,1:T(1,128)}, f32[1,1,1024]{2,0,1:T(1,128)S(1)}, u32[]{:S(2)}) copy-start(f32[1,1,1024]{2,0,1:T(1,128)S(1)} %get-tuple-element.96) | copy-start | bytes 12292
  12.9 866.8 %copy-start.107 = (f32[1,1,1024]{2,0,1:T(1,128)}, f32[1,1,1024]{2,0,1:T(1,128)S(1)}, u32[]{:S(2)}) copy-start(f32[1,1,1024]{2,0,1:T(1,128)S(1)} %get-tuple-element.93) | copy-start | bytes 12292
  15.7 561.3 %reduce-scatter.9.cloned.1.call-start = ((), (), s32[]{:S(2)}) async-start(), calls=%async_computation.9 | async-start | bytes 13107200 | tf_op jit(solution)/shard_map/reduce_scatter | solution.py:105
  396.1 333.7 %all-gather.21.cloned.1.call-start = ((), (), s32[]{:S(2)}) async-start(), calls=%async_computation.20 | async-start | bytes 10485760 | tf_op jit(solution)/shard_map/all_gather | solution.py:227
  400.9 478.8 %all-gather.23.cloned.1.call-start = ((), (), s32[]{:S(2)}) async-start(), calls=%async_computation.21 | async-start | bytes 10485760 | tf_op jit(solution)/shard_map/all_gather | solution.py:228
  405.9 879.0 %all-gather.15.cloned.1.call-start = ((), (), s32[]{:S(2)}) async-start(), calls=%async_computation.10 | async-start | bytes 13107200 | tf_op jit(solution)/shard_map/all_gather | solution.py:99
  910.0 702.0 %reduce-scatter.11.cloned.1.call-start = ((), (), s32[]{:S(2)}) async-start(), calls=%async_computation.11 | async-start | bytes 13107200 | tf_op jit(solution)/shard_map/reduce_scatter | solution.py:105
  1435.5 176.4 %copy-start.92 = (f32[1,1,1024]{2,0,1:T(1,128)S(1)}, f32[1,1,1024]{2,0,1:T(1,128)}, u32[]{:S(2)}) copy-start(f32[1,1,1024]{2,0,1:T(1,128)} %get-tuple-element.90) | copy-start | bytes 12292
  1435.6 328.7 %all-gather.25.cloned.1.call-start = ((), (), s32[]{:S(2)}) async-start(), calls=%async_computation.22 | async-start | bytes 10485760 | tf_op jit(solution)/shard_map/all_gather | solution.py:227
  1436.3 477.9 %all-gather.27.cloned.1.call-start = ((), (), s32[]{:S(2)}) async-start(), calls=%async_computation.23 | async-start | bytes 10485760 | tf_op jit(solution)/shard_map/all_gather | solution.py:228
  1437.1 737.8 %all-gather.17.cloned.1.call-start = ((), (), s32[]{:S(2)}) async-start(), calls=%async_computation.12 | async-start | bytes 13107200 | tf_op jit(solution)/shard_map/all_gather | solution.py:102
  1437.3 550.5 %copy-start.54 = (f32[1280]{0:T(1024)}, f32[1280]{0:T(1024)S(1)}, u32[]{:S(2)}) copy-start(f32[1280]{0:T(1024)S(1)} %fusion.182) | copy-start | bytes 15364
  1616.4 345.9 %copy-start.74 = (f32[1280]{0:T(1024)}, f32[1280]{0:T(1024)S(1)}, u32[]{:S(2)}) copy-start(f32[1280]{0:T(1024)S(1)} %broadcast_multiply_fusion) | copy-start | bytes 15364
  1619.4 342.9 %copy-start.93 = (f32[1280]{0:T(1024)}, f32[1280]{0:T(1024)S(1)}, u32[]{:S(2)}) copy-start(f32[1280]{0:T(1024)S(1)} %fusion.186) | copy-start | bytes 15364
  1764.2 179.8 %slice-start.4 = ((s8[5242880]{0:T(1024)(128)(4,1)}), s8[1048576]{0:T(1024)(128)(4,1)S(1)}, s32[]{:S(2)}) async-start(s8[5242880]{0:T(1024)(128)(4,1)} %bitcast.325), calls=%async_computation.29 | async-start | bytes 2097152
  1992.6 533.8 %reduce-scatter.13.cloned.1.call-start = ((), (), s32[]{:S(2)}) async-start(), calls=%async_computation.13 | async-start | bytes 13107200 | tf_op jit(solution)/shard_map/reduce_scatter | solution.py:113
  2350.0 180.9 %copy-start.82 = (f32[1280]{0:T(1024)S(1)}, f32[1280]{0:T(1024)}, u32[]{:S(2)}) copy-start(f32[1280]{0:T(1024)} %copy-done.81) | copy-start | bytes 15364
  2350.0 181.0 %copy-start.67 = (f32[1280]{0:T(1024)S(1)}, f32[1280]{0:T(1024)}, u32[]{:S(2)}) copy-start(f32[1280]{0:T(1024)} %copy-done.66) | copy-start | bytes 15364
  2350.0 432.9 %all-gather.19.cloned.1.call-start = ((), (), s32[]{:S(2)}) async-start(), calls=%async_computation.14 | async-start | bytes 13107200 | tf_op jit(solution)/shard_map/all_gather | solution.py:102
  2597.7 343.8 %reduce-scatter.19.cloned.1.call-start = ((), (), s32[]{:S(2)}) async-start(), calls=%async_computation.17 | async-start | bytes 10485760 | tf_op jit(solution)/shard_map/reduce_scatter | solution.py:271
  2616.6 459.9 %reduce-scatter.17.cloned.1.call-start = ((), (), s32[]{:S(2)}) async-start(), calls=%async_computation.16 | async-start | bytes 10485760 | tf_op jit(solution)/shard_map/reduce_scatter | solution.py:271
  2636.8 587.2 %reduce-scatter.23.cloned.1.call-start = ((), (), s32[]{:S(2)}) async-start(), calls=%async_computation.19 | async-start | bytes 10485760 | tf_op jit(solution)/shard_map/reduce_scatter | solution.py:274
  2661.5 709.9 %reduce-scatter.21.cloned.1.call-start = ((), (), s32[]{:S(2)}) async-start(), calls=%async_computation.18 | async-start | bytes 10485760 | tf_op jit(solution)/shard_map/reduce_scatter | solution.py:274
  2685.5 1715.8 %all-reduce.4.cloned.1.call-start = ((), (), s32[]{:S(2)}) async-start(), calls=%async_computation.24 | async-start | bytes 25165824 | tf_op jit(solution)/shard_map/psum | solution.py:331
  3376.0 1043.0 %reduce-scatter.15.cloned.1.call-start = ((), (), s32[]{:S(2)}) async-start(), calls=%async_computation.15 | async-start | bytes 13107200 | tf_op jit(solution)/shard_map/reduce_scatter | solution.py:113
  3422.4 548.2 %slice-start = ((s8[5242880]{0:T(1024)(128)(4,1)}), s8[1048576]{0:T(1024)(128)(4,1)S(1)}, s32[]{:S(2)}) async-start(s8[5242880]{0:T(1024)(128)(4,1)} %bitcast.320), calls=%async_computation.25 | async-start | bytes 2097152
  3422.4 548.2 %copy-start.51 = (f32[1280]{0:T(1024)S(1)}, f32[1280]{0:T(1024)}, u32[]{:S(2)}) copy-start(f32[1280]{0:T(1024)} %copy-done.49) | copy-start | bytes 15364
  3422.4 548.2 %copy-start.68 = (f32[1280]{0:T(1024)S(1)}, f32[1280]{0:T(1024)}, u32[]{:S(2)}) copy-start(f32[1280]{0:T(1024)} %copy-done.66) | copy-start | bytes 15364
  (125 other events, 2385.0 us)
Sparse Core Ops, SparseCore 0:
  15.8 186.6 all-gather.12
  396.2 180.6 reduce-scatter.8
  579.1 150.6 all-gather.20
  731.8 147.8 all-gather.22
  910.1 182.1 all-gather.14
  1435.7 176.2 reduce-scatter.10
  1613.5 150.6 all-gather.24
  1766.4 147.8 all-gather.26
  1992.7 182.1 all-gather.16
  2350.1 176.1 reduce-scatter.12
  2597.8 184.9 all-gather.18
  2785.6 142.6 reduce-scatter.18
  2931.3 145.1 reduce-scatter.16
  3078.7 145.1 reduce-scatter.22
  3226.1 145.1 reduce-scatter.20
  3376.1 174.1 all-reduce.3
  3552.6 178.0 reduce-scatter.14
where the time goes:
time: 4500 us; the launch traced here: 4490 us
  waiting for transfers between devices  1760 us (39%)
  other arithmetic  1090 us (24%)
  local copies, waits for them, and re-layouts  1000 us (22%)
  matrix products  572 us (13%)
  blocking collectives  50.6 us (1%)
    scatter-add x2, other arithmetic, attend_back(): jax.ops.segment_sum(table_terms.T, rel_index.reshape(-1), num_segments=ta...  890 us
    gather x4, local copies, waits for them, and re-layouts, logits_of(): logits = logits + table_arg[:, rel_index][None]  609 us
    reduce_scatter x2, waiting for transfers between devices, rows_out(): lax.psum_scatter(jnp.dot(full_rows, weight, preferred_element_type=jnp.fl...  346 us
    all_gather x2, waiting for transfers between devices, forward_block(): lax.all_gather(w_up[block_id], 'head', axis=1, tiled=True)  292 us
    reduce_scatter x2, waiting for transfers between devices, backward_block(): lax.psum_scatter(grad_down.astype(jnp.bfloat16), 'head', scatter_dimensio...  290 us
    all_gather x2, waiting for transfers between devices, forward_block(): lax.all_gather(w_down[block_id], 'head', axis=0, tiled=True)  259 us
    all_gather x2, waiting for transfers between devices, grads_in(): return lax.all_gather(values, 'head', axis=0, tiled=True)  256 us
    reduce_scatter x2, waiting for transfers between devices, grads_out(): lax.psum_scatter(jnp.einsum(einsum_form, full_rows, weight, preferred_ele...  176 us
  transfers between devices with their start and end apart: 17, of which 12 were waited for; matrix products, arithmetic and copies ran while one was open for 43% of the time, Pallas kernels for 0%

commit v1 on v0

--- a/solution.py
+++ b/solution.py
@@ -1,6 +1,8 @@
 import jax
 import jax.numpy as jnp
 from jax import lax
+from jax.experimental import pallas as pl
+from jax.experimental.pallas import tpu as pltpu
 from jax.sharding import PartitionSpec as P
 
 HD = 64
@@ -356,9 +358,954 @@
     )
 
 
+F32 = jnp.float32
+BF16 = jnp.bfloat16
+VMEM_LIMIT = 58 * 1024 * 1024
+NZ = 4
+D = 1024
+HPZ = 4
+CONST = pl.Buffered(1)
+
+
+def dot_nn(a, b):
+    return lax.dot_general(a, b, (((1,), (0,)), ((), ())), preferred_element_type=F32)
+
+
+def dot_nt(a, b):
+    return lax.dot_general(a, b, (((1,), (1,)), ((), ())), preferred_element_type=F32)
+
+
+def dot_tn(a, b):
+    return lax.dot_general(a, b, (((0,), (0,)), ((), ())), preferred_element_type=F32)
+
+
+def call(kernel, name, grid, in_specs, out_specs, out_shape, scratch, flops, nbytes):
+    return pl.pallas_call(
+        kernel,
+        name=name,
+        grid=grid,
+        in_specs=in_specs,
+        out_specs=out_specs,
+        out_shape=out_shape,
+        scratch_shapes=scratch,
+        compiler_params=pltpu.CompilerParams(
+            dimension_semantics=("arbitrary",) * len(grid), vmem_limit_bytes=VMEM_LIMIT
+        ),
+        cost_estimate=pl.CostEstimate(flops=flops, bytes_accessed=nbytes, transcendentals=0),
+    )
+
+
+def full(shape):
+    return pl.BlockSpec(shape, lambda *ids: (0,) * len(shape), pipeline_mode=CONST)
+
+
+def chunk_rows(i, size):
+    return pl.ds(pl.multiple_of(i * size, size), size)
+
+
+def ln_stats(x):
+    mean = jnp.mean(x, axis=-1, keepdims=True)
+    centred = x - mean
+    rstd = lax.rsqrt(jnp.mean(centred * centred, axis=-1, keepdims=True) + EPS)
+    return centred * rstd, rstd
+
+
+def ln_back(grad, hat, rstd, scale):
+    gh = grad * (1.0 + scale)
+    m1 = jnp.mean(gh, axis=-1, keepdims=True)
+    m2 = jnp.mean(gh * hat, axis=-1, keepdims=True)
+    return rstd * (gh - m1 - hat * m2)
+
+
+def piece_specs(k, row, count):
+    tail = (count, D)
+    return [
+        pl.BlockSpec((2, 4) + tail, lambda d: (0, 0, row, 0), pipeline_mode=CONST),
+        pl.BlockSpec((4, 1) + tail, lambda d: (0, jnp.maximum(d - 1, 0), row, 0)),
+        pl.BlockSpec((4, 1) + tail, lambda d: (0, jnp.maximum(d - 1, 0), row, 0)),
+    ]
+
+
+def by_offset(d, body, local_ref, own_ref, other_ref):
+    @pl.when(d == 0)
+    def _():
+        body(lambda m, r, n: local_ref[0, m, r : r + n, :], lambda m, r, n: local_ref[1, m, r : r + n, :])
+
+    @pl.when(d > 0)
+    def _():
+        body(lambda m, r, n: own_ref[m, 0, r : r + n, :], lambda m, r, n: other_ref[m, 0, r : r + n, :])
+
+
+def head_rows(own, other, row):
+    parts = []
+    for m in range(4):
+        parts += [own(m, row, 32), other(m, row, 32)]
+    return jnp.concatenate(parts, axis=0)
+
+
+def unit_rows(get, row, count):
+    return jnp.concatenate([get(m, row, count) for m in range(4)], axis=0)
+
+
+def ln_qkv(hidden, mods, weights, base):
+    rows = hidden.shape[0]
+    step = 256
+
+    def kernel(h_ref, m_ref, l_ref, w_ref, v_ref, normed_ref, qkv_ref):
+        d = pl.program_id(0)
+
+        @pl.when(d == 0)
+        def _():
+            def body(i, carry):
+                sl = chunk_rows(i, step)
+                hat, _ = ln_stats(h_ref[sl, :].astype(F32))
+                normed_ref[sl, :] = (
+                    hat * (1.0 + m_ref[base + 1 : base + 2, :]) + m_ref[base : base + 1, :]
+                ).astype(BF16)
+                return carry
+
+            lax.fori_loop(0, rows // step, body, 0)
+
+        def work(own, other):
+            for t in range(3):
+                qkv_ref[:, t * 256 : (t + 1) * 256] = dot_nt(
+                    normed_ref[...], head_rows(own, other, t * 32)
+                ).astype(BF16)
+
+        by_offset(d, work, l_ref, w_ref, v_ref)
+
+    return call(
+        kernel,
+        "ln_qkv",
+        (NZ,),
+        [full((rows, D)), full((12, D))] + piece_specs(128, 0, 96),
+        [full((rows, D)), pl.BlockSpec((rows, 768), lambda z: (0, z))],
+        [jax.ShapeDtypeStruct((rows, D), BF16), jax.ShapeDtypeStruct((rows, 3 * D), BF16)],
+        [],
+        2 * rows * D * 3 * D,
+        rows * D * 12 + 6 * D * D,
+    )(hidden, mods, *weights)
+
+
+def build_bias(base_ref, bias_ref, fc_ref, slides, width, lanes_step):
+    rows_step = width // slides
+    for h in range(HPZ):
+        for s in range(slides):
+            off = (slides - 1 - s) * lanes_step
+            tile = base_ref[h, :, off : off + width]
+            if fc_ref is not None:
+                tile = jnp.where(s < fc_ref[0], tile, NEGATIVE)
+            bias_ref[h, s * rows_step : (s + 1) * rows_step, :] = tile
+
+
+def attn_fwd(qkv, base, fc, slides, width, lanes_step, masked):
+    rows = qkv.shape[0]
+    windows = rows // width
+    r_step, lanes = base.shape[1], base.shape[2]
+
+    def kernel(x_ref, b_ref, fc_ref, o_ref, bias_ref):
+        @pl.when(pl.program_id(1) == 0)
+        def _():
+            build_bias(b_ref, bias_ref, fc_ref if masked else None, slides, width, lanes_step)
+
+        for h in range(HPZ):
+            q = x_ref[:, h * HD : (h + 1) * HD] * 0.125
+            k = x_ref[:, 256 + h * HD : 256 + (h + 1) * HD]
+            v = x_ref[:, 512 + h * HD : 512 + (h + 1) * HD]
+            score = dot_nt(k, q) + bias_ref[h]
+            expo = jnp.exp(score - jnp.max(score, axis=0, keepdims=True))
+            inv = 1.0 / jnp.sum(expo, axis=0, keepdims=True)
+            probs = (expo * inv).astype(BF16)
+            o_ref[:, h * HD : (h + 1) * HD] = dot_tn(probs, v).astype(BF16)
+
+    return call(
+        kernel,
+        "attn_fwd",
+        (NZ, windows),
+        [
+            pl.BlockSpec((width, 768), lambda z, w: (w, z)),
+            pl.BlockSpec((HPZ, r_step, lanes), lambda z, w: (z, 0, 0)),
+            pl.BlockSpec(memory_space=pltpu.SMEM),
+        ],
+        pl.BlockSpec((width, 256), lambda z, w: (w, z)),
+        jax.ShapeDtypeStruct((rows, D), BF16),
+        [pltpu.VMEM((HPZ, width, width), F32)],
+        windows * 16 * width * width * HD * 16,
+        rows * D * 8,
+    )(qkv, base, fc)
+
+
+def attn_bwd(qkv, grad_att, base, fc, slides, width, lanes_step, masked):
+    rows = qkv.shape[0]
+    windows = rows // width
+    r_step, lanes = base.shape[1], base.shape[2]
+
+    def kernel(x_ref, d_ref, b_ref, fc_ref, o_ref, gb_ref, bias_ref, acc_ref):
+        @pl.when(pl.program_id(1) == 0)
+        def _():
+            build_bias(b_ref, bias_ref, fc_ref if masked else None, slides, width, lanes_step)
+            acc_ref[...] = jnp.zeros_like(acc_ref)
+
+        for h in range(HPZ):
+            q = x_ref[:, h * HD : (h + 1) * HD] * 0.125
+            k = x_ref[:, 256 + h * HD : 256 + (h + 1) * HD]
+            v = x_ref[:, 512 + h * HD : 512 + (h + 1) * HD]
+            da = d_ref[:, h * HD : (h + 1) * HD]
+            score = dot_nt(k, q) + bias_ref[h]
+            expo = jnp.exp(score - jnp.max(score, axis=0, keepdims=True))
+            inv = 1.0 / jnp.sum(expo, axis=0, keepdims=True)
+            probs = expo * inv
+            dp = dot_nt(v, da)
+            row = jnp.sum(dp * probs, axis=0, keepdims=True)
+            dl = (probs * (dp - row)).astype(BF16)
+            acc_ref[h] += dl.astype(F32)
+            o_ref[:, h * HD : (h + 1) * HD] = (dot_tn(dl, k) * 0.125).astype(BF16)
+            o_ref[:, 256 + h * HD : 256 + (h + 1) * HD] = dot_nn(dl, q).astype(BF16)
+            o_ref[:, 512 + h * HD : 512 + (h + 1) * HD] = dot_nn(probs.astype(BF16), da).astype(
+                BF16
+            )
+
+        @pl.when(pl.program_id(1) == windows - 1)
+        def _():
+            gb_ref[...] = jnp.zeros_like(gb_ref)
+            for h in range(HPZ):
+                for s in range(slides):
+                    off = (slides - 1 - s) * lanes_step
+                    gb_ref[h, :, off : off + width] += acc_ref[h, s * r_step : (s + 1) * r_step, :]
+
+    return call(
+        kernel,
+        "attn_bwd",
+        (NZ, windows),
+        [
+            pl.BlockSpec((width, 768), lambda z, w: (w, z)),
+            pl.BlockSpec((width, 256), lambda z, w: (w, z)),
+            pl.BlockSpec((HPZ, r_step, lanes), lambda z, w: (z, 0, 0)),
+            pl.BlockSpec(memory_space=pltpu.SMEM),
+        ],
+        [
+            pl.BlockSpec((width, 768), lambda z, w: (w, z)),
+            pl.BlockSpec((HPZ, r_step, lanes), lambda z, w: (z, 0, 0)),
+        ],
+        [
+            jax.ShapeDtypeStruct((rows, 3 * D), BF16),
+            jax.ShapeDtypeStruct(base.shape, F32),
+        ],
+        [pltpu.VMEM((HPZ, width, width), F32), pltpu.VMEM((HPZ, width, width), F32)],
+        windows * 16 * width * width * HD * 40,
+        rows * D * 16,
+    )(qkv, grad_att, base, fc)
+
+
+def out_specs_of(row_block):
+    return [
+        pl.BlockSpec((2, 4, 32, D), lambda i: (0, 0, row_block, 0), pipeline_mode=CONST),
+        pl.BlockSpec((4, 3, 32, D), lambda i: (0, 0, row_block, 0), pipeline_mode=CONST),
+        pl.BlockSpec((4, 3, 32, D), lambda i: (0, 0, row_block, 0), pipeline_mode=CONST),
+    ]
+
+
+def out_rows(d, l_ref, w_ref, v_ref):
+    if d == 0:
+        return head_rows(
+            lambda m, r, n: l_ref[0, m, :, :], lambda m, r, n: l_ref[1, m, :, :], 0
+        )
+    return head_rows(
+        lambda m, r, n: w_ref[m, d - 1, :, :], lambda m, r, n: v_ref[m, d - 1, :, :], 0
+    )
+
+
+def out_proj(attended, weights, hidden, mods, base):
+    rows = attended.shape[0]
+    step = 256
+
+    def kernel(a_ref, l_ref, w_ref, v_ref, h_ref, m_ref, br_ref, mid_ref, sh_ref):
+        branch = jnp.zeros((step, D), F32)
+        for d in range(NZ):
+            branch += dot_nn(a_ref[:, d * 256 : (d + 1) * 256], out_rows(d, l_ref, w_ref, v_ref))
+        br_ref[...] = branch.astype(BF16)
+        middle = h_ref[...].astype(F32) + m_ref[base + 2 : base + 3, :] * branch
+        mid_ref[...] = middle
+        hat, _ = ln_stats(middle)
+        sh_ref[...] = (
+            hat * (1.0 + m_ref[base + 4 : base + 5, :]) + m_ref[base + 3 : base + 4, :]
+        ).astype(BF16)
+
+    tile = pl.BlockSpec((step, D), lambda i: (i, 0))
+    return call(
+        kernel,
+        "out_proj",
+        (rows // step,),
+        [tile] + out_specs_of(3) + [tile, full((12, D))],
+        [tile, tile, tile],
+        [
+            jax.ShapeDtypeStruct((rows, D), BF16),
+            jax.ShapeDtypeStruct((rows, D), F32),
+            jax.ShapeDtypeStruct((rows, D), BF16),
+        ],
+        [],
+        2 * rows * D * D,
+        rows * D * 14 + 2 * D * D,
+    )(attended, *weights, hidden, mods)
+
+
+GELU_C = 0.7978845608028654
+GELU_A = 0.044715
+
+
+def gelu_of(x):
+    return 0.5 * x * (1.0 + jnp.tanh(GELU_C * (x + GELU_A * x * x * x)))
+
+
+def gelu_both(x):
+    x2 = x * x
+    th = jnp.tanh(GELU_C * (x + GELU_A * x * x2))
+    half = 0.5 * (1.0 + th)
+    slope = half + 0.5 * x * (1.0 - th * th) * (GELU_C * (1.0 + 3.0 * GELU_A * x2))
+    return x * half, slope
+
+
+def ffn_fwd(shifted, weights, middle, mods, base):
+    rows = shifted.shape[0]
+    step = 256
+
+    def kernel(x_ref, l_ref, w_ref, v_ref, mid_ref, m_ref, pre_ref, feed_ref, nx_ref, acc_ref):
+        z = pl.program_id(0)
+
+        def work(own, other):
+            halves = (own, other)
+
+            def body(i, carry):
+                sl = chunk_rows(i, step)
+                part = jnp.zeros((step, D), F32)
+                for j, get in enumerate(halves):
+                    pre = dot_nt(x_ref[sl, :], unit_rows(get, 0, 128))
+                    pre_ref[sl, j * 512 : (j + 1) * 512] = pre.astype(BF16)
+                    part += dot_nn(gelu_of(pre).astype(BF16), unit_rows(get, 128, 128))
+
+                @pl.when(z == 0)
+                def _():
+                    acc_ref[sl, :] = part
+
+                @pl.when((z > 0) & (z < NZ - 1))
+                def _():
+                    acc_ref[sl, :] += part
+
+                @pl.when(z == NZ - 1)
+                def _():
+                    feed = acc_ref[sl, :] + part
+                    feed_ref[sl, :] = feed.astype(BF16)
+                    nx_ref[sl, :] = (
+                        mid_ref[sl, :] + m_ref[base + 5 : base + 6, :] * feed
+                    ).astype(BF16)
+
+                return carry
+
+            lax.fori_loop(0, rows // step, body, 0)
+
+        by_offset(z, work, l_ref, w_ref, v_ref)
+
+    return call(
+        kernel,
+        "ffn_fwd",
+        (NZ,),
+        [full((rows, D))] + piece_specs(256, 0, 256) + [full((rows, D)), full((12, D))],
+        [pl.BlockSpec((rows, D), lambda z: (0, z)), full((rows, D)), full((rows, D))],
+        [
+            jax.ShapeDtypeStruct((rows, 4 * D), BF16),
+            jax.ShapeDtypeStruct((rows, D), BF16),
+            jax.ShapeDtypeStruct((rows, D), BF16),
+        ],
+        [pltpu.VMEM((rows, D), F32)],
+        16 * rows * D * D,
+        rows * D * 20 + 16 * D * D,
+    )(shifted, *weights, middle, mods)
+
+
+def ffn_bwd(grad, pre, shifted, weights, mods, base):
+    rows = grad.shape[0]
+    step = 256
+
+    def kernel(
+        g_ref, p_ref, x_ref, l_ref, w_ref, v_ref, m_ref, keep_ref, send_ref, gs_ref, gf_ref, act_ref, gp_ref
+    ):
+        z = pl.program_id(0)
+
+        @pl.when(z == 0)
+        def _():
+            def body(i, carry):
+                sl = chunk_rows(i, step)
+                gf_ref[sl, :] = (
+                    g_ref[sl, :].astype(F32) * m_ref[base + 5 : base + 6, :]
+                ).astype(BF16)
+                gs_ref[sl, :] = jnp.zeros((step, D), F32)
+                return carry
+
+            lax.fori_loop(0, rows // step, body, 0)
+
+        def work(own, other):
+            halves = (own, other)
+
+            def body(i, carry):
+                sl = chunk_rows(i, step)
+                part = jnp.zeros((step, D), F32)
+                for j, get in enumerate(halves):
+                    cols = slice(j * 512, (j + 1) * 512)
+                    act, slope = gelu_both(p_ref[sl, cols].astype(F32))
+                    act_ref[sl, cols] = act.astype(BF16)
+                    gpre = (dot_nt(gf_ref[sl, :], unit_rows(get, 128, 128)) * slope).astype(BF16)
+                    gp_ref[sl, cols] = gpre
+                    part += dot_nn(gpre, unit_rows(get, 0, 128))
+                gs_ref[sl, :] += part
+                return carry
+
+            lax.fori_loop(0, rows // step, body, 0)
+
+        by_offset(z, work, l_ref, w_ref, v_ref)
+        for j, out_ref in enumerate((keep_ref, send_ref)):
+            for i in range(2):
+                cols = slice(j * 512 + i * 256, j * 512 + (i + 1) * 256)
+                gd = dot_tn(act_ref[:, cols], gf_ref[...]).astype(BF16)
+                gu = dot_tn(gp_ref[:, cols], x_ref[...]).astype(BF16)
+                out_ref[2 * i : 2 * i + 2, 0, 0:128] = gu.reshape(2, 128, D)
+                out_ref[2 * i : 2 * i + 2, 0, 128:256] = gd.reshape(2, 128, D)
+
+    gspec = pl.BlockSpec((4, 1, 256, D), lambda z: (0, z, 0, 0))
+    gshape = jax.ShapeDtypeStruct((4, NZ, 256, D), BF16)
+    return call(
+        kernel,
+        "ffn_bwd",
+        (NZ,),
+        [
+            full((rows, D)),
+            pl.BlockSpec((rows, D), lambda z: (0, z)),
+            full((rows, D)),
+        ]
+        + piece_specs(256, 0, 256)
+        + [full((12, D))],
+        [gspec, gspec, full((rows, D))],
+        [gshape, gshape, jax.ShapeDtypeStruct((rows, D), F32)],
+        [pltpu.VMEM((rows, D), BF16)] * 3,
+        32 * rows * D * D,
+        rows * D * 16 + 32 * D * D,
+    )(grad, pre, shifted, *weights, mods)
+
+
+def split_heads(value, keep_ref, send_ref, d, row):
+    for m in range(4):
+        keep_ref[m, d, row : row + 32] = value[m * 64 : m * 64 + 32]
+        send_ref[m, d, row : row + 32] = value[m * 64 + 32 : m * 64 + 64]
+
+
+def out_bwd(grad, grad_shifted, middle, feed, branch, attended, weights, mods, base):
+    rows = grad.shape[0]
+    step = 256
+    steps = rows // step
+
+    def kernel(
+        g_ref, gs_ref, mid_ref, f_ref, b_ref, a_ref, l_ref, w_ref, v_ref, m_ref, gm_ref, ga_ref,
+        keep_ref, send_ref, s_ref, gb_ref,
+    ):
+        i = pl.program_id(0)
+
+        @pl.when(i == 0)
+        def _():
+            s_ref[...] = jnp.zeros_like(s_ref)
+
+        g = g_ref[...].astype(F32)
+        gs = gs_ref[...]
+        hat, rstd = ln_stats(mid_ref[...])
+        gm = g + ln_back(gs, hat, rstd, m_ref[base + 4 : base + 5, :])
+        gm_ref[...] = gm
+        s_ref[0:1, :] += jnp.sum(gs, axis=0, keepdims=True)
+        s_ref[1:2, :] += jnp.sum(gs * hat, axis=0, keepdims=True)
+        s_ref[2:3, :] += jnp.sum(gm * b_ref[...].astype(F32), axis=0, keepdims=True)
+        s_ref[3:4, :] += jnp.sum(g * f_ref[...].astype(F32), axis=0, keepdims=True)
+        gb = (gm * m_ref[base + 2 : base + 3, :]).astype(BF16)
+        gb_ref[chunk_rows(i, step), :] = gb
+        for d in range(NZ):
+            ga_ref[:, d * 256 : (d + 1) * 256] = dot_nt(
+                gb, out_rows(d, l_ref, w_ref, v_ref)
+            ).astype(BF16)
+
+        @pl.when(i == steps - 1)
+        def _():
+            for d in range(NZ):
+                gw = dot_tn(a_ref[:, d * 256 : (d + 1) * 256], gb_ref[...]).astype(BF16)
+                split_heads(gw, keep_ref, send_ref, d, 0)
+
+    tile = pl.BlockSpec((step, D), lambda i: (i, 0))
+    gshape = jax.ShapeDtypeStruct((4, NZ, 32, D), BF16)
+    return call(
+        kernel,
+        "out_bwd",
+        (steps,),
+        [tile, tile, tile, tile, tile, full((rows, D))] + out_specs_of(3) + [full((12, D))],
+        [tile, tile, full(gshape.shape), full(gshape.shape), full((8, D))],
+        [
+            jax.ShapeDtypeStruct((rows, D), F32),
+            jax.ShapeDtypeStruct((rows, D), BF16),
+            gshape,
+            gshape,
+            jax.ShapeDtypeStruct((8, D), F32),
+        ],
+        [pltpu.VMEM((rows, D), BF16)],
+        4 * rows * D * D,
+        rows * D * 24 + 4 * D * D,
+    )(grad, grad_shifted, middle, feed, branch, attended, *weights, mods)
+
+
+def qkv_bwd(
+    grad_proj, normed, weights, out_keep, out_send, table_rows, hidden, grad_middle, mods, base, out_dtype
+):
+    rows = normed.shape[0]
+    step = 256
+
+    def kernel(
+        p_ref, n_ref, l_ref, w_ref, v_ref, ok_ref, os_ref, t_ref, h_ref, gm_ref, m_ref, keep_ref,
+        send_ref, gh_ref, s_ref, acc_ref,
+    ):
+        z = pl.program_id(0)
+        for t in range(3):
+            gw = dot_tn(p_ref[:, t * 256 : (t + 1) * 256], n_ref[...]).astype(BF16)
+            split_heads(gw, keep_ref, send_ref, 0, t * 32)
+        keep_ref[:, :, 96:128] = ok_ref[...]
+        send_ref[:, :, 96:128] = os_ref[...]
+        keep_ref[:, :, 128:144] = t_ref[...]
+        send_ref[:, :, 128:144] = t_ref[...]
+
+        @pl.when(z == 0)
+        def _():
+            acc_ref[...] = jnp.zeros_like(acc_ref)
+            s_ref[...] = jnp.zeros_like(s_ref)
+
+        def work(own, other):
+            def body(i, carry):
+                sl = chunk_rows(i, step)
+                part = jnp.zeros((step, D), F32)
+                for t in range(3):
+                    part += dot_nn(
+                        p_ref[sl, t * 256 : (t + 1) * 256], head_rows(own, other, t * 32)
+                    )
+                acc_ref[sl, :] += part
+                return carry
+
+            lax.fori_loop(0, rows // step, body, 0)
+
+        by_offset(z, work, l_ref, w_ref, v_ref)
+
+        @pl.when(z == NZ - 1)
+        def _():
+            def tail(i, carry):
+                sl = chunk_rows(i, step)
+                gn = acc_ref[sl, :]
+                hat, rstd = ln_stats(h_ref[sl, :].astype(F32))
+                gh = gm_ref[sl, :] + ln_back(gn, hat, rstd, m_ref[base + 1 : base + 2, :])
+                gh_ref[sl, :] = gh.astype(out_dtype)
+                s_ref[0:1, :] += jnp.sum(gn, axis=0, keepdims=True)
+                s_ref[1:2, :] += jnp.sum(gn * hat, axis=0, keepdims=True)
+                return carry
+
+            lax.fori_loop(0, rows // step, tail, 0)
+
+    gspec = pl.BlockSpec((4, 1, 144, D), lambda z: (0, z, 0, 0))
+    ospec = pl.BlockSpec((4, 1, 32, D), lambda z: (0, z, 0, 0))
+    tspec = pl.BlockSpec((4, 1, 16, D), lambda z: (0, z, 0, 0))
+    gshape = jax.ShapeDtypeStruct((4, NZ, 144, D), BF16)
+    return call(
+        kernel,
+        "qkv_bwd",
+        (NZ,),
+        [pl.BlockSpec((rows, 768), lambda z: (0, z)), full((rows, D))]
+        + piece_specs(128, 0, 96)
+        + [ospec, ospec, tspec, full((rows, D)), full((rows, D)), full((12, D))],
+        [gspec, gspec, full((rows, D)), full((8, D))],
+        [
+            gshape,
+            gshape,
+            jax.ShapeDtypeStruct((rows, D), out_dtype),
+            jax.ShapeDtypeStruct((8, D), F32),
+        ],
+        [pltpu.VMEM((rows, D), F32)],
+        12 * rows * D * D,
+        rows * D * 20 + 12 * D * D,
+    )(grad_proj, normed, *weights, out_keep, out_send, table_rows, hidden, grad_middle, mods)
+
+
+def partner(values):
+    return lax.ppermute(values, "head", [(i, i ^ 1) for i in range(NZ)])
+
+
+def rows_to_spatial(rows, odd):
+    cols = rows.shape[1]
+    whole = lax.dynamic_slice(rows, (256 * odd, 0), (1024, cols))
+    part = lax.dynamic_slice(rows, (1024 * (1 - odd), 0), (256, cols)).reshape(8, 2, 16, cols)
+    wins = whole.reshape(2, 16, 2, 16, cols).transpose(0, 2, 1, 3, 4).reshape(1024, cols)
+    left, right = part[:, 0].reshape(128, cols), part[:, 1].reshape(128, cols)
+    keep = jnp.where(odd == 0, left, right)
+    got = partner(jnp.where(odd == 0, right, left))
+    top, bottom = jnp.where(odd == 0, keep, got), jnp.where(odd == 0, got, keep)
+    return jnp.concatenate([wins, top, bottom], axis=0)
+
+
+def spatial_to_rows(wins, odd):
+    cols = wins.shape[1]
+    whole = wins[:1024].reshape(2, 2, 16, 16, cols).transpose(0, 2, 1, 3, 4).reshape(1024, cols)
+    top, bottom = wins[1024:1152], wins[1152:]
+    keep = jnp.where(odd == 0, top, bottom)
+    got = partner(jnp.where(odd == 0, bottom, top))
+    left, right = jnp.where(odd == 0, keep, got), jnp.where(odd == 0, got, keep)
+    part = jnp.stack([left.reshape(8, 16, cols), right.reshape(8, 16, cols)], axis=1)
+    part = part.reshape(256, cols)
+    return jnp.where(
+        odd == 0,
+        jnp.concatenate([whole, part], axis=0),
+        jnp.concatenate([part, whole], axis=0),
+    )
+
+
+def block_order():
+    places = {}
+    for z in range(NZ):
+        first = 5 * (z // 2)
+        halves = (first, first + 1) if z % 2 == 0 else (first + 3, first + 4)
+        listed = [(h, x) for h in halves for x in (0, 1)] + [(first + 2, z % 2)]
+        for k, item in enumerate(listed):
+            places[item] = z * 5 + k
+    return [places[(2 * t + wy, wx)] for wy in (0, 1) for wx in (0, 1) for t in range(PADF)]
+
+
+def exchange(values):
+    return lax.all_to_all(values, "head", 0, 0, tiled=True)
+
+
+def spatial_to_tubes(wins):
+    cols = wins.shape[1]
+    quads = wins.reshape(5, 2, 8, 2, 8, cols).transpose(1, 3, 0, 2, 4, 5).reshape(1280, cols)
+    got = exchange(quads)
+    return jnp.concatenate([got[64 * b : 64 * (b + 1)] for b in block_order()], axis=0)
+
+
+def tubes_to_spatial(tubes):
+    cols = tubes.shape[1]
+    order = block_order()
+    back = [order.index(b) for b in range(20)]
+    got = exchange(jnp.concatenate([tubes[64 * b : 64 * (b + 1)] for b in back], axis=0))
+    quads = got.reshape(2, 2, 5, 8, 8, cols).transpose(2, 0, 3, 1, 4, 5)
+    return quads.reshape(1280, cols)
+
+
+def toeplitz(side):
+    span = 2 * side - 1
+    b = lax.broadcasted_iota(jnp.int32, (span, side, side), 0)
+    j = lax.broadcasted_iota(jnp.int32, (span, side, side), 1)
+    i = lax.broadcasted_iota(jnp.int32, (span, side, side), 2)
+    return (b == i - j + side - 1).astype(F32)
+
+
+def toeplitz_pair(side):
+    span = 2 * side - 1
+    shape = (span * span, side * side, side * side)
+    r = lax.broadcasted_iota(jnp.int32, shape, 0)
+    j = lax.broadcasted_iota(jnp.int32, shape, 1)
+    i = lax.broadcasted_iota(jnp.int32, shape, 2)
+    dy = i // side - j // side + side - 1
+    dx = i % side - j % side + side - 1
+    return (r == dy * span + dx).astype(F32)
+
+
+CORE, ROW_X, ROW_Y = 1, 2, 4
+
+
+def swap(values, bit):
+    return lax.ppermute(values, "clip", [(i, i ^ bit) for i in range(8)])
+
+
+def from_z(values, d):
+    return lax.ppermute(values, "head", [((i + d) % NZ, i) for i in range(NZ)])
+
+
+def to_z(values, d):
+    return lax.ppermute(values, "head", [(i, (i + d) % NZ) for i in range(NZ)])
+
+
+def sync(*values):
+    return lax.optimization_barrier(values)
+
+
+def add(first, second):
+    return (first.astype(F32) + second.astype(F32)).astype(BF16)
+
+
+def line_stage(piece):
+    return jnp.stack([from_z(piece, d) for d in (1, 2, 3)])
+
+
+def cross_stage(own):
+    return own, swap(own, ROW_X), swap(own, ROW_Y)
+
+
+def corner_stage(crossed, axis):
+    own, by_x, by_y = crossed
+    half = own.shape[axis] // 2
+    first = swap(lax.slice_in_dim(by_x, 0, half, axis=axis), ROW_Y)
+    second = swap(lax.slice_in_dim(by_y, half, 2 * half, axis=axis), ROW_X)
+    return jnp.stack([own, by_x, by_y, jnp.concatenate([first, second], axis=axis)])
+
+
+def sum_core(pair):
+    return add(pair[0], swap(pair[1], CORE))
+
+
+def sum_cross(total):
+    k = total.shape[2]
+    total = total.reshape(2, 2, NZ, k, D)
+    first, second = total[:, :, :, : k // 2], total[:, :, :, k // 2 :]
+    first = add(first[:, 0], swap(first[:, 1], ROW_X))
+    second = add(second[0], swap(second[1], ROW_Y))
+    return first, second
+
+
+def sum_corner(halves):
+    first, second = halves
+    first = add(first[0], swap(first[1], ROW_Y))
+    second = add(second[0], swap(second[1], ROW_X))
+    return first, second
+
+
+def sum_line(halves):
+    first, second = halves
+    mine = jnp.concatenate([first[0], second[0]], axis=0).astype(F32)
+    for d in (1, 2, 3):
+        part = to_z(jnp.concatenate([first[d], second[d]], axis=0), d)
+        mine = mine + part.astype(F32)
+    return mine.astype(BF16)
+
+
+def sum_z(values):
+    total = values
+    for d in (1, 2, 3):
+        total = total + from_z(values, d)
+    return total
+
+
+def by_place(blocks, c):
+    return jnp.concatenate(
+        [lax.dynamic_slice_in_dim(blocks, c ^ i, 1, axis=0) for i in range(8)], axis=0
+    )
+
+
+def on_device_windows(
+    tokens, d_out, modulation, frame_counts, w_qkv, w_out, w_up, w_down, table_s, table_t
+):
+    z = lax.axis_index("head")
+    c = lax.axis_index("clip")
+    chip = c // 2
+    odd = z % 2
+    mods = modulation[0]
+    n_s, n_t = table_s.shape[1], table_t.shape[1]
+    hot_s, hot_t = toeplitz(SWIN), toeplitz_pair(TWIN)
+
+    def own_pieces(b):
+        qkv = lax.dynamic_slice_in_dim(w_qkv[b], c * 32, 32, 2).transpose(0, 2, 1)
+        out = lax.dynamic_slice_in_dim(w_out[b], c * 32, 32, 0)
+        up = lax.dynamic_slice_in_dim(w_up[b], c * 128, 128, 1).T
+        down = lax.dynamic_slice_in_dim(w_down[b], c * 128, 128, 0)
+        return (
+            jnp.concatenate([qkv.reshape(96, D), out], axis=0),
+            jnp.concatenate([up, down], axis=0),
+        )
+
+    def local_pieces(qkv, out, up, down):
+        up = up.T.reshape(8, 128, D)
+        down = down.reshape(8, 128, D)
+        qkv = qkv.transpose(0, 2, 1).reshape(3, 8, 32, D).transpose(1, 0, 2, 3)
+        attn = jnp.concatenate([qkv.reshape(8, 96, D), out.reshape(8, 32, D)], axis=1)
+        feed = jnp.concatenate([up, down], axis=1)
+        moved = [by_place(value, c) for value in (attn, feed)]
+        return [v.reshape((4, 2) + v.shape[1:]).transpose(1, 0, 2, 3) for v in moved]
+
+    def spatial_base(tables):
+        base = jnp.einsum(
+            "hab,bji->hjai", tables[:, :n_s].reshape(16, 31, 31), hot_s, precision=HIGHEST_PRECISION
+        ).reshape(16, 16, 496)
+        return jnp.pad(base, ((0, 0), (0, 0), (0, 16)))
+
+    def tube_base(tables):
+        base = jnp.einsum(
+            "htr,rjk->hjtk", tables[:, n_s:].reshape(16, 9, 225), hot_t, precision=HIGHEST_PRECISION
+        ).reshape(16, 64, 576)
+        return jnp.pad(base, ((0, 0), (0, 0), (0, 64)))
+
+    def table_rows(values):
+        values = jnp.pad(values, ((0, 0), (0, 16 * D - values.shape[1]))).astype(BF16)
+        return values.reshape(NZ, 4, 16, D).transpose(1, 0, 2, 3)
+
+    kinds = ((16, 256, 16, False), (5, 320, 64, True))
+
+    piece_a0, piece_f0 = own_pieces(0)
+    line_a0 = line_stage(piece_a0)
+    table_piece = jnp.concatenate([table_s, table_t], axis=1)
+    tables = jnp.stack([table_piece] + [from_z(table_piece, d) for d in (1, 2, 3)])
+    line_a0, piece_f0, tables = sync(line_a0, piece_f0, tables)
+    line_f0 = line_stage(piece_f0)
+    own_a0 = corner_stage(cross_stage(line_a0), 1)
+    other_a0 = swap(own_a0, CORE)
+    tables = jnp.concatenate(
+        [lax.dynamic_slice_in_dim(tables, chip ^ m, 1, axis=1) for m in range(4)], axis=1
+    ).reshape(16, n_s + n_t)
+    base_s = spatial_base(tables)
+    hidden0 = rows_to_spatial(tokens, odd)
+    local_a0, local_f0 = local_pieces(w_qkv[0], w_out[0], w_up[0], w_down[0])
+    own_a0, other_a0, line_f0, base_s, hidden0, local_a0, local_f0, tables = sync(
+        own_a0, other_a0, line_f0, base_s, hidden0, local_a0, local_f0, tables
+    )
+    weights_a0 = (local_a0, own_a0, other_a0)
+    cross_f0 = cross_stage(line_f0)
+    piece_a1, piece_f1 = own_pieces(1)
+    line_a1 = line_stage(piece_a1)
+    normed0, qkv0 = ln_qkv(hidden0, mods, weights_a0, 0)
+    attended0 = attn_fwd(qkv0, base_s, frame_counts, *kinds[0])
+    attended0, cross_f0, line_a1, piece_f1 = sync(attended0, cross_f0, line_a1, piece_f1)
+    own_f0 = corner_stage(cross_f0, 1)
+    other_f0 = swap(own_f0, CORE)
+    branch0, middle0, shifted0 = out_proj(attended0, weights_a0, hidden0, mods, 0)
+    shifted0, own_f0, other_f0, line_a1, piece_f1 = sync(
+        shifted0, own_f0, other_f0, line_a1, piece_f1
+    )
+    weights_f0 = (local_f0, own_f0, other_f0)
+    line_f1 = line_stage(piece_f1)
+    cross_a1 = cross_stage(line_a1)
+    pre0, feed0, hidden1 = ffn_fwd(shifted0, weights_f0, middle0, mods, 0)
+    hidden1, line_f1, cross_a1, tables, d_out, w_qkv, w_out, w_up, w_down = sync(
+        hidden1, line_f1, cross_a1, tables, d_out, w_qkv, w_out, w_up, w_down
+    )
+    tubes1 = spatial_to_tubes(hidden1)
+    own_a1 = corner_stage(cross_a1, 1)
+    other_a1 = swap(own_a1, CORE)
+    cross_f1 = cross_stage(line_f1)
+    local_a1, local_f1 = local_pieces(w_qkv[1], w_out[1], w_up[1], w_down[1])
+    base_t = tube_base(tables)
+    spatial_d = rows_to_spatial(d_out, odd)
+    tubes1, own_a1, other_a1, cross_f1, local_a1, local_f1, base_t, spatial_d = sync(
+        tubes1, own_a1, other_a1, cross_f1, local_a1, local_f1, base_t, spatial_d
+    )
+    weights_a1 = (local_a1, own_a1, other_a1)
+    own_f1 = corner_stage(cross_f1, 1)
+    tubes_d = spatial_to_tubes(spatial_d)
+    normed1, qkv1 = ln_qkv(tubes1, mods, weights_a1, 6)
+    qkv1, own_f1 = sync(qkv1, own_f1)
+    other_f1 = swap(own_f1, CORE)
+    attended1 = attn_fwd(qkv1, base_t, frame_counts, *kinds[1])
+    branch1, middle1, shifted1 = out_proj(attended1, weights_a1, tubes1, mods, 6)
+    shifted1, other_f1 = sync(shifted1, other_f1)
+    weights_f1 = (local_f1, own_f1, other_f1)
+    pre1, feed1, hidden2 = ffn_fwd(shifted1, weights_f1, middle1, mods, 6)
+    frame = lax.broadcasted_iota(jnp.int32, (1280, 1), 0) % 320 // 64
+    live = frame < frame_counts[0]
+    grad2 = jnp.where(live, tubes_d, 0)
+    hidden2, grad2 = sync(hidden2, grad2)
+    out_wins = tubes_to_spatial(jnp.where(live, hidden2, 0))
+    f1_keep, f1_send, g_shift1 = ffn_bwd(grad2, pre1, shifted1, weights_f1, mods, 6)
+    f1_keep, f1_send, g_shift1, out_wins = sync(f1_keep, f1_send, g_shift1, out_wins)
+    total_f1 = sum_core((f1_keep, f1_send))
+    g_mid1, g_att1, o1_keep, o1_send, sums_o1 = out_bwd(
+        grad2, g_shift1, middle1, feed1, branch1, attended1, weights_a1, mods, 6
+    )
+    g_att1, total_f1, out_wins = sync(g_att1, total_f1, out_wins)
+    half_f1 = sum_cross(total_f1)
+    g_proj1, g_base1 = attn_bwd(qkv1, g_att1, base_t, frame_counts, *kinds[1])
+    g_proj1, g_base1, half_f1 = sync(g_proj1, g_base1, half_f1)
+    half_f1 = sum_corner(half_f1)
+    gt_t = jnp.einsum(
+        "hjtk,rjk->htr",
+        g_base1[:, :, :576].reshape(16, 64, 9, 64),
+        hot_t,
+        precision=HIGHEST_PRECISION,
+    ).reshape(16, n_t)
+    a1_keep, a1_send, g_hid1, sums_q1 = qkv_bwd(
+        g_proj1, normed1, weights_a1, o1_keep, o1_send, table_rows(gt_t), tubes1, g_mid1, mods, 6, BF16
+    )
+    a1_keep, a1_send, g_hid1, half_f1 = sync(a1_keep, a1_send, g_hid1, half_f1)
+    grad1 = tubes_to_spatial(g_hid1)
+    half_a1 = sum_corner(sum_cross(sum_core((a1_keep, a1_send))))
+    mod1 = jnp.concatenate([sums_q1[0:2], sums_o1[2:3], sums_o1[0:2], sums_o1[3:4]], axis=0)
+    output = spatial_to_rows(out_wins, odd)
+    grad1, half_a1, half_f1, output = sync(grad1, half_a1, half_f1, output)
+    mine_f1, mine_a1 = sum_line(half_f1), sum_line(half_a1)
+    f0_keep, f0_send, g_shift0 = ffn_bwd(grad1, pre0, shifted0, weights_f0, mods, 0)
+    f0_keep, f0_send, g_shift0, mine_f1, mine_a1 = sync(
+        f0_keep, f0_send, g_shift0, mine_f1, mine_a1
+    )
+    total_f0 = sum_core((f0_keep, f0_send))
+    cross1 = cross_stage(jnp.concatenate([mine_f1, mine_a1], axis=0))
+    g_mid0, g_att0, o0_keep, o0_send, sums_o0 = out_bwd(
+        grad1, g_shift0, middle0, feed0, branch0, attended0, weights_a0, mods, 0
+    )
+    g_att0, total_f0, cross1 = sync(g_att0, total_f0, cross1)
+    half_f0 = sum_cross(total_f0)
+    g_proj0, g_base0 = attn_bwd(qkv0, g_att0, base_s, frame_counts, *kinds[0])
+    g_proj0, g_base0, half_f0, cross1 = sync(g_proj0, g_base0, half_f0, cross1)
+    half_f0 = sum_corner(half_f0)
+    plane1 = corner_stage(cross1, 0)
+    gt_s = jnp.einsum(
+        "hjai,bji->hab",
+        g_base0[:, :, :496].reshape(16, 16, 31, 16),
+        hot_s,
+        precision=HIGHEST_PRECISION,
+    ).reshape(16, n_s)
+    a0_keep, a0_send, grad0, sums_q0 = qkv_bwd(
+        g_proj0, normed0, weights_a0, o0_keep, o0_send, table_rows(gt_s), hidden0, g_mid0, mods, 0, F32
+    )
+    a0_keep, a0_send, grad0, half_f0, plane1, sums_q0 = sync(
+        a0_keep, a0_send, grad0, half_f0, plane1, sums_q0
+    )
+    mod0 = jnp.concatenate([sums_q0[0:2], sums_o0[2:3], sums_o0[0:2], sums_o0[3:4]], axis=0)
+    grad_tokens = spatial_to_rows(grad0, odd)
+    grad_mods = sum_z(jnp.concatenate([mod0, mod1], axis=0))[None]
+    mine_f0 = sum_line(half_f0)
+    mine_a0 = sum_line(sum_corner(sum_cross(sum_core((a0_keep, a0_send)))))
+    plane0f = corner_stage(cross_stage(mine_f0), 0)
+    plane0a = corner_stage(cross_stage(mine_a0), 0)
+
+    def placed(plane):
+        both = jnp.stack([plane, swap(plane, CORE)], axis=1)
+        return by_place(both.reshape((8,) + plane.shape[1:]), c)
+
+    done1 = placed(plane1)
+    pairs = ((placed(plane0f), placed(plane0a)), (done1[:, :256], done1[:, 256:]))
+    g_qkv, g_out, g_up, g_down = [], [], [], []
+    for feed, attn in pairs:
+        g_qkv.append(
+            attn[:, :96].reshape(8, 3, 32, D).transpose(1, 3, 0, 2).reshape(3, D, 256).astype(F32)
+        )
+        g_out.append(attn[:, 96:128].reshape(256, D).astype(F32))
+        g_up.append(feed[:, :128].reshape(D, D).T.astype(F32))
+        g_down.append(feed[:, 128:].reshape(D, D).astype(F32))
+
+    def table_of(attn, size):
+        return attn[::2, 128:144].reshape(4, 16 * D)[:, :size].astype(F32)
+
+    return (
+        output,
+        grad_tokens,
+        grad_mods,
+        jnp.stack(g_qkv),
+        jnp.stack(g_out),
+        jnp.stack(g_up),
+        jnp.stack(g_down),
+        table_of(pairs[0][1], n_s),
+        table_of(pairs[1][1], n_t),
+    )
+
+
 def solution(mesh):
+    if mesh.shape["head"] == NZ and mesh.shape["clip"] == 8:
+        body = on_device_windows
+    else:
+        body = on_device
     return jax.shard_map(
-        on_device,
+        body,
         mesh=mesh,
         in_specs=(
             P(("clip", "head"), None),

time: 4500 us -> 1300 us (0.29)
  waiting for transfers between devices: 1760 us -> 220 us
  other arithmetic: 1090 us -> 144 us
  local copies, waits for them, and re-layouts: 1000 us -> 221 us
  matrix products: 572 us -> 16.1 us
  Pallas kernels: 0 us -> 539 us
  starting transfers between devices: 0.87 us -> 141 us
  blocking collectives: 50.6 us -> 0 us
    reduce_scatter x8 -> x0, waiting for transfers between devices: 947 us -> none  [the longest x2 346 us: rows_out(): lax.psum_scatter(jnp.dot(full_rows, weight, preferred_element_type=jnp.fl...]
    scatter-add x2 -> x0, other arithmetic: 890 us -> none  [attend_back(): jax.ops.segment_sum(table_terms.T, rel_index.reshape(-1), num_segments=ta...]
    all_gather x8 -> x0, waiting for transfers between devices: 807 us -> none  [the longest x2 292 us: forward_block(): lax.all_gather(w_up[block_id], 'head', axis=1, tiled=True)]
    gather x4 -> x0, local copies, waits for them, and re-layouts: 609 us -> none  [logits_of(): logits = logits + table_arg[:, rel_index][None]]
    dot_general x38 -> x4, matrix products: 572 us -> 16.1 us  [the longest x1 5.62 us: tube_base(): jnp.einsum('htr,rjk->hjtk', tables[:, n_s:].reshape(16, 9, 225), hot_t, p...]
    pallas_call x0 -> x16, Pallas kernels: none -> 539 us  [the longest x2 141 us: ffn_bwd(): call(kernel, 'ffn_bwd', (NZ,), [full((rows, D)), pl.BlockSpec((rows, D),...]
    ppermute x0 -> x89, waiting for transfers between devices: none -> 206 us  [the longest x18 74.6 us: from_z(): return lax.ppermute(values, 'head', [((i + d) % NZ, i) for i in range(NZ)])]
    ppermute x0 -> x89, starting transfers between devices: none -> 122 us  [the longest x55 48.6 us: swap(): return lax.ppermute(values, 'clip', [(i, i ^ bit) for i in range(8)])]
  transfers between devices with their start and end apart: 17 -> 93, of which waited for: 12 -> 30; matrix products, arithmetic and copies ran while one was open for 43% -> 23% of each run, Pallas kernels for 0% -> 39%
where the time goes in v1:
time: 1300 us; the launch traced here: 1290 us
  Pallas kernels  539 us (41%)
  local copies, waits for them, and re-layouts  221 us (17%)
  waiting for transfers between devices  220 us (17%)
  other arithmetic  144 us (11%)
  starting transfers between devices  141 us (11%)
  matrix products  16.1 us (1%)
    pallas_call x2, Pallas kernels, ffn_bwd(): call(kernel, 'ffn_bwd', (NZ,), [full((rows, D)), pl.BlockSpec((rows, D),...  141 us
    pallas_call x2, Pallas kernels, attn_bwd(): call(kernel, 'attn_bwd', (NZ, windows), [pl.BlockSpec((width, 768), lambd...  97.1 us
    pallas_call x2, Pallas kernels, ffn_fwd(): call(kernel, 'ffn_fwd', (NZ,), [full((rows, D))] + piece_specs(256, 0, 25...  84.3 us
    ppermute x18, waiting for transfers between devices, from_z(): return lax.ppermute(values, 'head', [((i + d) % NZ, i) for i in range(NZ)])  74.6 us
    ppermute x55, waiting for transfers between devices, swap(): return lax.ppermute(values, 'clip', [(i, i ^ bit) for i in range(8)])  68.3 us
    pallas_call x2, Pallas kernels, qkv_bwd(): call(kernel, 'qkv_bwd', (NZ,), [pl.BlockSpec((rows, 768), lambda z: (0, z...  67.4 us
    unnamed x263, local copies, waits for them, and re-layouts  65.9 us
    pallas_call x2, Pallas kernels, attn_fwd(): call(kernel, 'attn_fwd', (NZ, windows), [pl.BlockSpec((width, 768), lambd...  61.2 us
  transfers between devices with their start and end apart: 93, of which 30 were waited for; matrix products, arithmetic and copies ran while one was open for 23% of the time, Pallas kernels for 39%

profile of v1, /device:TPU:0, one launch (start us, length us, event | category | flops | bytes accessed | tf_op | source)
XLA Modules:
  0.0 1285.5 jit_solution(8468711271331483112)
XLA Ops:
  38.7 7.0 collective-permute-done.2
  107.8 35.5 %collective-permute-done.12 = bf16[256,1024]{1,0:T(8,128)(2,1)} collective-permute-done((bf16[256,1024]{1,0:T(8,128)(2,1)}, bf16[256,1024]{1,0:T(8,128)(2,1)}, u32[]{:S(2)}, u32[]{:S(2)}) %collective-permute-start.12) | collective-permute-done | bytes 524320 | tf_op jit(solution)/shard_map/ppermute | solution.py:1025
  155.0 16.0 %ln_qkv.2 = (bf16[1280,1024]{1,0:T(8,128)(2,1)}, bf16[1280,3072]{1,0:T(8,128)(2,1)}) custom-call(bf16[1280,1024]{1,0:T(8,128)(2,1)} %pad_maximum_fusion.7.h_ref, f32[12,1024]{1,0:T(8,128)} %bitcast.660, bf16[2,4,128,1024]{3,2,1,0:T(8,128)(2,1)} %bitcast.546, bf16[4,3,128,1024]{3,2,1,0:T(8,128)(2,1)} %pad_maximum_fusion.5.w_ref, ...), custom_call_target="tpu_custom_call" | custom-call | flops 8053063680 | bytes 22020096 | tf_op jit(solution)/shard_map/ln_qkv/pallas_call | solution.py:477
  171.0 26.9 %attn_fwd.2.a_ref = bf16[1280,1024]{1,0:T(8,128)(2,1)} custom-call(bf16[1280,3072]{1,0:T(8,128)(2,1)} %get-tuple-element.155.x_ref, f32[16,16,512]{2,1,0:T(8,128)} %pad.18.b_ref, s32[1]{0:T(128)} %copy.310.fc_ref), custom_call_target="tpu_custom_call" | custom-call | flops 5368709120 | bytes 10485760 | tf_op jit(solution)/shard_map/attn_fwd/pallas_call | solution.py:521
  203.4 14.8 %collective-permute-done.20 = bf16[3,128,1024]{2,1,0:T(8,128)(2,1)S(1)} collective-permute-done((bf16[3,128,1024]{2,1,0:T(8,128)(2,1)S(1)}, bf16[3,128,1024]{2,1,0:T(8,128)(2,1)S(1)}, u32[]{:S(2)}, u32[]{:S(2)}) %collective-permute-start.20) | collective-permute-done | bytes 786464 | tf_op jit(solution)/shard_map/ppermute | solution.py:1021
  225.9 9.3 out_proj.2
  242.5 42.1 %ffn_fwd.2 = (bf16[1280,4096]{1,0:T(8,128)(2,1)}, bf16[1280,1024]{1,0:T(8,128)(2,1)}, bf16[1280,1024]{1,0:T(8,128)(2,1)}) custom-call(bf16[1280,1024]{1,0:T(8,128)(2,1)} %get-tuple-element.165.x_ref, bf16[2,4,256,1024]{3,2,1,0:T(8,128)(2,1)} %bitcast.631, bf16[4,3,256,1024]{3,2,1,0:T(8,128)(2,1)} %pad_maximum_fusion.1.w_ref, ...), custom_call_target="tpu_custom_call" | custom-call | flops 21474836480 | bytes 42991616 | tf_op jit(solution)/shard_map/ffn_fwd/pallas_call | solution.py:708
  348.9 9.8 all-to-all-done
  400.2 15.9 %ln_qkv.3 = (bf16[1280,1024]{1,0:T(8,128)(2,1)}, bf16[1280,3072]{1,0:T(8,128)(2,1)}) custom-call(bf16[1280,1024]{1,0:T(8,128)(2,1)} %constant_dynamic-update-slice_fusion.8.h_ref, f32[12,1024]{1,0:T(8,128)} %bitcast.663, bf16[2,4,128,1024]{3,2,1,0:T(8,128)(2,1)} %bitcast.550, bf16[4,3,128,1024]{3,2,1,0:T(8,128)(2,1)} %pad_maximum_fusion.6.w_ref, ...), custom_call_target="tpu_custom_call" | custom-call | flops 8053063680 | bytes 22020096 | tf_op jit(solution)/shard_map/ln_qkv/pallas_call | solution.py:477
  423.8 34.4 %attn_fwd.3.a_ref = bf16[1280,1024]{1,0:T(8,128)(2,1)} custom-call(bf16[1280,3072]{1,0:T(8,128)(2,1)} %get-tuple-element.193.x_ref, f32[16,64,640]{2,1,0:T(8,128)} %pad.19.b_ref, s32[1]{0:T(128)} %copy.310.fc_ref), custom_call_target="tpu_custom_call" | custom-call | flops 6710886400 | bytes 10485760 | tf_op jit(solution)/shard_map/attn_fwd/pallas_call | solution.py:521
  458.2 9.4 out_proj.3
  469.7 42.2 %ffn_fwd.3 = (bf16[1280,4096]{1,0:T(8,128)(2,1)}, bf16[1280,1024]{1,0:T(8,128)(2,1)}, bf16[1280,1024]{1,0:T(8,128)(2,1)}) custom-call(bf16[1280,1024]{1,0:T(8,128)(2,1)} %get-tuple-element.197.x_ref, bf16[2,4,256,1024]{3,2,1,0:T(8,128)(2,1)} %bitcast.633, bf16[4,3,256,1024]{3,2,1,0:T(8,128)(2,1)} %pad_maximum_fusion.2.w_ref, ...), custom_call_target="tpu_custom_call" | custom-call | flops 21474836480 | bytes 42991616 | tf_op jit(solution)/shard_map/ffn_fwd/pallas_call | solution.py:708
  520.8 70.2 %ffn_bwd.2 = (bf16[4,4,256,1024]{3,2,1,0:T(8,128)(2,1)}, bf16[4,4,256,1024]{3,2,1,0:T(8,128)(2,1)}, f32[1280,1024]{1,0:T(8,128)}) custom-call(bf16[1280,1024]{1,0:T(8,128)(2,1)} %broadcast_select_fusion.1.g_ref, bf16[1280,4096]{1,0:T(8,128)(2,1)} %get-tuple-element.204.p_ref, bf16[1280,1024]{1,0:T(8,128)(2,1)} %get-tuple-element.197.x_ref, ...), custom_call_target="tpu_custom_call" | custom-call | flops 42949672960 | bytes 54525952 | tf_op jit(solution)/shard_map/ffn_bwd/pallas_call | solution.py:775
  595.0 18.4 %out_bwd.2 = (f32[1280,1024]{1,0:T(8,128)}, bf16[1280,1024]{1,0:T(8,128)(2,1)}, bf16[4,4,32,1024]{3,2,1,0:T(8,128)(2,1)}, bf16[4,4,32,1024]{3,2,1,0:T(8,128)(2,1)}, f32[8,1024]{1,0:T(8,128)}) custom-call(bf16[1280,1024]{1,0:T(8,128)(2,1)} %broadcast_select_fusion.1.g_ref, f32[1280,1024]{1,0:T(8,128)} %get-tuple-element.209.gs_ref, ...), custom_call_target="tpu_custom_call" | custom-call | flops 5368709120 | bytes 35651584 | tf_op jit(solution)/shard_map/out_bwd/pallas_call | solution.py:839
  613.4 8.4 add_convert_fusion.1
  627.7 51.3 %attn_bwd.2 = (bf16[1280,3072]{1,0:T(8,128)(2,1)}, f32[16,64,640]{2,1,0:T(8,128)}) custom-call(bf16[1280,3072]{1,0:T(8,128)(2,1)} %get-tuple-element.193.x_ref, bf16[1280,1024]{1,0:T(8,128)(2,1)} %get-tuple-element.216.d_ref, f32[16,64,640]{2,1,0:T(8,128)} %pad.19.b_ref, s32[1]{0:T(128)} %copy.310.fc_ref), custom_call_target="tpu_custom_call" | custom-call | flops 16777216000 | bytes 20971520 | tf_op jit(solution)/shard_map/attn_bwd/pallas_call | solution.py:576
  707.4 33.2 %qkv_bwd.2 = (bf16[4,4,144,1024]{3,2,1,0:T(8,128)(2,1)}, bf16[4,4,144,1024]{3,2,1,0:T(8,128)(2,1)}, bf16[1280,1024]{1,0:T(8,128)(2,1)}, f32[8,1024]{1,0:T(8,128)}) custom-call(bf16[1280,3072]{1,0:T(8,128)(2,1)} %get-tuple-element.220.p_ref, bf16[1280,1024]{1,0:T(8,128)(2,1)} %get-tuple-element.221.n_ref, bf16[2,4,128,1024]{3,2,1,0:T(8,128)(2,1)} %bitcast.553, ...), custom_call_target="tpu_custom_call" | custom-call | flops 16106127360 | bytes 38797312 | tf_op jit(solution)/shard_map/qkv_bwd/pallas_call | solution.py:915
  765.0 36.7 %collective-permute-done.47 = bf16[128,1024]{1,0:T(8,128)(2,1)S(1)} collective-permute-done((bf16[128,1024]{1,0:T(8,128)(2,1)S(1)}, bf16[128,1024]{1,0:T(8,128)(2,1)S(1)}, u32[]{:S(2)}, u32[]{:S(2)}) %collective-permute-start.47) | collective-permute-done | bytes 262176 | tf_op jit(solution)/shard_map/ppermute | solution.py:936
  835.6 70.6 %ffn_bwd.3 = (bf16[4,4,256,1024]{3,2,1,0:T(8,128)(2,1)}, bf16[4,4,256,1024]{3,2,1,0:T(8,128)(2,1)}, f32[1280,1024]{1,0:T(8,128)}) custom-call(bf16[1280,1024]{1,0:T(8,128)(2,1)} %bitcast.577, bf16[1280,4096]{1,0:T(8,128)(2,1)} %get-tuple-element.239.p_ref, bf16[1280,1024]{1,0:T(8,128)(2,1)} %get-tuple-element.165.x_ref, bf16[2,4,256,1024]{3,2,1,0:T(8,128)(2,1)} %bitcast.632, ...), custom_call_target="tpu_custom_call" | custom-call | flops 42949672960 | bytes 54525952 | tf_op jit(solution)/shard_map/ffn_bwd/pallas_call | solution.py:775
  909.9 18.7 %out_bwd.3 = (f32[1280,1024]{1,0:T(8,128)}, bf16[1280,1024]{1,0:T(8,128)(2,1)}, bf16[4,4,32,1024]{3,2,1,0:T(8,128)(2,1)}, bf16[4,4,32,1024]{3,2,1,0:T(8,128)(2,1)}, f32[8,1024]{1,0:T(8,128)}) custom-call(bf16[1280,1024]{1,0:T(8,128)(2,1)} %bitcast.578, f32[1280,1024]{1,0:T(8,128)} %get-tuple-element.247.gs_ref, f32[1280,1024]{1,0:T(8,128)} %get-tuple-element.169.mid_ref, ...), custom_call_target="tpu_custom_call" | custom-call | flops 5368709120 | bytes 35651584 | tf_op jit(solution)/shard_map/out_bwd/pallas_call | solution.py:839
  928.6 8.0 add_convert_fusion
  942.7 45.8 %attn_bwd.3 = (bf16[1280,3072]{1,0:T(8,128)(2,1)}, f32[16,16,512]{2,1,0:T(8,128)}) custom-call(bf16[1280,3072]{1,0:T(8,128)(2,1)} %get-tuple-element.155.x_ref, bf16[1280,1024]{1,0:T(8,128)(2,1)} %get-tuple-element.255.d_ref, f32[16,16,512]{2,1,0:T(8,128)} %pad.18.b_ref, s32[1]{0:T(128)} %copy.310.fc_ref), custom_call_target="tpu_custom_call" | custom-call | flops 13421772800 | bytes 20971520 | tf_op jit(solution)/shard_map/attn_bwd/pallas_call | solution.py:576
  1011.2 34.1 %qkv_bwd.3 = (bf16[4,4,144,1024]{3,2,1,0:T(8,128)(2,1)}, bf16[4,4,144,1024]{3,2,1,0:T(8,128)(2,1)}, f32[1280,1024]{1,0:T(8,128)}, f32[8,1024]{1,0:T(8,128)}) custom-call(bf16[1280,3072]{1,0:T(8,128)(2,1)} %get-tuple-element.262.p_ref, bf16[1280,1024]{1,0:T(8,128)(2,1)} %get-tuple-element.263.n_ref, bf16[2,4,128,1024]{3,2,1,0:T(8,128)(2,1)} %bitcast.549, ...), custom_call_target="tpu_custom_call" | custom-call | flops 16106127360 | bytes 38797312 | tf_op jit(solution)/shard_map/qkv_bwd/pallas_call | solution.py:915
  1054.0 10.4 collective-permute-start.81
  1070.2 18.2 %collective-permute-done.64 = f32[12,1024]{1,0:T(8,128)S(1)} collective-permute-done((f32[12,1024]{1,0:T(8,128)S(1)}, f32[12,1024]{1,0:T(8,128)S(1)}, u32[]{:S(2)}, u32[]{:S(2)}) %collective-permute-start.64) | collective-permute-done | bytes 49184 | tf_op jit(solution)/shard_map/ppermute | solution.py:1025
  1094.0 11.6 collective-permute-start.63
  1110.1 7.4 collective-permute-done.83
  1120.2 10.4 collective-permute-done.66
  1135.1 10.5 collective-permute-done.85
  1175.7 19.6 %collective-permute-done.68 = bf16[2,4,72,1024]{3,2,1,0:T(8,128)(2,1)S(1)} collective-permute-done((bf16[2,4,72,1024]{3,2,1,0:T(8,128)(2,1)S(1)}, bf16[2,4,72,1024]{3,2,1,0:T(8,128)(2,1)S(1)}, u32[]{:S(2)}, u32[]{:S(2)}) %collective-permute-start.68) | collective-permute-done | bytes 1179680 | tf_op jit(solution)/shard_map/ppermute | solution.py:1021
  1228.1 9.9 collective-permute-done.73
  1275.3 6.7 copy.144
  (686 shorter events, 517.8 us)
Async XLA Ops:
  53.5 48.0 %collective-permute-start.14 = (bf16[128,1024]{1,0:T(8,128)(2,1)}, bf16[128,1024]{1,0:T(8,128)(2,1)}, u32[]{:S(2)}, u32[]{:S(2)}) collective-permute-start(bf16[128,1024]{1,0:T(8,128)(2,1)} %bitcast.29), channel_id=1, source_target_pairs={{0,1},{1,0},{2,3},{3,2},{4,5},{5,4},{6,7},{7,6},{8,9},{9,8},{10,11... | collective-permute-start | bytes 786440 | tf_op jit(solution)/shard_map/ppermute | solution.py:936
  60.3 90.2 %collective-permute-start.17 = (bf16[128,1024]{1,0:T(8,128)(2,1)}, bf16[128,1024]{1,0:T(8,128)(2,1)}, u32[]{:S(2)}, u32[]{:S(2)}) collective-permute-start(bf16[128,1024]{1,0:T(8,128)(2,1)} %pad_maximum_fusion.33), channel_id=1, source_target_pairs={{1,0},{2,1},{3,2},{0,3},{5,4},{6,5},{7,6},{4,7},{9,8},{10,9},{11,1... | collective-permute-start | bytes 786440 | tf_op jit(solution)/shard_map/ppermute | solution.py:1025
  84.6 60.4 %collective-permute-start.10 = (bf16[4,3,128,1024]{3,2,1,0:T(8,128)(2,1)}, bf16[4,3,128,1024]{3,2,1,0:T(8,128)(2,1)}, u32[]{:S(2)}, u32[]{:S(2)}) collective-permute-start(bf16[4,3,128,1024]{3,2,1,0:T(8,128)(2,1)} %pad_maximum_fusion.5.w_ref), channel_id=1, source_target_pairs={{0,4},{4,0},{8,12},{12,8},{16,20},{20,16},{24,28},{28,24},{1,5},{5... | collective-permute-start | bytes 9437192 | tf_op jit(solution)/shard_map/ppermute | solution.py:1021
  89.9 53.4 %collective-permute-start.12 = (bf16[256,1024]{1,0:T(8,128)(2,1)}, bf16[256,1024]{1,0:T(8,128)(2,1)}, u32[]{:S(2)}, u32[]{:S(2)}) collective-permute-start(bf16[256,1024]{1,0:T(8,128)(2,1)} %pad_maximum_fusion.17), channel_id=1, source_target_pairs={{2,0},{3,1},{0,2},{1,3},{6,4},{7,5},{4,6},{5,7},{10,8},{11,9},{8,1... | collective-permute-start | bytes 1572872 | tf_op jit(solution)/shard_map/ppermute | solution.py:1025
  145.0 52.8 %collective-permute-start.15 = (bf16[3,256,1024]{2,1,0:T(8,128)(2,1)S(1)}, bf16[3,256,1024]{2,1,0:T(8,128)(2,1)}, u32[]{:S(2)}, u32[]{:S(2)}) collective-permute-start(bf16[3,256,1024]{2,1,0:T(8,128)(2,1)S(1)} %pad_maximum_fusion.11), channel_id=1, source_target_pairs={{0,8},{4,12},{8,0},{12,4},{16,24},{20,28},{24,16},{28,20},{1,9},{5... | collective-permute-start | bytes 4718600 | tf_op jit(solution)/shard_map/ppermute | solution.py:1021
  146.6 51.3 %collective-permute-start.16 = (bf16[3,256,1024]{2,1,0:T(8,128)(2,1)S(1)}, bf16[3,256,1024]{2,1,0:T(8,128)(2,1)}, u32[]{:S(2)}, u32[]{:S(2)}) collective-permute-start(bf16[3,256,1024]{2,1,0:T(8,128)(2,1)S(1)} %pad_maximum_fusion.11), channel_id=1, source_target_pairs={{0,16},{4,20},{8,24},{12,28},{16,0},{20,4},{24,8},{28,12},{1,17},{... | collective-permute-start | bytes 4718600 | tf_op jit(solution)/shard_map/ppermute | solution.py:1021
  236.3 48.3 %collective-permute-start.23 = (bf16[256,1024]{1,0:T(8,128)(2,1)S(1)}, bf16[256,1024]{1,0:T(8,128)(2,1)S(1)}, u32[]{:S(2)}, u32[]{:S(2)}) collective-permute-start(bf16[256,1024]{1,0:T(8,128)(2,1)S(1)} %pad_maximum_fusion.18), channel_id=1, source_target_pairs={{1,0},{2,1},{3,2},{0,3},{5,4},{6,5},{7,6},{4,7},{9,8},{10,9},{11,1... | collective-permute-start | bytes 1572872 | tf_op jit(solution)/shard_map/ppermute | solution.py:1025
  240.5 47.7 %collective-permute-start.26 = (bf16[3,128,1024]{2,1,0:T(8,128)(2,1)S(1)}, bf16[3,128,1024]{2,1,0:T(8,128)(2,1)S(1)}, u32[]{:S(2)}, u32[]{:S(2)}) collective-permute-start(bf16[3,128,1024]{2,1,0:T(8,128)(2,1)S(1)} %pad_maximum_fusion.16), channel_id=1, source_target_pairs={{0,8},{4,12},{8,0},{12,4},{16,24},{20,28},{24,16},{28,20},{1,9},{5... | collective-permute-start | bytes 2359304 | tf_op jit(solution)/shard_map/ppermute | solution.py:1021
  288.3 101.7 %collective-permute-start.31 = (bf16[3,256,1024]{2,1,0:T(8,128)(2,1)}, bf16[3,256,1024]{2,1,0:T(8,128)(2,1)}, u32[]{:S(2)}, u32[]{:S(2)}) collective-permute-start(bf16[3,256,1024]{2,1,0:T(8,128)(2,1)} %pad_maximum_fusion.12), channel_id=1, source_target_pairs={{0,8},{4,12},{8,0},{12,4},{16,24},{20,28},{24,16},{28,20},{1,9},{5... | collective-permute-start | bytes 4718600 | tf_op jit(solution)/shard_map/ppermute | solution.py:1021
  289.7 100.3 %collective-permute-start.32 = (bf16[3,256,1024]{2,1,0:T(8,128)(2,1)}, bf16[3,256,1024]{2,1,0:T(8,128)(2,1)}, u32[]{:S(2)}, u32[]{:S(2)}) collective-permute-start(bf16[3,256,1024]{2,1,0:T(8,128)(2,1)} %pad_maximum_fusion.12), channel_id=1, source_target_pairs={{0,16},{4,20},{8,24},{12,28},{16,0},{20,4},{24,8},{28,12},{1,17},{... | collective-permute-start | bytes 4718600 | tf_op jit(solution)/shard_map/ppermute | solution.py:1021
  292.4 52.0 %collective-permute-start.33 = (bf16[128,1024]{1,0:T(8,128)(2,1)}, bf16[128,1024]{1,0:T(8,128)(2,1)}, u32[]{:S(2)}, u32[]{:S(2)}) collective-permute-start(bf16[128,1024]{1,0:T(8,128)(2,1)} %bitcast.93), channel_id=1, source_target_pairs={{0,1},{1,0},{2,3},{3,2},{4,5},{5,4},{6,7},{7,6},{8,9},{9,8},{10,11... | collective-permute-start | bytes 786440 | tf_op jit(solution)/shard_map/ppermute | solution.py:936
  295.5 63.1 %all-to-all-start = ((bf16[4,320,1024]{2,1,0:T(8,128)(2,1)}), bf16[4,320,1024]{2,1,0:T(8,128)(2,1)}, u32[]{:S(2)}, u32[]{:S(2)}) async-start(bf16[4,320,1024]{2,1,0:T(8,128)(2,1)} %bitcast.63), calls=%async_computation | async-start | bytes 5242880 | tf_op jit(solution)/shard_map/all_to_all | solution.py:979
  391.8 75.8 %all-to-all-start.1 = ((bf16[4,320,1024]{2,1,0:T(8,128)(2,1)}), bf16[4,320,1024]{2,1,0:T(8,128)(2,1)S(1)}, u32[]{:S(2)}, u32[]{:S(2)}) async-start(bf16[4,320,1024]{2,1,0:T(8,128)(2,1)} %bitcast.600), calls=%async_computation.1 | async-start | bytes 5242880 | tf_op jit(solution)/shard_map/all_to_all | solution.py:979
  515.8 75.2 %all-to-all-start.2 = ((bf16[4,320,1024]{2,1,0:T(8,128)(2,1)}), bf16[4,320,1024]{2,1,0:T(8,128)(2,1)S(1)}, u32[]{:S(2)}, u32[]{:S(2)}) async-start(bf16[4,320,1024]{2,1,0:T(8,128)(2,1)} %bitcast.637), calls=%async_computation.2 | async-start | bytes 5242880 | tf_op jit(solution)/shard_map/all_to_all | solution.py:979
  625.8 53.1 %collective-permute-start.38 = (bf16[2,4,128,1024]{3,2,1,0:T(8,128)(2,1)}, bf16[2,4,128,1024]{3,2,1,0:T(8,128)(2,1)}, u32[]{:S(2)}, u32[]{:S(2)}) collective-permute-start(bf16[2,4,128,1024]{3,2,1,0:T(8,128)(2,1)} %slice_bitcast_fusion.6), channel_id=1, source_target_pairs={{0,8},{4,12},{8,0},{12,4},{16,24},{20,28},{24,16},{28,20},{1,9},{5... | collective-permute-start | bytes 6291464 | tf_op jit(solution)/shard_map/ppermute | solution.py:1021
  626.4 52.6 %collective-permute-start.39 = (bf16[2,4,128,1024]{3,2,1,0:T(8,128)(2,1)S(1)}, bf16[2,4,128,1024]{3,2,1,0:T(8,128)(2,1)}, u32[]{:S(2)}, u32[]{:S(2)}) collective-permute-start(bf16[2,4,128,1024]{3,2,1,0:T(8,128)(2,1)S(1)} %slice_bitcast_fusion.4), channel_id=1, source_target_pairs={{0,16},{4,20},{8,24},{12,28},{16,0},{20,4},{24,8},{28,12},{1,17},{... | collective-permute-start | bytes 6291464 | tf_op jit(solution)/shard_map/ppermute | solution.py:1021
  685.8 54.9 %collective-permute-start.41 = (bf16[4,128,1024]{2,1,0:T(8,128)(2,1)}, bf16[4,128,1024]{2,1,0:T(8,128)(2,1)}, u32[]{:S(2)}, u32[]{:S(2)}) collective-permute-start(bf16[4,128,1024]{2,1,0:T(8,128)(2,1)} %slice_bitcast_fusion.19), channel_id=1, source_target_pairs={{0,8},{4,12},{8,0},{12,4},{16,24},{20,28},{24,16},{28,20},{1,9},{5... | collective-permute-start | bytes 3145736 | tf_op jit(solution)/shard_map/ppermute | solution.py:1021
  687.6 55.9 %collective-permute-start.40 = (bf16[4,128,1024]{2,1,0:T(8,128)(2,1)}, bf16[4,128,1024]{2,1,0:T(8,128)(2,1)}, u32[]{:S(2)}, u32[]{:S(2)}) collective-permute-start(bf16[4,128,1024]{2,1,0:T(8,128)(2,1)} %slice_bitcast_fusion.20), channel_id=1, source_target_pairs={{0,16},{4,20},{8,24},{12,28},{16,0},{20,4},{24,8},{28,12},{1,17},{... | collective-permute-start | bytes 3145736 | tf_op jit(solution)/shard_map/ppermute | solution.py:1021
  748.0 65.4 %all-to-all-start.3 = ((bf16[4,320,1024]{2,1,0:T(8,128)(2,1)}), bf16[4,320,1024]{2,1,0:T(8,128)(2,1)}, u32[]{:S(2)}, u32[]{:S(2)}) async-start(bf16[4,320,1024]{2,1,0:T(8,128)(2,1)} %bitcast.638), calls=%async_computation.3 | async-start | bytes 5242880 | tf_op jit(solution)/shard_map/all_to_all | solution.py:979
  823.4 82.8 %collective-permute-start.52 = (bf16[144,1024]{1,0:T(8,128)(2,1)S(1)}, bf16[144,1024]{1,0:T(8,128)(2,1)S(1)}, u32[]{:S(2)}, u32[]{:S(2)}) collective-permute-start(bf16[144,1024]{1,0:T(8,128)(2,1)S(1)} %pad_maximum_fusion.27), channel_id=1, source_target_pairs={{0,2},{1,3},{2,0},{3,1},{4,6},{5,7},{6,4},{7,5},{8,10},{9,11},{10,... | collective-permute-start | bytes 884744 | tf_op jit(solution)/shard_map/ppermute | solution.py:1029
  825.4 80.8 %collective-permute-start.53 = (bf16[144,1024]{1,0:T(8,128)(2,1)S(1)}, bf16[144,1024]{1,0:T(8,128)(2,1)}, u32[]{:S(2)}, u32[]{:S(2)}) collective-permute-start(bf16[144,1024]{1,0:T(8,128)(2,1)S(1)} %pad_maximum_fusion.28), channel_id=1, source_target_pairs={{0,3},{1,0},{2,1},{3,2},{4,7},{5,4},{6,5},{7,6},{8,11},{9,8},{10,9... | collective-permute-start | bytes 884744 | tf_op jit(solution)/shard_map/ppermute | solution.py:1029
  828.6 78.8 %collective-permute-start.48 = (bf16[256,1024]{1,0:T(8,128)(2,1)S(1)}, bf16[256,1024]{1,0:T(8,128)(2,1)S(1)}, u32[]{:S(2)}, u32[]{:S(2)}) collective-permute-start(bf16[256,1024]{1,0:T(8,128)(2,1)S(1)} %pad_maximum_fusion.20), channel_id=1, source_target_pairs={{0,1},{1,2},{2,3},{3,0},{4,5},{5,6},{6,7},{7,4},{8,9},{9,10},{10,1... | collective-permute-start | bytes 1572872 | tf_op jit(solution)/shard_map/ppermute | solution.py:1029
  828.7 78.7 %collective-permute-start.49 = (bf16[256,1024]{1,0:T(8,128)(2,1)S(1)}, bf16[256,1024]{1,0:T(8,128)(2,1)S(1)}, u32[]{:S(2)}, u32[]{:S(2)}) collective-permute-start(bf16[256,1024]{1,0:T(8,128)(2,1)S(1)} %pad_maximum_fusion.21), channel_id=1, source_target_pairs={{0,2},{1,3},{2,0},{3,1},{4,6},{5,7},{6,4},{7,5},{8,10},{9,11},{10,... | collective-permute-start | bytes 1572872 | tf_op jit(solution)/shard_map/ppermute | solution.py:1029
  832.8 74.7 %collective-permute-start.50 = (bf16[256,1024]{1,0:T(8,128)(2,1)S(1)}, bf16[256,1024]{1,0:T(8,128)(2,1)S(1)}, u32[]{:S(2)}, u32[]{:S(2)}) collective-permute-start(bf16[256,1024]{1,0:T(8,128)(2,1)S(1)} %pad_maximum_fusion.22), channel_id=1, source_target_pairs={{0,3},{1,0},{2,1},{3,2},{4,7},{5,4},{6,5},{7,6},{8,11},{9,8},{10,9... | collective-permute-start | bytes 1572872 | tf_op jit(solution)/shard_map/ppermute | solution.py:1029
  940.5 48.0 %collective-permute-start.57 = (bf16[2,4,128,1024]{3,2,1,0:T(8,128)(2,1)S(1)}, bf16[2,4,128,1024]{3,2,1,0:T(8,128)(2,1)}, u32[]{:S(2)}, u32[]{:S(2)}) collective-permute-start(bf16[2,4,128,1024]{3,2,1,0:T(8,128)(2,1)S(1)} %slice_bitcast_fusion.2), channel_id=1, source_target_pairs={{0,8},{4,12},{8,0},{12,4},{16,24},{20,28},{24,16},{28,20},{1,9},{5... | collective-permute-start | bytes 6291464 | tf_op jit(solution)/shard_map/ppermute | solution.py:1021
  995.7 49.6 %collective-permute-start.61 = (bf16[200,1024]{1,0:T(8,128)(2,1)}, bf16[200,1024]{1,0:T(8,128)(2,1)}, u32[]{:S(2)}, u32[]{:S(2)}) collective-permute-start(bf16[200,1024]{1,0:T(8,128)(2,1)} %slice.799), channel_id=1, source_target_pairs={{0,16},{4,20},{8,24},{12,28},{16,0},{20,4},{24,8},{28,12},{1,17},{... | collective-permute-start | bytes 1228808 | tf_op jit(solution)/shard_map/ppermute | solution.py:1021
  997.5 47.8 %collective-permute-start.62 = (bf16[200,1024]{1,0:T(8,128)(2,1)}, bf16[200,1024]{1,0:T(8,128)(2,1)}, u32[]{:S(2)}, u32[]{:S(2)}) collective-permute-start(bf16[200,1024]{1,0:T(8,128)(2,1)} %slice.800), channel_id=1, source_target_pairs={{0,8},{4,12},{8,0},{12,4},{16,24},{20,28},{24,16},{28,20},{1,9},{5... | collective-permute-start | bytes 1228808 | tf_op jit(solution)/shard_map/ppermute | solution.py:1021
  999.8 48.7 %collective-permute-start.60 = (bf16[4,128,1024]{2,1,0:T(8,128)(2,1)}, bf16[4,128,1024]{2,1,0:T(8,128)(2,1)}, u32[]{:S(2)}, u32[]{:S(2)}) collective-permute-start(bf16[4,128,1024]{2,1,0:T(8,128)(2,1)} %slice_bitcast_fusion.17), channel_id=1, source_target_pairs={{0,8},{4,12},{8,0},{12,4},{16,24},{20,28},{24,16},{28,20},{1,9},{5... | collective-permute-start | bytes 3145736 | tf_op jit(solution)/shard_map/ppermute | solution.py:1021
  1001.7 49.0 %collective-permute-start.59 = (bf16[4,128,1024]{2,1,0:T(8,128)(2,1)}, bf16[4,128,1024]{2,1,0:T(8,128)(2,1)}, u32[]{:S(2)}, u32[]{:S(2)}) collective-permute-start(bf16[4,128,1024]{2,1,0:T(8,128)(2,1)} %slice_bitcast_fusion.18), channel_id=1, source_target_pairs={{0,16},{4,20},{8,24},{12,28},{16,0},{20,4},{24,8},{28,12},{1,17},{... | collective-permute-start | bytes 3145736 | tf_op jit(solution)/shard_map/ppermute | solution.py:1021
  1052.3 108.0 %collective-permute-start.67 = (bf16[4,4,144,1024]{3,2,1,0:T(8,128)(2,1)}, bf16[4,4,144,1024]{3,2,1,0:T(8,128)(2,1)}, u32[]{:S(2)}, u32[]{:S(2)}) collective-permute-start(bf16[4,4,144,1024]{3,2,1,0:T(8,128)(2,1)} %get-tuple-element.283), channel_id=1, source_target_pairs={{0,4},{4,0},{8,12},{12,8},{16,20},{20,16},{24,28},{28,24},{1,5},{5... | collective-permute-start | bytes 14155784 | tf_op jit(solution)/shard_map/ppermute | solution.py:1021
  1053.2 100.5 %collective-permute-start.80 = (bf16[4,400,1024]{2,1,0:T(8,128)(2,1)}, bf16[4,400,1024]{2,1,0:T(8,128)(2,1)}, u32[]{:S(2)}, u32[]{:S(2)}) collective-permute-start(bf16[4,400,1024]{2,1,0:T(8,128)(2,1)} %pad_maximum_fusion.4), channel_id=1, source_target_pairs={{0,4},{4,0},{8,12},{12,8},{16,20},{20,16},{24,28},{28,24},{1,5},{5... | collective-permute-start | bytes 9830408 | tf_op jit(solution)/shard_map/ppermute | solution.py:1021
  1153.7 66.6 %collective-permute-start.88 = (bf16[4,256,1024]{2,1,0:T(8,128)(2,1)}, bf16[4,256,1024]{2,1,0:T(8,128)(2,1)}, u32[]{:S(2)}, u32[]{:S(2)}) collective-permute-start(bf16[4,256,1024]{2,1,0:T(8,128)(2,1)} %get-tuple-element.338), channel_id=1, source_target_pairs={{0,4},{4,0},{8,12},{12,8},{16,20},{20,16},{24,28},{28,24},{1,5},{5... | collective-permute-start | bytes 6291464 | tf_op jit(solution)/shard_map/ppermute | solution.py:1021
  (139 other events, 2532.3 us)

commit v2 on v1

--- a/solution.py
+++ b/solution.py
@@ -391,7 +391,9 @@
         compiler_params=pltpu.CompilerParams(
             dimension_semantics=("arbitrary",) * len(grid), vmem_limit_bytes=VMEM_LIMIT
         ),
-        cost_estimate=pl.CostEstimate(flops=flops, bytes_accessed=nbytes, transcendentals=0),
+        cost_estimate=pl.CostEstimate(
+            flops=flops // 4, bytes_accessed=nbytes // 4, transcendentals=0
+        ),
     )
 
 
@@ -443,13 +445,36 @@
     return jnp.concatenate(parts, axis=0)
 
 
-def unit_rows(get, row, count):
-    return jnp.concatenate([get(m, row, count) for m in range(4)], axis=0)
+def pair_rows(first, second):
+    return jnp.concatenate([get(m) for get in (first, second) for m in range(4)], axis=0)
+
+
+def feed_specs(down_block):
+    def spec(block):
+        return pl.BlockSpec((4, 1, 128, D), lambda d: (0, jnp.maximum(d - 1, 0), block, 0))
+
+    return [full((2, 4, 256, D)), spec(0), spec(0), spec(down_block), spec(down_block)]
+
+
+def feed_by_offset(d, body, l_ref, wu_ref, vu_ref, wd_ref, vd_ref):
+    @pl.when(d == 0)
+    def _():
+        body(
+            lambda: pair_rows(lambda m: l_ref[0, m, 0:128], lambda m: l_ref[1, m, 0:128]),
+            lambda: pair_rows(lambda m: l_ref[0, m, 128:256], lambda m: l_ref[1, m, 128:256]),
+        )
+
+    @pl.when(d > 0)
+    def _():
+        body(
+            lambda: pair_rows(lambda m: wu_ref[m, 0], lambda m: vu_ref[m, 0]),
+            lambda: pair_rows(lambda m: wd_ref[m, 0], lambda m: vd_ref[m, 0]),
+        )
 
 
 def ln_qkv(hidden, mods, weights, base):
     rows = hidden.shape[0]
-    step = 256
+    step = 640
 
     def kernel(h_ref, m_ref, l_ref, w_ref, v_ref, normed_ref, qkv_ref):
         d = pl.program_id(0)
@@ -498,103 +523,120 @@
             bias_ref[h, s * rows_step : (s + 1) * rows_step, :] = tile
 
 
-def attn_fwd(qkv, base, fc, slides, width, lanes_step, masked):
-    rows = qkv.shape[0]
-    windows = rows // width
+def window_view(values, kind):
+    parts, count, size = kind[0]
+    return values.reshape(parts, count, size, values.shape[-1])
+
+
+def attn_fwd(qkv, base, fc, kind):
+    (parts, count, size), slides, lanes_step, masked = kind
+    rows, width = qkv.shape[0], parts * size
     r_step, lanes = base.shape[1], base.shape[2]
 
     def kernel(x_ref, b_ref, fc_ref, o_ref, bias_ref):
-        @pl.when(pl.program_id(1) == 0)
-        def _():
-            build_bias(b_ref, bias_ref, fc_ref if masked else None, slides, width, lanes_step)
-
-        for h in range(HPZ):
-            q = x_ref[:, h * HD : (h + 1) * HD] * 0.125
-            k = x_ref[:, 256 + h * HD : 256 + (h + 1) * HD]
-            v = x_ref[:, 512 + h * HD : 512 + (h + 1) * HD]
-            score = dot_nt(k, q) + bias_ref[h]
-            expo = jnp.exp(score - jnp.max(score, axis=0, keepdims=True))
-            inv = 1.0 / jnp.sum(expo, axis=0, keepdims=True)
-            probs = (expo * inv).astype(BF16)
-            o_ref[:, h * HD : (h + 1) * HD] = dot_tn(probs, v).astype(BF16)
+        build_bias(b_ref, bias_ref, fc_ref if masked else None, slides, width, lanes_step)
+
+        def one(w, carry):
+            def cut(col):
+                return x_ref[:, w, :, col : col + HD].reshape(width, HD)
+
+            scores, probs = [], []
+            for h in range(HPZ):
+                scores.append(dot_nt(cut(256 + h * HD), cut(h * HD) * 0.125) + bias_ref[h])
+            for h in range(HPZ):
+                expo = jnp.exp(scores[h] - jnp.max(scores[h], axis=0, keepdims=True))
+                inv = 1.0 / jnp.sum(expo, axis=0, keepdims=True)
+                probs.append((expo * inv).astype(BF16))
+            for h in range(HPZ):
+                got = dot_tn(probs[h], cut(512 + h * HD)).astype(BF16)
+                o_ref[:, w, :, h * HD : (h + 1) * HD] = got.reshape(parts, size, HD)
+            return carry
+
+        lax.fori_loop(0, count, one, 0)
 
     return call(
         kernel,
         "attn_fwd",
-        (NZ, windows),
+        (NZ,),
         [
-            pl.BlockSpec((width, 768), lambda z, w: (w, z)),
-            pl.BlockSpec((HPZ, r_step, lanes), lambda z, w: (z, 0, 0)),
+            pl.BlockSpec((parts, count, size, 768), lambda z: (0, 0, 0, z)),
+            pl.BlockSpec((HPZ, r_step, lanes), lambda z: (z, 0, 0)),
             pl.BlockSpec(memory_space=pltpu.SMEM),
         ],
-        pl.BlockSpec((width, 256), lambda z, w: (w, z)),
-        jax.ShapeDtypeStruct((rows, D), BF16),
+        pl.BlockSpec((parts, count, size, 256), lambda z: (0, 0, 0, z)),
+        jax.ShapeDtypeStruct((parts, count, size, D), BF16),
         [pltpu.VMEM((HPZ, width, width), F32)],
-        windows * 16 * width * width * HD * 16,
+        count * 16 * width * width * HD * 16,
         rows * D * 8,
-    )(qkv, base, fc)
-
-
-def attn_bwd(qkv, grad_att, base, fc, slides, width, lanes_step, masked):
-    rows = qkv.shape[0]
-    windows = rows // width
+    )(window_view(qkv, kind), base, fc).reshape(rows, D)
+
+
+def attn_bwd(qkv, grad_att, base, fc, kind):
+    (parts, count, size), slides, lanes_step, masked = kind
+    rows, width = qkv.shape[0], parts * size
     r_step, lanes = base.shape[1], base.shape[2]
 
     def kernel(x_ref, d_ref, b_ref, fc_ref, o_ref, gb_ref, bias_ref, acc_ref):
-        @pl.when(pl.program_id(1) == 0)
-        def _():
-            build_bias(b_ref, bias_ref, fc_ref if masked else None, slides, width, lanes_step)
-            acc_ref[...] = jnp.zeros_like(acc_ref)
-
+        build_bias(b_ref, bias_ref, fc_ref if masked else None, slides, width, lanes_step)
+        acc_ref[...] = jnp.zeros_like(acc_ref)
+
+        def one(w, carry):
+            def cut(ref, col):
+                return ref[:, w, :, col : col + HD].reshape(width, HD)
+
+            def put(col, value):
+                o_ref[:, w, :, col : col + HD] = value.astype(BF16).reshape(parts, size, HD)
+
+            q = [cut(x_ref, h * HD) * 0.125 for h in range(HPZ)]
+            k = [cut(x_ref, 256 + h * HD) for h in range(HPZ)]
+            da = [cut(d_ref, h * HD) for h in range(HPZ)]
+            score = [dot_nt(k[h], q[h]) + bias_ref[h] for h in range(HPZ)]
+            dp = [dot_nt(cut(x_ref, 512 + h * HD), da[h]) for h in range(HPZ)]
+            probs, dl = [], []
+            for h in range(HPZ):
+                expo = jnp.exp(score[h] - jnp.max(score[h], axis=0, keepdims=True))
+                inv = 1.0 / jnp.sum(expo, axis=0, keepdims=True)
+                p = expo * inv
+                row = jnp.sum(dp[h] * p, axis=0, keepdims=True)
+                g = (p * (dp[h] - row)).astype(BF16)
+                acc_ref[h] += g.astype(F32)
+                probs.append(p.astype(BF16))
+                dl.append(g)
+            for h in range(HPZ):
+                put(h * HD, dot_tn(dl[h], k[h]) * 0.125)
+                put(256 + h * HD, dot_nn(dl[h], q[h]))
+                put(512 + h * HD, dot_nn(probs[h], da[h]))
+            return carry
+
+        lax.fori_loop(0, count, one, 0)
+        gb_ref[...] = jnp.zeros_like(gb_ref)
         for h in range(HPZ):
-            q = x_ref[:, h * HD : (h + 1) * HD] * 0.125
-            k = x_ref[:, 256 + h * HD : 256 + (h + 1) * HD]
-            v = x_ref[:, 512 + h * HD : 512 + (h + 1) * HD]
-            da = d_ref[:, h * HD : (h + 1) * HD]
-            score = dot_nt(k, q) + bias_ref[h]
-            expo = jnp.exp(score - jnp.max(score, axis=0, keepdims=True))
-            inv = 1.0 / jnp.sum(expo, axis=0, keepdims=True)
-            probs = expo * inv
-            dp = dot_nt(v, da)
-            row = jnp.sum(dp * probs, axis=0, keepdims=True)
-            dl = (probs * (dp - row)).astype(BF16)
-            acc_ref[h] += dl.astype(F32)
-            o_ref[:, h * HD : (h + 1) * HD] = (dot_tn(dl, k) * 0.125).astype(BF16)
-            o_ref[:, 256 + h * HD : 256 + (h + 1) * HD] = dot_nn(dl, q).astype(BF16)
-            o_ref[:, 512 + h * HD : 512 + (h + 1) * HD] = dot_nn(probs.astype(BF16), da).astype(
-                BF16
-            )
-
-        @pl.when(pl.program_id(1) == windows - 1)
-        def _():
-            gb_ref[...] = jnp.zeros_like(gb_ref)
-            for h in range(HPZ):
-                for s in range(slides):
-                    off = (slides - 1 - s) * lanes_step
-                    gb_ref[h, :, off : off + width] += acc_ref[h, s * r_step : (s + 1) * r_step, :]
-
-    return call(
+            for s in range(slides):
+                off = (slides - 1 - s) * lanes_step
+                gb_ref[h, :, off : off + width] += acc_ref[h, s * r_step : (s + 1) * r_step, :]
+
+    xspec = pl.BlockSpec((parts, count, size, 768), lambda z: (0, 0, 0, z))
+    bspec = pl.BlockSpec((HPZ, r_step, lanes), lambda z: (z, 0, 0))
+    proj, strips = call(
         kernel,
         "attn_bwd",
-        (NZ, windows),
+        (NZ,),
         [
-            pl.BlockSpec((width, 768), lambda z, w: (w, z)),
-            pl.BlockSpec((width, 256), lambda z, w: (w, z)),
-            pl.BlockSpec((HPZ, r_step, lanes), lambda z, w: (z, 0, 0)),
+            xspec,
+            pl.BlockSpec((parts, count, size, 256), lambda z: (0, 0, 0, z)),
+            bspec,
             pl.BlockSpec(memory_space=pltpu.SMEM),
         ],
+        [xspec, bspec],
         [
-            pl.BlockSpec((width, 768), lambda z, w: (w, z)),
-            pl.BlockSpec((HPZ, r_step, lanes), lambda z, w: (z, 0, 0)),
-        ],
-        [
-            jax.ShapeDtypeStruct((rows, 3 * D), BF16),
+            jax.ShapeDtypeStruct((parts, count, size, 3 * D), BF16),
             jax.ShapeDtypeStruct(base.shape, F32),
         ],
         [pltpu.VMEM((HPZ, width, width), F32), pltpu.VMEM((HPZ, width, width), F32)],
-        windows * 16 * width * width * HD * 40,
+        count * 16 * width * width * HD * 40,
         rows * D * 16,
-    )(qkv, grad_att, base, fc)
+    )(window_view(qkv, kind), window_view(grad_att, kind), base, fc)
+    return proj.reshape(rows, 3 * D), strips
 
 
 def out_specs_of(row_block):
@@ -665,23 +707,20 @@
     return x * half, slope
 
 
-def ffn_fwd(shifted, weights, middle, mods, base):
+def ffn_fwd(shifted, weights, down_block, middle, mods, base):
     rows = shifted.shape[0]
-    step = 256
-
-    def kernel(x_ref, l_ref, w_ref, v_ref, mid_ref, m_ref, pre_ref, feed_ref, nx_ref, acc_ref):
+    step = 640
+
+    def kernel(x_ref, *refs):
+        parts, (mid_ref, m_ref, pre_ref, feed_ref, nx_ref, acc_ref) = refs[:5], refs[5:]
         z = pl.program_id(0)
 
-        def work(own, other):
-            halves = (own, other)
-
+        def work(up, down):
             def body(i, carry):
                 sl = chunk_rows(i, step)
-                part = jnp.zeros((step, D), F32)
-                for j, get in enumerate(halves):
-                    pre = dot_nt(x_ref[sl, :], unit_rows(get, 0, 128))
-                    pre_ref[sl, j * 512 : (j + 1) * 512] = pre.astype(BF16)
-                    part += dot_nn(gelu_of(pre).astype(BF16), unit_rows(get, 128, 128))
+                pre = dot_nt(x_ref[sl, :], up())
+                pre_ref[sl, :] = pre.astype(BF16)
+                part = dot_nn(gelu_of(pre).astype(BF16), down())
 
                 @pl.when(z == 0)
                 def _():
@@ -703,13 +742,13 @@
 
             lax.fori_loop(0, rows // step, body, 0)
 
-        by_offset(z, work, l_ref, w_ref, v_ref)
+        feed_by_offset(z, work, *parts)
 
     return call(
         kernel,
         "ffn_fwd",
         (NZ,),
-        [full((rows, D))] + piece_specs(256, 0, 256) + [full((rows, D)), full((12, D))],
+        [full((rows, D))] + feed_specs(down_block) + [full((rows, D)), full((12, D))],
         [pl.BlockSpec((rows, D), lambda z: (0, z)), full((rows, D)), full((rows, D))],
         [
             jax.ShapeDtypeStruct((rows, 4 * D), BF16),
@@ -722,13 +761,13 @@
     )(shifted, *weights, middle, mods)
 
 
-def ffn_bwd(grad, pre, shifted, weights, mods, base):
+def ffn_bwd(grad, pre, shifted, weights, down_block, mods, base):
     rows = grad.shape[0]
-    step = 256
-
-    def kernel(
-        g_ref, p_ref, x_ref, l_ref, w_ref, v_ref, m_ref, keep_ref, send_ref, gs_ref, gf_ref, act_ref, gp_ref
-    ):
+    step = 640
+
+    def kernel(g_ref, p_ref, x_ref, *refs):
+        parts, refs = refs[:5], refs[5:]
+        m_ref, keep_ref, send_ref, gs_ref, gf_ref, act_ref, gp_ref = refs
         z = pl.program_id(0)
 
         @pl.when(z == 0)
@@ -743,32 +782,27 @@
 
             lax.fori_loop(0, rows // step, body, 0)
 
-        def work(own, other):
-            halves = (own, other)
-
+        def work(up, down):
             def body(i, carry):
                 sl = chunk_rows(i, step)
-                part = jnp.zeros((step, D), F32)
-                for j, get in enumerate(halves):
-                    cols = slice(j * 512, (j + 1) * 512)
-                    act, slope = gelu_both(p_ref[sl, cols].astype(F32))
-                    act_ref[sl, cols] = act.astype(BF16)
-                    gpre = (dot_nt(gf_ref[sl, :], unit_rows(get, 128, 128)) * slope).astype(BF16)
-                    gp_ref[sl, cols] = gpre
-                    part += dot_nn(gpre, unit_rows(get, 0, 128))
+                back = dot_nt(gf_ref[sl, :], down())
+                act, slope = gelu_both(p_ref[sl, :].astype(F32))
+                act_ref[sl, :] = act.astype(BF16)
+                gpre = (back * slope).astype(BF16)
+                gp_ref[sl, :] = gpre
+                part = dot_nn(gpre, up())
                 gs_ref[sl, :] += part
                 return carry
 
             lax.fori_loop(0, rows // step, body, 0)
 
-        by_offset(z, work, l_ref, w_ref, v_ref)
+        feed_by_offset(z, work, *parts)
         for j, out_ref in enumerate((keep_ref, send_ref)):
-            for i in range(2):
-                cols = slice(j * 512 + i * 256, j * 512 + (i + 1) * 256)
-                gd = dot_tn(act_ref[:, cols], gf_ref[...]).astype(BF16)
-                gu = dot_tn(gp_ref[:, cols], x_ref[...]).astype(BF16)
-                out_ref[2 * i : 2 * i + 2, 0, 0:128] = gu.reshape(2, 128, D)
-                out_ref[2 * i : 2 * i + 2, 0, 128:256] = gd.reshape(2, 128, D)
+            cols = slice(j * 512, (j + 1) * 512)
+            gd = dot_tn(act_ref[:, cols], gf_ref[...]).astype(BF16)
+            gu = dot_tn(gp_ref[:, cols], x_ref[...]).astype(BF16)
+            out_ref[:, 0, 0:128] = gu.reshape(4, 128, D)
+            out_ref[:, 0, 128:256] = gd.reshape(4, 128, D)
 
     gspec = pl.BlockSpec((4, 1, 256, D), lambda z: (0, z, 0, 0))
     gshape = jax.ShapeDtypeStruct((4, NZ, 256, D), BF16)
@@ -781,7 +815,7 @@
             pl.BlockSpec((rows, D), lambda z: (0, z)),
             full((rows, D)),
         ]
-        + piece_specs(256, 0, 256)
+        + feed_specs(down_block)
         + [full((12, D))],
         [gspec, gspec, full((rows, D))],
         [gshape, gshape, jax.ShapeDtypeStruct((rows, D), F32)],
@@ -855,81 +889,247 @@
     )(grad, grad_shifted, middle, feed, branch, attended, *weights, mods)
 
 
-def qkv_bwd(
-    grad_proj, normed, weights, out_keep, out_send, table_rows, hidden, grad_middle, mods, base, out_dtype
-):
+def qkv_back(grad_proj, weights, hidden, grad_middle, mods, base, out_dtype, pieces):
+    rows = hidden.shape[0]
+    step = 640
+
+    cols = D // pieces
+
+    def kernel(p_ref, l_ref, w_ref, v_ref, h_ref, gm_ref, m_ref, *refs):
+        gh_refs, (s_ref, acc_ref) = refs[:pieces], refs[pieces:]
+        z = pl.program_id(0)
+
+        @pl.when(z == 0)
+        def _():
+            acc_ref[...] = jnp.zeros_like(acc_ref)
+            s_ref[...] = jnp.zeros_like(s_ref)
+
+        def work(own, other):
+            def body(i, carry):
+                sl = chunk_rows(i, step)
+                rows_of = jnp.concatenate([head_rows(own, other, t * 32) for t in range(3)], axis=0)
+                acc_ref[sl, :] += dot_nn(p_ref[sl, :], rows_of)
+                return carry
+
+            lax.fori_loop(0, rows // step, body, 0)
+
+        by_offset(z, work, l_ref, w_ref, v_ref)
+
+        @pl.when(z == NZ - 1)
+        def _():
+            def tail(n, carry):
+                sl = chunk_rows(n, 256)
+                gn = acc_ref[sl, :]
+                hat, rstd = ln_stats(h_ref[sl, :].astype(F32))
+                gh = gm_ref[sl, :] + ln_back(gn, hat, rstd, m_ref[base + 1 : base + 2, :])
+                for i, gh_ref in enumerate(gh_refs):
+                    gh_ref[sl, :] = gh[:, i * cols : (i + 1) * cols].astype(out_dtype)
+                s_ref[0:1, :] += jnp.sum(gn, axis=0, keepdims=True)
+                s_ref[1:2, :] += jnp.sum(gn * hat, axis=0, keepdims=True)
+                return carry
+
+            lax.fori_loop(0, rows // 256, tail, 0)
+
+    return call(
+        kernel,
+        "qkv_back",
+        (NZ,),
+        [pl.BlockSpec((rows, 768), lambda z: (0, z))]
+        + piece_specs(128, 0, 96)
+        + [full((rows, D)), full((rows, D)), full((12, D))],
+        [full((rows, cols))] * pieces + [full((8, D))],
+        [jax.ShapeDtypeStruct((rows, cols), out_dtype)] * pieces
+        + [jax.ShapeDtypeStruct((8, D), F32)],
+        [pltpu.VMEM((rows, D), F32)],
+        6 * rows * D * D,
+        rows * D * 20 + 6 * D * D,
+    )(grad_proj, *weights, hidden, grad_middle, mods)
+
+
+def qkv_grad(grad_proj, normed, out_keep, out_send, table_rows):
     rows = normed.shape[0]
-    step = 256
-
-    def kernel(
-        p_ref, n_ref, l_ref, w_ref, v_ref, ok_ref, os_ref, t_ref, h_ref, gm_ref, m_ref, keep_ref,
-        send_ref, gh_ref, s_ref, acc_ref,
-    ):
-        z = pl.program_id(0)
+    k = 128 if table_rows is None else 144
+
+    def kernel(p_ref, n_ref, ok_ref, os_ref, *rest):
+        keep_ref, send_ref = rest[-2:]
         for t in range(3):
             gw = dot_tn(p_ref[:, t * 256 : (t + 1) * 256], n_ref[...]).astype(BF16)
             split_heads(gw, keep_ref, send_ref, 0, t * 32)
         keep_ref[:, :, 96:128] = ok_ref[...]
         send_ref[:, :, 96:128] = os_ref[...]
-        keep_ref[:, :, 128:144] = t_ref[...]
-        send_ref[:, :, 128:144] = t_ref[...]
-
-        @pl.when(z == 0)
-        def _():
-            acc_ref[...] = jnp.zeros_like(acc_ref)
-            s_ref[...] = jnp.zeros_like(s_ref)
-
-        def work(own, other):
-            def body(i, carry):
-                sl = chunk_rows(i, step)
-                part = jnp.zeros((step, D), F32)
-                for t in range(3):
-                    part += dot_nn(
-                        p_ref[sl, t * 256 : (t + 1) * 256], head_rows(own, other, t * 32)
-                    )
-                acc_ref[sl, :] += part
-                return carry
-
-            lax.fori_loop(0, rows // step, body, 0)
-
-        by_offset(z, work, l_ref, w_ref, v_ref)
-
-        @pl.when(z == NZ - 1)
-        def _():
-            def tail(i, carry):
-                sl = chunk_rows(i, step)
-                gn = acc_ref[sl, :]
-                hat, rstd = ln_stats(h_ref[sl, :].astype(F32))
-                gh = gm_ref[sl, :] + ln_back(gn, hat, rstd, m_ref[base + 1 : base + 2, :])
-                gh_ref[sl, :] = gh.astype(out_dtype)
-                s_ref[0:1, :] += jnp.sum(gn, axis=0, keepdims=True)
-                s_ref[1:2, :] += jnp.sum(gn * hat, axis=0, keepdims=True)
-                return carry
-
-            lax.fori_loop(0, rows // step, tail, 0)
-
-    gspec = pl.BlockSpec((4, 1, 144, D), lambda z: (0, z, 0, 0))
+        if table_rows is not None:
+            keep_ref[:, :, 128:144] = rest[0][...]
+            send_ref[:, :, 128:144] = rest[0][...]
+
+    gspec = pl.BlockSpec((4, 1, k, D), lambda z: (0, z, 0, 0))
     ospec = pl.BlockSpec((4, 1, 32, D), lambda z: (0, z, 0, 0))
     tspec = pl.BlockSpec((4, 1, 16, D), lambda z: (0, z, 0, 0))
-    gshape = jax.ShapeDtypeStruct((4, NZ, 144, D), BF16)
+    gshape = jax.ShapeDtypeStruct((4, NZ, k, D), BF16)
+    extra = () if table_rows is None else (table_rows,)
     return call(
         kernel,
-        "qkv_bwd",
+        "qkv_grad",
         (NZ,),
-        [pl.BlockSpec((rows, 768), lambda z: (0, z)), full((rows, D))]
-        + piece_specs(128, 0, 96)
-        + [ospec, ospec, tspec, full((rows, D)), full((rows, D)), full((12, D))],
-        [gspec, gspec, full((rows, D)), full((8, D))],
+        [pl.BlockSpec((rows, 768), lambda z: (0, z)), full((rows, D)), ospec, ospec]
+        + [tspec] * len(extra),
+        [gspec, gspec],
+        [gshape, gshape],
+        [],
+        6 * rows * D * D,
+        rows * D * 8 + 8 * D * D,
+    )(grad_proj, normed, out_keep, out_send, *extra)
+
+
+def place_call(kernel, name, in_specs, out_specs, out_shape, scratch, nbytes, aliases):
+    return pl.pallas_call(
+        kernel,
+        name=name,
+        grid_spec=pltpu.PrefetchScalarGridSpec(
+            num_scalar_prefetch=1,
+            grid=(8,),
+            in_specs=in_specs,
+            out_specs=out_specs,
+            scratch_shapes=scratch,
+        ),
+        out_shape=out_shape,
+        input_output_aliases=aliases,
+        compiler_params=pltpu.CompilerParams(
+            dimension_semantics=("arbitrary",), vmem_limit_bytes=VMEM_LIMIT
+        ),
+        cost_estimate=pl.CostEstimate(flops=0, bytes_accessed=nbytes, transcendentals=0),
+    )
+
+
+def rows_at(place):
+    return pl.ds(pl.multiple_of(place * 32, 32), 32)
+
+
+def prep_attn(place, w_qkv, w_out, b):
+    def kernel(c_ref, q_ref, o_ref, out_ref, t_ref):
+        r = pl.program_id(0)
+
+        @pl.when(r == 0)
+        def _():
+            for t in range(3):
+                t_ref[t] = q_ref[0, t].T
+
+        at = rows_at(c_ref[0] ^ r)
+        for t in range(3):
+            out_ref[0, 0, t * 32 : (t + 1) * 32, :] = t_ref[t, at, :]
+        out_ref[0, 0, 96:128, :] = o_ref[0, at, :]
+
+    return place_call(
+        kernel,
+        "prep_attn",
         [
-            gshape,
-            gshape,
-            jax.ShapeDtypeStruct((rows, D), out_dtype),
-            jax.ShapeDtypeStruct((8, D), F32),
+            pl.BlockSpec((1, 3, D, 256), lambda r, c: (b, 0, 0, 0)),
+            pl.BlockSpec((1, 256, D), lambda r, c: (b, 0, 0)),
         ],
-        [pltpu.VMEM((rows, D), F32)],
-        12 * rows * D * D,
-        rows * D * 20 + 12 * D * D,
-    )(grad_proj, normed, *weights, out_keep, out_send, table_rows, hidden, grad_middle, mods)
+        pl.BlockSpec((1, 1, 128, D), lambda r, c: (r % 2, r // 2, 0, 0)),
+        jax.ShapeDtypeStruct((2, 4, 128, D), BF16),
+        [pltpu.VMEM((3, 256, D), BF16)],
+        4 * D * D,
+        {},
+    )(place, w_qkv, w_out)
+
+
+def prep_feed(place, w_up, w_down, b):
+    def kernel(c_ref, u_ref, d_ref, out_ref):
+        out_ref[0, 0, 0:128, :] = u_ref[0].T
+        out_ref[0, 0, 128:256, :] = d_ref[0]
+
+    return place_call(
+        kernel,
+        "prep_feed",
+        [
+            pl.BlockSpec((1, D, 128), lambda r, c: (b, 0, c[0] ^ r)),
+            pl.BlockSpec((1, 128, D), lambda r, c: (b, c[0] ^ r, 0)),
+        ],
+        pl.BlockSpec((1, 1, 256, D), lambda r, c: (r % 2, r // 2, 0, 0)),
+        jax.ShapeDtypeStruct((2, 4, 256, D), BF16),
+        [],
+        8 * D * D,
+        {},
+    )(place, w_up, w_down)
+
+
+def finish_attn(place, own, other, b, earlier, block):
+
+    def kernel(c_ref, own_ref, oth_ref, *rest):
+        gq_ref, go_ref, t_ref = rest[-3:]
+        r = pl.program_id(0)
+        at = rows_at(c_ref[0] ^ r)
+
+        def store(ref):
+            for t in range(3):
+                t_ref[t, at, :] = ref[0, t * 32 : (t + 1) * 32, :]
+            go_ref[0, at, :] = ref[0, 96:128, :].astype(F32)
+
+        @pl.when(r % 2 == 0)
+        def _():
+            store(own_ref)
+
+        @pl.when(r % 2 == 1)
+        def _():
+            store(oth_ref)
+
+        @pl.when(r == 7)
+        def _():
+            for t in range(3):
+                gq_ref[0, t] = t_ref[t].T.astype(F32)
+
+    piece = pl.BlockSpec((1, 128, D), lambda r, c: (r // 2, block, 0))
+    anywhere = pl.BlockSpec(memory_space=pl.ANY)
+    return place_call(
+        kernel,
+        "finish_attn",
+        [piece, piece] + [anywhere] * len(earlier),
+        [
+            pl.BlockSpec((1, 3, D, 256), lambda r, c: (b, 0, 0, 0)),
+            pl.BlockSpec((1, 256, D), lambda r, c: (b, 0, 0)),
+        ],
+        [
+            jax.ShapeDtypeStruct((2, 3, D, 256), F32),
+            jax.ShapeDtypeStruct((2, 256, D), F32),
+        ],
+        [pltpu.VMEM((3, 256, D), BF16)],
+        6 * D * D,
+        {3 + i: i for i in range(len(earlier))},
+    )(place, own, other, *earlier)
+
+
+def finish_feed(place, own, other, b, earlier):
+    def kernel(c_ref, own_ref, oth_ref, *rest):
+        gu_ref, gd_ref = rest[-2:]
+        r = pl.program_id(0)
+
+        def store(ref):
+            gu_ref[0] = ref[0, 0:128, :].T.astype(F32)
+            gd_ref[0] = ref[0, 128:256, :].astype(F32)
+
+        @pl.when(r % 2 == 0)
+        def _():
+            store(own_ref)
+
+        @pl.when(r % 2 == 1)
+        def _():
+            store(oth_ref)
+
+    piece = pl.BlockSpec((1, 256, D), lambda r, c: (r // 2, 0, 0))
+    anywhere = pl.BlockSpec(memory_space=pl.ANY)
+    return place_call(
+        kernel,
+        "finish_feed",
+        [piece, piece] + [anywhere] * len(earlier),
+        [
+            pl.BlockSpec((1, D, 128), lambda r, c: (b, 0, c[0] ^ r)),
+            pl.BlockSpec((1, 128, D), lambda r, c: (b, c[0] ^ r, 0)),
+        ],
+        [jax.ShapeDtypeStruct((2, D, D), F32), jax.ShapeDtypeStruct((2, D, D), F32)],
+        [],
+        12 * D * D,
+        {3 + i: i for i in range(len(earlier))},
+    )(place, own, other, *earlier)
 
 
 def partner(values):
@@ -945,15 +1145,21 @@
     keep = jnp.where(odd == 0, left, right)
     got = partner(jnp.where(odd == 0, right, left))
     top, bottom = jnp.where(odd == 0, keep, got), jnp.where(odd == 0, got, keep)
-    return jnp.concatenate([wins, top, bottom], axis=0)
+    part = jnp.concatenate([top, bottom], axis=0)
+    return jnp.where(
+        odd == 0,
+        jnp.concatenate([wins, part], axis=0),
+        jnp.concatenate([part, wins], axis=0),
+    )
 
 
 def spatial_to_rows(wins, odd):
     cols = wins.shape[1]
-    whole = wins[:1024].reshape(2, 2, 16, 16, cols).transpose(0, 2, 1, 3, 4).reshape(1024, cols)
-    top, bottom = wins[1024:1152], wins[1152:]
-    keep = jnp.where(odd == 0, top, bottom)
-    got = partner(jnp.where(odd == 0, bottom, top))
+    whole = lax.dynamic_slice(wins, (256 * odd, 0), (1024, cols))
+    part = lax.dynamic_slice(wins, (1024 * (1 - odd), 0), (256, cols))
+    whole = whole.reshape(2, 2, 16, 16, cols).transpose(0, 2, 1, 3, 4).reshape(1024, cols)
+    keep = jnp.where(odd == 0, part[:128], part[128:])
+    got = partner(jnp.where(odd == 0, part[128:], part[:128]))
     left, right = jnp.where(odd == 0, keep, got), jnp.where(odd == 0, got, keep)
     part = jnp.stack([left.reshape(8, 16, cols), right.reshape(8, 16, cols)], axis=1)
     part = part.reshape(256, cols)
@@ -964,35 +1170,20 @@
     )
 
 
-def block_order():
-    places = {}
-    for z in range(NZ):
-        first = 5 * (z // 2)
-        halves = (first, first + 1) if z % 2 == 0 else (first + 3, first + 4)
-        listed = [(h, x) for h in halves for x in (0, 1)] + [(first + 2, z % 2)]
-        for k, item in enumerate(listed):
-            places[item] = z * 5 + k
-    return [places[(2 * t + wy, wx)] for wy in (0, 1) for wx in (0, 1) for t in range(PADF)]
-
-
 def exchange(values):
     return lax.all_to_all(values, "head", 0, 0, tiled=True)
 
 
 def spatial_to_tubes(wins):
     cols = wins.shape[1]
-    quads = wins.reshape(5, 2, 8, 2, 8, cols).transpose(1, 3, 0, 2, 4, 5).reshape(1280, cols)
-    got = exchange(quads)
-    return jnp.concatenate([got[64 * b : 64 * (b + 1)] for b in block_order()], axis=0)
-
-
-def tubes_to_spatial(tubes):
-    cols = tubes.shape[1]
-    order = block_order()
-    back = [order.index(b) for b in range(20)]
-    got = exchange(jnp.concatenate([tubes[64 * b : 64 * (b + 1)] for b in back], axis=0))
-    quads = got.reshape(2, 2, 5, 8, 8, cols).transpose(2, 0, 3, 1, 4, 5)
-    return quads.reshape(1280, cols)
+    return exchange(
+        wins.reshape(5, 2, 8, 2, 8, cols).transpose(1, 3, 0, 2, 4, 5).reshape(1280, cols)
+    )
+
+
+def from_quads(quads):
+    cols = quads.shape[1]
+    return quads.reshape(2, 2, 5, 8, 8, cols).transpose(2, 0, 3, 1, 4, 5).reshape(1280, cols)
 
 
 def toeplitz(side):
@@ -1025,10 +1216,6 @@
     return lax.ppermute(values, "head", [((i + d) % NZ, i) for i in range(NZ)])
 
 
-def to_z(values, d):
-    return lax.ppermute(values, "head", [(i, (i + d) % NZ) for i in range(NZ)])
-
-
 def sync(*values):
     return lax.optimization_barrier(values)
 
@@ -1038,61 +1225,66 @@
 
 
 def line_stage(piece):
-    return jnp.stack([from_z(piece, d) for d in (1, 2, 3)])
+    return [from_z(piece, d) for d in (1, 2, 3)]
+
+
+def others(by_z, z):
+    return [lax.dynamic_index_in_dim(by_z, (z + d) % NZ, 0, keepdims=False) for d in (1, 2, 3)]
 
 
 def cross_stage(own):
-    return own, swap(own, ROW_X), swap(own, ROW_Y)
-
-
-def corner_stage(crossed, axis):
-    own, by_x, by_y = crossed
-    half = own.shape[axis] // 2
-    first = swap(lax.slice_in_dim(by_x, 0, half, axis=axis), ROW_Y)
-    second = swap(lax.slice_in_dim(by_y, half, 2 * half, axis=axis), ROW_X)
-    return jnp.stack([own, by_x, by_y, jnp.concatenate([first, second], axis=axis)])
-
-
-def sum_core(pair):
-    return add(pair[0], swap(pair[1], CORE))
-
-
-def sum_cross(total):
-    k = total.shape[2]
-    total = total.reshape(2, 2, NZ, k, D)
-    first, second = total[:, :, :, : k // 2], total[:, :, :, k // 2 :]
-    first = add(first[:, 0], swap(first[:, 1], ROW_X))
-    second = add(second[0], swap(second[1], ROW_Y))
+    return [own] + [swap(own, m * 2) for m in (1, 2, 3)]
+
+
+def sum_core(keep, got):
+    return [add(keep[m], got[m]) for m in range(4)]
+
+
+def send_plane(totals, offsets):
+    return [swap(totals[m], m * 2) for m in offsets]
+
+
+def to_places(total, z):
+    twice = jnp.concatenate([total, total[: NZ - 1]], axis=0)
+    return lax.dynamic_slice_in_dim(twice, (NZ - z) % NZ, NZ, axis=0)
+
+
+def sum_plane(totals, got, z):
+    total = totals[0].astype(F32)
+    for value in got:
+        total = total + value.astype(F32)
+    return to_places(total.astype(BF16), z)
+
+
+def send_cross(totals):
+    half = totals[0].shape[1] // 2
+    first = [t[:, :half] for t in totals]
+    second = [t[:, half:] for t in totals]
+    by_x = swap(jnp.stack([first[1], first[3]]), ROW_X)
+    by_y = swap(jnp.stack([second[2], second[3]]), ROW_Y)
+    return by_x, by_y
+
+
+def sum_cross(totals, got):
+    half = totals[0].shape[1] // 2
+    by_x, by_y = got
+    first = [add(totals[0][:, :half], by_x[0]), add(totals[2][:, :half], by_x[1])]
+    second = [add(totals[0][:, half:], by_y[0]), add(totals[1][:, half:], by_y[1])]
     return first, second
 
 
-def sum_corner(halves):
-    first, second = halves
-    first = add(first[0], swap(first[1], ROW_Y))
-    second = add(second[0], swap(second[1], ROW_X))
-    return first, second
-
-
-def sum_line(halves):
-    first, second = halves
-    mine = jnp.concatenate([first[0], second[0]], axis=0).astype(F32)
-    for d in (1, 2, 3):
-        part = to_z(jnp.concatenate([first[d], second[d]], axis=0), d)
-        mine = mine + part.astype(F32)
-    return mine.astype(BF16)
-
-
-def sum_z(values):
-    total = values
-    for d in (1, 2, 3):
-        total = total + from_z(values, d)
-    return total
-
-
-def by_place(blocks, c):
-    return jnp.concatenate(
-        [lax.dynamic_slice_in_dim(blocks, c ^ i, 1, axis=0) for i in range(8)], axis=0
-    )
+def send_corner(halves):
+    return swap(halves[0][1], ROW_Y), swap(halves[1][1], ROW_X)
+
+
+def sum_corner(halves, got, z):
+    first = add(halves[0][0], got[0])
+    second = add(halves[1][0], got[1])
+    return to_places(jnp.concatenate([first, second], axis=1), z)
+
+
+def sum_line(by_z):
+    return lax.psum_scatter(by_z, "head", scatter_dimension=0)
 
 
 def on_device_windows(
@@ -1100,30 +1292,13 @@
 ):
     z = lax.axis_index("head")
     c = lax.axis_index("clip")
+    place = c.astype(jnp.int32).reshape(1)
     chip = c // 2
     odd = z % 2
     mods = modulation[0]
     n_s, n_t = table_s.shape[1], table_t.shape[1]
     hot_s, hot_t = toeplitz(SWIN), toeplitz_pair(TWIN)
-
-    def own_pieces(b):
-        qkv = lax.dynamic_slice_in_dim(w_qkv[b], c * 32, 32, 2).transpose(0, 2, 1)
-        out = lax.dynamic_slice_in_dim(w_out[b], c * 32, 32, 0)
-        up = lax.dynamic_slice_in_dim(w_up[b], c * 128, 128, 1).T
-        down = lax.dynamic_slice_in_dim(w_down[b], c * 128, 128, 0)
-        return (
-            jnp.concatenate([qkv.reshape(96, D), out], axis=0),
-            jnp.concatenate([up, down], axis=0),
-        )
-
-    def local_pieces(qkv, out, up, down):
-        up = up.T.reshape(8, 128, D)
-        down = down.reshape(8, 128, D)
-        qkv = qkv.transpose(0, 2, 1).reshape(3, 8, 32, D).transpose(1, 0, 2, 3)
-        attn = jnp.concatenate([qkv.reshape(8, 96, D), out.reshape(8, 32, D)], axis=1)
-        feed = jnp.concatenate([up, down], axis=1)
-        moved = [by_place(value, c) for value in (attn, feed)]
-        return [v.reshape((4, 2) + v.shape[1:]).transpose(1, 0, 2, 3) for v in moved]
+    fc = frame_counts
 
     def spatial_base(tables):
         base = jnp.einsum(
@@ -1137,165 +1312,200 @@
         ).reshape(16, 64, 576)
         return jnp.pad(base, ((0, 0), (0, 0), (0, 64)))
 
-    def table_rows(values):
-        values = jnp.pad(values, ((0, 0), (0, 16 * D - values.shape[1]))).astype(BF16)
+    def table_rows(first, second):
+        first = jnp.pad(first, ((0, 0), (0, D - n_s)))
+        second = jnp.pad(second, ((0, 0), (0, 15 * D - n_t)))
+        values = jnp.concatenate([first, second], axis=1).astype(BF16)
         return values.reshape(NZ, 4, 16, D).transpose(1, 0, 2, 3)
 
-    kinds = ((16, 256, 16, False), (5, 320, 64, True))
-
-    piece_a0, piece_f0 = own_pieces(0)
-    line_a0 = line_stage(piece_a0)
+    spatial = ((1, 5, 256), 16, 16, False)
+    tube = ((5, 4, 64), 5, 64, True)
+
+    local_a0 = prep_attn(place, w_qkv, w_out, 0)
+    line_a0 = line_stage(local_a0[0, 0])
     table_piece = jnp.concatenate([table_s, table_t], axis=1)
-    tables = jnp.stack([table_piece] + [from_z(table_piece, d) for d in (1, 2, 3)])
-    line_a0, piece_f0, tables = sync(line_a0, piece_f0, tables)
-    line_f0 = line_stage(piece_f0)
-    own_a0 = corner_stage(cross_stage(line_a0), 1)
-    other_a0 = swap(own_a0, CORE)
+    tables = [from_z(table_piece, d) for d in (1, 2)]
+    local_f0 = prep_feed(place, w_up, w_down, 0)
+    local_a1 = prep_attn(place, w_qkv, w_out, 1)
+    local_f1 = prep_feed(place, w_up, w_down, 1)
+    line_a0, local_f0, local_a1, local_f1, tables, tokens, table_piece = sync(
+        line_a0, local_f0, local_a1, local_f1, tables, tokens, table_piece
+    )
+    own_a0 = cross_stage(jnp.stack(line_a0))
+    z_u0 = lax.all_gather(local_f0[0, 0, :128], "head")
+    z_d0 = lax.all_gather(local_f0[0, 0, 128:], "head")
+    tables = jnp.stack([table_piece] + tables + [from_z(table_piece, 3)])
     tables = jnp.concatenate(
         [lax.dynamic_slice_in_dim(tables, chip ^ m, 1, axis=1) for m in range(4)], axis=1
     ).reshape(16, n_s + n_t)
     base_s = spatial_base(tables)
     hidden0 = rows_to_spatial(tokens, odd)
-    local_a0, local_f0 = local_pieces(w_qkv[0], w_out[0], w_up[0], w_down[0])
-    own_a0, other_a0, line_f0, base_s, hidden0, local_a0, local_f0, tables = sync(
-        own_a0, other_a0, line_f0, base_s, hidden0, local_a0, local_f0, tables
-    )
+    own_a0, hidden0, tables, base_s, z_u0 = sync(own_a0, hidden0, tables, base_s, z_u0)
+    own_a0 = jnp.stack(own_a0)
+    other_a0 = swap(own_a0, CORE)
+    own_u0 = cross_stage(jnp.stack(others(z_u0, z)))
+    own_a0, other_a0 = sync(own_a0, other_a0)
     weights_a0 = (local_a0, own_a0, other_a0)
-    cross_f0 = cross_stage(line_f0)
-    piece_a1, piece_f1 = own_pieces(1)
-    line_a1 = line_stage(piece_a1)
     normed0, qkv0 = ln_qkv(hidden0, mods, weights_a0, 0)
-    attended0 = attn_fwd(qkv0, base_s, frame_counts, *kinds[0])
-    attended0, cross_f0, line_a1, piece_f1 = sync(attended0, cross_f0, line_a1, piece_f1)
-    own_f0 = corner_stage(cross_f0, 1)
-    other_f0 = swap(own_f0, CORE)
+    qkv0, own_u0, z_d0 = sync(qkv0, own_u0, z_d0)
+    own_d0 = cross_stage(jnp.stack(others(z_d0, z)))
+    own_u0 = jnp.stack(own_u0)
+    other_u0 = swap(own_u0, CORE)
+    z_a1 = lax.all_gather(local_a1[0, 0], "head")
+    attended0 = attn_fwd(qkv0, base_s, fc, spatial)
     branch0, middle0, shifted0 = out_proj(attended0, weights_a0, hidden0, mods, 0)
-    shifted0, own_f0, other_f0, line_a1, piece_f1 = sync(
-        shifted0, own_f0, other_f0, line_a1, piece_f1
-    )
-    weights_f0 = (local_f0, own_f0, other_f0)
-    line_f1 = line_stage(piece_f1)
-    cross_a1 = cross_stage(line_a1)
-    pre0, feed0, hidden1 = ffn_fwd(shifted0, weights_f0, middle0, mods, 0)
-    hidden1, line_f1, cross_a1, tables, d_out, w_qkv, w_out, w_up, w_down = sync(
-        hidden1, line_f1, cross_a1, tables, d_out, w_qkv, w_out, w_up, w_down
-    )
+    shifted0, own_d0, other_u0, z_a1 = sync(shifted0, own_d0, other_u0, z_a1)
+    own_d0 = jnp.stack(own_d0)
+    other_d0 = swap(own_d0, CORE)
+    z_f1 = lax.all_gather(local_f1[0, 0], "head")
+    own_a1 = jnp.stack(others(z_a1, z))
+    shifted0, other_d0, own_a1 = sync(shifted0, other_d0, own_a1)
+    own_a1 = cross_stage(own_a1)
+    weights_f0 = (local_f0, own_u0, other_u0, own_d0, other_d0)
+    pre0, feed0, hidden1 = ffn_fwd(shifted0, weights_f0, 0, middle0, mods, 0)
+    hidden1, z_f1, own_a1, tables, d_out = sync(hidden1, z_f1, own_a1, tables, d_out)
     tubes1 = spatial_to_tubes(hidden1)
-    own_a1 = corner_stage(cross_a1, 1)
+    own_a1 = jnp.stack(own_a1)
     other_a1 = swap(own_a1, CORE)
-    cross_f1 = cross_stage(line_f1)
-    local_a1, local_f1 = local_pieces(w_qkv[1], w_out[1], w_up[1], w_down[1])
+    own_f1 = cross_stage(jnp.stack(others(z_f1, z)))
     base_t = tube_base(tables)
     spatial_d = rows_to_spatial(d_out, odd)
-    tubes1, own_a1, other_a1, cross_f1, local_a1, local_f1, base_t, spatial_d = sync(
-        tubes1, own_a1, other_a1, cross_f1, local_a1, local_f1, base_t, spatial_d
-    )
+    tubes1, other_a1, base_t, spatial_d = sync(tubes1, other_a1, base_t, spatial_d)
     weights_a1 = (local_a1, own_a1, other_a1)
-    own_f1 = corner_stage(cross_f1, 1)
     tubes_d = spatial_to_tubes(spatial_d)
     normed1, qkv1 = ln_qkv(tubes1, mods, weights_a1, 6)
     qkv1, own_f1 = sync(qkv1, own_f1)
+    own_f1 = jnp.stack(own_f1)
     other_f1 = swap(own_f1, CORE)
-    attended1 = attn_fwd(qkv1, base_t, frame_counts, *kinds[1])
+    attended1 = attn_fwd(qkv1, base_t, fc, tube)
     branch1, middle1, shifted1 = out_proj(attended1, weights_a1, tubes1, mods, 6)
     shifted1, other_f1 = sync(shifted1, other_f1)
-    weights_f1 = (local_f1, own_f1, other_f1)
-    pre1, feed1, hidden2 = ffn_fwd(shifted1, weights_f1, middle1, mods, 6)
-    frame = lax.broadcasted_iota(jnp.int32, (1280, 1), 0) % 320 // 64
-    live = frame < frame_counts[0]
+    weights_f1 = (local_f1, own_f1, other_f1, own_f1, other_f1)
+    pre1, feed1, hidden2 = ffn_fwd(shifted1, weights_f1, 1, middle1, mods, 6)
+    hidden2, tubes_d = sync(hidden2, tubes_d)
+    live = lax.broadcasted_iota(jnp.int32, (1280, 1), 0) // 256 < fc[0]
     grad2 = jnp.where(live, tubes_d, 0)
-    hidden2, grad2 = sync(hidden2, grad2)
-    out_wins = tubes_to_spatial(jnp.where(live, hidden2, 0))
-    f1_keep, f1_send, g_shift1 = ffn_bwd(grad2, pre1, shifted1, weights_f1, mods, 6)
+    out_wins = exchange(jnp.where(live, hidden2, 0))
+    f1_keep, f1_send, g_shift1 = ffn_bwd(grad2, pre1, shifted1, weights_f1, 1, mods, 6)
     f1_keep, f1_send, g_shift1, out_wins = sync(f1_keep, f1_send, g_shift1, out_wins)
-    total_f1 = sum_core((f1_keep, f1_send))
+    f1_got = swap(f1_send, CORE)
     g_mid1, g_att1, o1_keep, o1_send, sums_o1 = out_bwd(
         grad2, g_shift1, middle1, feed1, branch1, attended1, weights_a1, mods, 6
     )
-    g_att1, total_f1, out_wins = sync(g_att1, total_f1, out_wins)
-    half_f1 = sum_cross(total_f1)
-    g_proj1, g_base1 = attn_bwd(qkv1, g_att1, base_t, frame_counts, *kinds[1])
-    g_proj1, g_base1, half_f1 = sync(g_proj1, g_base1, half_f1)
-    half_f1 = sum_corner(half_f1)
+    g_att1, f1_got = sync(g_att1, f1_got)
+    total_f1 = sum_core(f1_keep, f1_got)
+    g_att1, total_f1 = sync(g_att1, total_f1)
+    got_f1 = send_plane(total_f1, (1, 2))
+    g_proj1, g_base1 = attn_bwd(qkv1, g_att1, base_t, fc, tube)
+    g_proj1, g_base1, got_f1 = sync(g_proj1, g_base1, got_f1)
+    g_hid1a, g_hid1b, sums_q1 = qkv_back(
+        g_proj1, weights_a1, tubes1, g_mid1, mods, 6, BF16, 2
+    )
+    g_hid1a, g_hid1b, g_proj1, out_wins, g_base1 = sync(
+        g_hid1a, g_hid1b, g_proj1, out_wins, g_base1
+    )
+    grad1a = exchange(g_hid1a)
+    corner_a = swap(total_f1[3][:, :128], ROW_X + ROW_Y)
+    a1_keep, a1_send = qkv_grad(g_proj1, normed1, o1_keep, o1_send, None)
     gt_t = jnp.einsum(
         "hjtk,rjk->htr",
         g_base1[:, :, :576].reshape(16, 64, 9, 64),
         hot_t,
         precision=HIGHEST_PRECISION,
     ).reshape(16, n_t)
-    a1_keep, a1_send, g_hid1, sums_q1 = qkv_bwd(
-        g_proj1, normed1, weights_a1, o1_keep, o1_send, table_rows(gt_t), tubes1, g_mid1, mods, 6, BF16
-    )
-    a1_keep, a1_send, g_hid1, half_f1 = sync(a1_keep, a1_send, g_hid1, half_f1)
-    grad1 = tubes_to_spatial(g_hid1)
-    half_a1 = sum_corner(sum_cross(sum_core((a1_keep, a1_send))))
-    mod1 = jnp.concatenate([sums_q1[0:2], sums_o1[2:3], sums_o1[0:2], sums_o1[3:4]], axis=0)
-    output = spatial_to_rows(out_wins, odd)
-    grad1, half_a1, half_f1, output = sync(grad1, half_a1, half_f1, output)
-    mine_f1, mine_a1 = sum_line(half_f1), sum_line(half_a1)
-    f0_keep, f0_send, g_shift0 = ffn_bwd(grad1, pre0, shifted0, weights_f0, mods, 0)
-    f0_keep, f0_send, g_shift0, mine_f1, mine_a1 = sync(
-        f0_keep, f0_send, g_shift0, mine_f1, mine_a1
-    )
-    total_f0 = sum_core((f0_keep, f0_send))
-    cross1 = cross_stage(jnp.concatenate([mine_f1, mine_a1], axis=0))
+    grad1a, corner_a, a1_keep, a1_send, gt_t, g_hid1b, out_wins = sync(
+        grad1a, corner_a, a1_keep, a1_send, gt_t, g_hid1b, out_wins
+    )
+    grad1b = exchange(g_hid1b)
+    corner_b = swap(total_f1[3][:, 128:], ROW_X + ROW_Y)
+    a1_got = swap(a1_send, CORE)
+    output = spatial_to_rows(from_quads(out_wins), odd)
+    grad1b, a1_got, corner_b, output = sync(grad1b, a1_got, corner_b, output)
+    grad1 = from_quads(jnp.concatenate([grad1a, grad1b], axis=1))
+    got_f1 = got_f1 + [jnp.concatenate([corner_a, corner_b], axis=1)]
+    z_f1 = sum_plane(total_f1, got_f1, z)
+    total_a1 = sum_core(a1_keep, a1_got)
+    grad1, z_f1, total_a1 = sync(grad1, z_f1, total_a1)
+    mine_f1 = sum_line(z_f1)
+    got_a1 = send_plane(total_a1, (1, 2, 3))
+    f0_keep, f0_send, g_shift0 = ffn_bwd(grad1, pre0, shifted0, weights_f0, 0, mods, 0)
+    f0_keep, f0_send, g_shift0, mine_f1, got_a1 = sync(f0_keep, f0_send, g_shift0, mine_f1, got_a1)
+    f0_got = swap(f0_send, CORE)
+    own_gf1 = cross_stage(mine_f1)
+    mine_a1 = sum_line(sum_plane(total_a1, got_a1, z))
     g_mid0, g_att0, o0_keep, o0_send, sums_o0 = out_bwd(
         grad1, g_shift0, middle0, feed0, branch0, attended0, weights_a0, mods, 0
     )
-    g_att0, total_f0, cross1 = sync(g_att0, total_f0, cross1)
-    half_f0 = sum_cross(total_f0)
-    g_proj0, g_base0 = attn_bwd(qkv0, g_att0, base_s, frame_counts, *kinds[0])
-    g_proj0, g_base0, half_f0, cross1 = sync(g_proj0, g_base0, half_f0, cross1)
-    half_f0 = sum_corner(half_f0)
-    plane1 = corner_stage(cross1, 0)
+    g_att0, f0_got, own_gf1 = sync(g_att0, f0_got, own_gf1)
+    total_f0 = sum_core(f0_keep, f0_got)
+    own_gf1 = jnp.stack(own_gf1)
+    g_att0, total_f0, own_gf1 = sync(g_att0, total_f0, own_gf1)
+    got_f0 = send_cross(total_f0)
+    other_gf1 = swap(own_gf1, CORE)
+    g_proj0, g_base0 = attn_bwd(qkv0, g_att0, base_s, fc, spatial)
     gt_s = jnp.einsum(
         "hjai,bji->hab",
         g_base0[:, :, :496].reshape(16, 16, 31, 16),
         hot_s,
         precision=HIGHEST_PRECISION,
     ).reshape(16, n_s)
-    a0_keep, a0_send, grad0, sums_q0 = qkv_bwd(
-        g_proj0, normed0, weights_a0, o0_keep, o0_send, table_rows(gt_s), hidden0, g_mid0, mods, 0, F32
-    )
-    a0_keep, a0_send, grad0, half_f0, plane1, sums_q0 = sync(
-        a0_keep, a0_send, grad0, half_f0, plane1, sums_q0
-    )
-    mod0 = jnp.concatenate([sums_q0[0:2], sums_o0[2:3], sums_o0[0:2], sums_o0[3:4]], axis=0)
+    a0_keep, a0_send = qkv_grad(g_proj0, normed0, o0_keep, o0_send, table_rows(gt_s, gt_t))
+    a0_keep, a0_send, got_f0, mine_a1, other_gf1, g_proj0 = sync(
+        a0_keep, a0_send, got_f0, mine_a1, other_gf1, g_proj0
+    )
+    a0_got = swap(a0_send, CORE)
+    half_f0 = sum_cross(total_f0, got_f0)
+    got_f0 = send_corner(half_f0)
+    g_feed = finish_feed(place, own_gf1, other_gf1, 1, ())
+    half_f0, got_f0, a0_got, g_feed, g_proj0 = sync(half_f0, got_f0, a0_got, g_feed, g_proj0)
+    total_a0 = sum_core(a0_keep, a0_got)
+    z_f0 = sum_corner(half_f0, got_f0, z)
+    total_a0, z_f0, g_proj0 = sync(total_a0, z_f0, g_proj0)
+    got_a0 = send_cross(total_a0)
+    mine_f0 = sum_line(z_f0)
+    grad0, sums_q0 = qkv_back(g_proj0, weights_a0, hidden0, g_mid0, mods, 0, F32, 1)
+    grad0, sums_q0, got_a0 = sync(grad0, sums_q0, got_a0)
+    half_a0 = sum_cross(total_a0, got_a0)
+    half_a0, grad0, sums_q0 = sync(half_a0, grad0, sums_q0)
+    got_a0 = send_corner(half_a0)
     grad_tokens = spatial_to_rows(grad0, odd)
-    grad_mods = sum_z(jnp.concatenate([mod0, mod1], axis=0))[None]
-    mine_f0 = sum_line(half_f0)
-    mine_a0 = sum_line(sum_corner(sum_cross(sum_core((a0_keep, a0_send)))))
-    plane0f = corner_stage(cross_stage(mine_f0), 0)
-    plane0a = corner_stage(cross_stage(mine_a0), 0)
-
-    def placed(plane):
-        both = jnp.stack([plane, swap(plane, CORE)], axis=1)
-        return by_place(both.reshape((8,) + plane.shape[1:]), c)
-
-    done1 = placed(plane1)
-    pairs = ((placed(plane0f), placed(plane0a)), (done1[:, :256], done1[:, 256:]))
-    g_qkv, g_out, g_up, g_down = [], [], [], []
-    for feed, attn in pairs:
-        g_qkv.append(
-            attn[:, :96].reshape(8, 3, 32, D).transpose(1, 3, 0, 2).reshape(3, D, 256).astype(F32)
-        )
-        g_out.append(attn[:, 96:128].reshape(256, D).astype(F32))
-        g_up.append(feed[:, :128].reshape(D, D).T.astype(F32))
-        g_down.append(feed[:, 128:].reshape(D, D).astype(F32))
-
-    def table_of(attn, size):
-        return attn[::2, 128:144].reshape(4, 16 * D)[:, :size].astype(F32)
-
+    mod_rows = jnp.concatenate(
+        [
+            sums_q0[0:2], sums_o0[2:3], sums_o0[0:2], sums_o0[3:4],
+            sums_q1[0:2], sums_o1[2:3], sums_o1[0:2], sums_o1[3:4],
+        ],
+        axis=0,
+    )
+    got_a0, mine_f0, mod_rows, grad_tokens = sync(got_a0, mine_f0, mod_rows, grad_tokens)
+    mine_a0 = sum_line(sum_corner(half_a0, got_a0, z))
+    crossed = cross_stage(jnp.concatenate([mine_f0, mine_a1], axis=0))
+    mod_got = [from_z(mod_rows, 1), from_z(mod_rows, 2)]
+    mine_a0, crossed, mod_got = sync(mine_a0, crossed, mod_got)
+    own_ga0 = cross_stage(mine_a0)
+    crossed = jnp.stack(crossed)
+    other_crossed = swap(crossed, CORE)
+    mod_got = mod_got + [from_z(mod_rows, 3)]
+    own_ga0, other_crossed, mod_got = sync(own_ga0, other_crossed, mod_got)
+    own_ga0 = jnp.stack(own_ga0)
+    other_ga0 = swap(own_ga0, CORE)
+    g_feed = finish_feed(place, crossed, other_crossed, 0, g_feed)
+    g_attn = finish_attn(place, crossed, other_crossed, 1, (), 2)
+    other_ga0, g_feed, g_attn = sync(other_ga0, g_feed, g_attn)
+    g_attn = finish_attn(place, own_ga0, other_ga0, 0, g_attn, 0)
+    tab = jnp.concatenate(
+        [lax.dynamic_slice_in_dim(own_ga0, chip ^ m, 1, axis=0) for m in range(4)], axis=0
+    )
+    tab = tab[:, 128:144].reshape(4, 16 * D).astype(F32)
     return (
         output,
         grad_tokens,
-        grad_mods,
-        jnp.stack(g_qkv),
-        jnp.stack(g_out),
-        jnp.stack(g_up),
-        jnp.stack(g_down),
-        table_of(pairs[0][1], n_s),
-        table_of(pairs[1][1], n_t),
+        (mod_rows + mod_got[0] + mod_got[1] + mod_got[2])[None],
+        g_attn[0],
+        g_attn[1],
+        g_feed[0],
+        g_feed[1],
+        tab[:, :n_s],
+        tab[:, D : D + n_t],
     )
 
 

time: 1300 us -> 1020 us (0.78)
  local copies, waits for them, and re-layouts: 221 us -> 89.6 us
  waiting for transfers between devices: 220 us -> 162 us
  starting transfers between devices: 141 us -> 93.1 us
  other arithmetic: 144 us -> 109 us
  Pallas kernels: 539 us -> 525 us
    ppermute x18 -> x9, waiting for transfers between devices: 74.6 us -> 15.8 us  [from_z(): return lax.ppermute(values, 'head', [((i + d) % NZ, i) for i in range(NZ)])]
    unnamed x263 -> x97, local copies, waits for them, and re-layouts: 65.9 us -> 12.5 us
    ppermute x12 -> x0, starting transfers between devices: 33.7 us -> none  [to_z(): return lax.ppermute(values, 'head', [(i, (i + d) % NZ) for i in range(NZ)])]
    slice x31 -> x9, local copies, waits for them, and re-layouts: 41.4 us -> 8.92 us  [the longest x1 2.27 us: on_device_windows(): z_f1 = lax.all_gather(local_f1[0, 0], 'head')]
    ppermute x12 -> x0, waiting for transfers between devices: 26.5 us -> none  [to_z(): return lax.ppermute(values, 'head', [(i, (i + d) % NZ) for i in range(NZ)])]
    another operation x27 -> x18, other arithmetic: 57.4 us -> 32 us  [the longest x1 6.74 us: on_device_windows(): own_f1 = jnp.stack(own_f1)]
    convert_element_type x16 -> x10, other arithmetic: 55.2 us -> 37.3 us  [add(): return (first.astype(F32) + second.astype(F32)).astype(BF16)]
    pallas_call x2, Pallas kernels: 141 us -> 123 us  [ffn_bwd(): call(kernel, 'ffn_bwd', (NZ,), [full((rows, D)), pl.BlockSpec((rows, D),...]
  transfers between devices with their start and end apart: 93 -> 77, of which waited for: 30 -> 30; matrix products, arithmetic and copies ran while one was open for 23% -> 14% of each run, Pallas kernels for 39% -> 49%
where the time goes in v2:
time: 1020 us; the launch traced here: 1010 us
  Pallas kernels  525 us (51%)
  waiting for transfers between devices  162 us (16%)
  other arithmetic  109 us (11%)
  starting transfers between devices  93.1 us (9%)
  local copies, waits for them, and re-layouts  89.6 us (9%)
  matrix products  17.4 us (2%)
  between operations  16.4 us (2%)
    pallas_call x2, Pallas kernels, ffn_bwd(): call(kernel, 'ffn_bwd', (NZ,), [full((rows, D)), pl.BlockSpec((rows, D),...  123 us
    ppermute x51, waiting for transfers between devices, swap(): return lax.ppermute(values, 'clip', [(i, i ^ bit) for i in range(8)])  83.1 us
    pallas_call x2, Pallas kernels, attn_bwd(): call(kernel, 'attn_bwd', (NZ,), [xspec, pl.BlockSpec((parts, count, size,...  75.6 us
    pallas_call x2, Pallas kernels, ffn_fwd(): call(kernel, 'ffn_fwd', (NZ,), [full((rows, D))] + feed_specs(down_block)...  70.1 us
    ppermute x51, starting transfers between devices, swap(): return lax.ppermute(values, 'clip', [(i, i ^ bit) for i in range(8)])  45.9 us
    pallas_call x2, Pallas kernels, attn_fwd(): call(kernel, 'attn_fwd', (NZ,), [pl.BlockSpec((parts, count, size, 768),...  43.2 us
    ppermute x4, waiting for transfers between devices, partner(): return lax.ppermute(values, 'head', [(i, i ^ 1) for i in range(NZ)])  43.2 us
    pallas_call x2, Pallas kernels, qkv_back(): call(kernel, 'qkv_back', (NZ,), [pl.BlockSpec((rows, 768), lambda z: (0,...  41.7 us
  transfers between devices with their start and end apart: 77, of which 30 were waited for; matrix products, arithmetic and copies ran while one was open for 14% of the time, Pallas kernels for 49%

profile of v2, /device:TPU:0, one launch (start us, length us, event | category | flops | bytes accessed | tf_op | source)
XLA Modules:
  0.0 1011.9 jit_solution(1214453937537584755)
XLA Ops:
  30.5 6.9 prep_feed.3.refs_0_
  71.9 10.7 %collective-permute-done.6 = bf16[3,128,1024]{2,1,0:T(8,128)(2,1)} collective-permute-done((bf16[3,128,1024]{2,1,0:T(8,128)(2,1)S(1)}, bf16[3,128,1024]{2,1,0:T(8,128)(2,1)}, u32[]{:S(2)}, u32[]{:S(2)}) %collective-permute-start.6) | collective-permute-done | bytes 786464 | tf_op jit(solution)/shard_map/ppermute | solution.py:1212
  94.9 16.0 %ln_qkv.2 = (bf16[1280,1024]{1,0:T(8,128)(2,1)}, bf16[1280,3072]{1,0:T(8,128)(2,1)}) custom-call(bf16[1280,1024]{1,0:T(8,128)(2,1)} %maximum_select_fusion.1.h_ref, f32[12,1024]{1,0:T(8,128)} %bitcast.264, bf16[2,4,128,1024]{3,2,1,0:T(8,128)(2,1)} %prep_attn.2.l_ref, bf16[4,3,128,1024]{3,2,1,0:T(8,128)(2,1)} %copy-done.2, ...), custom_call_target="tpu_custom_call" | custom-call | flops 2013265920 | bytes 5505024 | tf_op jit(solution)/shard_map/ln_qkv/pallas_call | solution.py:502
  115.4 13.1 %collective-permute-done.12 = bf16[3,128,1024]{2,1,0:T(8,128)(2,1)} collective-permute-done((bf16[3,128,1024]{2,1,0:T(8,128)(2,1)}, bf16[3,128,1024]{2,1,0:T(8,128)(2,1)}, u32[]{:S(2)}, u32[]{:S(2)}) %collective-permute-start.12) | collective-permute-done | bytes 786464 | tf_op jit(solution)/shard_map/ppermute | solution.py:1212
  139.4 20.4 %attn_fwd.2 = bf16[1,5,256,1024]{3,2,1,0:T(8,128)(2,1)} custom-call(bf16[1,5,256,3072]{3,2,1,0:T(8,128)(2,1)} %bitcast.284, f32[16,16,512]{2,1,0:T(8,128)} %pad.18.b_ref, s32[1]{0:T(128)} %copy.102.fc_ref), custom_call_target="tpu_custom_call" | custom-call | flops 1342177280 | bytes 2621440 | tf_op jit(solution)/shard_map/attn_fwd/pallas_call | solution.py:557
  159.8 9.3 out_proj.2
  184.5 35.0 %ffn_fwd.2 = (bf16[1280,4096]{1,0:T(8,128)(2,1)}, bf16[1280,1024]{1,0:T(8,128)(2,1)}, bf16[1280,1024]{1,0:T(8,128)(2,1)}) custom-call(bf16[1280,1024]{1,0:T(8,128)(2,1)} %get-tuple-element.263.x_ref, bf16[2,4,256,1024]{3,2,1,0:T(8,128)(2,1)} %prep_feed.2.refs_0_, bf16[4,3,128,1024]{3,2,1,0:T(8,128)(2,1)} %copy-done.8, ...), custom_call_target="tpu_custom_call" | custom-call | flops 5368709120 | bytes 10747904 | tf_op jit(solution)/shard_map/ffn_fwd/pallas_call | solution.py:747
  267.7 11.4 %collective-permute-done.23 = bf16[128,1024]{1,0:T(8,128)(2,1)} collective-permute-done((bf16[128,1024]{1,0:T(8,128)(2,1)}, bf16[128,1024]{1,0:T(8,128)(2,1)}, u32[]{:S(2)}, u32[]{:S(2)}) %collective-permute-start.23) | collective-permute-done | bytes 262176 | tf_op jit(solution)/shard_map/ppermute | solution.py:1136
  282.7 7.9 all-to-all-done
  290.6 16.1 %ln_qkv.3 = (bf16[1280,1024]{1,0:T(8,128)(2,1)}, bf16[1280,3072]{1,0:T(8,128)(2,1)}) custom-call(bf16[1280,1024]{1,0:T(8,128)(2,1)} %bitcast.39.h_ref, f32[12,1024]{1,0:T(8,128)} %bitcast.267, bf16[2,4,128,1024]{3,2,1,0:T(8,128)(2,1)} %prep_attn.3.l_ref, bf16[4,3,128,1024]{3,2,1,0:T(8,128)(2,1)} %copy-done.3, ...), custom_call_target="tpu_custom_call" | custom-call | flops 2013265920 | bytes 5505024 | tf_op jit(solution)/shard_map/ln_qkv/pallas_call | solution.py:502
  321.1 22.8 %attn_fwd.3 = bf16[5,4,64,1024]{3,2,1,0:T(8,128)(2,1)} custom-call(bf16[5,4,64,3072]{3,2,1,0:T(8,128)(2,1)} %bitcast.282, f32[16,64,640]{2,1,0:T(8,128)} %pad.19.b_ref, s32[1]{0:T(128)} %copy.102.fc_ref), custom_call_target="tpu_custom_call" | custom-call | flops 1677721600 | bytes 2621440 | tf_op jit(solution)/shard_map/attn_fwd/pallas_call | solution.py:557
  343.9 9.3 out_proj.3
  353.2 35.1 %ffn_fwd.3 = (bf16[1280,4096]{1,0:T(8,128)(2,1)}, bf16[1280,1024]{1,0:T(8,128)(2,1)}, bf16[1280,1024]{1,0:T(8,128)(2,1)}) custom-call(bf16[1280,1024]{1,0:T(8,128)(2,1)} %get-tuple-element.289.x_ref, bf16[2,4,256,1024]{3,2,1,0:T(8,128)(2,1)} %prep_feed.3.refs_0_, bf16[4,3,256,1024]{3,2,1,0:T(8,128)(2,1)} %pad_maximum_fusion.refs_1_.refs_3_, ...), custom_call_target="tpu_custom_call" | custom-call | flops 5368709120 | bytes 10747904 | tf_op jit(solution)/shard_map/ffn_fwd/pallas_call | solution.py:747
  397.8 61.3 %ffn_bwd.2 = (bf16[4,4,256,1024]{3,2,1,0:T(8,128)(2,1)}, bf16[4,4,256,1024]{3,2,1,0:T(8,128)(2,1)}, f32[1280,1024]{1,0:T(8,128)}) custom-call(bf16[1280,1024]{1,0:T(8,128)(2,1)} %get-tuple-element.549.g_ref, bf16[1280,4096]{1,0:T(8,128)(2,1)} %get-tuple-element.295.p_ref, bf16[1280,1024]{1,0:T(8,128)(2,1)} %get-tuple-element.289.x_ref, ...), custom_call_target="tpu_custom_call" | custom-call | flops 10737418240 | bytes 13631488 | tf_op jit(solution)/shard_map/ffn_bwd/pallas_call | solution.py:809
  459.2 19.1 %out_bwd.2 = (f32[1280,1024]{1,0:T(8,128)}, bf16[1280,1024]{1,0:T(8,128)(2,1)}, bf16[4,4,32,1024]{3,2,1,0:T(8,128)(2,1)}, bf16[4,4,32,1024]{3,2,1,0:T(8,128)(2,1)}, f32[8,1024]{1,0:T(8,128)}) custom-call(bf16[1280,1024]{1,0:T(8,128)(2,1)} %get-tuple-element.549.g_ref, f32[1280,1024]{1,0:T(8,128)} %get-tuple-element.300.gs_ref, ...), custom_call_target="tpu_custom_call" | custom-call | flops 1342177280 | bytes 8912896 | tf_op jit(solution)/shard_map/out_bwd/pallas_call | solution.py:873
  478.3 9.6 fusion.14
  489.9 42.7 %attn_bwd.2 = (bf16[5,4,64,3072]{3,2,1,0:T(8,128)(2,1)}, f32[16,64,640]{2,1,0:T(8,128)}) custom-call(bf16[5,4,64,3072]{3,2,1,0:T(8,128)(2,1)} %bitcast.283, bf16[5,4,64,1024]{3,2,1,0:T(8,128)(2,1)} %bitcast.329, f32[16,64,640]{2,1,0:T(8,128)} %pad.19.b_ref, s32[1]{0:T(128)} %copy.102.fc_ref), custom_call_target="tpu_custom_call" | custom-call | flops 4194304000 | bytes 5242880 | tf_op jit(solution)/shard_map/attn_bwd/pallas_call | solution.py:620
  536.5 20.2 %qkv_back.2 = (bf16[1280,512]{1,0:T(8,128)(2,1)}, bf16[1280,512]{1,0:T(8,128)(2,1)}, f32[8,1024]{1,0:T(8,128)}) custom-call(bf16[1280,3072]{1,0:T(8,128)(2,1)} %bitcast.244, bf16[2,4,128,1024]{3,2,1,0:T(8,128)(2,1)} %prep_attn.3.l_ref, bf16[4,3,128,1024]{3,2,1,0:T(8,128)(2,1)} %copy-done.3, bf16[4,3,128,1024]{3,2,1,0:T(8,128)(2,1)} %collective-permute-done.22.v_ref, ...), custom_call_target="tpu_custom_call" | custom-call | flops 2013265920 | bytes 8126464 | tf_op jit(solution)/shard_map/qkv_back/pallas_call | solution.py:933
  582.3 13.1 %qkv_grad.2 = (bf16[4,4,128,1024]{3,2,1,0:T(8,128)(2,1)}, bf16[4,4,128,1024]{3,2,1,0:T(8,128)(2,1)}) custom-call(bf16[1280,3072]{1,0:T(8,128)(2,1)} %bitcast.245, bf16[1280,1024]{1,0:T(8,128)(2,1)} %get-tuple-element.322.n_ref, bf16[4,4,32,1024]{3,2,1,0:T(8,128)(2,1)} %get-tuple-element.323.ok_ref, bf16[4,4,32,1024]{3,2,1,0:T(8,128)(2,1)} %get-tuple-element.324.os_ref), custom_call_target="tpu_custom_call" | custom-call | flops 2013265920 | bytes 4718592 | tf_op jit(solution)/shard_map/qkv_grad/pallas_call | solution.py:969
  606.5 21.6 %collective-permute-done.34 = bf16[128,1024]{1,0:T(8,128)(2,1)S(1)} collective-permute-done((bf16[128,1024]{1,0:T(8,128)(2,1)S(1)}, bf16[128,1024]{1,0:T(8,128)(2,1)S(1)}, u32[]{:S(2)}, u32[]{:S(2)}) %collective-permute-start.34) | collective-permute-done | bytes 262176 | tf_op jit(solution)/shard_map/ppermute | solution.py:1136
  654.3 62.2 %ffn_bwd.3 = (bf16[4,4,256,1024]{3,2,1,0:T(8,128)(2,1)}, bf16[4,4,256,1024]{3,2,1,0:T(8,128)(2,1)}, f32[1280,1024]{1,0:T(8,128)}) custom-call(bf16[1280,1024]{1,0:T(8,128)(2,1)} %bitcast.257, bf16[1280,4096]{1,0:T(8,128)(2,1)} %get-tuple-element.344.p_ref, bf16[1280,1024]{1,0:T(8,128)(2,1)} %get-tuple-element.263.x_ref, ...), custom_call_target="tpu_custom_call" | custom-call | flops 10737418240 | bytes 13631488 | tf_op jit(solution)/shard_map/ffn_bwd/pallas_call | solution.py:809
  723.8 18.5 %out_bwd.3 = (f32[1280,1024]{1,0:T(8,128)}, bf16[1280,1024]{1,0:T(8,128)(2,1)}, bf16[4,4,32,1024]{3,2,1,0:T(8,128)(2,1)}, bf16[4,4,32,1024]{3,2,1,0:T(8,128)(2,1)}, f32[8,1024]{1,0:T(8,128)}) custom-call(bf16[1280,1024]{1,0:T(8,128)(2,1)} %bitcast.258, f32[1280,1024]{1,0:T(8,128)} %get-tuple-element.352.gs_ref, ...), custom_call_target="tpu_custom_call" | custom-call | flops 1342177280 | bytes 8912896 | tf_op jit(solution)/shard_map/out_bwd/pallas_call | solution.py:873
  743.2 9.0 fusion.18
  761.1 32.9 %attn_bwd.3 = (bf16[1,5,256,3072]{3,2,1,0:T(8,128)(2,1)}, f32[16,16,512]{2,1,0:T(8,128)}) custom-call(bf16[1,5,256,3072]{3,2,1,0:T(8,128)(2,1)} %bitcast.285, bf16[1,5,256,1024]{3,2,1,0:T(8,128)(2,1)} %bitcast.328, f32[16,16,512]{2,1,0:T(8,128)} %pad.18.b_ref, s32[1]{0:T(128)} %copy.102.fc_ref), custom_call_target="tpu_custom_call" | custom-call | flops 3355443200 | bytes 5242880 | tf_op jit(solution)/shard_map/attn_bwd/pallas_call | solution.py:620
  803.5 13.4 %qkv_grad.3 = (bf16[4,4,144,1024]{3,2,1,0:T(8,128)(2,1)}, bf16[4,4,144,1024]{3,2,1,0:T(8,128)(2,1)}) custom-call(bf16[1280,3072]{1,0:T(8,128)(2,1)} %bitcast.242, bf16[1280,1024]{1,0:T(8,128)(2,1)} %get-tuple-element.367.n_ref, bf16[4,4,32,1024]{3,2,1,0:T(8,128)(2,1)} %get-tuple-element.368.ok_ref, bf16[4,4,32,1024]{3,2,1,0:T(8,128)(2,1)} %get-tuple-element.369.os_ref, ...), custom_call_target="tpu_custom_call" | custom-call | flops 2013265920 | bytes 4718592 | tf_op jit(solution)/shard_map/qkv_grad/pallas_call | solution.py:969
  824.7 9.0 finish_feed.2
  833.6 14.0 %collective-permute-done.45 = bf16[4,128,1024]{2,1,0:T(8,128)(2,1)S(1)} collective-permute-done((bf16[4,128,1024]{2,1,0:T(8,128)(2,1)}, bf16[4,128,1024]{2,1,0:T(8,128)(2,1)S(1)}, u32[]{:S(2)}, u32[]{:S(2)}) %collective-permute-start.45) | collective-permute-done | bytes 1048608 | tf_op jit(solution)/shard_map/ppermute | solution.py:1212
  864.7 21.4 %qkv_back.3 = (f32[1280,1024]{1,0:T(8,128)}, f32[8,1024]{1,0:T(8,128)}) custom-call(bf16[1280,3072]{1,0:T(8,128)(2,1)} %bitcast.243, bf16[2,4,128,1024]{3,2,1,0:T(8,128)(2,1)} %prep_attn.2.l_ref, bf16[4,3,128,1024]{3,2,1,0:T(8,128)(2,1)} %copy-done.2, bf16[4,3,128,1024]{3,2,1,0:T(8,128)(2,1)} %collective-permute-done.10.v_ref, ...), custom_call_target="tpu_custom_call" | custom-call | flops 2013265920 | bytes 8126464 | tf_op jit(solution)/shard_map/qkv_back/pallas_call | solution.py:933
  901.4 10.1 %collective-permute-done.52 = f32[128,1024]{1,0:T(8,128)S(1)} collective-permute-done((f32[128,1024]{1,0:T(8,128)S(1)}, f32[128,1024]{1,0:T(8,128)S(1)}, u32[]{:S(2)}, u32[]{:S(2)}) %collective-permute-start.52) | collective-permute-done | bytes 524320 | tf_op jit(solution)/shard_map/ppermute | solution.py:1136
  941.7 16.5 %collective-permute-done.54 = bf16[384,1024]{1,0:T(8,128)(2,1)S(1)} collective-permute-done((bf16[384,1024]{1,0:T(8,128)(2,1)S(1)}, bf16[384,1024]{1,0:T(8,128)(2,1)S(1)}, u32[]{:S(2)}, u32[]{:S(2)}) %collective-permute-start.54) | collective-permute-done | bytes 786464 | tf_op jit(solution)/shard_map/ppermute | solution.py:1212
  987.6 9.0 finish_feed.3
  997.6 7.0 finish_attn.3
  (380 shorter events, 370.7 us)
Async XLA Ops:
  7.2 78.3 %all-gather.9.cloned.1.call-start = ((), (), s32[]{:S(2)}) async-start(), calls=%async_computation.13 | async-start | bytes 1310720 | tf_op jit(solution)/shard_map/all_gather | solution.py:1335
  56.1 59.2 %all-gather.11.cloned.1.call-start = ((), (), s32[]{:S(2)}) async-start(), calls=%async_computation.14 | async-start | bytes 1310720 | tf_op jit(solution)/shard_map/all_gather | solution.py:1336
  87.6 81.5 %all-gather.13.cloned.1.call-start = ((), (), s32[]{:S(2)}) async-start(), calls=%async_computation.15 | async-start | bytes 1310720 | tf_op jit(solution)/shard_map/all_gather | solution.py:1354
  92.2 36.2 %collective-permute-start.12 = (bf16[3,128,1024]{2,1,0:T(8,128)(2,1)}, bf16[3,128,1024]{2,1,0:T(8,128)(2,1)}, u32[]{:S(2)}, u32[]{:S(2)}) collective-permute-start(bf16[3,128,1024]{2,1,0:T(8,128)(2,1)} %pad_maximum_fusion.16), channel_id=1, source_target_pairs={{0,16},{4,20},{8,24},{12,28},{16,0},{20,4},{24,8},{28,12},{1,17},{... | collective-permute-start | bytes 2359304 | tf_op jit(solution)/shard_map/ppermute | solution.py:1212
  130.5 42.5 %collective-permute-start.17 = (bf16[4,3,128,1024]{3,2,1,0:T(8,128)(2,1)S(1)}, bf16[4,3,128,1024]{3,2,1,0:T(8,128)(2,1)}, u32[]{:S(2)}, u32[]{:S(2)}) collective-permute-start(bf16[4,3,128,1024]{3,2,1,0:T(8,128)(2,1)S(1)} %pad_maximum_fusion.2.refs_1_), channel_id=1, source_target_pairs={{0,4},{4,0},{8,12},{12,8},{16,20},{20,16},{24,28},{28,24},{1,5},{5... | collective-permute-start | bytes 9437192 | tf_op jit(solution)/shard_map/ppermute | solution.py:1212
  132.5 90.0 %all-gather.15.cloned.1.call-start = ((), (), s32[]{:S(2)}) async-start(), calls=%async_computation.16 | async-start | bytes 2621440 | tf_op jit(solution)/shard_map/all_gather | solution.py:1360
  181.0 41.5 %collective-permute-start.19 = (bf16[3,128,1024]{2,1,0:T(8,128)(2,1)}, bf16[3,128,1024]{2,1,0:T(8,128)(2,1)}, u32[]{:S(2)}, u32[]{:S(2)}) collective-permute-start(bf16[3,128,1024]{2,1,0:T(8,128)(2,1)} %pad_maximum_fusion.18), channel_id=1, source_target_pairs={{0,8},{4,12},{8,0},{12,4},{16,24},{20,28},{24,16},{28,20},{1,9},{5... | collective-permute-start | bytes 2359304 | tf_op jit(solution)/shard_map/ppermute | solution.py:1212
  181.8 40.7 %collective-permute-start.20 = (bf16[3,128,1024]{2,1,0:T(8,128)(2,1)}, bf16[3,128,1024]{2,1,0:T(8,128)(2,1)}, u32[]{:S(2)}, u32[]{:S(2)}) collective-permute-start(bf16[3,128,1024]{2,1,0:T(8,128)(2,1)} %pad_maximum_fusion.18), channel_id=1, source_target_pairs={{0,16},{4,20},{8,24},{12,28},{16,0},{20,4},{24,8},{28,12},{1,17},{... | collective-permute-start | bytes 2359304 | tf_op jit(solution)/shard_map/ppermute | solution.py:1212
  183.3 39.2 %collective-permute-start.21 = (bf16[3,128,1024]{2,1,0:T(8,128)(2,1)}, bf16[3,128,1024]{2,1,0:T(8,128)(2,1)}, u32[]{:S(2)}, u32[]{:S(2)}) collective-permute-start(bf16[3,128,1024]{2,1,0:T(8,128)(2,1)} %pad_maximum_fusion.18), channel_id=1, source_target_pairs={{0,24},{4,28},{8,16},{12,20},{16,8},{20,12},{24,0},{28,4},{1,25},{... | collective-permute-start | bytes 2359304 | tf_op jit(solution)/shard_map/ppermute | solution.py:1212
  226.1 64.5 %all-to-all-start = ((bf16[4,320,1024]{2,1,0:T(8,128)(2,1)}), bf16[4,320,1024]{2,1,0:T(8,128)(2,1)}, u32[]{:S(2)}, u32[]{:S(2)}) async-start(bf16[4,320,1024]{2,1,0:T(8,128)(2,1)} %bitcast.38), calls=%async_computation | async-start | bytes 5242880 | tf_op jit(solution)/shard_map/all_to_all | solution.py:1174
  233.1 49.6 %collective-permute-start.22 = (bf16[4,3,128,1024]{3,2,1,0:T(8,128)(2,1)S(1)}, bf16[4,3,128,1024]{3,2,1,0:T(8,128)(2,1)}, u32[]{:S(2)}, u32[]{:S(2)}) collective-permute-start(bf16[4,3,128,1024]{3,2,1,0:T(8,128)(2,1)S(1)} %pad_maximum_fusion.4.w_ref), channel_id=1, source_target_pairs={{0,4},{4,0},{8,12},{12,8},{16,20},{20,16},{24,28},{28,24},{1,5},{5... | collective-permute-start | bytes 9437192 | tf_op jit(solution)/shard_map/ppermute | solution.py:1212
  235.3 71.3 %collective-permute-start.24 = (bf16[3,256,1024]{2,1,0:T(8,128)(2,1)}, bf16[3,256,1024]{2,1,0:T(8,128)(2,1)}, u32[]{:S(2)}, u32[]{:S(2)}) collective-permute-start(bf16[3,256,1024]{2,1,0:T(8,128)(2,1)} %pad_maximum_fusion.10), channel_id=1, source_target_pairs={{0,8},{4,12},{8,0},{12,4},{16,24},{20,28},{24,16},{28,20},{1,9},{5... | collective-permute-start | bytes 4718600 | tf_op jit(solution)/shard_map/ppermute | solution.py:1212
  236.8 70.6 %collective-permute-start.25 = (bf16[3,256,1024]{2,1,0:T(8,128)(2,1)}, bf16[3,256,1024]{2,1,0:T(8,128)(2,1)}, u32[]{:S(2)}, u32[]{:S(2)}) collective-permute-start(bf16[3,256,1024]{2,1,0:T(8,128)(2,1)} %pad_maximum_fusion.10), channel_id=1, source_target_pairs={{0,16},{4,20},{8,24},{12,28},{16,0},{20,4},{24,8},{28,12},{1,17},{... | collective-permute-start | bytes 4718600 | tf_op jit(solution)/shard_map/ppermute | solution.py:1212
  238.3 69.2 %collective-permute-start.26 = (bf16[3,256,1024]{2,1,0:T(8,128)(2,1)}, bf16[3,256,1024]{2,1,0:T(8,128)(2,1)}, u32[]{:S(2)}, u32[]{:S(2)}) collective-permute-start(bf16[3,256,1024]{2,1,0:T(8,128)(2,1)} %pad_maximum_fusion.10), channel_id=1, source_target_pairs={{0,24},{4,28},{8,16},{12,20},{16,8},{20,12},{24,0},{28,4},{1,25},{... | collective-permute-start | bytes 4718600 | tf_op jit(solution)/shard_map/ppermute | solution.py:1212
  240.7 38.5 %collective-permute-start.23 = (bf16[128,1024]{1,0:T(8,128)(2,1)}, bf16[128,1024]{1,0:T(8,128)(2,1)}, u32[]{:S(2)}, u32[]{:S(2)}) collective-permute-start(bf16[128,1024]{1,0:T(8,128)(2,1)} %bitcast.54), channel_id=1, source_target_pairs={{0,1},{1,0},{2,3},{3,2},{4,5},{5,4},{6,7},{7,6},{8,9},{9,8},{10,11... | collective-permute-start | bytes 786440 | tf_op jit(solution)/shard_map/ppermute | solution.py:1136
  314.2 39.0 %collective-permute-start.27 = (bf16[4,3,256,1024]{3,2,1,0:T(8,128)(2,1)}, bf16[4,3,256,1024]{3,2,1,0:T(8,128)(2,1)}, u32[]{:S(2)}, u32[]{:S(2)}) collective-permute-start(bf16[4,3,256,1024]{3,2,1,0:T(8,128)(2,1)} %pad_maximum_fusion.refs_1_.refs_3_), channel_id=1, source_target_pairs={{0,4},{4,0},{8,12},{12,8},{16,20},{20,16},{24,28},{28,24},{1,5},{5... | collective-permute-start | bytes 18874376 | tf_op jit(solution)/shard_map/ppermute | solution.py:1212
  316.0 72.3 %all-to-all-start.1 = ((bf16[4,320,1024]{2,1,0:T(8,128)(2,1)}), bf16[4,320,1024]{2,1,0:T(8,128)(2,1)S(1)}, u32[]{:S(2)}, u32[]{:S(2)}) async-start(bf16[4,320,1024]{2,1,0:T(8,128)(2,1)} %bitcast.64), calls=%async_computation.1 | async-start | bytes 5242880 | tf_op jit(solution)/shard_map/all_to_all | solution.py:1174
  392.3 66.8 %all-to-all-start.2 = ((bf16[4,320,1024]{2,1,0:T(8,128)(2,1)}), bf16[4,320,1024]{2,1,0:T(8,128)(2,1)S(1)}, u32[]{:S(2)}, u32[]{:S(2)}) async-start(bf16[4,320,1024]{2,1,0:T(8,128)(2,1)} %bitcast.263), calls=%async_computation.2 | async-start | bytes 5242880 | tf_op jit(solution)/shard_map/all_to_all | solution.py:1174
  487.9 47.6 %collective-permute-start.29 = (bf16[4,256,1024]{2,1,0:T(8,128)(2,1)}, bf16[4,256,1024]{2,1,0:T(8,128)(2,1)S(1)}, u32[]{:S(2)}, u32[]{:S(2)}) collective-permute-start(bf16[4,256,1024]{2,1,0:T(8,128)(2,1)} %get-tuple-element.311), channel_id=1, source_target_pairs={{0,8},{4,12},{8,0},{12,4},{16,24},{20,28},{24,16},{28,20},{1,9},{5... | collective-permute-start | bytes 6291464 | tf_op jit(solution)/shard_map/ppermute | solution.py:1212
  489.1 47.4 %collective-permute-start.30 = (bf16[4,256,1024]{2,1,0:T(8,128)(2,1)}, bf16[4,256,1024]{2,1,0:T(8,128)(2,1)}, u32[]{:S(2)}, u32[]{:S(2)}) collective-permute-start(bf16[4,256,1024]{2,1,0:T(8,128)(2,1)} %get-tuple-element.312), channel_id=1, source_target_pairs={{0,16},{4,20},{8,24},{12,28},{16,0},{20,4},{24,8},{28,12},{1,17},{... | collective-permute-start | bytes 6291464 | tf_op jit(solution)/shard_map/ppermute | solution.py:1212
  556.8 38.7 %all-to-all-start.3 = ((bf16[4,320,512]{2,1,0:T(8,128)(2,1)}), bf16[4,320,512]{2,1,0:T(8,128)(2,1)S(1)}, u32[]{:S(2)}, u32[]{:S(2)}) async-start(bf16[4,320,512]{2,1,0:T(8,128)(2,1)} %bitcast.300), calls=%async_computation.3 | async-start | bytes 2621440 | tf_op jit(solution)/shard_map/all_to_all | solution.py:1174
  595.4 37.3 %collective-permute-start.32 = (bf16[4,4,128,1024]{3,2,1,0:T(8,128)(2,1)}, bf16[4,4,128,1024]{3,2,1,0:T(8,128)(2,1)}, u32[]{:S(2)}, u32[]{:S(2)}) collective-permute-start(bf16[4,4,128,1024]{3,2,1,0:T(8,128)(2,1)} %get-tuple-element.331), channel_id=1, source_target_pairs={{0,4},{4,0},{8,12},{12,8},{16,20},{20,16},{24,28},{28,24},{1,5},{5... | collective-permute-start | bytes 12582920 | tf_op jit(solution)/shard_map/ppermute | solution.py:1212
  595.5 37.2 %all-to-all-start.4 = ((bf16[4,320,512]{2,1,0:T(8,128)(2,1)}), bf16[4,320,512]{2,1,0:T(8,128)(2,1)}, u32[]{:S(2)}, u32[]{:S(2)}) async-start(bf16[4,320,512]{2,1,0:T(8,128)(2,1)} %bitcast.79), calls=%async_computation.4 | async-start | bytes 2621440 | tf_op jit(solution)/shard_map/all_to_all | solution.py:1174
  600.6 115.9 %reduce-scatter.5.cloned.1.call-start = ((), (), s32[]{:S(2)}) async-start(), calls=%async_computation.9 | async-start | bytes 2621440 | tf_op jit(solution)/shard_map/reduce_scatter | solution.py:1287
  650.7 166.2 %reduce-scatter.7.cloned.1.call-start = ((), (), s32[]{:S(2)}) async-start(), calls=%async_computation.10 | async-start | bytes 1310720 | tf_op jit(solution)/shard_map/reduce_scatter | solution.py:1287
  650.8 65.8 %collective-permute-start.35 = (bf16[4,128,1024]{2,1,0:T(8,128)(2,1)}, bf16[4,128,1024]{2,1,0:T(8,128)(2,1)S(1)}, u32[]{:S(2)}, u32[]{:S(2)}) collective-permute-start(bf16[4,128,1024]{2,1,0:T(8,128)(2,1)} %get-tuple-element.349), channel_id=1, source_target_pairs={{0,8},{4,12},{8,0},{12,4},{16,24},{20,28},{24,16},{28,20},{1,9},{5... | collective-permute-start | bytes 3145736 | tf_op jit(solution)/shard_map/ppermute | solution.py:1212
  651.7 64.8 %collective-permute-start.36 = (bf16[4,128,1024]{2,1,0:T(8,128)(2,1)}, bf16[4,128,1024]{2,1,0:T(8,128)(2,1)S(1)}, u32[]{:S(2)}, u32[]{:S(2)}) collective-permute-start(bf16[4,128,1024]{2,1,0:T(8,128)(2,1)} %get-tuple-element.350), channel_id=1, source_target_pairs={{0,16},{4,20},{8,24},{12,28},{16,0},{20,4},{24,8},{28,12},{1,17},{... | collective-permute-start | bytes 3145736 | tf_op jit(solution)/shard_map/ppermute | solution.py:1212
  652.6 64.0 %collective-permute-start.37 = (bf16[4,128,1024]{2,1,0:T(8,128)(2,1)}, bf16[4,128,1024]{2,1,0:T(8,128)(2,1)}, u32[]{:S(2)}, u32[]{:S(2)}) collective-permute-start(bf16[4,128,1024]{2,1,0:T(8,128)(2,1)} %get-tuple-element.351), channel_id=1, source_target_pairs={{0,24},{4,28},{8,16},{12,20},{16,8},{20,12},{24,0},{28,4},{1,25},{... | collective-permute-start | bytes 3145736 | tf_op jit(solution)/shard_map/ppermute | solution.py:1212
  723.8 194.3 %reduce-scatter.9.cloned.1.call-start = ((), (), s32[]{:S(2)}) async-start(), calls=%async_computation.11 | async-start | bytes 2621440 | tf_op jit(solution)/shard_map/reduce_scatter | solution.py:1287
  757.8 59.1 %collective-permute-start.43 = (bf16[2,4,128,1024]{3,2,1,0:T(8,128)(2,1)}, bf16[2,4,128,1024]{3,2,1,0:T(8,128)(2,1)}, u32[]{:S(2)}, u32[]{:S(2)}) collective-permute-start(bf16[2,4,128,1024]{3,2,1,0:T(8,128)(2,1)} %pad_maximum_fusion.9), channel_id=1, source_target_pairs={{0,16},{4,20},{8,24},{12,28},{16,0},{20,4},{24,8},{28,12},{1,17},{... | collective-permute-start | bytes 6291464 | tf_op jit(solution)/shard_map/ppermute | solution.py:1212
  760.2 56.7 %collective-permute-start.42 = (bf16[2,4,128,1024]{3,2,1,0:T(8,128)(2,1)}, bf16[2,4,128,1024]{3,2,1,0:T(8,128)(2,1)}, u32[]{:S(2)}, u32[]{:S(2)}) collective-permute-start(bf16[2,4,128,1024]{3,2,1,0:T(8,128)(2,1)} %pad_maximum_fusion.8), channel_id=1, source_target_pairs={{0,8},{4,12},{8,0},{12,4},{16,24},{20,28},{24,16},{28,20},{1,9},{5... | collective-permute-start | bytes 6291464 | tf_op jit(solution)/shard_map/ppermute | solution.py:1212
  859.2 99.1 %reduce-scatter.11.cloned.1.call-start = ((), (), s32[]{:S(2)}) async-start(), calls=%async_computation.12 | async-start | bytes 1474560 | tf_op jit(solution)/shard_map/reduce_scatter | solution.py:1287
  (92 other events, 1371.2 us)
Sparse Core Ops, SparseCore 0:
  56.3 29.1 all-gather.8
  87.8 27.5 all-gather.10
  132.7 26.5 all-gather.12
  177.6 44.8 all-gather.14
  650.8 43.1 reduce-scatter.4
  723.9 26.3 reduce-scatter.6
  859.3 46.3 reduce-scatter.8
  921.2 29.9 reduce-scatter.10

commit v3 on v2

--- a/solution.py
+++ b/solution.py
@@ -1236,6 +1236,19 @@
     return [own] + [swap(own, m * 2) for m in (1, 2, 3)]
 
 
+def sides_stage(own):
+    return [own, swap(own, ROW_X), swap(own, ROW_Y)]
+
+
+def corner_stage(sides):
+    half = sides[0].shape[1] // 2
+    return [swap(sides[1][:, :half], ROW_Y), swap(sides[2][:, half:], ROW_X)]
+
+
+def joined(sides, corner):
+    return jnp.stack(sides + [jnp.concatenate(corner, axis=1)])
+
+
 def sum_core(keep, got):
     return [add(keep[m], got[m]) for m in range(4)]
 
@@ -1343,19 +1356,22 @@
     own_a0, hidden0, tables, base_s, z_u0 = sync(own_a0, hidden0, tables, base_s, z_u0)
     own_a0 = jnp.stack(own_a0)
     other_a0 = swap(own_a0, CORE)
-    own_u0 = cross_stage(jnp.stack(others(z_u0, z)))
+    own_u0 = sides_stage(jnp.stack(others(z_u0, z)))
     own_a0, other_a0 = sync(own_a0, other_a0)
     weights_a0 = (local_a0, own_a0, other_a0)
     normed0, qkv0 = ln_qkv(hidden0, mods, weights_a0, 0)
     qkv0, own_u0, z_d0 = sync(qkv0, own_u0, z_d0)
-    own_d0 = cross_stage(jnp.stack(others(z_d0, z)))
-    own_u0 = jnp.stack(own_u0)
-    other_u0 = swap(own_u0, CORE)
+    corner_u0 = corner_stage(own_u0)
+    own_d0 = sides_stage(jnp.stack(others(z_d0, z)))
     z_a1 = lax.all_gather(local_a1[0, 0], "head")
     attended0 = attn_fwd(qkv0, base_s, fc, spatial)
+    attended0, corner_u0, own_d0 = sync(attended0, corner_u0, own_d0)
+    corner_d0 = corner_stage(own_d0)
+    own_u0 = joined(own_u0, corner_u0)
+    other_u0 = swap(own_u0, CORE)
     branch0, middle0, shifted0 = out_proj(attended0, weights_a0, hidden0, mods, 0)
-    shifted0, own_d0, other_u0, z_a1 = sync(shifted0, own_d0, other_u0, z_a1)
-    own_d0 = jnp.stack(own_d0)
+    shifted0, corner_d0, other_u0, z_a1 = sync(shifted0, corner_d0, other_u0, z_a1)
+    own_d0 = joined(own_d0, corner_d0)
     other_d0 = swap(own_d0, CORE)
     z_f1 = lax.all_gather(local_f1[0, 0], "head")
     own_a1 = jnp.stack(others(z_a1, z))
@@ -1395,17 +1411,20 @@
     g_att1, f1_got = sync(g_att1, f1_got)
     total_f1 = sum_core(f1_keep, f1_got)
     g_att1, total_f1 = sync(g_att1, total_f1)
-    got_f1 = send_plane(total_f1, (1, 2))
+    got_f1 = send_cross(total_f1)
     g_proj1, g_base1 = attn_bwd(qkv1, g_att1, base_t, fc, tube)
     g_proj1, g_base1, got_f1 = sync(g_proj1, g_base1, got_f1)
+    half_f1 = sum_cross(total_f1, got_f1)
+    half_f1, g_proj1 = sync(half_f1, g_proj1)
+    got_f1 = send_corner(half_f1)
     g_hid1a, g_hid1b, sums_q1 = qkv_back(
         g_proj1, weights_a1, tubes1, g_mid1, mods, 6, BF16, 2
     )
-    g_hid1a, g_hid1b, g_proj1, out_wins, g_base1 = sync(
-        g_hid1a, g_hid1b, g_proj1, out_wins, g_base1
+    g_hid1a, g_hid1b, g_proj1, out_wins, g_base1, got_f1 = sync(
+        g_hid1a, g_hid1b, g_proj1, out_wins, g_base1, got_f1
     )
     grad1a = exchange(g_hid1a)
-    corner_a = swap(total_f1[3][:, :128], ROW_X + ROW_Y)
+    z_f1 = sum_corner(half_f1, got_f1, z)
     a1_keep, a1_send = qkv_grad(g_proj1, normed1, o1_keep, o1_send, None)
     gt_t = jnp.einsum(
         "hjtk,rjk->htr",
@@ -1413,19 +1432,14 @@
         hot_t,
         precision=HIGHEST_PRECISION,
     ).reshape(16, n_t)
-    grad1a, corner_a, a1_keep, a1_send, gt_t, g_hid1b, out_wins = sync(
-        grad1a, corner_a, a1_keep, a1_send, gt_t, g_hid1b, out_wins
+    grad1a, z_f1, a1_keep, a1_send, gt_t, g_hid1b, out_wins = sync(
+        grad1a, z_f1, a1_keep, a1_send, gt_t, g_hid1b, out_wins
     )
     grad1b = exchange(g_hid1b)
-    corner_b = swap(total_f1[3][:, 128:], ROW_X + ROW_Y)
-    a1_got = swap(a1_send, CORE)
+    total_a1 = sum_core(a1_keep, swap(a1_send, CORE))
     output = spatial_to_rows(from_quads(out_wins), odd)
-    grad1b, a1_got, corner_b, output = sync(grad1b, a1_got, corner_b, output)
+    grad1b, total_a1, output, z_f1 = sync(grad1b, total_a1, output, z_f1)
     grad1 = from_quads(jnp.concatenate([grad1a, grad1b], axis=1))
-    got_f1 = got_f1 + [jnp.concatenate([corner_a, corner_b], axis=1)]
-    z_f1 = sum_plane(total_f1, got_f1, z)
-    total_a1 = sum_core(a1_keep, a1_got)
-    grad1, z_f1, total_a1 = sync(grad1, z_f1, total_a1)
     mine_f1 = sum_line(z_f1)
     got_a1 = send_plane(total_a1, (1, 2, 3))
     f0_keep, f0_send, g_shift0 = ffn_bwd(grad1, pre0, shifted0, weights_f0, 0, mods, 0)
@@ -1436,12 +1450,12 @@
     g_mid0, g_att0, o0_keep, o0_send, sums_o0 = out_bwd(
         grad1, g_shift0, middle0, feed0, branch0, attended0, weights_a0, mods, 0
     )
-    g_att0, f0_got, own_gf1 = sync(g_att0, f0_got, own_gf1)
+    g_att0, f0_got, own_gf1, mine_a1 = sync(g_att0, f0_got, own_gf1, mine_a1)
     total_f0 = sum_core(f0_keep, f0_got)
     own_gf1 = jnp.stack(own_gf1)
     g_att0, total_f0, own_gf1 = sync(g_att0, total_f0, own_gf1)
     got_f0 = send_cross(total_f0)
-    other_gf1 = swap(own_gf1, CORE)
+    own_ga1 = cross_stage(mine_a1)
     g_proj0, g_base0 = attn_bwd(qkv0, g_att0, base_s, fc, spatial)
     gt_s = jnp.einsum(
         "hjai,bji->hab",
@@ -1450,14 +1464,17 @@
         precision=HIGHEST_PRECISION,
     ).reshape(16, n_s)
     a0_keep, a0_send = qkv_grad(g_proj0, normed0, o0_keep, o0_send, table_rows(gt_s, gt_t))
-    a0_keep, a0_send, got_f0, mine_a1, other_gf1, g_proj0 = sync(
-        a0_keep, a0_send, got_f0, mine_a1, other_gf1, g_proj0
-    )
+    a0_keep, a0_send, got_f0, own_ga1, g_proj0 = sync(a0_keep, a0_send, got_f0, own_ga1, g_proj0)
     a0_got = swap(a0_send, CORE)
     half_f0 = sum_cross(total_f0, got_f0)
     got_f0 = send_corner(half_f0)
+    own_ga1 = jnp.stack(own_ga1)
+    other_gf1, other_ga1 = swap(own_gf1, CORE), swap(own_ga1, CORE)
     g_feed = finish_feed(place, own_gf1, other_gf1, 1, ())
-    half_f0, got_f0, a0_got, g_feed, g_proj0 = sync(half_f0, got_f0, a0_got, g_feed, g_proj0)
+    g_attn = finish_attn(place, own_ga1, other_ga1, 1, (), 0)
+    half_f0, got_f0, a0_got, g_feed, g_attn, g_proj0 = sync(
+        half_f0, got_f0, a0_got, g_feed, g_attn, g_proj0
+    )
     total_a0 = sum_core(a0_keep, a0_got)
     z_f0 = sum_corner(half_f0, got_f0, z)
     total_a0, z_f0, g_proj0 = sync(total_a0, z_f0, g_proj0)
@@ -1478,19 +1495,17 @@
     )
     got_a0, mine_f0, mod_rows, grad_tokens = sync(got_a0, mine_f0, mod_rows, grad_tokens)
     mine_a0 = sum_line(sum_corner(half_a0, got_a0, z))
-    crossed = cross_stage(jnp.concatenate([mine_f0, mine_a1], axis=0))
+    own_gf0 = cross_stage(mine_f0)
     mod_got = [from_z(mod_rows, 1), from_z(mod_rows, 2)]
-    mine_a0, crossed, mod_got = sync(mine_a0, crossed, mod_got)
+    mine_a0, own_gf0, mod_got = sync(mine_a0, own_gf0, mod_got)
     own_ga0 = cross_stage(mine_a0)
-    crossed = jnp.stack(crossed)
-    other_crossed = swap(crossed, CORE)
+    own_gf0 = jnp.stack(own_gf0)
+    other_gf0 = swap(own_gf0, CORE)
     mod_got = mod_got + [from_z(mod_rows, 3)]
-    own_ga0, other_crossed, mod_got = sync(own_ga0, other_crossed, mod_got)
+    g_feed = finish_feed(place, own_gf0, other_gf0, 0, g_feed)
+    own_ga0, g_feed, mod_got = sync(own_ga0, g_feed, mod_got)
     own_ga0 = jnp.stack(own_ga0)
     other_ga0 = swap(own_ga0, CORE)
-    g_feed = finish_feed(place, crossed, other_crossed, 0, g_feed)
-    g_attn = finish_attn(place, crossed, other_crossed, 1, (), 2)
-    other_ga0, g_feed, g_attn = sync(other_ga0, g_feed, g_attn)
     g_attn = finish_attn(place, own_ga0, other_ga0, 0, g_attn, 0)
     tab = jnp.concatenate(
         [lax.dynamic_slice_in_dim(own_ga0, chip ^ m, 1, axis=0) for m in range(4)], axis=0

time: 1020 us -> 1020 us (level)
  waiting for transfers between devices: 162 us -> 147 us
  other arithmetic: 109 us -> 120 us
    ppermute x51 -> x57, waiting for transfers between devices: 83.1 us -> 54 us  [swap(): return lax.ppermute(values, 'clip', [(i, i ^ bit) for i in range(8)])]
    all_gather x1, waiting for transfers between devices: 0.01 us -> 12.4 us  [on_device_windows(): z_a1 = lax.all_gather(local_a1[0, 0], 'head')]
    convert_element_type x10 -> x13, other arithmetic: 37.3 us -> 46 us  [add(): return (first.astype(F32) + second.astype(F32)).astype(BF16)]
    ppermute x51 -> x57, starting transfers between devices: 45.9 us -> 49.9 us  [swap(): return lax.ppermute(values, 'clip', [(i, i ^ bit) for i in range(8)])]
  transfers between devices with their start and end apart: 77 -> 83, of which waited for: 30 -> 31; matrix products, arithmetic and copies ran while one was open for 14% -> 16% of each run, Pallas kernels for 49% -> 50%
where the time goes in v3:
time: 1020 us; the launch traced here: 1010 us
  Pallas kernels  524 us (51%)
  waiting for transfers between devices  147 us (14%)
  other arithmetic  120 us (12%)
  starting transfers between devices  98 us (10%)
  local copies, waits for them, and re-layouts  91.4 us (9%)
  matrix products  17.3 us (2%)
  between operations  16.5 us (2%)
    pallas_call x2, Pallas kernels, ffn_bwd(): call(kernel, 'ffn_bwd', (NZ,), [full((rows, D)), pl.BlockSpec((rows, D),...  123 us
    pallas_call x2, Pallas kernels, attn_bwd(): call(kernel, 'attn_bwd', (NZ,), [xspec, pl.BlockSpec((parts, count, size,...  76 us
    pallas_call x2, Pallas kernels, ffn_fwd(): call(kernel, 'ffn_fwd', (NZ,), [full((rows, D))] + feed_specs(down_block)...  70.1 us
    ppermute x57, waiting for transfers between devices, swap(): return lax.ppermute(values, 'clip', [(i, i ^ bit) for i in range(8)])  54 us
    ppermute x57, starting transfers between devices, swap(): return lax.ppermute(values, 'clip', [(i, i ^ bit) for i in range(8)])  49.9 us
    convert_element_type x13, other arithmetic, add(): return (first.astype(F32) + second.astype(F32)).astype(BF16)  46 us
    ppermute x4, waiting for transfers between devices, partner(): return lax.ppermute(values, 'head', [(i, i ^ 1) for i in range(NZ)])  45.3 us
    pallas_call x2, Pallas kernels, attn_fwd(): call(kernel, 'attn_fwd', (NZ,), [pl.BlockSpec((parts, count, size, 768),...  43.3 us
  transfers between devices with their start and end apart: 83, of which 31 were waited for; matrix products, arithmetic and copies ran while one was open for 16% of the time, Pallas kernels for 50%

profile of v3, /device:TPU:0, one launch (start us, length us, event | category | flops | bytes accessed | tf_op | source)
XLA Modules:
  0.0 1014.0 jit_solution(2519444341799017697)
XLA Ops:
  23.6 6.9 prep_feed.2.refs_0_
  30.5 6.9 prep_feed.3.refs_0_
  72.0 10.7 %collective-permute-done.6 = bf16[3,128,1024]{2,1,0:T(8,128)(2,1)} collective-permute-done((bf16[3,128,1024]{2,1,0:T(8,128)(2,1)S(1)}, bf16[3,128,1024]{2,1,0:T(8,128)(2,1)}, u32[]{:S(2)}, u32[]{:S(2)}) %collective-permute-start.6) | collective-permute-done | bytes 786464 | tf_op jit(solution)/shard_map/ppermute | solution.py:1212
  94.3 16.1 %ln_qkv.2 = (bf16[1280,1024]{1,0:T(8,128)(2,1)}, bf16[1280,3072]{1,0:T(8,128)(2,1)}) custom-call(bf16[1280,1024]{1,0:T(8,128)(2,1)} %maximum_select_fusion.1.h_ref, f32[12,1024]{1,0:T(8,128)} %bitcast.290, bf16[2,4,128,1024]{3,2,1,0:T(8,128)(2,1)} %prep_attn.2.l_ref, bf16[4,3,128,1024]{3,2,1,0:T(8,128)(2,1)} %copy-done.2, ...), custom_call_target="tpu_custom_call" | custom-call | flops 2013265920 | bytes 5505024 | tf_op jit(solution)/shard_map/ln_qkv/pallas_call | solution.py:502
  123.6 20.4 %attn_fwd.2 = bf16[1,5,256,1024]{3,2,1,0:T(8,128)(2,1)} custom-call(bf16[1,5,256,3072]{3,2,1,0:T(8,128)(2,1)} %bitcast.310, f32[16,16,512]{2,1,0:T(8,128)} %pad.18.b_ref, s32[1]{0:T(128)} %copy.101.fc_ref), custom_call_target="tpu_custom_call" | custom-call | flops 1342177280 | bytes 2621440 | tf_op jit(solution)/shard_map/attn_fwd/pallas_call | solution.py:557
  155.1 9.4 out_proj.2
  164.5 12.4 %all-gather.13.cloned.1.call-done = bf16[4,1,128,1024]{3,2,1,0:T(8,128)(2,1)} async-done(((bf16[1,1,128,1024]{3,2,1,0:T(8,128)(2,1)}), bf16[4,1,128,1024]{3,2,1,0:T(8,128)(2,1)}) %all-gather.13.cloned.1.call-update) | async-done | bytes 1048592 | tf_op jit(solution)/shard_map/all_gather | solution.py:1366
  189.3 35.1 %ffn_fwd.2 = (bf16[1280,4096]{1,0:T(8,128)(2,1)}, bf16[1280,1024]{1,0:T(8,128)(2,1)}, bf16[1280,1024]{1,0:T(8,128)(2,1)}) custom-call(bf16[1280,1024]{1,0:T(8,128)(2,1)} %get-tuple-element.274.x_ref, bf16[2,4,256,1024]{3,2,1,0:T(8,128)(2,1)} %prep_feed.2.refs_0_, bf16[4,3,128,1024]{3,2,1,0:T(8,128)(2,1)} %copy-done.5, ...), custom_call_target="tpu_custom_call" | custom-call | flops 5368709120 | bytes 10747904 | tf_op jit(solution)/shard_map/ffn_fwd/pallas_call | solution.py:747
  273.4 11.5 %collective-permute-done.25 = bf16[128,1024]{1,0:T(8,128)(2,1)} collective-permute-done((bf16[128,1024]{1,0:T(8,128)(2,1)}, bf16[128,1024]{1,0:T(8,128)(2,1)}, u32[]{:S(2)}, u32[]{:S(2)}) %collective-permute-start.25) | collective-permute-done | bytes 262176 | tf_op jit(solution)/shard_map/ppermute | solution.py:1136
  288.4 7.9 all-to-all-done
  296.4 15.9 %ln_qkv.3 = (bf16[1280,1024]{1,0:T(8,128)(2,1)}, bf16[1280,3072]{1,0:T(8,128)(2,1)}) custom-call(bf16[1280,1024]{1,0:T(8,128)(2,1)} %bitcast.40.h_ref, f32[12,1024]{1,0:T(8,128)} %bitcast.293, bf16[2,4,128,1024]{3,2,1,0:T(8,128)(2,1)} %prep_attn.3.l_ref, bf16[4,3,128,1024]{3,2,1,0:T(8,128)(2,1)} %copy-done.3, ...), custom_call_target="tpu_custom_call" | custom-call | flops 2013265920 | bytes 5505024 | tf_op jit(solution)/shard_map/ln_qkv/pallas_call | solution.py:502
  326.8 22.9 %attn_fwd.3 = bf16[5,4,64,1024]{3,2,1,0:T(8,128)(2,1)} custom-call(bf16[5,4,64,3072]{3,2,1,0:T(8,128)(2,1)} %bitcast.308, f32[16,64,640]{2,1,0:T(8,128)} %pad.19.b_ref, s32[1]{0:T(128)} %copy.101.fc_ref), custom_call_target="tpu_custom_call" | custom-call | flops 1677721600 | bytes 2621440 | tf_op jit(solution)/shard_map/attn_fwd/pallas_call | solution.py:557
  349.7 9.3 out_proj.3
  359.0 35.0 %ffn_fwd.3 = (bf16[1280,4096]{1,0:T(8,128)(2,1)}, bf16[1280,1024]{1,0:T(8,128)(2,1)}, bf16[1280,1024]{1,0:T(8,128)(2,1)}) custom-call(bf16[1280,1024]{1,0:T(8,128)(2,1)} %get-tuple-element.300.x_ref, bf16[2,4,256,1024]{3,2,1,0:T(8,128)(2,1)} %prep_feed.3.refs_0_, bf16[4,3,256,1024]{3,2,1,0:T(8,128)(2,1)} %pad_maximum_fusion.refs_1_.refs_3_, ...), custom_call_target="tpu_custom_call" | custom-call | flops 5368709120 | bytes 10747904 | tf_op jit(solution)/shard_map/ffn_fwd/pallas_call | solution.py:747
  403.4 61.2 %ffn_bwd.2 = (bf16[4,4,256,1024]{3,2,1,0:T(8,128)(2,1)}, bf16[4,4,256,1024]{3,2,1,0:T(8,128)(2,1)}, f32[1280,1024]{1,0:T(8,128)}) custom-call(bf16[1280,1024]{1,0:T(8,128)(2,1)} %get-tuple-element.569.g_ref, bf16[1280,4096]{1,0:T(8,128)(2,1)} %get-tuple-element.306.p_ref, bf16[1280,1024]{1,0:T(8,128)(2,1)} %get-tuple-element.300.x_ref, ...), custom_call_target="tpu_custom_call" | custom-call | flops 10737418240 | bytes 13631488 | tf_op jit(solution)/shard_map/ffn_bwd/pallas_call | solution.py:809
  464.7 18.7 %out_bwd.2 = (f32[1280,1024]{1,0:T(8,128)}, bf16[1280,1024]{1,0:T(8,128)(2,1)}, bf16[4,4,32,1024]{3,2,1,0:T(8,128)(2,1)}, bf16[4,4,32,1024]{3,2,1,0:T(8,128)(2,1)}, f32[8,1024]{1,0:T(8,128)}) custom-call(bf16[1280,1024]{1,0:T(8,128)(2,1)} %get-tuple-element.569.g_ref, f32[1280,1024]{1,0:T(8,128)} %get-tuple-element.311.gs_ref, ...), custom_call_target="tpu_custom_call" | custom-call | flops 1342177280 | bytes 8912896 | tf_op jit(solution)/shard_map/out_bwd/pallas_call | solution.py:873
  483.4 9.0 fusion.16
  498.0 42.8 %attn_bwd.2 = (bf16[5,4,64,3072]{3,2,1,0:T(8,128)(2,1)}, f32[16,64,640]{2,1,0:T(8,128)}) custom-call(bf16[5,4,64,3072]{3,2,1,0:T(8,128)(2,1)} %bitcast.309, bf16[5,4,64,1024]{3,2,1,0:T(8,128)(2,1)} %bitcast.365, f32[16,64,640]{2,1,0:T(8,128)} %pad.19.b_ref, s32[1]{0:T(128)} %copy.101.fc_ref), custom_call_target="tpu_custom_call" | custom-call | flops 4194304000 | bytes 5242880 | tf_op jit(solution)/shard_map/attn_bwd/pallas_call | solution.py:620
  552.4 20.3 %qkv_back.2 = (bf16[1280,512]{1,0:T(8,128)(2,1)}, bf16[1280,512]{1,0:T(8,128)(2,1)}, f32[8,1024]{1,0:T(8,128)}) custom-call(bf16[1280,3072]{1,0:T(8,128)(2,1)} %bitcast.270, bf16[2,4,128,1024]{3,2,1,0:T(8,128)(2,1)} %prep_attn.3.l_ref, bf16[4,3,128,1024]{3,2,1,0:T(8,128)(2,1)} %copy-done.3, bf16[4,3,128,1024]{3,2,1,0:T(8,128)(2,1)} %collective-permute-done.24.v_ref, ...), custom_call_target="tpu_custom_call" | custom-call | flops 2013265920 | bytes 8126464 | tf_op jit(solution)/shard_map/qkv_back/pallas_call | solution.py:933
  598.0 13.2 %qkv_grad.2 = (bf16[4,4,128,1024]{3,2,1,0:T(8,128)(2,1)}, bf16[4,4,128,1024]{3,2,1,0:T(8,128)(2,1)}) custom-call(bf16[1280,3072]{1,0:T(8,128)(2,1)} %bitcast.271, bf16[1280,1024]{1,0:T(8,128)(2,1)} %get-tuple-element.343.n_ref, bf16[4,4,32,1024]{3,2,1,0:T(8,128)(2,1)} %get-tuple-element.344.ok_ref, bf16[4,4,32,1024]{3,2,1,0:T(8,128)(2,1)} %get-tuple-element.345.os_ref), custom_call_target="tpu_custom_call" | custom-call | flops 2013265920 | bytes 4718592 | tf_op jit(solution)/shard_map/qkv_grad/pallas_call | solution.py:969
  626.5 24.7 %collective-permute-done.36 = bf16[128,1024]{1,0:T(8,128)(2,1)S(1)} collective-permute-done((bf16[128,1024]{1,0:T(8,128)(2,1)S(1)}, bf16[128,1024]{1,0:T(8,128)(2,1)S(1)}, u32[]{:S(2)}, u32[]{:S(2)}) %collective-permute-start.36) | collective-permute-done | bytes 262176 | tf_op jit(solution)/shard_map/ppermute | solution.py:1136
  666.3 61.4 %ffn_bwd.3 = (bf16[4,4,256,1024]{3,2,1,0:T(8,128)(2,1)}, bf16[4,4,256,1024]{3,2,1,0:T(8,128)(2,1)}, f32[1280,1024]{1,0:T(8,128)}) custom-call(bf16[1280,1024]{1,0:T(8,128)(2,1)} %bitcast.283, bf16[1280,4096]{1,0:T(8,128)(2,1)} %get-tuple-element.359.p_ref, bf16[1280,1024]{1,0:T(8,128)(2,1)} %get-tuple-element.274.x_ref, ...), custom_call_target="tpu_custom_call" | custom-call | flops 10737418240 | bytes 13631488 | tf_op jit(solution)/shard_map/ffn_bwd/pallas_call | solution.py:809
  737.5 18.5 %out_bwd.3 = (f32[1280,1024]{1,0:T(8,128)}, bf16[1280,1024]{1,0:T(8,128)(2,1)}, bf16[4,4,32,1024]{3,2,1,0:T(8,128)(2,1)}, bf16[4,4,32,1024]{3,2,1,0:T(8,128)(2,1)}, f32[8,1024]{1,0:T(8,128)}) custom-call(bf16[1280,1024]{1,0:T(8,128)(2,1)} %bitcast.284, f32[1280,1024]{1,0:T(8,128)} %get-tuple-element.367.gs_ref, ...), custom_call_target="tpu_custom_call" | custom-call | flops 1342177280 | bytes 8912896 | tf_op jit(solution)/shard_map/out_bwd/pallas_call | solution.py:873
  766.1 9.0 fusion.20
  784.4 33.1 %attn_bwd.3 = (bf16[1,5,256,3072]{3,2,1,0:T(8,128)(2,1)}, f32[16,16,512]{2,1,0:T(8,128)}) custom-call(bf16[1,5,256,3072]{3,2,1,0:T(8,128)(2,1)} %bitcast.311, bf16[1,5,256,1024]{3,2,1,0:T(8,128)(2,1)} %bitcast.364, f32[16,16,512]{2,1,0:T(8,128)} %pad.18.b_ref, s32[1]{0:T(128)} %copy.101.fc_ref), custom_call_target="tpu_custom_call" | custom-call | flops 3355443200 | bytes 5242880 | tf_op jit(solution)/shard_map/attn_bwd/pallas_call | solution.py:620
  826.9 13.6 %qkv_grad.3 = (bf16[4,4,144,1024]{3,2,1,0:T(8,128)(2,1)}, bf16[4,4,144,1024]{3,2,1,0:T(8,128)(2,1)}) custom-call(bf16[1280,3072]{1,0:T(8,128)(2,1)} %bitcast.268, bf16[1280,1024]{1,0:T(8,128)(2,1)} %get-tuple-element.386.n_ref, bf16[4,4,32,1024]{3,2,1,0:T(8,128)(2,1)} %get-tuple-element.387.ok_ref, bf16[4,4,32,1024]{3,2,1,0:T(8,128)(2,1)} %get-tuple-element.388.os_ref, ...), custom_call_target="tpu_custom_call" | custom-call | flops 2013265920 | bytes 4718592 | tf_op jit(solution)/shard_map/qkv_grad/pallas_call | solution.py:969
  852.6 9.0 finish_feed.2
  892.3 21.1 %qkv_back.3 = (f32[1280,1024]{1,0:T(8,128)}, f32[8,1024]{1,0:T(8,128)}) custom-call(bf16[1280,3072]{1,0:T(8,128)(2,1)} %bitcast.269, bf16[2,4,128,1024]{3,2,1,0:T(8,128)(2,1)} %prep_attn.2.l_ref, bf16[4,3,128,1024]{3,2,1,0:T(8,128)(2,1)} %copy-done.2, bf16[4,3,128,1024]{3,2,1,0:T(8,128)(2,1)} %collective-permute-done.10.v_ref, ...), custom_call_target="tpu_custom_call" | custom-call | flops 2013265920 | bytes 8126464 | tf_op jit(solution)/shard_map/qkv_back/pallas_call | solution.py:933
  929.6 9.0 collective-permute-done.58
  963.3 9.9 collective-permute-done.60
  985.6 9.0 finish_feed.3
  999.7 7.0 finish_attn.3
  (413 shorter events, 386.7 us)
Async XLA Ops:
  7.2 78.3 %all-gather.9.cloned.1.call-start = ((), (), s32[]{:S(2)}) async-start(), calls=%async_computation.13 | async-start | bytes 1310720 | tf_op jit(solution)/shard_map/all_gather | solution.py:1348
  56.2 59.2 %all-gather.11.cloned.1.call-start = ((), (), s32[]{:S(2)}) async-start(), calls=%async_computation.14 | async-start | bytes 1310720 | tf_op jit(solution)/shard_map/all_gather | solution.py:1349
  87.7 89.2 %all-gather.13.cloned.1.call-start = ((), (), s32[]{:S(2)}) async-start(), calls=%async_computation.15 | async-start | bytes 1310720 | tf_op jit(solution)/shard_map/all_gather | solution.py:1366
  149.9 78.1 %all-gather.15.cloned.1.call-start = ((), (), s32[]{:S(2)}) async-start(), calls=%async_computation.16 | async-start | bytes 2621440 | tf_op jit(solution)/shard_map/all_gather | solution.py:1376
  185.8 42.2 %collective-permute-start.21 = (bf16[3,128,1024]{2,1,0:T(8,128)(2,1)}, bf16[3,128,1024]{2,1,0:T(8,128)(2,1)}, u32[]{:S(2)}, u32[]{:S(2)}) collective-permute-start(bf16[3,128,1024]{2,1,0:T(8,128)(2,1)} %pad_maximum_fusion.21), channel_id=1, source_target_pairs={{0,8},{4,12},{8,0},{12,4},{16,24},{20,28},{24,16},{28,20},{1,9},{5... | collective-permute-start | bytes 2359304 | tf_op jit(solution)/shard_map/ppermute | solution.py:1212
  187.2 40.7 %collective-permute-start.22 = (bf16[3,128,1024]{2,1,0:T(8,128)(2,1)}, bf16[3,128,1024]{2,1,0:T(8,128)(2,1)}, u32[]{:S(2)}, u32[]{:S(2)}) collective-permute-start(bf16[3,128,1024]{2,1,0:T(8,128)(2,1)} %pad_maximum_fusion.21), channel_id=1, source_target_pairs={{0,16},{4,20},{8,24},{12,28},{16,0},{20,4},{24,8},{28,12},{1,17},{... | collective-permute-start | bytes 2359304 | tf_op jit(solution)/shard_map/ppermute | solution.py:1212
  188.7 39.3 %collective-permute-start.23 = (bf16[3,128,1024]{2,1,0:T(8,128)(2,1)}, bf16[3,128,1024]{2,1,0:T(8,128)(2,1)}, u32[]{:S(2)}, u32[]{:S(2)}) collective-permute-start(bf16[3,128,1024]{2,1,0:T(8,128)(2,1)} %pad_maximum_fusion.21), channel_id=1, source_target_pairs={{0,24},{4,28},{8,16},{12,20},{16,8},{20,12},{24,0},{28,4},{1,25},{... | collective-permute-start | bytes 2359304 | tf_op jit(solution)/shard_map/ppermute | solution.py:1212
  231.6 64.8 %all-to-all-start = ((bf16[4,320,1024]{2,1,0:T(8,128)(2,1)}), bf16[4,320,1024]{2,1,0:T(8,128)(2,1)}, u32[]{:S(2)}, u32[]{:S(2)}) async-start(bf16[4,320,1024]{2,1,0:T(8,128)(2,1)} %bitcast.39), calls=%async_computation | async-start | bytes 5242880 | tf_op jit(solution)/shard_map/all_to_all | solution.py:1174
  238.9 49.6 %collective-permute-start.24 = (bf16[4,3,128,1024]{3,2,1,0:T(8,128)(2,1)S(1)}, bf16[4,3,128,1024]{3,2,1,0:T(8,128)(2,1)}, u32[]{:S(2)}, u32[]{:S(2)}) collective-permute-start(bf16[4,3,128,1024]{3,2,1,0:T(8,128)(2,1)S(1)} %pad_maximum_fusion.4.w_ref), channel_id=1, source_target_pairs={{0,4},{4,0},{8,12},{12,8},{16,20},{20,16},{24,28},{28,24},{1,5},{5... | collective-permute-start | bytes 9437192 | tf_op jit(solution)/shard_map/ppermute | solution.py:1212
  241.1 71.2 %collective-permute-start.26 = (bf16[3,256,1024]{2,1,0:T(8,128)(2,1)}, bf16[3,256,1024]{2,1,0:T(8,128)(2,1)}, u32[]{:S(2)}, u32[]{:S(2)}) collective-permute-start(bf16[3,256,1024]{2,1,0:T(8,128)(2,1)} %pad_maximum_fusion.12), channel_id=1, source_target_pairs={{0,8},{4,12},{8,0},{12,4},{16,24},{20,28},{24,16},{28,20},{1,9},{5... | collective-permute-start | bytes 4718600 | tf_op jit(solution)/shard_map/ppermute | solution.py:1212
  242.6 70.6 %collective-permute-start.27 = (bf16[3,256,1024]{2,1,0:T(8,128)(2,1)}, bf16[3,256,1024]{2,1,0:T(8,128)(2,1)}, u32[]{:S(2)}, u32[]{:S(2)}) collective-permute-start(bf16[3,256,1024]{2,1,0:T(8,128)(2,1)} %pad_maximum_fusion.12), channel_id=1, source_target_pairs={{0,16},{4,20},{8,24},{12,28},{16,0},{20,4},{24,8},{28,12},{1,17},{... | collective-permute-start | bytes 4718600 | tf_op jit(solution)/shard_map/ppermute | solution.py:1212
  244.1 69.2 %collective-permute-start.28 = (bf16[3,256,1024]{2,1,0:T(8,128)(2,1)}, bf16[3,256,1024]{2,1,0:T(8,128)(2,1)}, u32[]{:S(2)}, u32[]{:S(2)}) collective-permute-start(bf16[3,256,1024]{2,1,0:T(8,128)(2,1)} %pad_maximum_fusion.12), channel_id=1, source_target_pairs={{0,24},{4,28},{8,16},{12,20},{16,8},{20,12},{24,0},{28,4},{1,25},{... | collective-permute-start | bytes 4718600 | tf_op jit(solution)/shard_map/ppermute | solution.py:1212
  246.4 38.5 %collective-permute-start.25 = (bf16[128,1024]{1,0:T(8,128)(2,1)}, bf16[128,1024]{1,0:T(8,128)(2,1)}, u32[]{:S(2)}, u32[]{:S(2)}) collective-permute-start(bf16[128,1024]{1,0:T(8,128)(2,1)} %bitcast.55), channel_id=1, source_target_pairs={{0,1},{1,0},{2,3},{3,2},{4,5},{5,4},{6,7},{7,6},{8,9},{9,8},{10,11... | collective-permute-start | bytes 786440 | tf_op jit(solution)/shard_map/ppermute | solution.py:1136
  320.0 39.0 %collective-permute-start.29 = (bf16[4,3,256,1024]{3,2,1,0:T(8,128)(2,1)}, bf16[4,3,256,1024]{3,2,1,0:T(8,128)(2,1)}, u32[]{:S(2)}, u32[]{:S(2)}) collective-permute-start(bf16[4,3,256,1024]{3,2,1,0:T(8,128)(2,1)} %pad_maximum_fusion.refs_1_.refs_3_), channel_id=1, source_target_pairs={{0,4},{4,0},{8,12},{12,8},{16,20},{20,16},{24,28},{28,24},{1,5},{5... | collective-permute-start | bytes 18874376 | tf_op jit(solution)/shard_map/ppermute | solution.py:1212
  321.7 72.2 %all-to-all-start.1 = ((bf16[4,320,1024]{2,1,0:T(8,128)(2,1)}), bf16[4,320,1024]{2,1,0:T(8,128)(2,1)S(1)}, u32[]{:S(2)}, u32[]{:S(2)}) async-start(bf16[4,320,1024]{2,1,0:T(8,128)(2,1)} %bitcast.64), calls=%async_computation.1 | async-start | bytes 5242880 | tf_op jit(solution)/shard_map/all_to_all | solution.py:1174
  398.1 66.5 %all-to-all-start.2 = ((bf16[4,320,1024]{2,1,0:T(8,128)(2,1)}), bf16[4,320,1024]{2,1,0:T(8,128)(2,1)S(1)}, u32[]{:S(2)}, u32[]{:S(2)}) async-start(bf16[4,320,1024]{2,1,0:T(8,128)(2,1)} %bitcast.289), calls=%async_computation.2 | async-start | bytes 5242880 | tf_op jit(solution)/shard_map/all_to_all | solution.py:1174
  494.4 48.3 %collective-permute-start.32 = (bf16[2,4,128,1024]{3,2,1,0:T(8,128)(2,1)}, bf16[2,4,128,1024]{3,2,1,0:T(8,128)(2,1)}, u32[]{:S(2)}, u32[]{:S(2)}) collective-permute-start(bf16[2,4,128,1024]{3,2,1,0:T(8,128)(2,1)} %pad_maximum_fusion.7), channel_id=1, source_target_pairs={{0,16},{4,20},{8,24},{12,28},{16,0},{20,4},{24,8},{28,12},{1,17},{... | collective-permute-start | bytes 6291464 | tf_op jit(solution)/shard_map/ppermute | solution.py:1212
  497.4 48.0 %collective-permute-start.31 = (bf16[2,4,128,1024]{3,2,1,0:T(8,128)(2,1)}, bf16[2,4,128,1024]{3,2,1,0:T(8,128)(2,1)}, u32[]{:S(2)}, u32[]{:S(2)}) collective-permute-start(bf16[2,4,128,1024]{3,2,1,0:T(8,128)(2,1)} %pad_maximum_fusion.6), channel_id=1, source_target_pairs={{0,8},{4,12},{8,0},{12,4},{16,24},{20,28},{24,16},{28,20},{1,9},{5... | collective-permute-start | bytes 6291464 | tf_op jit(solution)/shard_map/ppermute | solution.py:1212
  575.7 42.8 %all-to-all-start.3 = ((bf16[4,320,512]{2,1,0:T(8,128)(2,1)}), bf16[4,320,512]{2,1,0:T(8,128)(2,1)}, u32[]{:S(2)}, u32[]{:S(2)}) async-start(bf16[4,320,512]{2,1,0:T(8,128)(2,1)} %bitcast.328), calls=%async_computation.3 | async-start | bytes 2621440 | tf_op jit(solution)/shard_map/all_to_all | solution.py:1174
  618.6 40.2 %all-to-all-start.4 = ((bf16[4,320,512]{2,1,0:T(8,128)(2,1)}), bf16[4,320,512]{2,1,0:T(8,128)(2,1)}, u32[]{:S(2)}, u32[]{:S(2)}) async-start(bf16[4,320,512]{2,1,0:T(8,128)(2,1)} %bitcast.327), calls=%async_computation.4 | async-start | bytes 2621440 | tf_op jit(solution)/shard_map/all_to_all | solution.py:1174
  623.7 106.0 %reduce-scatter.5.cloned.1.call-start = ((), (), s32[]{:S(2)}) async-start(), calls=%async_computation.9 | async-start | bytes 2621440 | tf_op jit(solution)/shard_map/reduce_scatter | solution.py:1300
  658.8 103.8 %reduce-scatter.7.cloned.1.call-start = ((), (), s32[]{:S(2)}) async-start(), calls=%async_computation.10 | async-start | bytes 1310720 | tf_op jit(solution)/shard_map/reduce_scatter | solution.py:1300
  658.8 68.9 %collective-permute-start.37 = (bf16[4,128,1024]{2,1,0:T(8,128)(2,1)}, bf16[4,128,1024]{2,1,0:T(8,128)(2,1)S(1)}, u32[]{:S(2)}, u32[]{:S(2)}) collective-permute-start(bf16[4,128,1024]{2,1,0:T(8,128)(2,1)} %get-tuple-element.364), channel_id=1, source_target_pairs={{0,8},{4,12},{8,0},{12,4},{16,24},{20,28},{24,16},{28,20},{1,9},{5... | collective-permute-start | bytes 3145736 | tf_op jit(solution)/shard_map/ppermute | solution.py:1212
  660.1 67.7 %collective-permute-start.38 = (bf16[4,128,1024]{2,1,0:T(8,128)(2,1)S(1)}, bf16[4,128,1024]{2,1,0:T(8,128)(2,1)S(1)}, u32[]{:S(2)}, u32[]{:S(2)}) collective-permute-start(bf16[4,128,1024]{2,1,0:T(8,128)(2,1)S(1)} %get-tuple-element.365), channel_id=1, source_target_pairs={{0,16},{4,20},{8,24},{12,28},{16,0},{20,4},{24,8},{28,12},{1,17},{... | collective-permute-start | bytes 3145736 | tf_op jit(solution)/shard_map/ppermute | solution.py:1212
  660.9 68.8 %collective-permute-start.39 = (bf16[4,128,1024]{2,1,0:T(8,128)(2,1)S(1)}, bf16[4,128,1024]{2,1,0:T(8,128)(2,1)}, u32[]{:S(2)}, u32[]{:S(2)}) collective-permute-start(bf16[4,128,1024]{2,1,0:T(8,128)(2,1)S(1)} %get-tuple-element.366), channel_id=1, source_target_pairs={{0,24},{4,28},{8,16},{12,20},{16,8},{20,12},{24,0},{28,4},{1,25},{... | collective-permute-start | bytes 3145736 | tf_op jit(solution)/shard_map/ppermute | solution.py:1212
  733.9 211.3 %reduce-scatter.9.cloned.1.call-start = ((), (), s32[]{:S(2)}) async-start(), calls=%async_computation.11 | async-start | bytes 2621440 | tf_op jit(solution)/shard_map/reduce_scatter | solution.py:1300
  762.6 77.9 %collective-permute-start.46 = (bf16[128,1024]{1,0:T(8,128)(2,1)}, bf16[128,1024]{1,0:T(8,128)(2,1)S(1)}, u32[]{:S(2)}, u32[]{:S(2)}) collective-permute-start(bf16[128,1024]{1,0:T(8,128)(2,1)} %bitcast.357), channel_id=1, source_target_pairs={{0,8},{4,12},{8,0},{12,4},{16,24},{20,28},{24,16},{28,20},{1,9},{5... | collective-permute-start | bytes 786440 | tf_op jit(solution)/shard_map/ppermute | solution.py:1212
  764.1 76.5 %collective-permute-start.47 = (bf16[128,1024]{1,0:T(8,128)(2,1)}, bf16[128,1024]{1,0:T(8,128)(2,1)}, u32[]{:S(2)}, u32[]{:S(2)}) collective-permute-start(bf16[128,1024]{1,0:T(8,128)(2,1)} %bitcast.358), channel_id=1, source_target_pairs={{0,16},{4,20},{8,24},{12,28},{16,0},{20,4},{24,8},{28,12},{1,17},{... | collective-permute-start | bytes 786440 | tf_op jit(solution)/shard_map/ppermute | solution.py:1212
  765.5 75.0 %collective-permute-start.48 = (bf16[128,1024]{1,0:T(8,128)(2,1)}, bf16[128,1024]{1,0:T(8,128)(2,1)}, u32[]{:S(2)}, u32[]{:S(2)}) collective-permute-start(bf16[128,1024]{1,0:T(8,128)(2,1)} %bitcast.359), channel_id=1, source_target_pairs={{0,24},{4,28},{8,16},{12,20},{16,8},{20,12},{24,0},{28,4},{1,25},{... | collective-permute-start | bytes 786440 | tf_op jit(solution)/shard_map/ppermute | solution.py:1212
  779.9 60.6 %collective-permute-start.45 = (bf16[2,4,128,1024]{3,2,1,0:T(8,128)(2,1)}, bf16[2,4,128,1024]{3,2,1,0:T(8,128)(2,1)}, u32[]{:S(2)}, u32[]{:S(2)}) collective-permute-start(bf16[2,4,128,1024]{3,2,1,0:T(8,128)(2,1)} %pad_maximum_fusion.10), channel_id=1, source_target_pairs={{0,16},{4,20},{8,24},{12,28},{16,0},{20,4},{24,8},{28,12},{1,17},{... | collective-permute-start | bytes 6291464 | tf_op jit(solution)/shard_map/ppermute | solution.py:1212
  783.0 57.6 %collective-permute-start.44 = (bf16[2,4,128,1024]{3,2,1,0:T(8,128)(2,1)}, bf16[2,4,128,1024]{3,2,1,0:T(8,128)(2,1)}, u32[]{:S(2)}, u32[]{:S(2)}) collective-permute-start(bf16[2,4,128,1024]{3,2,1,0:T(8,128)(2,1)} %pad_maximum_fusion.9), channel_id=1, source_target_pairs={{0,8},{4,12},{8,0},{12,4},{16,24},{20,28},{24,16},{28,20},{1,9},{5... | collective-permute-start | bytes 6291464 | tf_op jit(solution)/shard_map/ppermute | solution.py:1212
  886.7 91.5 %reduce-scatter.11.cloned.1.call-start = ((), (), s32[]{:S(2)}) async-start(), calls=%async_computation.12 | async-start | bytes 1474560 | tf_op jit(solution)/shard_map/reduce_scatter | solution.py:1300
  (103 other events, 1441.1 us)
Sparse Core Ops, SparseCore 0:
  56.3 29.1 all-gather.8
  87.8 27.5 all-gather.10
  150.0 26.7 all-gather.12
  182.4 45.5 all-gather.14
  658.9 45.1 reduce-scatter.4
  734.0 28.5 reduce-scatter.6
  886.9 44.5 reduce-scatter.8
  948.3 29.9 reduce-scatter.10

commit v4 on v3

--- a/solution.py
+++ b/solution.py
@@ -1053,17 +1053,17 @@
     )(place, w_up, w_down)
 
 
-def finish_attn(place, own, other, b, earlier, block):
-
-    def kernel(c_ref, own_ref, oth_ref, *rest):
-        gq_ref, go_ref, t_ref = rest[-3:]
+def finish_attn(place, own, other):
+    def kernel(c_ref, own_ref, oth_ref, gq_ref, go_ref, t_ref):
         r = pl.program_id(0)
         at = rows_at(c_ref[0] ^ r)
 
         def store(ref):
-            for t in range(3):
-                t_ref[t, at, :] = ref[0, t * 32 : (t + 1) * 32, :]
-            go_ref[0, at, :] = ref[0, 96:128, :].astype(F32)
+            for b in range(2):
+                row = 128 * b
+                for t in range(3):
+                    t_ref[b, t, at, :] = ref[0, row + t * 32 : row + (t + 1) * 32, :]
+                go_ref[b, at, :] = ref[0, row + 96 : row + 128, :].astype(F32)
 
         @pl.when(r % 2 == 0)
         def _():
@@ -1075,27 +1075,27 @@
 
         @pl.when(r == 7)
         def _():
-            for t in range(3):
-                gq_ref[0, t] = t_ref[t].T.astype(F32)
-
-    piece = pl.BlockSpec((1, 128, D), lambda r, c: (r // 2, block, 0))
-    anywhere = pl.BlockSpec(memory_space=pl.ANY)
+            for b in range(2):
+                for t in range(3):
+                    gq_ref[b, t] = t_ref[b, t].T.astype(F32)
+
+    piece = pl.BlockSpec((1, 256, D), lambda r, c: (r // 2, 0, 0))
     return place_call(
         kernel,
         "finish_attn",
-        [piece, piece] + [anywhere] * len(earlier),
+        [piece, piece],
         [
-            pl.BlockSpec((1, 3, D, 256), lambda r, c: (b, 0, 0, 0)),
-            pl.BlockSpec((1, 256, D), lambda r, c: (b, 0, 0)),
+            pl.BlockSpec((2, 3, D, 256), lambda r, c: (0, 0, 0, 0), pipeline_mode=CONST),
+            pl.BlockSpec((2, 256, D), lambda r, c: (0, 0, 0), pipeline_mode=CONST),
         ],
         [
             jax.ShapeDtypeStruct((2, 3, D, 256), F32),
             jax.ShapeDtypeStruct((2, 256, D), F32),
         ],
-        [pltpu.VMEM((3, 256, D), BF16)],
-        6 * D * D,
-        {3 + i: i for i in range(len(earlier))},
-    )(place, own, other, *earlier)
+        [pltpu.VMEM((2, 3, 256, D), BF16)],
+        12 * D * D,
+        {},
+    )(place, own, other)
 
 
 def finish_feed(place, own, other, b, earlier):
@@ -1365,17 +1365,17 @@
     own_d0 = sides_stage(jnp.stack(others(z_d0, z)))
     z_a1 = lax.all_gather(local_a1[0, 0], "head")
     attended0 = attn_fwd(qkv0, base_s, fc, spatial)
-    attended0, corner_u0, own_d0 = sync(attended0, corner_u0, own_d0)
+    attended0, corner_u0, own_d0, z_a1 = sync(attended0, corner_u0, own_d0, z_a1)
     corner_d0 = corner_stage(own_d0)
     own_u0 = joined(own_u0, corner_u0)
     other_u0 = swap(own_u0, CORE)
     branch0, middle0, shifted0 = out_proj(attended0, weights_a0, hidden0, mods, 0)
-    shifted0, corner_d0, other_u0, z_a1 = sync(shifted0, corner_d0, other_u0, z_a1)
+    own_a1 = jnp.stack(others(z_a1, z))
+    shifted0, corner_d0, other_u0, own_a1 = sync(shifted0, corner_d0, other_u0, own_a1)
     own_d0 = joined(own_d0, corner_d0)
     other_d0 = swap(own_d0, CORE)
     z_f1 = lax.all_gather(local_f1[0, 0], "head")
-    own_a1 = jnp.stack(others(z_a1, z))
-    shifted0, other_d0, own_a1 = sync(shifted0, other_d0, own_a1)
+    shifted0, other_d0 = sync(shifted0, other_d0)
     own_a1 = cross_stage(own_a1)
     weights_f0 = (local_f0, own_u0, other_u0, own_d0, other_d0)
     pre0, feed0, hidden1 = ffn_fwd(shifted0, weights_f0, 0, middle0, mods, 0)
@@ -1445,17 +1445,14 @@
     f0_keep, f0_send, g_shift0 = ffn_bwd(grad1, pre0, shifted0, weights_f0, 0, mods, 0)
     f0_keep, f0_send, g_shift0, mine_f1, got_a1 = sync(f0_keep, f0_send, g_shift0, mine_f1, got_a1)
     f0_got = swap(f0_send, CORE)
-    own_gf1 = cross_stage(mine_f1)
     mine_a1 = sum_line(sum_plane(total_a1, got_a1, z))
     g_mid0, g_att0, o0_keep, o0_send, sums_o0 = out_bwd(
         grad1, g_shift0, middle0, feed0, branch0, attended0, weights_a0, mods, 0
     )
-    g_att0, f0_got, own_gf1, mine_a1 = sync(g_att0, f0_got, own_gf1, mine_a1)
+    g_att0, f0_got = sync(g_att0, f0_got)
     total_f0 = sum_core(f0_keep, f0_got)
-    own_gf1 = jnp.stack(own_gf1)
-    g_att0, total_f0, own_gf1 = sync(g_att0, total_f0, own_gf1)
+    g_att0, total_f0 = sync(g_att0, total_f0)
     got_f0 = send_cross(total_f0)
-    own_ga1 = cross_stage(mine_a1)
     g_proj0, g_base0 = attn_bwd(qkv0, g_att0, base_s, fc, spatial)
     gt_s = jnp.einsum(
         "hjai,bji->hab",
@@ -1464,27 +1461,27 @@
         precision=HIGHEST_PRECISION,
     ).reshape(16, n_s)
     a0_keep, a0_send = qkv_grad(g_proj0, normed0, o0_keep, o0_send, table_rows(gt_s, gt_t))
-    a0_keep, a0_send, got_f0, own_ga1, g_proj0 = sync(a0_keep, a0_send, got_f0, own_ga1, g_proj0)
+    a0_keep, a0_send, got_f0, mine_a1, g_proj0 = sync(a0_keep, a0_send, got_f0, mine_a1, g_proj0)
     a0_got = swap(a0_send, CORE)
     half_f0 = sum_cross(total_f0, got_f0)
     got_f0 = send_corner(half_f0)
-    own_ga1 = jnp.stack(own_ga1)
-    other_gf1, other_ga1 = swap(own_gf1, CORE), swap(own_ga1, CORE)
-    g_feed = finish_feed(place, own_gf1, other_gf1, 1, ())
-    g_attn = finish_attn(place, own_ga1, other_ga1, 1, (), 0)
-    half_f0, got_f0, a0_got, g_feed, g_attn, g_proj0 = sync(
-        half_f0, got_f0, a0_got, g_feed, g_attn, g_proj0
-    )
+    half_f0, got_f0, a0_got, g_proj0 = sync(half_f0, got_f0, a0_got, g_proj0)
+    z_f0 = sum_corner(half_f0, got_f0, z)
     total_a0 = sum_core(a0_keep, a0_got)
-    z_f0 = sum_corner(half_f0, got_f0, z)
     total_a0, z_f0, g_proj0 = sync(total_a0, z_f0, g_proj0)
+    mine_f0 = sum_line(z_f0)
     got_a0 = send_cross(total_a0)
-    mine_f0 = sum_line(z_f0)
     grad0, sums_q0 = qkv_back(g_proj0, weights_a0, hidden0, g_mid0, mods, 0, F32, 1)
     grad0, sums_q0, got_a0 = sync(grad0, sums_q0, got_a0)
     half_a0 = sum_cross(total_a0, got_a0)
     half_a0, grad0, sums_q0 = sync(half_a0, grad0, sums_q0)
     got_a0 = send_corner(half_a0)
+    own_gf1 = cross_stage(mine_f1)
+    got_a0, own_gf1, mine_f0 = sync(got_a0, own_gf1, mine_f0)
+    mine_a0 = sum_line(sum_corner(half_a0, got_a0, z))
+    own_gf0 = cross_stage(mine_f0)
+    own_gf1 = jnp.stack(own_gf1)
+    other_gf1 = swap(own_gf1, CORE)
     grad_tokens = spatial_to_rows(grad0, odd)
     mod_rows = jnp.concatenate(
         [
@@ -1493,24 +1490,25 @@
         ],
         axis=0,
     )
-    got_a0, mine_f0, mod_rows, grad_tokens = sync(got_a0, mine_f0, mod_rows, grad_tokens)
-    mine_a0 = sum_line(sum_corner(half_a0, got_a0, z))
-    own_gf0 = cross_stage(mine_f0)
-    mod_got = [from_z(mod_rows, 1), from_z(mod_rows, 2)]
-    mine_a0, own_gf0, mod_got = sync(mine_a0, own_gf0, mod_got)
-    own_ga0 = cross_stage(mine_a0)
+    mine_a0, own_gf0, other_gf1, grad_tokens = sync(mine_a0, own_gf0, other_gf1, grad_tokens)
+    mine_a = jnp.concatenate([mine_a0[:128], mine_a1, mine_a0[128:]], axis=0)
+    own_ga = cross_stage(mine_a)
     own_gf0 = jnp.stack(own_gf0)
     other_gf0 = swap(own_gf0, CORE)
-    mod_got = mod_got + [from_z(mod_rows, 3)]
+    mod_got = [from_z(mod_rows, 1)]
+    g_feed = finish_feed(place, own_gf1, other_gf1, 1, ())
+    own_ga, other_gf0, g_feed, mod_got = sync(own_ga, other_gf0, g_feed, mod_got)
+    own_ga = jnp.stack(own_ga)
+    other_ga = swap(own_ga, CORE)
+    mod_got = mod_got + [from_z(mod_rows, 2), from_z(mod_rows, 3)]
     g_feed = finish_feed(place, own_gf0, other_gf0, 0, g_feed)
-    own_ga0, g_feed, mod_got = sync(own_ga0, g_feed, mod_got)
-    own_ga0 = jnp.stack(own_ga0)
-    other_ga0 = swap(own_ga0, CORE)
-    g_attn = finish_attn(place, own_ga0, other_ga0, 0, g_attn, 0)
+    own_ga, other_ga, g_feed, mod_got = sync(own_ga, other_ga, g_feed, mod_got)
+    own_ga0 = own_ga
+    g_attn = finish_attn(place, own_ga, other_ga)
     tab = jnp.concatenate(
         [lax.dynamic_slice_in_dim(own_ga0, chip ^ m, 1, axis=0) for m in range(4)], axis=0
     )
-    tab = tab[:, 128:144].reshape(4, 16 * D).astype(F32)
+    tab = tab[:, 256:272].reshape(4, 16 * D).astype(F32)
     return (
         output,
         grad_tokens,

time: 1020 us -> 1050 us (1.029)
  waiting for transfers between devices: 147 us -> 187 us
    ppermute x57 -> x53, waiting for transfers between devices: 54 us -> 105 us  [swap(): return lax.ppermute(values, 'clip', [(i, i ^ bit) for i in range(8)])]
    ppermute x4, waiting for transfers between devices: 45.3 us -> 60.1 us  [partner(): return lax.ppermute(values, 'head', [(i, i ^ 1) for i in range(NZ)])]
    all_gather x1, waiting for transfers between devices: 12.4 us -> 0.85 us  [on_device_windows(): z_a1 = lax.all_gather(local_a1[0, 0], 'head')]
    ppermute x57 -> x53, starting transfers between devices: 49.9 us -> 47.5 us  [swap(): return lax.ppermute(values, 'clip', [(i, i ^ bit) for i in range(8)])]
  transfers between devices with their start and end apart: 83 -> 79, of which waited for: 31 -> 25; matrix products, arithmetic and copies ran while one was open for 16% -> 14% of each run, Pallas kernels for 50% -> 48%
where the time goes in v4:
time: 1050 us; the launch traced here: 1040 us
  Pallas kernels  520 us (50%)
  waiting for transfers between devices  187 us (18%)
  other arithmetic  118 us (11%)
  starting transfers between devices  103 us (10%)
  local copies, waits for them, and re-layouts  81.8 us (8%)
  matrix products  17.4 us (2%)
  between operations  16.4 us (2%)
    pallas_call x2, Pallas kernels, ffn_bwd(): call(kernel, 'ffn_bwd', (NZ,), [full((rows, D)), pl.BlockSpec((rows, D),...  123 us
    ppermute x53, waiting for transfers between devices, swap(): return lax.ppermute(values, 'clip', [(i, i ^ bit) for i in range(8)])  105 us
    pallas_call x2, Pallas kernels, attn_bwd(): call(kernel, 'attn_bwd', (NZ,), [xspec, pl.BlockSpec((parts, count, size,...  75.7 us
    pallas_call x2, Pallas kernels, ffn_fwd(): call(kernel, 'ffn_fwd', (NZ,), [full((rows, D))] + feed_specs(down_block)...  70.7 us
    ppermute x4, waiting for transfers between devices, partner(): return lax.ppermute(values, 'head', [(i, i ^ 1) for i in range(NZ)])  60.1 us
    ppermute x53, starting transfers between devices, swap(): return lax.ppermute(values, 'clip', [(i, i ^ bit) for i in range(8)])  47.5 us
    convert_element_type x13, other arithmetic, add(): return (first.astype(F32) + second.astype(F32)).astype(BF16)  46.1 us
    pallas_call x2, Pallas kernels, attn_fwd(): call(kernel, 'attn_fwd', (NZ,), [pl.BlockSpec((parts, count, size, 768),...  43.4 us
  transfers between devices with their start and end apart: 79, of which 25 were waited for; matrix products, arithmetic and copies ran while one was open for 14% of the time, Pallas kernels for 48%

profile of v4, /device:TPU:0, one launch (start us, length us, event | category | flops | bytes accessed | tf_op | source)
XLA Modules:
  0.0 1044.6 jit_solution(13129033418080399292)
XLA Ops:
  71.9 10.7 %collective-permute-done.6 = bf16[3,128,1024]{2,1,0:T(8,128)(2,1)} collective-permute-done((bf16[3,128,1024]{2,1,0:T(8,128)(2,1)S(1)}, bf16[3,128,1024]{2,1,0:T(8,128)(2,1)}, u32[]{:S(2)}, u32[]{:S(2)}) %collective-permute-start.6) | collective-permute-done | bytes 786464 | tf_op jit(solution)/shard_map/ppermute | solution.py:1212
  96.0 15.9 %ln_qkv.2 = (bf16[1280,1024]{1,0:T(8,128)(2,1)}, bf16[1280,3072]{1,0:T(8,128)(2,1)}) custom-call(bf16[1280,1024]{1,0:T(8,128)(2,1)} %maximum_select_fusion.1.h_ref, f32[12,1024]{1,0:T(8,128)} %bitcast.286, bf16[2,4,128,1024]{3,2,1,0:T(8,128)(2,1)} %prep_attn.2.l_ref, bf16[4,3,128,1024]{3,2,1,0:T(8,128)(2,1)} %copy-done.2, ...), custom_call_target="tpu_custom_call" | custom-call | flops 2013265920 | bytes 5505024 | tf_op jit(solution)/shard_map/ln_qkv/pallas_call | solution.py:502
  123.6 20.5 %attn_fwd.2 = bf16[1,5,256,1024]{3,2,1,0:T(8,128)(2,1)} custom-call(bf16[1,5,256,3072]{3,2,1,0:T(8,128)(2,1)} %bitcast.306, f32[16,16,512]{2,1,0:T(8,128)} %pad.18.b_ref, s32[1]{0:T(128)} %copy.97.fc_ref), custom_call_target="tpu_custom_call" | custom-call | flops 1342177280 | bytes 2621440 | tf_op jit(solution)/shard_map/attn_fwd/pallas_call | solution.py:557
  152.3 9.3 out_proj.2
  171.4 35.6 %ffn_fwd.2 = (bf16[1280,4096]{1,0:T(8,128)(2,1)}, bf16[1280,1024]{1,0:T(8,128)(2,1)}, bf16[1280,1024]{1,0:T(8,128)(2,1)}) custom-call(bf16[1280,1024]{1,0:T(8,128)(2,1)} %get-tuple-element.267.x_ref, bf16[2,4,256,1024]{3,2,1,0:T(8,128)(2,1)} %prep_feed.2.refs_0_, bf16[4,3,128,1024]{3,2,1,0:T(8,128)(2,1)} %copy-done.5, ...), custom_call_target="tpu_custom_call" | custom-call | flops 5368709120 | bytes 10747904 | tf_op jit(solution)/shard_map/ffn_fwd/pallas_call | solution.py:747
  258.0 11.5 %collective-permute-done.25 = bf16[128,1024]{1,0:T(8,128)(2,1)} collective-permute-done((bf16[128,1024]{1,0:T(8,128)(2,1)}, bf16[128,1024]{1,0:T(8,128)(2,1)}, u32[]{:S(2)}, u32[]{:S(2)}) %collective-permute-start.25) | collective-permute-done | bytes 262176 | tf_op jit(solution)/shard_map/ppermute | solution.py:1136
  280.9 15.9 %ln_qkv.3 = (bf16[1280,1024]{1,0:T(8,128)(2,1)}, bf16[1280,3072]{1,0:T(8,128)(2,1)}) custom-call(bf16[1280,1024]{1,0:T(8,128)(2,1)} %bitcast.40.h_ref, f32[12,1024]{1,0:T(8,128)} %bitcast.289, bf16[2,4,128,1024]{3,2,1,0:T(8,128)(2,1)} %prep_attn.3.l_ref, bf16[4,3,128,1024]{3,2,1,0:T(8,128)(2,1)} %copy-done.3, ...), custom_call_target="tpu_custom_call" | custom-call | flops 2013265920 | bytes 5505024 | tf_op jit(solution)/shard_map/ln_qkv/pallas_call | solution.py:502
  311.4 22.9 %attn_fwd.3 = bf16[5,4,64,1024]{3,2,1,0:T(8,128)(2,1)} custom-call(bf16[5,4,64,3072]{3,2,1,0:T(8,128)(2,1)} %bitcast.304, f32[16,64,640]{2,1,0:T(8,128)} %pad.19.b_ref, s32[1]{0:T(128)} %copy.97.fc_ref), custom_call_target="tpu_custom_call" | custom-call | flops 1677721600 | bytes 2621440 | tf_op jit(solution)/shard_map/attn_fwd/pallas_call | solution.py:557
  334.3 9.3 out_proj.3
  343.6 35.1 %ffn_fwd.3 = (bf16[1280,4096]{1,0:T(8,128)(2,1)}, bf16[1280,1024]{1,0:T(8,128)(2,1)}, bf16[1280,1024]{1,0:T(8,128)(2,1)}) custom-call(bf16[1280,1024]{1,0:T(8,128)(2,1)} %get-tuple-element.293.x_ref, bf16[2,4,256,1024]{3,2,1,0:T(8,128)(2,1)} %prep_feed.3.refs_0_, bf16[4,3,256,1024]{3,2,1,0:T(8,128)(2,1)} %pad_maximum_fusion.refs_1_.refs_3_, ...), custom_call_target="tpu_custom_call" | custom-call | flops 5368709120 | bytes 10747904 | tf_op jit(solution)/shard_map/ffn_fwd/pallas_call | solution.py:747
  388.0 61.2 %ffn_bwd.2 = (bf16[4,4,256,1024]{3,2,1,0:T(8,128)(2,1)}, bf16[4,4,256,1024]{3,2,1,0:T(8,128)(2,1)}, f32[1280,1024]{1,0:T(8,128)}) custom-call(bf16[1280,1024]{1,0:T(8,128)(2,1)} %get-tuple-element.555.g_ref, bf16[1280,4096]{1,0:T(8,128)(2,1)} %get-tuple-element.299.p_ref, bf16[1280,1024]{1,0:T(8,128)(2,1)} %get-tuple-element.293.x_ref, ...), custom_call_target="tpu_custom_call" | custom-call | flops 10737418240 | bytes 13631488 | tf_op jit(solution)/shard_map/ffn_bwd/pallas_call | solution.py:809
  449.3 18.7 %out_bwd.2 = (f32[1280,1024]{1,0:T(8,128)}, bf16[1280,1024]{1,0:T(8,128)(2,1)}, bf16[4,4,32,1024]{3,2,1,0:T(8,128)(2,1)}, bf16[4,4,32,1024]{3,2,1,0:T(8,128)(2,1)}, f32[8,1024]{1,0:T(8,128)}) custom-call(bf16[1280,1024]{1,0:T(8,128)(2,1)} %get-tuple-element.555.g_ref, f32[1280,1024]{1,0:T(8,128)} %get-tuple-element.304.gs_ref, ...), custom_call_target="tpu_custom_call" | custom-call | flops 1342177280 | bytes 8912896 | tf_op jit(solution)/shard_map/out_bwd/pallas_call | solution.py:873
  468.1 9.0 fusion.16
  482.7 42.9 %attn_bwd.2 = (bf16[5,4,64,3072]{3,2,1,0:T(8,128)(2,1)}, f32[16,64,640]{2,1,0:T(8,128)}) custom-call(bf16[5,4,64,3072]{3,2,1,0:T(8,128)(2,1)} %bitcast.305, bf16[5,4,64,1024]{3,2,1,0:T(8,128)(2,1)} %bitcast.358, f32[16,64,640]{2,1,0:T(8,128)} %pad.19.b_ref, s32[1]{0:T(128)} %copy.97.fc_ref), custom_call_target="tpu_custom_call" | custom-call | flops 4194304000 | bytes 5242880 | tf_op jit(solution)/shard_map/attn_bwd/pallas_call | solution.py:620
  537.1 20.3 %qkv_back.2 = (bf16[1280,512]{1,0:T(8,128)(2,1)}, bf16[1280,512]{1,0:T(8,128)(2,1)}, f32[8,1024]{1,0:T(8,128)}) custom-call(bf16[1280,3072]{1,0:T(8,128)(2,1)} %bitcast.266, bf16[2,4,128,1024]{3,2,1,0:T(8,128)(2,1)} %prep_attn.3.l_ref, bf16[4,3,128,1024]{3,2,1,0:T(8,128)(2,1)} %copy-done.3, bf16[4,3,128,1024]{3,2,1,0:T(8,128)(2,1)} %collective-permute-done.24.v_ref, ...), custom_call_target="tpu_custom_call" | custom-call | flops 2013265920 | bytes 8126464 | tf_op jit(solution)/shard_map/qkv_back/pallas_call | solution.py:933
  582.6 13.2 %qkv_grad.2 = (bf16[4,4,128,1024]{3,2,1,0:T(8,128)(2,1)}, bf16[4,4,128,1024]{3,2,1,0:T(8,128)(2,1)}) custom-call(bf16[1280,3072]{1,0:T(8,128)(2,1)} %bitcast.267, bf16[1280,1024]{1,0:T(8,128)(2,1)} %get-tuple-element.336.n_ref, bf16[4,4,32,1024]{3,2,1,0:T(8,128)(2,1)} %get-tuple-element.337.ok_ref, bf16[4,4,32,1024]{3,2,1,0:T(8,128)(2,1)} %get-tuple-element.338.os_ref), custom_call_target="tpu_custom_call" | custom-call | flops 2013265920 | bytes 4718592 | tf_op jit(solution)/shard_map/qkv_grad/pallas_call | solution.py:969
  611.2 24.7 %collective-permute-done.36 = bf16[128,1024]{1,0:T(8,128)(2,1)S(1)} collective-permute-done((bf16[128,1024]{1,0:T(8,128)(2,1)S(1)}, bf16[128,1024]{1,0:T(8,128)(2,1)S(1)}, u32[]{:S(2)}, u32[]{:S(2)}) %collective-permute-start.36) | collective-permute-done | bytes 262176 | tf_op jit(solution)/shard_map/ppermute | solution.py:1136
  650.7 61.6 %ffn_bwd.3 = (bf16[4,4,256,1024]{3,2,1,0:T(8,128)(2,1)}, bf16[4,4,256,1024]{3,2,1,0:T(8,128)(2,1)}, f32[1280,1024]{1,0:T(8,128)}) custom-call(bf16[1280,1024]{1,0:T(8,128)(2,1)} %bitcast.279, bf16[1280,4096]{1,0:T(8,128)(2,1)} %get-tuple-element.352.p_ref, bf16[1280,1024]{1,0:T(8,128)(2,1)} %get-tuple-element.267.x_ref, ...), custom_call_target="tpu_custom_call" | custom-call | flops 10737418240 | bytes 13631488 | tf_op jit(solution)/shard_map/ffn_bwd/pallas_call | solution.py:809
  718.6 18.5 %out_bwd.3 = (f32[1280,1024]{1,0:T(8,128)}, bf16[1280,1024]{1,0:T(8,128)(2,1)}, bf16[4,4,32,1024]{3,2,1,0:T(8,128)(2,1)}, bf16[4,4,32,1024]{3,2,1,0:T(8,128)(2,1)}, f32[8,1024]{1,0:T(8,128)}) custom-call(bf16[1280,1024]{1,0:T(8,128)(2,1)} %bitcast.280, f32[1280,1024]{1,0:T(8,128)} %get-tuple-element.360.gs_ref, ...), custom_call_target="tpu_custom_call" | custom-call | flops 1342177280 | bytes 8912896 | tf_op jit(solution)/shard_map/out_bwd/pallas_call | solution.py:873
  737.1 9.0 fusion.20
  751.8 32.8 %attn_bwd.3 = (bf16[1,5,256,3072]{3,2,1,0:T(8,128)(2,1)}, f32[16,16,512]{2,1,0:T(8,128)}) custom-call(bf16[1,5,256,3072]{3,2,1,0:T(8,128)(2,1)} %bitcast.307, bf16[1,5,256,1024]{3,2,1,0:T(8,128)(2,1)} %bitcast.357, f32[16,16,512]{2,1,0:T(8,128)} %pad.18.b_ref, s32[1]{0:T(128)} %copy.97.fc_ref), custom_call_target="tpu_custom_call" | custom-call | flops 3355443200 | bytes 5242880 | tf_op jit(solution)/shard_map/attn_bwd/pallas_call | solution.py:620
  794.1 13.4 %qkv_grad.3 = (bf16[4,4,144,1024]{3,2,1,0:T(8,128)(2,1)}, bf16[4,4,144,1024]{3,2,1,0:T(8,128)(2,1)}) custom-call(bf16[1280,3072]{1,0:T(8,128)(2,1)} %bitcast.264, bf16[1280,1024]{1,0:T(8,128)(2,1)} %get-tuple-element.370.n_ref, bf16[4,4,32,1024]{3,2,1,0:T(8,128)(2,1)} %get-tuple-element.371.ok_ref, bf16[4,4,32,1024]{3,2,1,0:T(8,128)(2,1)} %get-tuple-element.372.os_ref, ...), custom_call_target="tpu_custom_call" | custom-call | flops 2013265920 | bytes 4718592 | tf_op jit(solution)/shard_map/qkv_grad/pallas_call | solution.py:969
  813.7 23.5 %collective-permute-done.43 = bf16[4,128,1024]{2,1,0:T(8,128)(2,1)S(1)} collective-permute-done((bf16[4,128,1024]{2,1,0:T(8,128)(2,1)S(1)}, bf16[4,128,1024]{2,1,0:T(8,128)(2,1)S(1)}, u32[]{:S(2)}, u32[]{:S(2)}) %collective-permute-start.43) | collective-permute-done | bytes 1048608 | tf_op jit(solution)/shard_map/ppermute | solution.py:1212
  854.5 21.8 %qkv_back.3 = (f32[1280,1024]{1,0:T(8,128)}, f32[8,1024]{1,0:T(8,128)}) custom-call(bf16[1280,3072]{1,0:T(8,128)(2,1)} %bitcast.265, bf16[2,4,128,1024]{3,2,1,0:T(8,128)(2,1)} %prep_attn.2.l_ref, bf16[4,3,128,1024]{3,2,1,0:T(8,128)(2,1)} %copy-done.2, bf16[4,3,128,1024]{3,2,1,0:T(8,128)(2,1)} %collective-permute-done.10.v_ref, ...), custom_call_target="tpu_custom_call" | custom-call | flops 2013265920 | bytes 8126464 | tf_op jit(solution)/shard_map/qkv_back/pallas_call | solution.py:933
  888.0 23.0 %collective-permute-done.50 = bf16[256,1024]{1,0:T(8,128)(2,1)S(1)} collective-permute-done((bf16[256,1024]{1,0:T(8,128)(2,1)S(1)}, bf16[256,1024]{1,0:T(8,128)(2,1)S(1)}, u32[]{:S(2)}, u32[]{:S(2)}) %collective-permute-start.50) | collective-permute-done | bytes 524320 | tf_op jit(solution)/shard_map/ppermute | solution.py:1212
  911.1 8.7 collective-permute-done.52
  930.9 23.9 %collective-permute-done.57 = f32[128,1024]{1,0:T(8,128)S(1)} collective-permute-done((f32[128,1024]{1,0:T(8,128)S(1)}, f32[128,1024]{1,0:T(8,128)S(1)}, u32[]{:S(2)}, u32[]{:S(2)}) %collective-permute-start.57) | collective-permute-done | bytes 524320 | tf_op jit(solution)/shard_map/ppermute | solution.py:1136
  962.0 8.1 collective-permute-done.53
  990.1 9.0 finish_feed.2
  999.1 8.5 collective-permute-done.59
  1015.6 9.0 finish_feed.3
  1027.4 9.4 finish_attn.1
  (398 shorter events, 371.3 us)
Async XLA Ops:
  7.2 78.3 %all-gather.9.cloned.1.call-start = ((), (), s32[]{:S(2)}) async-start(), calls=%async_computation.13 | async-start | bytes 1310720 | tf_op jit(solution)/shard_map/all_gather | solution.py:1348
  56.1 59.2 %all-gather.11.cloned.1.call-start = ((), (), s32[]{:S(2)}) async-start(), calls=%async_computation.14 | async-start | bytes 1310720 | tf_op jit(solution)/shard_map/all_gather | solution.py:1349
  87.6 57.3 %all-gather.13.cloned.1.call-start = ((), (), s32[]{:S(2)}) async-start(), calls=%async_computation.15 | async-start | bytes 1310720 | tf_op jit(solution)/shard_map/all_gather | solution.py:1366
  95.1 117.5 %all-gather.15.cloned.1.call-start = ((), (), s32[]{:S(2)}) async-start(), calls=%async_computation.16 | async-start | bytes 2621440 | tf_op jit(solution)/shard_map/all_gather | solution.py:1377
  167.8 44.8 %collective-permute-start.21 = (bf16[3,128,1024]{2,1,0:T(8,128)(2,1)}, bf16[3,128,1024]{2,1,0:T(8,128)(2,1)}, u32[]{:S(2)}, u32[]{:S(2)}) collective-permute-start(bf16[3,128,1024]{2,1,0:T(8,128)(2,1)} %pad_maximum_fusion.20), channel_id=1, source_target_pairs={{0,8},{4,12},{8,0},{12,4},{16,24},{20,28},{24,16},{28,20},{1,9},{5... | collective-permute-start | bytes 2359304 | tf_op jit(solution)/shard_map/ppermute | solution.py:1212
  168.9 43.7 %collective-permute-start.22 = (bf16[3,128,1024]{2,1,0:T(8,128)(2,1)}, bf16[3,128,1024]{2,1,0:T(8,128)(2,1)}, u32[]{:S(2)}, u32[]{:S(2)}) collective-permute-start(bf16[3,128,1024]{2,1,0:T(8,128)(2,1)} %pad_maximum_fusion.20), channel_id=1, source_target_pairs={{0,16},{4,20},{8,24},{12,28},{16,0},{20,4},{24,8},{28,12},{1,17},{... | collective-permute-start | bytes 2359304 | tf_op jit(solution)/shard_map/ppermute | solution.py:1212
  169.7 42.9 %collective-permute-start.23 = (bf16[3,128,1024]{2,1,0:T(8,128)(2,1)}, bf16[3,128,1024]{2,1,0:T(8,128)(2,1)}, u32[]{:S(2)}, u32[]{:S(2)}) collective-permute-start(bf16[3,128,1024]{2,1,0:T(8,128)(2,1)} %pad_maximum_fusion.20), channel_id=1, source_target_pairs={{0,24},{4,28},{8,16},{12,20},{16,8},{20,12},{24,0},{28,4},{1,25},{... | collective-permute-start | bytes 2359304 | tf_op jit(solution)/shard_map/ppermute | solution.py:1212
  216.2 64.7 %all-to-all-start = ((bf16[4,320,1024]{2,1,0:T(8,128)(2,1)}), bf16[4,320,1024]{2,1,0:T(8,128)(2,1)}, u32[]{:S(2)}, u32[]{:S(2)}) async-start(bf16[4,320,1024]{2,1,0:T(8,128)(2,1)} %bitcast.39), calls=%async_computation | async-start | bytes 5242880 | tf_op jit(solution)/shard_map/all_to_all | solution.py:1174
  223.4 49.6 %collective-permute-start.24 = (bf16[4,3,128,1024]{3,2,1,0:T(8,128)(2,1)S(1)}, bf16[4,3,128,1024]{3,2,1,0:T(8,128)(2,1)}, u32[]{:S(2)}, u32[]{:S(2)}) collective-permute-start(bf16[4,3,128,1024]{3,2,1,0:T(8,128)(2,1)S(1)} %pad_maximum_fusion.4.w_ref), channel_id=1, source_target_pairs={{0,4},{4,0},{8,12},{12,8},{16,20},{20,16},{24,28},{28,24},{1,5},{5... | collective-permute-start | bytes 9437192 | tf_op jit(solution)/shard_map/ppermute | solution.py:1212
  225.7 71.2 %collective-permute-start.26 = (bf16[3,256,1024]{2,1,0:T(8,128)(2,1)}, bf16[3,256,1024]{2,1,0:T(8,128)(2,1)}, u32[]{:S(2)}, u32[]{:S(2)}) collective-permute-start(bf16[3,256,1024]{2,1,0:T(8,128)(2,1)} %pad_maximum_fusion.13), channel_id=1, source_target_pairs={{0,8},{4,12},{8,0},{12,4},{16,24},{20,28},{24,16},{28,20},{1,9},{5... | collective-permute-start | bytes 4718600 | tf_op jit(solution)/shard_map/ppermute | solution.py:1212
  227.1 70.8 %collective-permute-start.27 = (bf16[3,256,1024]{2,1,0:T(8,128)(2,1)}, bf16[3,256,1024]{2,1,0:T(8,128)(2,1)}, u32[]{:S(2)}, u32[]{:S(2)}) collective-permute-start(bf16[3,256,1024]{2,1,0:T(8,128)(2,1)} %pad_maximum_fusion.13), channel_id=1, source_target_pairs={{0,16},{4,20},{8,24},{12,28},{16,0},{20,4},{24,8},{28,12},{1,17},{... | collective-permute-start | bytes 4718600 | tf_op jit(solution)/shard_map/ppermute | solution.py:1212
  228.6 69.3 %collective-permute-start.28 = (bf16[3,256,1024]{2,1,0:T(8,128)(2,1)}, bf16[3,256,1024]{2,1,0:T(8,128)(2,1)}, u32[]{:S(2)}, u32[]{:S(2)}) collective-permute-start(bf16[3,256,1024]{2,1,0:T(8,128)(2,1)} %pad_maximum_fusion.13), channel_id=1, source_target_pairs={{0,24},{4,28},{8,16},{12,20},{16,8},{20,12},{24,0},{28,4},{1,25},{... | collective-permute-start | bytes 4718600 | tf_op jit(solution)/shard_map/ppermute | solution.py:1212
  231.0 38.5 %collective-permute-start.25 = (bf16[128,1024]{1,0:T(8,128)(2,1)}, bf16[128,1024]{1,0:T(8,128)(2,1)}, u32[]{:S(2)}, u32[]{:S(2)}) collective-permute-start(bf16[128,1024]{1,0:T(8,128)(2,1)} %bitcast.55), channel_id=1, source_target_pairs={{0,1},{1,0},{2,3},{3,2},{4,5},{5,4},{6,7},{7,6},{8,9},{9,8},{10,11... | collective-permute-start | bytes 786440 | tf_op jit(solution)/shard_map/ppermute | solution.py:1136
  304.6 39.0 %collective-permute-start.29 = (bf16[4,3,256,1024]{3,2,1,0:T(8,128)(2,1)}, bf16[4,3,256,1024]{3,2,1,0:T(8,128)(2,1)}, u32[]{:S(2)}, u32[]{:S(2)}) collective-permute-start(bf16[4,3,256,1024]{3,2,1,0:T(8,128)(2,1)} %pad_maximum_fusion.refs_1_.refs_3_), channel_id=1, source_target_pairs={{0,4},{4,0},{8,12},{12,8},{16,20},{20,16},{24,28},{28,24},{1,5},{5... | collective-permute-start | bytes 18874376 | tf_op jit(solution)/shard_map/ppermute | solution.py:1212
  306.4 72.3 %all-to-all-start.1 = ((bf16[4,320,1024]{2,1,0:T(8,128)(2,1)}), bf16[4,320,1024]{2,1,0:T(8,128)(2,1)S(1)}, u32[]{:S(2)}, u32[]{:S(2)}) async-start(bf16[4,320,1024]{2,1,0:T(8,128)(2,1)} %bitcast.64), calls=%async_computation.1 | async-start | bytes 5242880 | tf_op jit(solution)/shard_map/all_to_all | solution.py:1174
  382.7 66.5 %all-to-all-start.2 = ((bf16[4,320,1024]{2,1,0:T(8,128)(2,1)}), bf16[4,320,1024]{2,1,0:T(8,128)(2,1)S(1)}, u32[]{:S(2)}, u32[]{:S(2)}) async-start(bf16[4,320,1024]{2,1,0:T(8,128)(2,1)} %bitcast.285), calls=%async_computation.2 | async-start | bytes 5242880 | tf_op jit(solution)/shard_map/all_to_all | solution.py:1174
  479.0 48.3 %collective-permute-start.32 = (bf16[2,4,128,1024]{3,2,1,0:T(8,128)(2,1)}, bf16[2,4,128,1024]{3,2,1,0:T(8,128)(2,1)}, u32[]{:S(2)}, u32[]{:S(2)}) collective-permute-start(bf16[2,4,128,1024]{3,2,1,0:T(8,128)(2,1)} %pad_maximum_fusion.8), channel_id=1, source_target_pairs={{0,16},{4,20},{8,24},{12,28},{16,0},{20,4},{24,8},{28,12},{1,17},{... | collective-permute-start | bytes 6291464 | tf_op jit(solution)/shard_map/ppermute | solution.py:1212
  482.1 48.0 %collective-permute-start.31 = (bf16[2,4,128,1024]{3,2,1,0:T(8,128)(2,1)}, bf16[2,4,128,1024]{3,2,1,0:T(8,128)(2,1)}, u32[]{:S(2)}, u32[]{:S(2)}) collective-permute-start(bf16[2,4,128,1024]{3,2,1,0:T(8,128)(2,1)} %pad_maximum_fusion.7), channel_id=1, source_target_pairs={{0,8},{4,12},{8,0},{12,4},{16,24},{20,28},{24,16},{28,20},{1,9},{5... | collective-permute-start | bytes 6291464 | tf_op jit(solution)/shard_map/ppermute | solution.py:1212
  560.4 42.8 %all-to-all-start.3 = ((bf16[4,320,512]{2,1,0:T(8,128)(2,1)}), bf16[4,320,512]{2,1,0:T(8,128)(2,1)}, u32[]{:S(2)}, u32[]{:S(2)}) async-start(bf16[4,320,512]{2,1,0:T(8,128)(2,1)} %bitcast.326), calls=%async_computation.3 | async-start | bytes 2621440 | tf_op jit(solution)/shard_map/all_to_all | solution.py:1174
  603.2 40.0 %all-to-all-start.4 = ((bf16[4,320,512]{2,1,0:T(8,128)(2,1)}), bf16[4,320,512]{2,1,0:T(8,128)(2,1)}, u32[]{:S(2)}, u32[]{:S(2)}) async-start(bf16[4,320,512]{2,1,0:T(8,128)(2,1)} %bitcast.325), calls=%async_computation.4 | async-start | bytes 2621440 | tf_op jit(solution)/shard_map/all_to_all | solution.py:1174
  608.3 106.0 %reduce-scatter.5.cloned.1.call-start = ((), (), s32[]{:S(2)}) async-start(), calls=%async_computation.9 | async-start | bytes 2621440 | tf_op jit(solution)/shard_map/reduce_scatter | solution.py:1300
  643.2 164.2 %reduce-scatter.7.cloned.1.call-start = ((), (), s32[]{:S(2)}) async-start(), calls=%async_computation.10 | async-start | bytes 1310720 | tf_op jit(solution)/shard_map/reduce_scatter | solution.py:1300
  643.3 69.1 %collective-permute-start.37 = (bf16[4,128,1024]{2,1,0:T(8,128)(2,1)}, bf16[4,128,1024]{2,1,0:T(8,128)(2,1)S(1)}, u32[]{:S(2)}, u32[]{:S(2)}) collective-permute-start(bf16[4,128,1024]{2,1,0:T(8,128)(2,1)} %get-tuple-element.357), channel_id=1, source_target_pairs={{0,8},{4,12},{8,0},{12,4},{16,24},{20,28},{24,16},{28,20},{1,9},{5... | collective-permute-start | bytes 3145736 | tf_op jit(solution)/shard_map/ppermute | solution.py:1212
  644.5 67.9 %collective-permute-start.38 = (bf16[4,128,1024]{2,1,0:T(8,128)(2,1)S(1)}, bf16[4,128,1024]{2,1,0:T(8,128)(2,1)S(1)}, u32[]{:S(2)}, u32[]{:S(2)}) collective-permute-start(bf16[4,128,1024]{2,1,0:T(8,128)(2,1)S(1)} %get-tuple-element.358), channel_id=1, source_target_pairs={{0,16},{4,20},{8,24},{12,28},{16,0},{20,4},{24,8},{28,12},{1,17},{... | collective-permute-start | bytes 3145736 | tf_op jit(solution)/shard_map/ppermute | solution.py:1212
  645.4 69.0 %collective-permute-start.39 = (bf16[4,128,1024]{2,1,0:T(8,128)(2,1)S(1)}, bf16[4,128,1024]{2,1,0:T(8,128)(2,1)}, u32[]{:S(2)}, u32[]{:S(2)}) collective-permute-start(bf16[4,128,1024]{2,1,0:T(8,128)(2,1)S(1)} %get-tuple-element.359), channel_id=1, source_target_pairs={{0,24},{4,28},{8,16},{12,20},{16,8},{20,12},{24,0},{28,4},{1,25},{... | collective-permute-start | bytes 3145736 | tf_op jit(solution)/shard_map/ppermute | solution.py:1212
  718.6 201.3 %reduce-scatter.9.cloned.1.call-start = ((), (), s32[]{:S(2)}) async-start(), calls=%async_computation.11 | async-start | bytes 2621440 | tf_op jit(solution)/shard_map/reduce_scatter | solution.py:1300
  748.1 59.4 %collective-permute-start.42 = (bf16[2,4,128,1024]{3,2,1,0:T(8,128)(2,1)}, bf16[2,4,128,1024]{3,2,1,0:T(8,128)(2,1)}, u32[]{:S(2)}, u32[]{:S(2)}) collective-permute-start(bf16[2,4,128,1024]{3,2,1,0:T(8,128)(2,1)} %pad_maximum_fusion.10), channel_id=1, source_target_pairs={{0,16},{4,20},{8,24},{12,28},{16,0},{20,4},{24,8},{28,12},{1,17},{... | collective-permute-start | bytes 6291464 | tf_op jit(solution)/shard_map/ppermute | solution.py:1212
  751.0 56.5 %collective-permute-start.41 = (bf16[2,4,128,1024]{3,2,1,0:T(8,128)(2,1)}, bf16[2,4,128,1024]{3,2,1,0:T(8,128)(2,1)}, u32[]{:S(2)}, u32[]{:S(2)}) collective-permute-start(bf16[2,4,128,1024]{3,2,1,0:T(8,128)(2,1)} %pad_maximum_fusion.9), channel_id=1, source_target_pairs={{0,8},{4,12},{8,0},{12,4},{16,24},{20,28},{24,16},{28,20},{1,9},{5... | collective-permute-start | bytes 6291464 | tf_op jit(solution)/shard_map/ppermute | solution.py:1212
  848.6 129.3 %reduce-scatter.11.cloned.1.call-start = ((), (), s32[]{:S(2)}) async-start(), calls=%async_computation.12 | async-start | bytes 1474560 | tf_op jit(solution)/shard_map/reduce_scatter | solution.py:1300
  882.6 37.2 %collective-permute-start.48 = (bf16[4,72,1024]{2,1,0:T(8,128)(2,1)S(1)}, bf16[4,72,1024]{2,1,0:T(8,128)(2,1)S(1)}, u32[]{:S(2)}, u32[]{:S(2)}) collective-permute-start(bf16[4,72,1024]{2,1,0:T(8,128)(2,1)S(1)} %get-tuple-element.409), channel_id=1, source_target_pairs={{0,16},{4,20},{8,24},{12,28},{16,0},{20,4},{24,8},{28,12},{1,17},{... | collective-permute-start | bytes 1769480 | tf_op jit(solution)/shard_map/ppermute | solution.py:1212
  883.6 36.3 %collective-permute-start.49 = (bf16[4,72,1024]{2,1,0:T(8,128)(2,1)S(1)}, bf16[4,72,1024]{2,1,0:T(8,128)(2,1)S(1)}, u32[]{:S(2)}, u32[]{:S(2)}) collective-permute-start(bf16[4,72,1024]{2,1,0:T(8,128)(2,1)S(1)} %get-tuple-element.410), channel_id=1, source_target_pairs={{0,8},{4,12},{8,0},{12,4},{16,24},{20,28},{24,16},{28,20},{1,9},{5... | collective-permute-start | bytes 1769480 | tf_op jit(solution)/shard_map/ppermute | solution.py:1212
  925.3 52.5 %collective-permute-start.56 = (bf16[4,256,1024]{2,1,0:T(8,128)(2,1)S(1)}, bf16[4,256,1024]{2,1,0:T(8,128)(2,1)}, u32[]{:S(2)}, u32[]{:S(2)}) collective-permute-start(bf16[4,256,1024]{2,1,0:T(8,128)(2,1)S(1)} %pad_maximum_fusion.11.own_ref), channel_id=1, source_target_pairs={{0,4},{4,0},{8,12},{12,8},{16,20},{20,16},{24,28},{28,24},{1,5},{5... | collective-permute-start | bytes 6291464 | tf_op jit(solution)/shard_map/ppermute | solution.py:1212
  (95 other events, 1432.2 us)
Sparse Core Ops, SparseCore 0:
  56.3 29.1 all-gather.8
  87.8 27.5 all-gather.10
  117.5 27.4 all-gather.12
  167.9 44.6 all-gather.14
  643.4 45.1 reduce-scatter.4
  718.7 28.5 reduce-scatter.6
  848.7 45.7 reduce-scatter.8
  925.1 39.4 reduce-scatter.10

commit v5 on v4

--- a/solution.py
+++ b/solution.py
@@ -1445,14 +1445,16 @@
     f0_keep, f0_send, g_shift0 = ffn_bwd(grad1, pre0, shifted0, weights_f0, 0, mods, 0)
     f0_keep, f0_send, g_shift0, mine_f1, got_a1 = sync(f0_keep, f0_send, g_shift0, mine_f1, got_a1)
     f0_got = swap(f0_send, CORE)
+    sides_f1 = sides_stage(mine_f1[None])
     mine_a1 = sum_line(sum_plane(total_a1, got_a1, z))
     g_mid0, g_att0, o0_keep, o0_send, sums_o0 = out_bwd(
         grad1, g_shift0, middle0, feed0, branch0, attended0, weights_a0, mods, 0
     )
-    g_att0, f0_got = sync(g_att0, f0_got)
+    g_att0, f0_got, sides_f1 = sync(g_att0, f0_got, sides_f1)
     total_f0 = sum_core(f0_keep, f0_got)
     g_att0, total_f0 = sync(g_att0, total_f0)
     got_f0 = send_cross(total_f0)
+    corner_f1 = corner_stage(sides_f1)
     g_proj0, g_base0 = attn_bwd(qkv0, g_att0, base_s, fc, spatial)
     gt_s = jnp.einsum(
         "hjai,bji->hab",
@@ -1461,11 +1463,15 @@
         precision=HIGHEST_PRECISION,
     ).reshape(16, n_s)
     a0_keep, a0_send = qkv_grad(g_proj0, normed0, o0_keep, o0_send, table_rows(gt_s, gt_t))
-    a0_keep, a0_send, got_f0, mine_a1, g_proj0 = sync(a0_keep, a0_send, got_f0, mine_a1, g_proj0)
+    a0_keep, a0_send, got_f0, corner_f1, mine_a1, g_proj0 = sync(
+        a0_keep, a0_send, got_f0, corner_f1, mine_a1, g_proj0
+    )
     a0_got = swap(a0_send, CORE)
     half_f0 = sum_cross(total_f0, got_f0)
     got_f0 = send_corner(half_f0)
-    half_f0, got_f0, a0_got, g_proj0 = sync(half_f0, got_f0, a0_got, g_proj0)
+    own_gf1 = joined(sides_f1, corner_f1).reshape(4, 256, D)
+    g_feed = finish_feed(place, own_gf1, swap(own_gf1, CORE), 1, ())
+    half_f0, got_f0, a0_got, g_proj0, g_feed = sync(half_f0, got_f0, a0_got, g_proj0, g_feed)
     z_f0 = sum_corner(half_f0, got_f0, z)
     total_a0 = sum_core(a0_keep, a0_got)
     total_a0, z_f0, g_proj0 = sync(total_a0, z_f0, g_proj0)
@@ -1476,13 +1482,13 @@
     half_a0 = sum_cross(total_a0, got_a0)
     half_a0, grad0, sums_q0 = sync(half_a0, grad0, sums_q0)
     got_a0 = send_corner(half_a0)
-    own_gf1 = cross_stage(mine_f1)
-    got_a0, own_gf1, mine_f0 = sync(got_a0, own_gf1, mine_f0)
-    mine_a0 = sum_line(sum_corner(half_a0, got_a0, z))
+    sides_a1 = sides_stage(mine_a1[None])
+    got_a0, sides_a1, mine_f0 = sync(got_a0, sides_a1, mine_f0)
+    z_a0 = sum_corner(half_a0, got_a0, z)
+    z_a0, mine_f0 = sync(z_a0, mine_f0)
+    mine_a0 = sum_line(z_a0)
     own_gf0 = cross_stage(mine_f0)
-    own_gf1 = jnp.stack(own_gf1)
-    other_gf1 = swap(own_gf1, CORE)
-    grad_tokens = spatial_to_rows(grad0, odd)
+    corner_a1 = corner_stage(sides_a1)
     mod_rows = jnp.concatenate(
         [
             sums_q0[0:2], sums_o0[2:3], sums_o0[0:2], sums_o0[3:4],
@@ -1490,21 +1496,20 @@
         ],
         axis=0,
     )
-    mine_a0, own_gf0, other_gf1, grad_tokens = sync(mine_a0, own_gf0, other_gf1, grad_tokens)
-    mine_a = jnp.concatenate([mine_a0[:128], mine_a1, mine_a0[128:]], axis=0)
-    own_ga = cross_stage(mine_a)
+    mine_a0, own_gf0, corner_a1, mod_rows, grad0 = sync(mine_a0, own_gf0, corner_a1, mod_rows, grad0)
+    own_ga0 = cross_stage(mine_a0)
     own_gf0 = jnp.stack(own_gf0)
-    other_gf0 = swap(own_gf0, CORE)
-    mod_got = [from_z(mod_rows, 1)]
-    g_feed = finish_feed(place, own_gf1, other_gf1, 1, ())
-    own_ga, other_gf0, g_feed, mod_got = sync(own_ga, other_gf0, g_feed, mod_got)
-    own_ga = jnp.stack(own_ga)
-    other_ga = swap(own_ga, CORE)
-    mod_got = mod_got + [from_z(mod_rows, 2), from_z(mod_rows, 3)]
-    g_feed = finish_feed(place, own_gf0, other_gf0, 0, g_feed)
-    own_ga, other_ga, g_feed, mod_got = sync(own_ga, other_ga, g_feed, mod_got)
+    grad_tokens = spatial_to_rows(grad0, odd)
+    own_ga1 = joined(sides_a1, corner_a1).reshape(4, 128, D)
+    g_feed = finish_feed(place, own_gf0, swap(own_gf0, CORE), 0, g_feed)
+    own_ga0, g_feed, grad_tokens, mod_rows, own_ga1 = sync(
+        own_ga0, g_feed, grad_tokens, mod_rows, own_ga1
+    )
+    own_ga0 = jnp.stack(own_ga0)
+    own_ga = jnp.concatenate([own_ga0[:, :128], own_ga1, own_ga0[:, 128:]], axis=1)
+    mod_got = [from_z(mod_rows, d) for d in (1, 2, 3)]
     own_ga0 = own_ga
-    g_attn = finish_attn(place, own_ga, other_ga)
+    g_attn = finish_attn(place, own_ga, swap(own_ga, CORE))
     tab = jnp.concatenate(
         [lax.dynamic_slice_in_dim(own_ga0, chip ^ m, 1, axis=0) for m in range(4)], axis=0
     )

time: 1050 us -> 1020 us (0.971)
  waiting for transfers between devices: 187 us -> 149 us
    ppermute x53 -> x58, waiting for transfers between devices: 105 us -> 75 us  [swap(): return lax.ppermute(values, 'clip', [(i, i ^ bit) for i in range(8)])]
    ppermute x4, waiting for transfers between devices: 60.1 us -> 42.4 us  [partner(): return lax.ppermute(values, 'head', [(i, i ^ 1) for i in range(NZ)])]
    ppermute x53 -> x58, starting transfers between devices: 47.5 us -> 49.7 us  [swap(): return lax.ppermute(values, 'clip', [(i, i ^ bit) for i in range(8)])]
  transfers between devices with their start and end apart: 79 -> 84, of which waited for: 25 -> 25; matrix products, arithmetic and copies ran while one was open for 14% -> 16% of each run, Pallas kernels for 48% -> 50%
where the time goes in v5:
time: 1020 us; the launch traced here: 1010 us
  Pallas kernels  520 us (51%)
  waiting for transfers between devices  149 us (15%)
  other arithmetic  123 us (12%)
  starting transfers between devices  95.5 us (9%)
  local copies, waits for them, and re-layouts  85.5 us (8%)
  matrix products  17.4 us (2%)
  between operations  16.5 us (2%)
    pallas_call x2, Pallas kernels, ffn_bwd(): call(kernel, 'ffn_bwd', (NZ,), [full((rows, D)), pl.BlockSpec((rows, D),...  123 us
    pallas_call x2, Pallas kernels, attn_bwd(): call(kernel, 'attn_bwd', (NZ,), [xspec, pl.BlockSpec((parts, count, size,...  75.6 us
    ppermute x58, waiting for transfers between devices, swap(): return lax.ppermute(values, 'clip', [(i, i ^ bit) for i in range(8)])  75 us
    pallas_call x2, Pallas kernels, ffn_fwd(): call(kernel, 'ffn_fwd', (NZ,), [full((rows, D))] + feed_specs(down_block)...  70.6 us
    ppermute x58, starting transfers between devices, swap(): return lax.ppermute(values, 'clip', [(i, i ^ bit) for i in range(8)])  49.7 us
    convert_element_type x13, other arithmetic, add(): return (first.astype(F32) + second.astype(F32)).astype(BF16)  48.2 us
    pallas_call x2, Pallas kernels, attn_fwd(): call(kernel, 'attn_fwd', (NZ,), [pl.BlockSpec((parts, count, size, 768),...  43.3 us
    ppermute x4, waiting for transfers between devices, partner(): return lax.ppermute(values, 'head', [(i, i ^ 1) for i in range(NZ)])  42.4 us
  transfers between devices with their start and end apart: 84, of which 25 were waited for; matrix products, arithmetic and copies ran while one was open for 16% of the time, Pallas kernels for 50%

profile of v5, /device:TPU:0, one launch (start us, length us, event | category | flops | bytes accessed | tf_op | source)
XLA Modules:
  0.0 1007.4 jit_solution(13669334557861321616)
XLA Ops:
  23.6 6.9 prep_feed.2.refs_0_
  30.6 6.9 prep_feed.3.refs_0_
  72.0 10.7 %collective-permute-done.6 = bf16[3,128,1024]{2,1,0:T(8,128)(2,1)} collective-permute-done((bf16[3,128,1024]{2,1,0:T(8,128)(2,1)S(1)}, bf16[3,128,1024]{2,1,0:T(8,128)(2,1)}, u32[]{:S(2)}, u32[]{:S(2)}) %collective-permute-start.6) | collective-permute-done | bytes 786464 | tf_op jit(solution)/shard_map/ppermute | solution.py:1212
  96.0 16.0 %ln_qkv.2 = (bf16[1280,1024]{1,0:T(8,128)(2,1)}, bf16[1280,3072]{1,0:T(8,128)(2,1)}) custom-call(bf16[1280,1024]{1,0:T(8,128)(2,1)} %maximum_select_fusion.1.h_ref, f32[12,1024]{1,0:T(8,128)} %bitcast.310, bf16[2,4,128,1024]{3,2,1,0:T(8,128)(2,1)} %prep_attn.2.l_ref, bf16[4,3,128,1024]{3,2,1,0:T(8,128)(2,1)} %copy-done.2, ...), custom_call_target="tpu_custom_call" | custom-call | flops 2013265920 | bytes 5505024 | tf_op jit(solution)/shard_map/ln_qkv/pallas_call | solution.py:502
  123.6 20.5 %attn_fwd.2 = bf16[1,5,256,1024]{3,2,1,0:T(8,128)(2,1)} custom-call(bf16[1,5,256,3072]{3,2,1,0:T(8,128)(2,1)} %bitcast.330, f32[16,16,512]{2,1,0:T(8,128)} %pad.18.b_ref, s32[1]{0:T(128)} %copy.115.fc_ref), custom_call_target="tpu_custom_call" | custom-call | flops 1342177280 | bytes 2621440 | tf_op jit(solution)/shard_map/attn_fwd/pallas_call | solution.py:557
  152.3 9.3 out_proj.2
  171.4 35.6 %ffn_fwd.2 = (bf16[1280,4096]{1,0:T(8,128)(2,1)}, bf16[1280,1024]{1,0:T(8,128)(2,1)}, bf16[1280,1024]{1,0:T(8,128)(2,1)}) custom-call(bf16[1280,1024]{1,0:T(8,128)(2,1)} %get-tuple-element.271.x_ref, bf16[2,4,256,1024]{3,2,1,0:T(8,128)(2,1)} %prep_feed.2.refs_0_, bf16[4,3,128,1024]{3,2,1,0:T(8,128)(2,1)} %copy-done.5, ...), custom_call_target="tpu_custom_call" | custom-call | flops 5368709120 | bytes 10747904 | tf_op jit(solution)/shard_map/ffn_fwd/pallas_call | solution.py:747
  258.1 11.4 %collective-permute-done.25 = bf16[128,1024]{1,0:T(8,128)(2,1)} collective-permute-done((bf16[128,1024]{1,0:T(8,128)(2,1)}, bf16[128,1024]{1,0:T(8,128)(2,1)}, u32[]{:S(2)}, u32[]{:S(2)}) %collective-permute-start.25) | collective-permute-done | bytes 262176 | tf_op jit(solution)/shard_map/ppermute | solution.py:1136
  273.0 7.9 all-to-all-done
  281.0 15.9 %ln_qkv.3 = (bf16[1280,1024]{1,0:T(8,128)(2,1)}, bf16[1280,3072]{1,0:T(8,128)(2,1)}) custom-call(bf16[1280,1024]{1,0:T(8,128)(2,1)} %bitcast.40.h_ref, f32[12,1024]{1,0:T(8,128)} %bitcast.313, bf16[2,4,128,1024]{3,2,1,0:T(8,128)(2,1)} %prep_attn.3.l_ref, bf16[4,3,128,1024]{3,2,1,0:T(8,128)(2,1)} %copy-done.3, ...), custom_call_target="tpu_custom_call" | custom-call | flops 2013265920 | bytes 5505024 | tf_op jit(solution)/shard_map/ln_qkv/pallas_call | solution.py:502
  311.4 22.8 %attn_fwd.3 = bf16[5,4,64,1024]{3,2,1,0:T(8,128)(2,1)} custom-call(bf16[5,4,64,3072]{3,2,1,0:T(8,128)(2,1)} %bitcast.328, f32[16,64,640]{2,1,0:T(8,128)} %pad.19.b_ref, s32[1]{0:T(128)} %copy.115.fc_ref), custom_call_target="tpu_custom_call" | custom-call | flops 1677721600 | bytes 2621440 | tf_op jit(solution)/shard_map/attn_fwd/pallas_call | solution.py:557
  334.2 9.3 out_proj.3
  343.5 35.0 %ffn_fwd.3 = (bf16[1280,4096]{1,0:T(8,128)(2,1)}, bf16[1280,1024]{1,0:T(8,128)(2,1)}, bf16[1280,1024]{1,0:T(8,128)(2,1)}) custom-call(bf16[1280,1024]{1,0:T(8,128)(2,1)} %get-tuple-element.297.x_ref, bf16[2,4,256,1024]{3,2,1,0:T(8,128)(2,1)} %prep_feed.3.refs_0_, bf16[4,3,256,1024]{3,2,1,0:T(8,128)(2,1)} %pad_maximum_fusion.refs_1_.refs_3_, ...), custom_call_target="tpu_custom_call" | custom-call | flops 5368709120 | bytes 10747904 | tf_op jit(solution)/shard_map/ffn_fwd/pallas_call | solution.py:747
  387.9 61.2 %ffn_bwd.2 = (bf16[4,4,256,1024]{3,2,1,0:T(8,128)(2,1)}, bf16[4,4,256,1024]{3,2,1,0:T(8,128)(2,1)}, f32[1280,1024]{1,0:T(8,128)}) custom-call(bf16[1280,1024]{1,0:T(8,128)(2,1)} %get-tuple-element.563.g_ref, bf16[1280,4096]{1,0:T(8,128)(2,1)} %get-tuple-element.303.p_ref, bf16[1280,1024]{1,0:T(8,128)(2,1)} %get-tuple-element.297.x_ref, ...), custom_call_target="tpu_custom_call" | custom-call | flops 10737418240 | bytes 13631488 | tf_op jit(solution)/shard_map/ffn_bwd/pallas_call | solution.py:809
  449.2 18.7 %out_bwd.2 = (f32[1280,1024]{1,0:T(8,128)}, bf16[1280,1024]{1,0:T(8,128)(2,1)}, bf16[4,4,32,1024]{3,2,1,0:T(8,128)(2,1)}, bf16[4,4,32,1024]{3,2,1,0:T(8,128)(2,1)}, f32[8,1024]{1,0:T(8,128)}) custom-call(bf16[1280,1024]{1,0:T(8,128)(2,1)} %get-tuple-element.563.g_ref, f32[1280,1024]{1,0:T(8,128)} %get-tuple-element.308.gs_ref, ...), custom_call_target="tpu_custom_call" | custom-call | flops 1342177280 | bytes 8912896 | tf_op jit(solution)/shard_map/out_bwd/pallas_call | solution.py:873
  467.9 9.0 fusion.24
  482.5 42.7 %attn_bwd.2 = (bf16[5,4,64,3072]{3,2,1,0:T(8,128)(2,1)}, f32[16,64,640]{2,1,0:T(8,128)}) custom-call(bf16[5,4,64,3072]{3,2,1,0:T(8,128)(2,1)} %bitcast.329, bf16[5,4,64,1024]{3,2,1,0:T(8,128)(2,1)} %bitcast.382, f32[16,64,640]{2,1,0:T(8,128)} %pad.19.b_ref, s32[1]{0:T(128)} %copy.115.fc_ref), custom_call_target="tpu_custom_call" | custom-call | flops 4194304000 | bytes 5242880 | tf_op jit(solution)/shard_map/attn_bwd/pallas_call | solution.py:620
  536.9 20.3 %qkv_back.2 = (bf16[1280,512]{1,0:T(8,128)(2,1)}, bf16[1280,512]{1,0:T(8,128)(2,1)}, f32[8,1024]{1,0:T(8,128)}) custom-call(bf16[1280,3072]{1,0:T(8,128)(2,1)} %bitcast.290, bf16[2,4,128,1024]{3,2,1,0:T(8,128)(2,1)} %prep_attn.3.l_ref, bf16[4,3,128,1024]{3,2,1,0:T(8,128)(2,1)} %copy-done.3, bf16[4,3,128,1024]{3,2,1,0:T(8,128)(2,1)} %collective-permute-done.24.v_ref, ...), custom_call_target="tpu_custom_call" | custom-call | flops 2013265920 | bytes 8126464 | tf_op jit(solution)/shard_map/qkv_back/pallas_call | solution.py:933
  582.4 13.2 %qkv_grad.2 = (bf16[4,4,128,1024]{3,2,1,0:T(8,128)(2,1)}, bf16[4,4,128,1024]{3,2,1,0:T(8,128)(2,1)}) custom-call(bf16[1280,3072]{1,0:T(8,128)(2,1)} %bitcast.291, bf16[1280,1024]{1,0:T(8,128)(2,1)} %get-tuple-element.340.n_ref, bf16[4,4,32,1024]{3,2,1,0:T(8,128)(2,1)} %get-tuple-element.341.ok_ref, bf16[4,4,32,1024]{3,2,1,0:T(8,128)(2,1)} %get-tuple-element.342.os_ref), custom_call_target="tpu_custom_call" | custom-call | flops 2013265920 | bytes 4718592 | tf_op jit(solution)/shard_map/qkv_grad/pallas_call | solution.py:969
  611.0 24.7 %collective-permute-done.36 = bf16[128,1024]{1,0:T(8,128)(2,1)S(1)} collective-permute-done((bf16[128,1024]{1,0:T(8,128)(2,1)S(1)}, bf16[128,1024]{1,0:T(8,128)(2,1)S(1)}, u32[]{:S(2)}, u32[]{:S(2)}) %collective-permute-start.36) | collective-permute-done | bytes 262176 | tf_op jit(solution)/shard_map/ppermute | solution.py:1136
  650.8 61.7 %ffn_bwd.3 = (bf16[4,4,256,1024]{3,2,1,0:T(8,128)(2,1)}, bf16[4,4,256,1024]{3,2,1,0:T(8,128)(2,1)}, f32[1280,1024]{1,0:T(8,128)}) custom-call(bf16[1280,1024]{1,0:T(8,128)(2,1)} %bitcast.303, bf16[1280,4096]{1,0:T(8,128)(2,1)} %get-tuple-element.356.p_ref, bf16[1280,1024]{1,0:T(8,128)(2,1)} %get-tuple-element.271.x_ref, ...), custom_call_target="tpu_custom_call" | custom-call | flops 10737418240 | bytes 13631488 | tf_op jit(solution)/shard_map/ffn_bwd/pallas_call | solution.py:809
  719.0 18.8 %out_bwd.3 = (f32[1280,1024]{1,0:T(8,128)}, bf16[1280,1024]{1,0:T(8,128)(2,1)}, bf16[4,4,32,1024]{3,2,1,0:T(8,128)(2,1)}, bf16[4,4,32,1024]{3,2,1,0:T(8,128)(2,1)}, f32[8,1024]{1,0:T(8,128)}) custom-call(bf16[1280,1024]{1,0:T(8,128)(2,1)} %bitcast.304, f32[1280,1024]{1,0:T(8,128)} %get-tuple-element.364.gs_ref, ...), custom_call_target="tpu_custom_call" | custom-call | flops 1342177280 | bytes 8912896 | tf_op jit(solution)/shard_map/out_bwd/pallas_call | solution.py:873
  737.9 9.0 fusion.28
  751.5 32.9 %attn_bwd.3 = (bf16[1,5,256,3072]{3,2,1,0:T(8,128)(2,1)}, f32[16,16,512]{2,1,0:T(8,128)}) custom-call(bf16[1,5,256,3072]{3,2,1,0:T(8,128)(2,1)} %bitcast.331, bf16[1,5,256,1024]{3,2,1,0:T(8,128)(2,1)} %bitcast.381, f32[16,16,512]{2,1,0:T(8,128)} %pad.18.b_ref, s32[1]{0:T(128)} %copy.115.fc_ref), custom_call_target="tpu_custom_call" | custom-call | flops 3355443200 | bytes 5242880 | tf_op jit(solution)/shard_map/attn_bwd/pallas_call | solution.py:620
  798.2 13.4 %qkv_grad.3 = (bf16[4,4,144,1024]{3,2,1,0:T(8,128)(2,1)}, bf16[4,4,144,1024]{3,2,1,0:T(8,128)(2,1)}) custom-call(bf16[1280,3072]{1,0:T(8,128)(2,1)} %bitcast.288, bf16[1280,1024]{1,0:T(8,128)(2,1)} %get-tuple-element.375.n_ref, bf16[4,4,32,1024]{3,2,1,0:T(8,128)(2,1)} %get-tuple-element.376.ok_ref, bf16[4,4,32,1024]{3,2,1,0:T(8,128)(2,1)} %get-tuple-element.377.os_ref, ...), custom_call_target="tpu_custom_call" | custom-call | flops 2013265920 | bytes 4718592 | tf_op jit(solution)/shard_map/qkv_grad/pallas_call | solution.py:969
  822.8 9.0 finish_feed.2
  831.7 13.2 %collective-permute-done.47 = bf16[4,128,1024]{2,1,0:T(8,128)(2,1)S(1)} collective-permute-done((bf16[4,128,1024]{2,1,0:T(8,128)(2,1)}, bf16[4,128,1024]{2,1,0:T(8,128)(2,1)S(1)}, u32[]{:S(2)}, u32[]{:S(2)}) %collective-permute-start.47) | collective-permute-done | bytes 1048608 | tf_op jit(solution)/shard_map/ppermute | solution.py:1212
  863.1 21.8 %qkv_back.3 = (f32[1280,1024]{1,0:T(8,128)}, f32[8,1024]{1,0:T(8,128)}) custom-call(bf16[1280,3072]{1,0:T(8,128)(2,1)} %bitcast.289, bf16[2,4,128,1024]{3,2,1,0:T(8,128)(2,1)} %prep_attn.2.l_ref, bf16[4,3,128,1024]{3,2,1,0:T(8,128)(2,1)} %copy-done.2, bf16[4,3,128,1024]{3,2,1,0:T(8,128)(2,1)} %collective-permute-done.10.v_ref, ...), custom_call_target="tpu_custom_call" | custom-call | flops 2013265920 | bytes 8126464 | tf_op jit(solution)/shard_map/qkv_back/pallas_call | solution.py:933
  895.6 16.6 %collective-permute-done.55 = bf16[1,128,1024]{2,1,0:T(8,128)(2,1)S(1)} collective-permute-done((bf16[1,128,1024]{2,1,0:T(8,128)(2,1)S(1)}, bf16[1,128,1024]{2,1,0:T(8,128)(2,1)S(1)}, u32[]{:S(2)}, u32[]{:S(2)}) %collective-permute-start.55) | collective-permute-done | bytes 262176 | tf_op jit(solution)/shard_map/ppermute | solution.py:1212
  924.8 18.1 %collective-permute-done.60 = bf16[1,64,1024]{2,1,0:T(8,128)(2,1)S(1)} collective-permute-done((bf16[1,64,1024]{2,1,0:T(8,128)(2,1)S(1)}, bf16[1,64,1024]{2,1,0:T(8,128)(2,1)S(1)}, u32[]{:S(2)}, u32[]{:S(2)}) %collective-permute-start.60) | collective-permute-done | bytes 131104 | tf_op jit(solution)/shard_map/ppermute | solution.py:1212
  969.6 9.0 finish_feed.3
  991.0 9.4 finish_attn.1
  (426 shorter events, 360.2 us)
Async XLA Ops:
  7.2 78.3 %all-gather.9.cloned.1.call-start = ((), (), s32[]{:S(2)}) async-start(), calls=%async_computation.13 | async-start | bytes 1310720 | tf_op jit(solution)/shard_map/all_gather | solution.py:1348
  47.6 35.1 %collective-permute-start.6 = (bf16[3,128,1024]{2,1,0:T(8,128)(2,1)S(1)}, bf16[3,128,1024]{2,1,0:T(8,128)(2,1)}, u32[]{:S(2)}, u32[]{:S(2)}) collective-permute-start(bf16[3,128,1024]{2,1,0:T(8,128)(2,1)S(1)} %pad_maximum_fusion.16), channel_id=1, source_target_pairs={{0,16},{4,20},{8,24},{12,28},{16,0},{20,4},{24,8},{28,12},{1,17},{... | collective-permute-start | bytes 2359304 | tf_op jit(solution)/shard_map/ppermute | solution.py:1212
  49.1 33.6 %collective-permute-start.7 = (bf16[3,128,1024]{2,1,0:T(8,128)(2,1)S(1)}, bf16[3,128,1024]{2,1,0:T(8,128)(2,1)}, u32[]{:S(2)}, u32[]{:S(2)}) collective-permute-start(bf16[3,128,1024]{2,1,0:T(8,128)(2,1)S(1)} %pad_maximum_fusion.16), channel_id=1, source_target_pairs={{0,24},{4,28},{8,16},{12,20},{16,8},{20,12},{24,0},{28,4},{1,25},{... | collective-permute-start | bytes 2359304 | tf_op jit(solution)/shard_map/ppermute | solution.py:1212
  56.2 59.2 %all-gather.11.cloned.1.call-start = ((), (), s32[]{:S(2)}) async-start(), calls=%async_computation.14 | async-start | bytes 1310720 | tf_op jit(solution)/shard_map/all_gather | solution.py:1349
  87.7 57.3 %all-gather.13.cloned.1.call-start = ((), (), s32[]{:S(2)}) async-start(), calls=%async_computation.15 | async-start | bytes 1310720 | tf_op jit(solution)/shard_map/all_gather | solution.py:1366
  95.1 117.5 %all-gather.15.cloned.1.call-start = ((), (), s32[]{:S(2)}) async-start(), calls=%async_computation.16 | async-start | bytes 2621440 | tf_op jit(solution)/shard_map/all_gather | solution.py:1377
  167.8 44.8 %collective-permute-start.21 = (bf16[3,128,1024]{2,1,0:T(8,128)(2,1)}, bf16[3,128,1024]{2,1,0:T(8,128)(2,1)}, u32[]{:S(2)}, u32[]{:S(2)}) collective-permute-start(bf16[3,128,1024]{2,1,0:T(8,128)(2,1)} %pad_maximum_fusion.19), channel_id=1, source_target_pairs={{0,8},{4,12},{8,0},{12,4},{16,24},{20,28},{24,16},{28,20},{1,9},{5... | collective-permute-start | bytes 2359304 | tf_op jit(solution)/shard_map/ppermute | solution.py:1212
  168.9 43.7 %collective-permute-start.22 = (bf16[3,128,1024]{2,1,0:T(8,128)(2,1)}, bf16[3,128,1024]{2,1,0:T(8,128)(2,1)}, u32[]{:S(2)}, u32[]{:S(2)}) collective-permute-start(bf16[3,128,1024]{2,1,0:T(8,128)(2,1)} %pad_maximum_fusion.19), channel_id=1, source_target_pairs={{0,16},{4,20},{8,24},{12,28},{16,0},{20,4},{24,8},{28,12},{1,17},{... | collective-permute-start | bytes 2359304 | tf_op jit(solution)/shard_map/ppermute | solution.py:1212
  169.7 42.9 %collective-permute-start.23 = (bf16[3,128,1024]{2,1,0:T(8,128)(2,1)}, bf16[3,128,1024]{2,1,0:T(8,128)(2,1)}, u32[]{:S(2)}, u32[]{:S(2)}) collective-permute-start(bf16[3,128,1024]{2,1,0:T(8,128)(2,1)} %pad_maximum_fusion.19), channel_id=1, source_target_pairs={{0,24},{4,28},{8,16},{12,20},{16,8},{20,12},{24,0},{28,4},{1,25},{... | collective-permute-start | bytes 2359304 | tf_op jit(solution)/shard_map/ppermute | solution.py:1212
  216.2 64.8 %all-to-all-start = ((bf16[4,320,1024]{2,1,0:T(8,128)(2,1)}), bf16[4,320,1024]{2,1,0:T(8,128)(2,1)}, u32[]{:S(2)}, u32[]{:S(2)}) async-start(bf16[4,320,1024]{2,1,0:T(8,128)(2,1)} %bitcast.39), calls=%async_computation | async-start | bytes 5242880 | tf_op jit(solution)/shard_map/all_to_all | solution.py:1174
  223.4 49.6 %collective-permute-start.24 = (bf16[4,3,128,1024]{3,2,1,0:T(8,128)(2,1)S(1)}, bf16[4,3,128,1024]{3,2,1,0:T(8,128)(2,1)}, u32[]{:S(2)}, u32[]{:S(2)}) collective-permute-start(bf16[4,3,128,1024]{3,2,1,0:T(8,128)(2,1)S(1)} %pad_maximum_fusion.4.w_ref), channel_id=1, source_target_pairs={{0,4},{4,0},{8,12},{12,8},{16,20},{20,16},{24,28},{28,24},{1,5},{5... | collective-permute-start | bytes 9437192 | tf_op jit(solution)/shard_map/ppermute | solution.py:1212
  225.8 71.1 %collective-permute-start.26 = (bf16[3,256,1024]{2,1,0:T(8,128)(2,1)}, bf16[3,256,1024]{2,1,0:T(8,128)(2,1)}, u32[]{:S(2)}, u32[]{:S(2)}) collective-permute-start(bf16[3,256,1024]{2,1,0:T(8,128)(2,1)} %pad_maximum_fusion.11), channel_id=1, source_target_pairs={{0,8},{4,12},{8,0},{12,4},{16,24},{20,28},{24,16},{28,20},{1,9},{5... | collective-permute-start | bytes 4718600 | tf_op jit(solution)/shard_map/ppermute | solution.py:1212
  227.2 70.6 %collective-permute-start.27 = (bf16[3,256,1024]{2,1,0:T(8,128)(2,1)}, bf16[3,256,1024]{2,1,0:T(8,128)(2,1)}, u32[]{:S(2)}, u32[]{:S(2)}) collective-permute-start(bf16[3,256,1024]{2,1,0:T(8,128)(2,1)} %pad_maximum_fusion.11), channel_id=1, source_target_pairs={{0,16},{4,20},{8,24},{12,28},{16,0},{20,4},{24,8},{28,12},{1,17},{... | collective-permute-start | bytes 4718600 | tf_op jit(solution)/shard_map/ppermute | solution.py:1212
  228.7 69.1 %collective-permute-start.28 = (bf16[3,256,1024]{2,1,0:T(8,128)(2,1)}, bf16[3,256,1024]{2,1,0:T(8,128)(2,1)}, u32[]{:S(2)}, u32[]{:S(2)}) collective-permute-start(bf16[3,256,1024]{2,1,0:T(8,128)(2,1)} %pad_maximum_fusion.11), channel_id=1, source_target_pairs={{0,24},{4,28},{8,16},{12,20},{16,8},{20,12},{24,0},{28,4},{1,25},{... | collective-permute-start | bytes 4718600 | tf_op jit(solution)/shard_map/ppermute | solution.py:1212
  231.1 38.5 %collective-permute-start.25 = (bf16[128,1024]{1,0:T(8,128)(2,1)}, bf16[128,1024]{1,0:T(8,128)(2,1)}, u32[]{:S(2)}, u32[]{:S(2)}) collective-permute-start(bf16[128,1024]{1,0:T(8,128)(2,1)} %bitcast.55), channel_id=1, source_target_pairs={{0,1},{1,0},{2,3},{3,2},{4,5},{5,4},{6,7},{7,6},{8,9},{9,8},{10,11... | collective-permute-start | bytes 786440 | tf_op jit(solution)/shard_map/ppermute | solution.py:1136
  304.6 38.9 %collective-permute-start.29 = (bf16[4,3,256,1024]{3,2,1,0:T(8,128)(2,1)}, bf16[4,3,256,1024]{3,2,1,0:T(8,128)(2,1)}, u32[]{:S(2)}, u32[]{:S(2)}) collective-permute-start(bf16[4,3,256,1024]{3,2,1,0:T(8,128)(2,1)} %pad_maximum_fusion.refs_1_.refs_3_), channel_id=1, source_target_pairs={{0,4},{4,0},{8,12},{12,8},{16,20},{20,16},{24,28},{28,24},{1,5},{5... | collective-permute-start | bytes 18874376 | tf_op jit(solution)/shard_map/ppermute | solution.py:1212
  306.3 72.2 %all-to-all-start.1 = ((bf16[4,320,1024]{2,1,0:T(8,128)(2,1)}), bf16[4,320,1024]{2,1,0:T(8,128)(2,1)S(1)}, u32[]{:S(2)}, u32[]{:S(2)}) async-start(bf16[4,320,1024]{2,1,0:T(8,128)(2,1)} %bitcast.64), calls=%async_computation.1 | async-start | bytes 5242880 | tf_op jit(solution)/shard_map/all_to_all | solution.py:1174
  382.6 66.5 %all-to-all-start.2 = ((bf16[4,320,1024]{2,1,0:T(8,128)(2,1)}), bf16[4,320,1024]{2,1,0:T(8,128)(2,1)S(1)}, u32[]{:S(2)}, u32[]{:S(2)}) async-start(bf16[4,320,1024]{2,1,0:T(8,128)(2,1)} %bitcast.309), calls=%async_computation.2 | async-start | bytes 5242880 | tf_op jit(solution)/shard_map/all_to_all | solution.py:1174
  478.9 48.3 %collective-permute-start.32 = (bf16[2,4,128,1024]{3,2,1,0:T(8,128)(2,1)}, bf16[2,4,128,1024]{3,2,1,0:T(8,128)(2,1)}, u32[]{:S(2)}, u32[]{:S(2)}) collective-permute-start(bf16[2,4,128,1024]{3,2,1,0:T(8,128)(2,1)} %pad_maximum_fusion.7), channel_id=1, source_target_pairs={{0,16},{4,20},{8,24},{12,28},{16,0},{20,4},{24,8},{28,12},{1,17},{... | collective-permute-start | bytes 6291464 | tf_op jit(solution)/shard_map/ppermute | solution.py:1212
  481.9 48.0 %collective-permute-start.31 = (bf16[2,4,128,1024]{3,2,1,0:T(8,128)(2,1)}, bf16[2,4,128,1024]{3,2,1,0:T(8,128)(2,1)}, u32[]{:S(2)}, u32[]{:S(2)}) collective-permute-start(bf16[2,4,128,1024]{3,2,1,0:T(8,128)(2,1)} %pad_maximum_fusion.6), channel_id=1, source_target_pairs={{0,8},{4,12},{8,0},{12,4},{16,24},{20,28},{24,16},{28,20},{1,9},{5... | collective-permute-start | bytes 6291464 | tf_op jit(solution)/shard_map/ppermute | solution.py:1212
  560.2 42.8 %all-to-all-start.3 = ((bf16[4,320,512]{2,1,0:T(8,128)(2,1)}), bf16[4,320,512]{2,1,0:T(8,128)(2,1)}, u32[]{:S(2)}, u32[]{:S(2)}) async-start(bf16[4,320,512]{2,1,0:T(8,128)(2,1)} %bitcast.349), calls=%async_computation.3 | async-start | bytes 2621440 | tf_op jit(solution)/shard_map/all_to_all | solution.py:1174
  603.1 35.7 %collective-permute-start.35 = (bf16[4,4,128,1024]{3,2,1,0:T(8,128)(2,1)}, bf16[4,4,128,1024]{3,2,1,0:T(8,128)(2,1)}, u32[]{:S(2)}, u32[]{:S(2)}) collective-permute-start(bf16[4,4,128,1024]{3,2,1,0:T(8,128)(2,1)} %get-tuple-element.350), channel_id=1, source_target_pairs={{0,4},{4,0},{8,12},{12,8},{16,20},{20,16},{24,28},{28,24},{1,5},{5... | collective-permute-start | bytes 12582920 | tf_op jit(solution)/shard_map/ppermute | solution.py:1212
  603.1 40.2 %all-to-all-start.4 = ((bf16[4,320,512]{2,1,0:T(8,128)(2,1)}), bf16[4,320,512]{2,1,0:T(8,128)(2,1)}, u32[]{:S(2)}, u32[]{:S(2)}) async-start(bf16[4,320,512]{2,1,0:T(8,128)(2,1)} %bitcast.348), calls=%async_computation.4 | async-start | bytes 2621440 | tf_op jit(solution)/shard_map/all_to_all | solution.py:1174
  608.2 104.4 %reduce-scatter.5.cloned.1.call-start = ((), (), s32[]{:S(2)}) async-start(), calls=%async_computation.9 | async-start | bytes 2621440 | tf_op jit(solution)/shard_map/reduce_scatter | solution.py:1300
  643.3 168.4 %reduce-scatter.7.cloned.1.call-start = ((), (), s32[]{:S(2)}) async-start(), calls=%async_computation.10 | async-start | bytes 1310720 | tf_op jit(solution)/shard_map/reduce_scatter | solution.py:1300
  643.3 69.2 %collective-permute-start.37 = (bf16[4,128,1024]{2,1,0:T(8,128)(2,1)}, bf16[4,128,1024]{2,1,0:T(8,128)(2,1)S(1)}, u32[]{:S(2)}, u32[]{:S(2)}) collective-permute-start(bf16[4,128,1024]{2,1,0:T(8,128)(2,1)} %get-tuple-element.361), channel_id=1, source_target_pairs={{0,8},{4,12},{8,0},{12,4},{16,24},{20,28},{24,16},{28,20},{1,9},{5... | collective-permute-start | bytes 3145736 | tf_op jit(solution)/shard_map/ppermute | solution.py:1212
  644.6 67.9 %collective-permute-start.38 = (bf16[4,128,1024]{2,1,0:T(8,128)(2,1)}, bf16[4,128,1024]{2,1,0:T(8,128)(2,1)}, u32[]{:S(2)}, u32[]{:S(2)}) collective-permute-start(bf16[4,128,1024]{2,1,0:T(8,128)(2,1)} %get-tuple-element.362), channel_id=1, source_target_pairs={{0,16},{4,20},{8,24},{12,28},{16,0},{20,4},{24,8},{28,12},{1,17},{... | collective-permute-start | bytes 3145736 | tf_op jit(solution)/shard_map/ppermute | solution.py:1212
  645.4 67.1 %collective-permute-start.39 = (bf16[4,128,1024]{2,1,0:T(8,128)(2,1)S(1)}, bf16[4,128,1024]{2,1,0:T(8,128)(2,1)}, u32[]{:S(2)}, u32[]{:S(2)}) collective-permute-start(bf16[4,128,1024]{2,1,0:T(8,128)(2,1)S(1)} %get-tuple-element.363), channel_id=1, source_target_pairs={{0,24},{4,28},{8,16},{12,20},{16,8},{20,12},{24,0},{28,4},{1,25},{... | collective-permute-start | bytes 3145736 | tf_op jit(solution)/shard_map/ppermute | solution.py:1212
  719.0 193.2 %reduce-scatter.9.cloned.1.call-start = ((), (), s32[]{:S(2)}) async-start(), calls=%async_computation.11 | async-start | bytes 2621440 | tf_op jit(solution)/shard_map/reduce_scatter | solution.py:1300
  748.9 62.7 %collective-permute-start.44 = (bf16[2,4,128,1024]{3,2,1,0:T(8,128)(2,1)}, bf16[2,4,128,1024]{3,2,1,0:T(8,128)(2,1)}, u32[]{:S(2)}, u32[]{:S(2)}) collective-permute-start(bf16[2,4,128,1024]{3,2,1,0:T(8,128)(2,1)} %pad_maximum_fusion.9), channel_id=1, source_target_pairs={{0,16},{4,20},{8,24},{12,28},{16,0},{20,4},{24,8},{28,12},{1,17},{... | collective-permute-start | bytes 6291464 | tf_op jit(solution)/shard_map/ppermute | solution.py:1212
  750.8 60.8 %collective-permute-start.43 = (bf16[2,4,128,1024]{3,2,1,0:T(8,128)(2,1)}, bf16[2,4,128,1024]{3,2,1,0:T(8,128)(2,1)}, u32[]{:S(2)}, u32[]{:S(2)}) collective-permute-start(bf16[2,4,128,1024]{3,2,1,0:T(8,128)(2,1)} %pad_maximum_fusion.8), channel_id=1, source_target_pairs={{0,8},{4,12},{8,0},{12,4},{16,24},{20,28},{24,16},{28,20},{1,9},{5... | collective-permute-start | bytes 6291464 | tf_op jit(solution)/shard_map/ppermute | solution.py:1212
  857.9 89.8 %reduce-scatter.11.cloned.1.call-start = ((), (), s32[]{:S(2)}) async-start(), calls=%async_computation.12 | async-start | bytes 1474560 | tf_op jit(solution)/shard_map/reduce_scatter | solution.py:1300
  (106 other events, 1432.0 us)
Sparse Core Ops, SparseCore 0:
  56.3 29.1 all-gather.8
  87.8 27.5 all-gather.10
  117.5 27.4 all-gather.12
  168.0 44.6 all-gather.14
  643.4 45.1 reduce-scatter.4
  719.1 28.0 reduce-scatter.6
  858.0 44.7 reduce-scatter.8
  917.5 30.1 reduce-scatter.10

commit v6 on v5

--- a/solution.py
+++ b/solution.py
@@ -946,34 +946,46 @@
     )(grad_proj, *weights, hidden, grad_middle, mods)
 
 
-def qkv_grad(grad_proj, normed, out_keep, out_send, table_rows):
+def qkv_grad(grad_proj, normed, out_keep, out_send, table_rows, apart=False):
     rows = normed.shape[0]
     k = 128 if table_rows is None else 144
 
     def kernel(p_ref, n_ref, ok_ref, os_ref, *rest):
-        keep_ref, send_ref = rest[-2:]
+        if apart:
+            keep_ref, send_refs = rest[-5], rest[-4:]
+        else:
+            keep_ref, send_ref = rest[-2:]
+            send_refs = [send_ref.at[m : m + 1] for m in range(4)]
         for t in range(3):
             gw = dot_tn(p_ref[:, t * 256 : (t + 1) * 256], n_ref[...]).astype(BF16)
-            split_heads(gw, keep_ref, send_ref, 0, t * 32)
+            for m in range(4):
+                keep_ref[m, 0, t * 32 : t * 32 + 32] = gw[m * 64 : m * 64 + 32]
+                send_refs[m][0, 0, t * 32 : t * 32 + 32] = gw[m * 64 + 32 : m * 64 + 64]
         keep_ref[:, :, 96:128] = ok_ref[...]
-        send_ref[:, :, 96:128] = os_ref[...]
+        for m in range(4):
+            send_refs[m][0, :, 96:128] = os_ref[m]
         if table_rows is not None:
             keep_ref[:, :, 128:144] = rest[0][...]
-            send_ref[:, :, 128:144] = rest[0][...]
+            for m in range(4):
+                send_refs[m][0, :, 128:144] = rest[0][m]
 
     gspec = pl.BlockSpec((4, 1, k, D), lambda z: (0, z, 0, 0))
     ospec = pl.BlockSpec((4, 1, 32, D), lambda z: (0, z, 0, 0))
     tspec = pl.BlockSpec((4, 1, 16, D), lambda z: (0, z, 0, 0))
     gshape = jax.ShapeDtypeStruct((4, NZ, k, D), BF16)
     extra = () if table_rows is None else (table_rows,)
+    sends, send_shapes = [gspec], [gshape]
+    if apart:
+        sends = [pl.BlockSpec((1, 1, k, D), lambda z: (0, z, 0, 0))] * 4
+        send_shapes = [jax.ShapeDtypeStruct((1, NZ, k, D), BF16)] * 4
     return call(
         kernel,
         "qkv_grad",
         (NZ,),
         [pl.BlockSpec((rows, 768), lambda z: (0, z)), full((rows, D)), ospec, ospec]
         + [tspec] * len(extra),
-        [gspec, gspec],
-        [gshape, gshape],
+        [gspec] + sends,
+        [gshape] + send_shapes,
         [],
         6 * rows * D * D,
         rows * D * 8 + 8 * D * D,
@@ -1153,13 +1165,16 @@
     )
 
 
-def spatial_to_rows(wins, odd):
+def last_window(wins, odd):
+    part = lax.dynamic_slice(wins, (1024 * (1 - odd), 0), (256, wins.shape[1]))
+    keep = jnp.where(odd == 0, part[:128], part[128:])
+    return keep, jnp.where(odd == 0, part[128:], part[:128])
+
+
+def spatial_to_rows(wins, keep, got, odd):
     cols = wins.shape[1]
     whole = lax.dynamic_slice(wins, (256 * odd, 0), (1024, cols))
-    part = lax.dynamic_slice(wins, (1024 * (1 - odd), 0), (256, cols))
     whole = whole.reshape(2, 2, 16, 16, cols).transpose(0, 2, 1, 3, 4).reshape(1024, cols)
-    keep = jnp.where(odd == 0, part[:128], part[128:])
-    got = partner(jnp.where(odd == 0, part[128:], part[:128]))
     left, right = jnp.where(odd == 0, keep, got), jnp.where(odd == 0, got, keep)
     part = jnp.stack([left.reshape(8, 16, cols), right.reshape(8, 16, cols)], axis=1)
     part = part.reshape(256, cols)
@@ -1250,7 +1265,7 @@
 
 
 def sum_core(keep, got):
-    return [add(keep[m], got[m]) for m in range(4)]
+    return [add(keep[m], got[m].reshape(keep.shape[1:])) for m in range(4)]
 
 
 def send_plane(totals, offsets):
@@ -1417,33 +1432,33 @@
     half_f1 = sum_cross(total_f1, got_f1)
     half_f1, g_proj1 = sync(half_f1, g_proj1)
     got_f1 = send_corner(half_f1)
-    g_hid1a, g_hid1b, sums_q1 = qkv_back(
-        g_proj1, weights_a1, tubes1, g_mid1, mods, 6, BF16, 2
-    )
-    g_hid1a, g_hid1b, g_proj1, out_wins, g_base1, got_f1 = sync(
-        g_hid1a, g_hid1b, g_proj1, out_wins, g_base1, got_f1
-    )
-    grad1a = exchange(g_hid1a)
+    g_hid1, sums_q1 = qkv_back(g_proj1, weights_a1, tubes1, g_mid1, mods, 6, BF16, 1)
+    g_hid1, g_proj1, out_wins, g_base1, got_f1 = sync(g_hid1, g_proj1, out_wins, g_base1, got_f1)
+    grad1 = exchange(g_hid1)
     z_f1 = sum_corner(half_f1, got_f1, z)
-    a1_keep, a1_send = qkv_grad(g_proj1, normed1, o1_keep, o1_send, None)
+    a1_keep, *a1_send = qkv_grad(g_proj1, normed1, o1_keep, o1_send, None, True)
+    a1_got = [swap(v, CORE) for v in a1_send]
     gt_t = jnp.einsum(
         "hjtk,rjk->htr",
         g_base1[:, :, :576].reshape(16, 64, 9, 64),
         hot_t,
         precision=HIGHEST_PRECISION,
     ).reshape(16, n_t)
-    grad1a, z_f1, a1_keep, a1_send, gt_t, g_hid1b, out_wins = sync(
-        grad1a, z_f1, a1_keep, a1_send, gt_t, g_hid1b, out_wins
-    )
-    grad1b = exchange(g_hid1b)
-    total_a1 = sum_core(a1_keep, swap(a1_send, CORE))
-    output = spatial_to_rows(from_quads(out_wins), odd)
-    grad1b, total_a1, output, z_f1 = sync(grad1b, total_a1, output, z_f1)
-    grad1 = from_quads(jnp.concatenate([grad1a, grad1b], axis=1))
+    out_wins = from_quads(out_wins)
+    out_keep, out_send = last_window(out_wins, odd)
+    grad1, a1_got, z_f1, gt_t, out_wins, out_keep, out_send = sync(
+        grad1, a1_got, z_f1, gt_t, out_wins, out_keep, out_send
+    )
+    grad1 = from_quads(grad1)
+    total_a1 = sum_core(a1_keep, a1_got)
+    grad1, total_a1 = sync(grad1, total_a1)
     mine_f1 = sum_line(z_f1)
+    out_got = partner(out_send)
     got_a1 = send_plane(total_a1, (1, 2, 3))
     f0_keep, f0_send, g_shift0 = ffn_bwd(grad1, pre0, shifted0, weights_f0, 0, mods, 0)
-    f0_keep, f0_send, g_shift0, mine_f1, got_a1 = sync(f0_keep, f0_send, g_shift0, mine_f1, got_a1)
+    f0_keep, f0_send, g_shift0, mine_f1, got_a1, out_got = sync(
+        f0_keep, f0_send, g_shift0, mine_f1, got_a1, out_got
+    )
     f0_got = swap(f0_send, CORE)
     sides_f1 = sides_stage(mine_f1[None])
     mine_a1 = sum_line(sum_plane(total_a1, got_a1, z))
@@ -1483,12 +1498,6 @@
     half_a0, grad0, sums_q0 = sync(half_a0, grad0, sums_q0)
     got_a0 = send_corner(half_a0)
     sides_a1 = sides_stage(mine_a1[None])
-    got_a0, sides_a1, mine_f0 = sync(got_a0, sides_a1, mine_f0)
-    z_a0 = sum_corner(half_a0, got_a0, z)
-    z_a0, mine_f0 = sync(z_a0, mine_f0)
-    mine_a0 = sum_line(z_a0)
-    own_gf0 = cross_stage(mine_f0)
-    corner_a1 = corner_stage(sides_a1)
     mod_rows = jnp.concatenate(
         [
             sums_q0[0:2], sums_o0[2:3], sums_o0[0:2], sums_o0[3:4],
@@ -1496,19 +1505,32 @@
         ],
         axis=0,
     )
-    mine_a0, own_gf0, corner_a1, mod_rows, grad0 = sync(mine_a0, own_gf0, corner_a1, mod_rows, grad0)
+    mod_got = partner(mod_rows)
+    got_a0, sides_a1, mine_f0, mod_got, mod_rows = sync(
+        got_a0, sides_a1, mine_f0, mod_got, mod_rows
+    )
+    z_a0 = sum_corner(half_a0, got_a0, z)
+    mod_sum = mod_rows + mod_got
+    z_a0, mine_f0, mod_sum = sync(z_a0, mine_f0, mod_sum)
+    mine_a0 = sum_line(z_a0)
+    own_gf0 = cross_stage(mine_f0)
+    corner_a1 = corner_stage(sides_a1)
+    output = spatial_to_rows(out_wins, out_keep, out_got, odd)
+    rows_keep, rows_send = last_window(grad0, odd)
+    mine_a0, own_gf0, corner_a1, rows_keep, rows_send, output = sync(
+        mine_a0, own_gf0, corner_a1, rows_keep, rows_send, output
+    )
     own_ga0 = cross_stage(mine_a0)
+    rows_got = partner(rows_send)
     own_gf0 = jnp.stack(own_gf0)
-    grad_tokens = spatial_to_rows(grad0, odd)
     own_ga1 = joined(sides_a1, corner_a1).reshape(4, 128, D)
     g_feed = finish_feed(place, own_gf0, swap(own_gf0, CORE), 0, g_feed)
-    own_ga0, g_feed, grad_tokens, mod_rows, own_ga1 = sync(
-        own_ga0, g_feed, grad_tokens, mod_rows, own_ga1
-    )
+    own_ga0, g_feed, rows_got, own_ga1, mod_sum = sync(own_ga0, g_feed, rows_got, own_ga1, mod_sum)
     own_ga0 = jnp.stack(own_ga0)
     own_ga = jnp.concatenate([own_ga0[:, :128], own_ga1, own_ga0[:, 128:]], axis=1)
-    mod_got = [from_z(mod_rows, d) for d in (1, 2, 3)]
     own_ga0 = own_ga
+    mod_got = lax.ppermute(mod_sum, "head", [(i, i ^ 2) for i in range(NZ)])
+    grad_tokens = spatial_to_rows(grad0, rows_keep, rows_got, odd)
     g_attn = finish_attn(place, own_ga, swap(own_ga, CORE))
     tab = jnp.concatenate(
         [lax.dynamic_slice_in_dim(own_ga0, chip ^ m, 1, axis=0) for m in range(4)], axis=0
@@ -1517,7 +1539,7 @@
     return (
         output,
         grad_tokens,
-        (mod_rows + mod_got[0] + mod_got[1] + mod_got[2])[None],
+        (mod_sum + mod_got)[None],
         g_attn[0],
         g_attn[1],
         g_feed[0],

time: 1020 us -> 1000 us (0.980)
  waiting for transfers between devices: 149 us -> 116 us
  local copies, waits for them, and re-layouts: 85.5 us -> 102 us
    ppermute x4 -> x5, waiting for transfers between devices: 42.4 us -> 11.5 us  [partner(): return lax.ppermute(values, 'head', [(i, i ^ 1) for i in range(NZ)])]
    all_to_all x5 -> x4, waiting for transfers between devices: 7.95 us -> 29.8 us  [exchange(): return lax.all_to_all(values, 'head', 0, 0, tiled=True)]
    ppermute x58 -> x61, waiting for transfers between devices: 75 us -> 60 us  [swap(): return lax.ppermute(values, 'clip', [(i, i ^ bit) for i in range(8)])]
    all_to_all x5 -> x4, starting transfers between devices: 25.7 us -> 20.6 us  [exchange(): return lax.all_to_all(values, 'head', 0, 0, tiled=True)]
    ppermute x58 -> x61, starting transfers between devices: 49.7 us -> 53.4 us  [swap(): return lax.ppermute(values, 'clip', [(i, i ^ bit) for i in range(8)])]
  transfers between devices with their start and end apart: 84 -> 85, of which waited for: 25 -> 24; matrix products, arithmetic and copies ran while one was open for 16% -> 17% of each run, Pallas kernels for 50% -> 51%
where the time goes in v6:
time: 1000 us; the launch traced here: 992 us
  Pallas kernels  521 us (52%)
  other arithmetic  128 us (13%)
  waiting for transfers between devices  116 us (12%)
  local copies, waits for them, and re-layouts  102 us (10%)
  starting transfers between devices  93.6 us (9%)
  between operations  16.4 us (2%)
  matrix products  15.6 us (2%)
    pallas_call x2, Pallas kernels, ffn_bwd(): call(kernel, 'ffn_bwd', (NZ,), [full((rows, D)), pl.BlockSpec((rows, D),...  123 us
    pallas_call x2, Pallas kernels, attn_bwd(): call(kernel, 'attn_bwd', (NZ,), [xspec, pl.BlockSpec((parts, count, size,...  75.9 us
    pallas_call x2, Pallas kernels, ffn_fwd(): call(kernel, 'ffn_fwd', (NZ,), [full((rows, D))] + feed_specs(down_block)...  70.7 us
    ppermute x61, waiting for transfers between devices, swap(): return lax.ppermute(values, 'clip', [(i, i ^ bit) for i in range(8)])  60 us
    ppermute x61, starting transfers between devices, swap(): return lax.ppermute(values, 'clip', [(i, i ^ bit) for i in range(8)])  53.4 us
    convert_element_type x13, other arithmetic, add(): return (first.astype(F32) + second.astype(F32)).astype(BF16)  51 us
    pallas_call x2, Pallas kernels, attn_fwd(): call(kernel, 'attn_fwd', (NZ,), [pl.BlockSpec((parts, count, size, 768),...  43.4 us
    pallas_call x2, Pallas kernels, qkv_back(): call(kernel, 'qkv_back', (NZ,), [pl.BlockSpec((rows, 768), lambda z: (0,...  41.8 us
  transfers between devices with their start and end apart: 85, of which 24 were waited for; matrix products, arithmetic and copies ran while one was open for 17% of the time, Pallas kernels for 51%

profile of v6, /device:TPU:0, one launch (start us, length us, event | category | flops | bytes accessed | tf_op | source)
XLA Modules:
  0.0 992.1 jit_solution(10782621444052586337)
XLA Ops:
  23.6 6.9 prep_feed.2.refs_0_
  30.5 6.9 prep_feed.3.refs_0_
  71.9 10.8 %collective-permute-done.6 = bf16[3,128,1024]{2,1,0:T(8,128)(2,1)} collective-permute-done((bf16[3,128,1024]{2,1,0:T(8,128)(2,1)S(1)}, bf16[3,128,1024]{2,1,0:T(8,128)(2,1)}, u32[]{:S(2)}, u32[]{:S(2)}) %collective-permute-start.6) | collective-permute-done | bytes 786464 | tf_op jit(solution)/shard_map/ppermute | solution.py:1227
  96.0 15.9 %ln_qkv.2 = (bf16[1280,1024]{1,0:T(8,128)(2,1)}, bf16[1280,3072]{1,0:T(8,128)(2,1)}) custom-call(bf16[1280,1024]{1,0:T(8,128)(2,1)} %maximum_select_fusion.1.h_ref, f32[12,1024]{1,0:T(8,128)} %bitcast.306, bf16[2,4,128,1024]{3,2,1,0:T(8,128)(2,1)} %prep_attn.2.l_ref, bf16[4,3,128,1024]{3,2,1,0:T(8,128)(2,1)} %copy-done.2, ...), custom_call_target="tpu_custom_call" | custom-call | flops 2013265920 | bytes 5505024 | tf_op jit(solution)/shard_map/ln_qkv/pallas_call | solution.py:502
  123.6 20.6 %attn_fwd.2 = bf16[1,5,256,1024]{3,2,1,0:T(8,128)(2,1)} custom-call(bf16[1,5,256,3072]{3,2,1,0:T(8,128)(2,1)} %bitcast.326, f32[16,16,512]{2,1,0:T(8,128)} %pad.18.b_ref, s32[1]{0:T(128)} %copy.115.fc_ref), custom_call_target="tpu_custom_call" | custom-call | flops 1342177280 | bytes 2621440 | tf_op jit(solution)/shard_map/attn_fwd/pallas_call | solution.py:557
  152.3 9.3 out_proj.2
  171.4 35.6 %ffn_fwd.2 = (bf16[1280,4096]{1,0:T(8,128)(2,1)}, bf16[1280,1024]{1,0:T(8,128)(2,1)}, bf16[1280,1024]{1,0:T(8,128)(2,1)}) custom-call(bf16[1280,1024]{1,0:T(8,128)(2,1)} %get-tuple-element.278.x_ref, bf16[2,4,256,1024]{3,2,1,0:T(8,128)(2,1)} %prep_feed.2.refs_0_, bf16[4,3,128,1024]{3,2,1,0:T(8,128)(2,1)} %copy-done.5, ...), custom_call_target="tpu_custom_call" | custom-call | flops 5368709120 | bytes 10747904 | tf_op jit(solution)/shard_map/ffn_fwd/pallas_call | solution.py:747
  258.0 11.5 %collective-permute-done.25 = bf16[128,1024]{1,0:T(8,128)(2,1)} collective-permute-done((bf16[128,1024]{1,0:T(8,128)(2,1)}, bf16[128,1024]{1,0:T(8,128)(2,1)}, u32[]{:S(2)}, u32[]{:S(2)}) %collective-permute-start.25) | collective-permute-done | bytes 262176 | tf_op jit(solution)/shard_map/ppermute | solution.py:1148
  273.0 7.9 all-to-all-done
  280.9 15.9 %ln_qkv.3 = (bf16[1280,1024]{1,0:T(8,128)(2,1)}, bf16[1280,3072]{1,0:T(8,128)(2,1)}) custom-call(bf16[1280,1024]{1,0:T(8,128)(2,1)} %bitcast.40.h_ref, f32[12,1024]{1,0:T(8,128)} %bitcast.309, bf16[2,4,128,1024]{3,2,1,0:T(8,128)(2,1)} %prep_attn.3.l_ref, bf16[4,3,128,1024]{3,2,1,0:T(8,128)(2,1)} %copy-done.3, ...), custom_call_target="tpu_custom_call" | custom-call | flops 2013265920 | bytes 5505024 | tf_op jit(solution)/shard_map/ln_qkv/pallas_call | solution.py:502
  311.3 22.9 %attn_fwd.3 = bf16[5,4,64,1024]{3,2,1,0:T(8,128)(2,1)} custom-call(bf16[5,4,64,3072]{3,2,1,0:T(8,128)(2,1)} %bitcast.324, f32[16,64,640]{2,1,0:T(8,128)} %pad.19.b_ref, s32[1]{0:T(128)} %copy.115.fc_ref), custom_call_target="tpu_custom_call" | custom-call | flops 1677721600 | bytes 2621440 | tf_op jit(solution)/shard_map/attn_fwd/pallas_call | solution.py:557
  334.2 9.3 out_proj.3
  343.5 35.1 %ffn_fwd.3 = (bf16[1280,4096]{1,0:T(8,128)(2,1)}, bf16[1280,1024]{1,0:T(8,128)(2,1)}, bf16[1280,1024]{1,0:T(8,128)(2,1)}) custom-call(bf16[1280,1024]{1,0:T(8,128)(2,1)} %get-tuple-element.304.x_ref, bf16[2,4,256,1024]{3,2,1,0:T(8,128)(2,1)} %prep_feed.3.refs_0_, bf16[4,3,256,1024]{3,2,1,0:T(8,128)(2,1)} %pad_maximum_fusion.refs_1_.refs_3_, ...), custom_call_target="tpu_custom_call" | custom-call | flops 5368709120 | bytes 10747904 | tf_op jit(solution)/shard_map/ffn_fwd/pallas_call | solution.py:747
  388.0 61.2 %ffn_bwd.2 = (bf16[4,4,256,1024]{3,2,1,0:T(8,128)(2,1)}, bf16[4,4,256,1024]{3,2,1,0:T(8,128)(2,1)}, f32[1280,1024]{1,0:T(8,128)}) custom-call(bf16[1280,1024]{1,0:T(8,128)(2,1)} %get-tuple-element.581.g_ref, bf16[1280,4096]{1,0:T(8,128)(2,1)} %get-tuple-element.310.p_ref, bf16[1280,1024]{1,0:T(8,128)(2,1)} %get-tuple-element.304.x_ref, ...), custom_call_target="tpu_custom_call" | custom-call | flops 10737418240 | bytes 13631488 | tf_op jit(solution)/shard_map/ffn_bwd/pallas_call | solution.py:809
  449.3 19.1 %out_bwd.2 = (f32[1280,1024]{1,0:T(8,128)}, bf16[1280,1024]{1,0:T(8,128)(2,1)}, bf16[4,4,32,1024]{3,2,1,0:T(8,128)(2,1)}, bf16[4,4,32,1024]{3,2,1,0:T(8,128)(2,1)}, f32[8,1024]{1,0:T(8,128)}) custom-call(bf16[1280,1024]{1,0:T(8,128)(2,1)} %get-tuple-element.581.g_ref, f32[1280,1024]{1,0:T(8,128)} %get-tuple-element.315.gs_ref, ...), custom_call_target="tpu_custom_call" | custom-call | flops 1342177280 | bytes 8912896 | tf_op jit(solution)/shard_map/out_bwd/pallas_call | solution.py:873
  468.5 9.1 fusion.24
  483.0 42.7 %attn_bwd.2 = (bf16[5,4,64,3072]{3,2,1,0:T(8,128)(2,1)}, f32[16,64,640]{2,1,0:T(8,128)}) custom-call(bf16[5,4,64,3072]{3,2,1,0:T(8,128)(2,1)} %bitcast.325, bf16[5,4,64,1024]{3,2,1,0:T(8,128)(2,1)} %bitcast.371, f32[16,64,640]{2,1,0:T(8,128)} %pad.19.b_ref, s32[1]{0:T(128)} %copy.115.fc_ref), custom_call_target="tpu_custom_call" | custom-call | flops 4194304000 | bytes 5242880 | tf_op jit(solution)/shard_map/attn_bwd/pallas_call | solution.py:620
  536.7 20.4 %qkv_back.2 = (bf16[1280,1024]{1,0:T(8,128)(2,1)}, f32[8,1024]{1,0:T(8,128)}) custom-call(bf16[1280,3072]{1,0:T(8,128)(2,1)} %bitcast.288, bf16[2,4,128,1024]{3,2,1,0:T(8,128)(2,1)} %prep_attn.3.l_ref, bf16[4,3,128,1024]{3,2,1,0:T(8,128)(2,1)} %copy-done.3, bf16[4,3,128,1024]{3,2,1,0:T(8,128)(2,1)} %collective-permute-done.24.v_ref, ...), custom_call_target="tpu_custom_call" | custom-call | flops 2013265920 | bytes 8126464 | tf_op jit(solution)/shard_map/qkv_back/pallas_call | solution.py:933
  575.7 13.2 %qkv_grad.2 = (bf16[4,4,128,1024]{3,2,1,0:T(8,128)(2,1)}, bf16[1,4,128,1024]{3,2,1,0:T(8,128)(2,1)}, bf16[1,4,128,1024]{3,2,1,0:T(8,128)(2,1)}, bf16[1,4,128,102...) custom-call(bf16[1280,3072]{1,0:T(8,128)(2,1)} %bitcast.289, bf16[1280,1024]{1,0:T(8,128)(2,1)} %get-tuple-element.342.n_ref, ...), custom_call_target="tpu_custom_call" | custom-call | flops 2013265920 | bytes 4718592 | tf_op jit(solution)/shard_map/qkv_grad/pallas_call | solution.py:981
  601.7 21.9 %all-to-all-done.3 = bf16[4,320,1024]{2,1,0:T(8,128)(2,1)} async-done(((bf16[4,320,1024]{2,1,0:T(8,128)(2,1)}), bf16[4,320,1024]{2,1,0:T(8,128)(2,1)}, u32[]{:S(2)}, u32[]{:S(2)}) %all-to-all-start.3) | async-done | bytes 2621472 | tf_op jit(solution)/shard_map/all_to_all | solution.py:1189
  637.0 61.5 %ffn_bwd.3 = (bf16[4,4,256,1024]{3,2,1,0:T(8,128)(2,1)}, bf16[4,4,256,1024]{3,2,1,0:T(8,128)(2,1)}, f32[1280,1024]{1,0:T(8,128)}) custom-call(bf16[1280,1024]{1,0:T(8,128)(2,1)} %bitcast.298, bf16[1280,4096]{1,0:T(8,128)(2,1)} %get-tuple-element.362.p_ref, bf16[1280,1024]{1,0:T(8,128)(2,1)} %get-tuple-element.278.x_ref, ...), custom_call_target="tpu_custom_call" | custom-call | flops 10737418240 | bytes 13631488 | tf_op jit(solution)/shard_map/ffn_bwd/pallas_call | solution.py:809
  705.9 18.4 %out_bwd.3 = (f32[1280,1024]{1,0:T(8,128)}, bf16[1280,1024]{1,0:T(8,128)(2,1)}, bf16[4,4,32,1024]{3,2,1,0:T(8,128)(2,1)}, bf16[4,4,32,1024]{3,2,1,0:T(8,128)(2,1)}, f32[8,1024]{1,0:T(8,128)}) custom-call(bf16[1280,1024]{1,0:T(8,128)(2,1)} %bitcast.299, f32[1280,1024]{1,0:T(8,128)} %get-tuple-element.371.gs_ref, ...), custom_call_target="tpu_custom_call" | custom-call | flops 1342177280 | bytes 8912896 | tf_op jit(solution)/shard_map/out_bwd/pallas_call | solution.py:873
  724.4 9.0 fusion.28
  739.9 33.1 %attn_bwd.3 = (bf16[1,5,256,3072]{3,2,1,0:T(8,128)(2,1)}, f32[16,16,512]{2,1,0:T(8,128)}) custom-call(bf16[1,5,256,3072]{3,2,1,0:T(8,128)(2,1)} %bitcast.327, bf16[1,5,256,1024]{3,2,1,0:T(8,128)(2,1)} %bitcast.370, f32[16,16,512]{2,1,0:T(8,128)} %pad.18.b_ref, s32[1]{0:T(128)} %copy.115.fc_ref), custom_call_target="tpu_custom_call" | custom-call | flops 3355443200 | bytes 5242880 | tf_op jit(solution)/shard_map/attn_bwd/pallas_call | solution.py:620
  788.6 13.4 %qkv_grad.3 = (bf16[4,4,144,1024]{3,2,1,0:T(8,128)(2,1)}, bf16[4,4,144,1024]{3,2,1,0:T(8,128)(2,1)}) custom-call(bf16[1280,3072]{1,0:T(8,128)(2,1)} %bitcast.286, bf16[1280,1024]{1,0:T(8,128)(2,1)} %get-tuple-element.382.n_ref, bf16[4,4,32,1024]{3,2,1,0:T(8,128)(2,1)} %get-tuple-element.383.ok_ref, bf16[4,4,32,1024]{3,2,1,0:T(8,128)(2,1)} %get-tuple-element.384.os_ref, ...), custom_call_target="tpu_custom_call" | custom-call | flops 2013265920 | bytes 4718592 | tf_op jit(solution)/shard_map/qkv_grad/pallas_call | solution.py:981
  813.2 9.0 finish_feed.2
  822.2 14.0 %collective-permute-done.50 = bf16[4,128,1024]{2,1,0:T(8,128)(2,1)} collective-permute-done((bf16[4,128,1024]{2,1,0:T(8,128)(2,1)}, bf16[4,128,1024]{2,1,0:T(8,128)(2,1)}, u32[]{:S(2)}, u32[]{:S(2)}) %collective-permute-start.50) | collective-permute-done | bytes 1048608 | tf_op jit(solution)/shard_map/ppermute | solution.py:1227
  857.7 21.4 %qkv_back.3 = (f32[1280,1024]{1,0:T(8,128)}, f32[8,1024]{1,0:T(8,128)}) custom-call(bf16[1280,3072]{1,0:T(8,128)(2,1)} %bitcast.287, bf16[2,4,128,1024]{3,2,1,0:T(8,128)(2,1)} %prep_attn.2.l_ref, bf16[4,3,128,1024]{3,2,1,0:T(8,128)(2,1)} %copy-done.2, bf16[4,3,128,1024]{3,2,1,0:T(8,128)(2,1)} %collective-permute-done.10.v_ref, ...), custom_call_target="tpu_custom_call" | custom-call | flops 2013265920 | bytes 8126464 | tf_op jit(solution)/shard_map/qkv_back/pallas_call | solution.py:933
  899.1 8.3 collective-permute-done.58
  929.3 13.1 %collective-permute-done.64 = bf16[1,64,1024]{2,1,0:T(8,128)(2,1)S(1)} collective-permute-done((bf16[1,64,1024]{2,1,0:T(8,128)(2,1)S(1)}, bf16[1,64,1024]{2,1,0:T(8,128)(2,1)S(1)}, u32[]{:S(2)}, u32[]{:S(2)}) %collective-permute-start.64) | collective-permute-done | bytes 131104 | tf_op jit(solution)/shard_map/ppermute | solution.py:1227
  952.7 9.0 finish_feed.3
  975.7 9.4 finish_attn.1
  (438 shorter events, 359.8 us)
Async XLA Ops:
  7.2 78.3 %all-gather.9.cloned.1.call-start = ((), (), s32[]{:S(2)}) async-start(), calls=%async_computation.12 | async-start | bytes 1310720 | tf_op jit(solution)/shard_map/all_gather | solution.py:1363
  47.6 35.1 %collective-permute-start.6 = (bf16[3,128,1024]{2,1,0:T(8,128)(2,1)S(1)}, bf16[3,128,1024]{2,1,0:T(8,128)(2,1)}, u32[]{:S(2)}, u32[]{:S(2)}) collective-permute-start(bf16[3,128,1024]{2,1,0:T(8,128)(2,1)S(1)} %pad_maximum_fusion.15), channel_id=1, source_target_pairs={{0,16},{4,20},{8,24},{12,28},{16,0},{20,4},{24,8},{28,12},{1,17},{... | collective-permute-start | bytes 2359304 | tf_op jit(solution)/shard_map/ppermute | solution.py:1227
  49.1 33.6 %collective-permute-start.7 = (bf16[3,128,1024]{2,1,0:T(8,128)(2,1)S(1)}, bf16[3,128,1024]{2,1,0:T(8,128)(2,1)}, u32[]{:S(2)}, u32[]{:S(2)}) collective-permute-start(bf16[3,128,1024]{2,1,0:T(8,128)(2,1)S(1)} %pad_maximum_fusion.15), channel_id=1, source_target_pairs={{0,24},{4,28},{8,16},{12,20},{16,8},{20,12},{24,0},{28,4},{1,25},{... | collective-permute-start | bytes 2359304 | tf_op jit(solution)/shard_map/ppermute | solution.py:1227
  56.1 59.2 %all-gather.11.cloned.1.call-start = ((), (), s32[]{:S(2)}) async-start(), calls=%async_computation.13 | async-start | bytes 1310720 | tf_op jit(solution)/shard_map/all_gather | solution.py:1364
  87.6 57.3 %all-gather.13.cloned.1.call-start = ((), (), s32[]{:S(2)}) async-start(), calls=%async_computation.14 | async-start | bytes 1310720 | tf_op jit(solution)/shard_map/all_gather | solution.py:1381
  95.1 117.5 %all-gather.15.cloned.1.call-start = ((), (), s32[]{:S(2)}) async-start(), calls=%async_computation.15 | async-start | bytes 2621440 | tf_op jit(solution)/shard_map/all_gather | solution.py:1392
  167.8 44.8 %collective-permute-start.21 = (bf16[3,128,1024]{2,1,0:T(8,128)(2,1)}, bf16[3,128,1024]{2,1,0:T(8,128)(2,1)}, u32[]{:S(2)}, u32[]{:S(2)}) collective-permute-start(bf16[3,128,1024]{2,1,0:T(8,128)(2,1)} %pad_maximum_fusion.18), channel_id=1, source_target_pairs={{0,8},{4,12},{8,0},{12,4},{16,24},{20,28},{24,16},{28,20},{1,9},{5... | collective-permute-start | bytes 2359304 | tf_op jit(solution)/shard_map/ppermute | solution.py:1227
  169.0 43.7 %collective-permute-start.22 = (bf16[3,128,1024]{2,1,0:T(8,128)(2,1)}, bf16[3,128,1024]{2,1,0:T(8,128)(2,1)}, u32[]{:S(2)}, u32[]{:S(2)}) collective-permute-start(bf16[3,128,1024]{2,1,0:T(8,128)(2,1)} %pad_maximum_fusion.18), channel_id=1, source_target_pairs={{0,16},{4,20},{8,24},{12,28},{16,0},{20,4},{24,8},{28,12},{1,17},{... | collective-permute-start | bytes 2359304 | tf_op jit(solution)/shard_map/ppermute | solution.py:1227
  169.8 42.9 %collective-permute-start.23 = (bf16[3,128,1024]{2,1,0:T(8,128)(2,1)}, bf16[3,128,1024]{2,1,0:T(8,128)(2,1)}, u32[]{:S(2)}, u32[]{:S(2)}) collective-permute-start(bf16[3,128,1024]{2,1,0:T(8,128)(2,1)} %pad_maximum_fusion.18), channel_id=1, source_target_pairs={{0,24},{4,28},{8,16},{12,20},{16,8},{20,12},{24,0},{28,4},{1,25},{... | collective-permute-start | bytes 2359304 | tf_op jit(solution)/shard_map/ppermute | solution.py:1227
  216.2 64.7 %all-to-all-start = ((bf16[4,320,1024]{2,1,0:T(8,128)(2,1)}), bf16[4,320,1024]{2,1,0:T(8,128)(2,1)}, u32[]{:S(2)}, u32[]{:S(2)}) async-start(bf16[4,320,1024]{2,1,0:T(8,128)(2,1)} %bitcast.39), calls=%async_computation | async-start | bytes 5242880 | tf_op jit(solution)/shard_map/all_to_all | solution.py:1189
  223.4 49.6 %collective-permute-start.24 = (bf16[4,3,128,1024]{3,2,1,0:T(8,128)(2,1)S(1)}, bf16[4,3,128,1024]{3,2,1,0:T(8,128)(2,1)}, u32[]{:S(2)}, u32[]{:S(2)}) collective-permute-start(bf16[4,3,128,1024]{3,2,1,0:T(8,128)(2,1)S(1)} %pad_maximum_fusion.4.w_ref), channel_id=1, source_target_pairs={{0,4},{4,0},{8,12},{12,8},{16,20},{20,16},{24,28},{28,24},{1,5},{5... | collective-permute-start | bytes 9437192 | tf_op jit(solution)/shard_map/ppermute | solution.py:1227
  225.7 71.2 %collective-permute-start.26 = (bf16[3,256,1024]{2,1,0:T(8,128)(2,1)}, bf16[3,256,1024]{2,1,0:T(8,128)(2,1)}, u32[]{:S(2)}, u32[]{:S(2)}) collective-permute-start(bf16[3,256,1024]{2,1,0:T(8,128)(2,1)} %pad_maximum_fusion.10), channel_id=1, source_target_pairs={{0,8},{4,12},{8,0},{12,4},{16,24},{20,28},{24,16},{28,20},{1,9},{5... | collective-permute-start | bytes 4718600 | tf_op jit(solution)/shard_map/ppermute | solution.py:1227
  227.1 70.6 %collective-permute-start.27 = (bf16[3,256,1024]{2,1,0:T(8,128)(2,1)}, bf16[3,256,1024]{2,1,0:T(8,128)(2,1)}, u32[]{:S(2)}, u32[]{:S(2)}) collective-permute-start(bf16[3,256,1024]{2,1,0:T(8,128)(2,1)} %pad_maximum_fusion.10), channel_id=1, source_target_pairs={{0,16},{4,20},{8,24},{12,28},{16,0},{20,4},{24,8},{28,12},{1,17},{... | collective-permute-start | bytes 4718600 | tf_op jit(solution)/shard_map/ppermute | solution.py:1227
  228.6 69.2 %collective-permute-start.28 = (bf16[3,256,1024]{2,1,0:T(8,128)(2,1)}, bf16[3,256,1024]{2,1,0:T(8,128)(2,1)}, u32[]{:S(2)}, u32[]{:S(2)}) collective-permute-start(bf16[3,256,1024]{2,1,0:T(8,128)(2,1)} %pad_maximum_fusion.10), channel_id=1, source_target_pairs={{0,24},{4,28},{8,16},{12,20},{16,8},{20,12},{24,0},{28,4},{1,25},{... | collective-permute-start | bytes 4718600 | tf_op jit(solution)/shard_map/ppermute | solution.py:1227
  231.0 38.5 %collective-permute-start.25 = (bf16[128,1024]{1,0:T(8,128)(2,1)}, bf16[128,1024]{1,0:T(8,128)(2,1)}, u32[]{:S(2)}, u32[]{:S(2)}) collective-permute-start(bf16[128,1024]{1,0:T(8,128)(2,1)} %bitcast.55), channel_id=1, source_target_pairs={{0,1},{1,0},{2,3},{3,2},{4,5},{5,4},{6,7},{7,6},{8,9},{9,8},{10,11... | collective-permute-start | bytes 786440 | tf_op jit(solution)/shard_map/ppermute | solution.py:1148
  304.5 39.0 %collective-permute-start.29 = (bf16[4,3,256,1024]{3,2,1,0:T(8,128)(2,1)}, bf16[4,3,256,1024]{3,2,1,0:T(8,128)(2,1)}, u32[]{:S(2)}, u32[]{:S(2)}) collective-permute-start(bf16[4,3,256,1024]{3,2,1,0:T(8,128)(2,1)} %pad_maximum_fusion.refs_1_.refs_3_), channel_id=1, source_target_pairs={{0,4},{4,0},{8,12},{12,8},{16,20},{20,16},{24,28},{28,24},{1,5},{5... | collective-permute-start | bytes 18874376 | tf_op jit(solution)/shard_map/ppermute | solution.py:1227
  306.3 72.3 %all-to-all-start.1 = ((bf16[4,320,1024]{2,1,0:T(8,128)(2,1)}), bf16[4,320,1024]{2,1,0:T(8,128)(2,1)S(1)}, u32[]{:S(2)}, u32[]{:S(2)}) async-start(bf16[4,320,1024]{2,1,0:T(8,128)(2,1)} %bitcast.64), calls=%async_computation.1 | async-start | bytes 5242880 | tf_op jit(solution)/shard_map/all_to_all | solution.py:1189
  382.7 66.6 %all-to-all-start.2 = ((bf16[4,320,1024]{2,1,0:T(8,128)(2,1)}), bf16[4,320,1024]{2,1,0:T(8,128)(2,1)S(1)}, u32[]{:S(2)}, u32[]{:S(2)}) async-start(bf16[4,320,1024]{2,1,0:T(8,128)(2,1)} %bitcast.305), calls=%async_computation.2 | async-start | bytes 5242880 | tf_op jit(solution)/shard_map/all_to_all | solution.py:1189
  479.4 48.0 %collective-permute-start.32 = (bf16[2,4,128,1024]{3,2,1,0:T(8,128)(2,1)}, bf16[2,4,128,1024]{3,2,1,0:T(8,128)(2,1)}, u32[]{:S(2)}, u32[]{:S(2)}) collective-permute-start(bf16[2,4,128,1024]{3,2,1,0:T(8,128)(2,1)} %pad_maximum_fusion.6), channel_id=1, source_target_pairs={{0,16},{4,20},{8,24},{12,28},{16,0},{20,4},{24,8},{28,12},{1,17},{... | collective-permute-start | bytes 6291464 | tf_op jit(solution)/shard_map/ppermute | solution.py:1227
  482.5 47.7 %collective-permute-start.31 = (bf16[2,4,128,1024]{3,2,1,0:T(8,128)(2,1)}, bf16[2,4,128,1024]{3,2,1,0:T(8,128)(2,1)}, u32[]{:S(2)}, u32[]{:S(2)}) collective-permute-start(bf16[2,4,128,1024]{3,2,1,0:T(8,128)(2,1)} %pad_maximum_fusion.5), channel_id=1, source_target_pairs={{0,8},{4,12},{8,0},{12,4},{16,24},{20,28},{24,16},{28,20},{1,9},{5... | collective-permute-start | bytes 6291464 | tf_op jit(solution)/shard_map/ppermute | solution.py:1227
  560.5 63.1 %all-to-all-start.3 = ((bf16[4,320,1024]{2,1,0:T(8,128)(2,1)}), bf16[4,320,1024]{2,1,0:T(8,128)(2,1)}, u32[]{:S(2)}, u32[]{:S(2)}) async-start(bf16[4,320,1024]{2,1,0:T(8,128)(2,1)} %bitcast.333), calls=%async_computation.3 | async-start | bytes 5242880 | tf_op jit(solution)/shard_map/all_to_all | solution.py:1189
  565.8 132.8 %reduce-scatter.5.cloned.1.call-start = ((), (), s32[]{:S(2)}) async-start(), calls=%async_computation.8 | async-start | bytes 2621440 | tf_op jit(solution)/shard_map/reduce_scatter | solution.py:1315
  623.6 178.4 %reduce-scatter.7.cloned.1.call-start = ((), (), s32[]{:S(2)}) async-start(), calls=%async_computation.9 | async-start | bytes 1310720 | tf_op jit(solution)/shard_map/reduce_scatter | solution.py:1315
  633.5 65.0 %collective-permute-start.39 = (bf16[4,128,1024]{2,1,0:T(8,128)(2,1)}, bf16[4,128,1024]{2,1,0:T(8,128)(2,1)}, u32[]{:S(2)}, u32[]{:S(2)}) collective-permute-start(bf16[4,128,1024]{2,1,0:T(8,128)(2,1)} %get-tuple-element.367), channel_id=1, source_target_pairs={{0,8},{4,12},{8,0},{12,4},{16,24},{20,28},{24,16},{28,20},{1,9},{5... | collective-permute-start | bytes 3145736 | tf_op jit(solution)/shard_map/ppermute | solution.py:1227
  634.5 64.0 %collective-permute-start.40 = (bf16[4,128,1024]{2,1,0:T(8,128)(2,1)S(1)}, bf16[4,128,1024]{2,1,0:T(8,128)(2,1)}, u32[]{:S(2)}, u32[]{:S(2)}) collective-permute-start(bf16[4,128,1024]{2,1,0:T(8,128)(2,1)S(1)} %get-tuple-element.368), channel_id=1, source_target_pairs={{0,16},{4,20},{8,24},{12,28},{16,0},{20,4},{24,8},{28,12},{1,17},{... | collective-permute-start | bytes 3145736 | tf_op jit(solution)/shard_map/ppermute | solution.py:1227
  635.6 62.9 %collective-permute-start.41 = (bf16[4,128,1024]{2,1,0:T(8,128)(2,1)S(1)}, bf16[4,128,1024]{2,1,0:T(8,128)(2,1)}, u32[]{:S(2)}, u32[]{:S(2)}) collective-permute-start(bf16[4,128,1024]{2,1,0:T(8,128)(2,1)S(1)} %get-tuple-element.369), channel_id=1, source_target_pairs={{0,24},{4,28},{8,16},{12,20},{16,8},{20,12},{24,0},{28,4},{1,25},{... | collective-permute-start | bytes 3145736 | tf_op jit(solution)/shard_map/ppermute | solution.py:1227
  637.0 61.5 %collective-permute-start.42 = (bf16[128,1024]{1,0:T(8,128)(2,1)S(1)}, bf16[128,1024]{1,0:T(8,128)(2,1)S(1)}, u32[]{:S(2)}, u32[]{:S(2)}) collective-permute-start(bf16[128,1024]{1,0:T(8,128)(2,1)S(1)} %get-tuple-element.370), channel_id=1, source_target_pairs={{0,1},{1,0},{2,3},{3,2},{4,5},{5,4},{6,7},{7,6},{8,9},{9,8},{10,11... | collective-permute-start | bytes 786440 | tf_op jit(solution)/shard_map/ppermute | solution.py:1148
  705.9 202.2 %reduce-scatter.9.cloned.1.call-start = ((), (), s32[]{:S(2)}) async-start(), calls=%async_computation.10 | async-start | bytes 2621440 | tf_op jit(solution)/shard_map/reduce_scatter | solution.py:1315
  736.2 65.8 %collective-permute-start.47 = (bf16[2,4,128,1024]{3,2,1,0:T(8,128)(2,1)}, bf16[2,4,128,1024]{3,2,1,0:T(8,128)(2,1)}, u32[]{:S(2)}, u32[]{:S(2)}) collective-permute-start(bf16[2,4,128,1024]{3,2,1,0:T(8,128)(2,1)} %pad_maximum_fusion.8), channel_id=1, source_target_pairs={{0,16},{4,20},{8,24},{12,28},{16,0},{20,4},{24,8},{28,12},{1,17},{... | collective-permute-start | bytes 6291464 | tf_op jit(solution)/shard_map/ppermute | solution.py:1227
  738.9 63.1 %collective-permute-start.46 = (bf16[2,4,128,1024]{3,2,1,0:T(8,128)(2,1)}, bf16[2,4,128,1024]{3,2,1,0:T(8,128)(2,1)}, u32[]{:S(2)}, u32[]{:S(2)}) collective-permute-start(bf16[2,4,128,1024]{3,2,1,0:T(8,128)(2,1)} %pad_maximum_fusion.7), channel_id=1, source_target_pairs={{0,8},{4,12},{8,0},{12,4},{16,24},{20,28},{24,16},{28,20},{1,9},{5... | collective-permute-start | bytes 6291464 | tf_op jit(solution)/shard_map/ppermute | solution.py:1227
  802.0 35.0 %collective-permute-start.52 = (bf16[4,4,144,1024]{3,2,1,0:T(8,128)(2,1)}, bf16[4,4,144,1024]{3,2,1,0:T(8,128)(2,1)}, u32[]{:S(2)}, u32[]{:S(2)}) collective-permute-start(bf16[4,4,144,1024]{3,2,1,0:T(8,128)(2,1)} %get-tuple-element.402), channel_id=1, source_target_pairs={{0,4},{4,0},{8,12},{12,8},{16,20},{20,16},{24,28},{28,24},{1,5},{5... | collective-permute-start | bytes 14155784 | tf_op jit(solution)/shard_map/ppermute | solution.py:1227
  850.6 92.3 %reduce-scatter.11.cloned.1.call-start = ((), (), s32[]{:S(2)}) async-start(), calls=%async_computation.11 | async-start | bytes 1474560 | tf_op jit(solution)/shard_map/reduce_scatter | solution.py:1315
  (112 other events, 1421.4 us)
Sparse Core Ops, SparseCore 0:
  56.3 29.1 all-gather.8
  87.8 27.5 all-gather.10
  117.5 27.4 all-gather.12
  168.0 44.6 all-gather.14
  623.7 47.1 reduce-scatter.4
  706.0 25.8 reduce-scatter.6
  850.7 42.6 reduce-scatter.8
  915.0 27.9 reduce-scatter.10

commit v7 on v6

--- a/solution.py
+++ b/solution.py
@@ -946,9 +946,9 @@
     )(grad_proj, *weights, hidden, grad_middle, mods)
 
 
-def qkv_grad(grad_proj, normed, out_keep, out_send, table_rows, apart=False):
+def qkv_grad(grad_proj, normed, out_keep, out_send, apart):
     rows = normed.shape[0]
-    k = 128 if table_rows is None else 144
+    k = 128
 
     def kernel(p_ref, n_ref, ok_ref, os_ref, *rest):
         if apart:
@@ -964,16 +964,10 @@
         keep_ref[:, :, 96:128] = ok_ref[...]
         for m in range(4):
             send_refs[m][0, :, 96:128] = os_ref[m]
-        if table_rows is not None:
-            keep_ref[:, :, 128:144] = rest[0][...]
-            for m in range(4):
-                send_refs[m][0, :, 128:144] = rest[0][m]
 
     gspec = pl.BlockSpec((4, 1, k, D), lambda z: (0, z, 0, 0))
     ospec = pl.BlockSpec((4, 1, 32, D), lambda z: (0, z, 0, 0))
-    tspec = pl.BlockSpec((4, 1, 16, D), lambda z: (0, z, 0, 0))
     gshape = jax.ShapeDtypeStruct((4, NZ, k, D), BF16)
-    extra = () if table_rows is None else (table_rows,)
     sends, send_shapes = [gspec], [gshape]
     if apart:
         sends = [pl.BlockSpec((1, 1, k, D), lambda z: (0, z, 0, 0))] * 4
@@ -982,14 +976,13 @@
         kernel,
         "qkv_grad",
         (NZ,),
-        [pl.BlockSpec((rows, 768), lambda z: (0, z)), full((rows, D)), ospec, ospec]
-        + [tspec] * len(extra),
+        [pl.BlockSpec((rows, 768), lambda z: (0, z)), full((rows, D)), ospec, ospec],
         [gspec] + sends,
         [gshape] + send_shapes,
         [],
         6 * rows * D * D,
         rows * D * 8 + 8 * D * D,
-    )(grad_proj, normed, out_keep, out_send, *extra)
+    )(grad_proj, normed, out_keep, out_send)
 
 
 def place_call(kernel, name, in_specs, out_specs, out_shape, scratch, nbytes, aliases):
@@ -1171,10 +1164,14 @@
     return keep, jnp.where(odd == 0, part[128:], part[:128])
 
 
-def spatial_to_rows(wins, keep, got, odd):
+def whole_windows(wins, odd):
     cols = wins.shape[1]
     whole = lax.dynamic_slice(wins, (256 * odd, 0), (1024, cols))
-    whole = whole.reshape(2, 2, 16, 16, cols).transpose(0, 2, 1, 3, 4).reshape(1024, cols)
+    return whole.reshape(2, 2, 16, 16, cols).transpose(0, 2, 1, 3, 4).reshape(1024, cols)
+
+
+def spatial_to_rows(whole, keep, got, odd):
+    cols = whole.shape[1]
     left, right = jnp.where(odd == 0, keep, got), jnp.where(odd == 0, got, keep)
     part = jnp.stack([left.reshape(8, 16, cols), right.reshape(8, 16, cols)], axis=1)
     part = part.reshape(256, cols)
@@ -1436,7 +1433,7 @@
     g_hid1, g_proj1, out_wins, g_base1, got_f1 = sync(g_hid1, g_proj1, out_wins, g_base1, got_f1)
     grad1 = exchange(g_hid1)
     z_f1 = sum_corner(half_f1, got_f1, z)
-    a1_keep, *a1_send = qkv_grad(g_proj1, normed1, o1_keep, o1_send, None, True)
+    a1_keep, *a1_send = qkv_grad(g_proj1, normed1, o1_keep, o1_send, True)
     a1_got = [swap(v, CORE) for v in a1_send]
     gt_t = jnp.einsum(
         "hjtk,rjk->htr",
@@ -1446,12 +1443,11 @@
     ).reshape(16, n_t)
     out_wins = from_quads(out_wins)
     out_keep, out_send = last_window(out_wins, odd)
-    grad1, a1_got, z_f1, gt_t, out_wins, out_keep, out_send = sync(
-        grad1, a1_got, z_f1, gt_t, out_wins, out_keep, out_send
+    total_a1 = sum_core(a1_keep, a1_got)
+    grad1, total_a1, z_f1, gt_t, out_wins, out_keep, out_send = sync(
+        grad1, total_a1, z_f1, gt_t, out_wins, out_keep, out_send
     )
     grad1 = from_quads(grad1)
-    total_a1 = sum_core(a1_keep, a1_got)
-    grad1, total_a1 = sync(grad1, total_a1)
     mine_f1 = sum_line(z_f1)
     out_got = partner(out_send)
     got_a1 = send_plane(total_a1, (1, 2, 3))
@@ -1471,33 +1467,39 @@
     got_f0 = send_cross(total_f0)
     corner_f1 = corner_stage(sides_f1)
     g_proj0, g_base0 = attn_bwd(qkv0, g_att0, base_s, fc, spatial)
+    a0_keep, a0_send = qkv_grad(g_proj0, normed0, o0_keep, o0_send, False)
+    a0_keep, a0_send, got_f0, corner_f1, mine_a1, g_proj0, g_base0 = sync(
+        a0_keep, a0_send, got_f0, corner_f1, mine_a1, g_proj0, g_base0
+    )
+    a0_got = swap(a0_send, CORE)
+    half_f0 = sum_cross(total_f0, got_f0)
+    half_f0, g_base0, sides_f1, corner_f1 = sync(half_f0, g_base0, sides_f1, corner_f1)
+    got_f0 = send_corner(half_f0)
+    own_gf1 = joined(sides_f1, corner_f1).reshape(4, 256, D)
+    g_feed = finish_feed(place, own_gf1, swap(own_gf1, CORE), 1, ())
     gt_s = jnp.einsum(
         "hjai,bji->hab",
         g_base0[:, :, :496].reshape(16, 16, 31, 16),
         hot_s,
         precision=HIGHEST_PRECISION,
     ).reshape(16, n_s)
-    a0_keep, a0_send = qkv_grad(g_proj0, normed0, o0_keep, o0_send, table_rows(gt_s, gt_t))
-    a0_keep, a0_send, got_f0, corner_f1, mine_a1, g_proj0 = sync(
-        a0_keep, a0_send, got_f0, corner_f1, mine_a1, g_proj0
-    )
-    a0_got = swap(a0_send, CORE)
-    half_f0 = sum_cross(total_f0, got_f0)
-    got_f0 = send_corner(half_f0)
-    own_gf1 = joined(sides_f1, corner_f1).reshape(4, 256, D)
-    g_feed = finish_feed(place, own_gf1, swap(own_gf1, CORE), 1, ())
-    half_f0, got_f0, a0_got, g_proj0, g_feed = sync(half_f0, got_f0, a0_got, g_proj0, g_feed)
+    gt = table_rows(gt_s, gt_t)
+    half_f0, got_f0, a0_got, g_proj0, g_feed, gt = sync(
+        half_f0, got_f0, a0_got, g_proj0, g_feed, gt
+    )
     z_f0 = sum_corner(half_f0, got_f0, z)
     total_a0 = sum_core(a0_keep, a0_got)
+    total_a0 = [jnp.concatenate([total_a0[m], gt[m]], axis=1) for m in range(4)]
     total_a0, z_f0, g_proj0 = sync(total_a0, z_f0, g_proj0)
     mine_f0 = sum_line(z_f0)
     got_a0 = send_cross(total_a0)
     grad0, sums_q0 = qkv_back(g_proj0, weights_a0, hidden0, g_mid0, mods, 0, F32, 1)
-    grad0, sums_q0, got_a0 = sync(grad0, sums_q0, got_a0)
+    sides_a1 = sides_stage(mine_a1[None])
+    grad0, sums_q0, got_a0, sides_a1 = sync(grad0, sums_q0, got_a0, sides_a1)
     half_a0 = sum_cross(total_a0, got_a0)
     half_a0, grad0, sums_q0 = sync(half_a0, grad0, sums_q0)
     got_a0 = send_corner(half_a0)
-    sides_a1 = sides_stage(mine_a1[None])
+    corner_a1 = corner_stage(sides_a1)
     mod_rows = jnp.concatenate(
         [
             sums_q0[0:2], sums_o0[2:3], sums_o0[0:2], sums_o0[3:4],
@@ -1506,36 +1508,37 @@
         axis=0,
     )
     mod_got = partner(mod_rows)
-    got_a0, sides_a1, mine_f0, mod_got, mod_rows = sync(
-        got_a0, sides_a1, mine_f0, mod_got, mod_rows
+    got_a0, corner_a1, mine_f0, mod_got, mod_rows = sync(
+        got_a0, corner_a1, mine_f0, mod_got, mod_rows
     )
     z_a0 = sum_corner(half_a0, got_a0, z)
     mod_sum = mod_rows + mod_got
     z_a0, mine_f0, mod_sum = sync(z_a0, mine_f0, mod_sum)
     mine_a0 = sum_line(z_a0)
     own_gf0 = cross_stage(mine_f0)
-    corner_a1 = corner_stage(sides_a1)
-    output = spatial_to_rows(out_wins, out_keep, out_got, odd)
+    own_ga1 = joined(sides_a1, corner_a1).reshape(4, 128, D)
+    rows_whole = whole_windows(grad0, odd)
+    output = spatial_to_rows(whole_windows(out_wins, odd), out_keep, out_got, odd)
     rows_keep, rows_send = last_window(grad0, odd)
-    mine_a0, own_gf0, corner_a1, rows_keep, rows_send, output = sync(
-        mine_a0, own_gf0, corner_a1, rows_keep, rows_send, output
+    mine_a0, own_gf0, own_ga1, rows_keep, rows_send, rows_whole, output = sync(
+        mine_a0, own_gf0, own_ga1, rows_keep, rows_send, rows_whole, output
     )
     own_ga0 = cross_stage(mine_a0)
     rows_got = partner(rows_send)
     own_gf0 = jnp.stack(own_gf0)
-    own_ga1 = joined(sides_a1, corner_a1).reshape(4, 128, D)
     g_feed = finish_feed(place, own_gf0, swap(own_gf0, CORE), 0, g_feed)
     own_ga0, g_feed, rows_got, own_ga1, mod_sum = sync(own_ga0, g_feed, rows_got, own_ga1, mod_sum)
     own_ga0 = jnp.stack(own_ga0)
     own_ga = jnp.concatenate([own_ga0[:, :128], own_ga1, own_ga0[:, 128:]], axis=1)
-    own_ga0 = own_ga
     mod_got = lax.ppermute(mod_sum, "head", [(i, i ^ 2) for i in range(NZ)])
-    grad_tokens = spatial_to_rows(grad0, rows_keep, rows_got, odd)
-    g_attn = finish_attn(place, own_ga, swap(own_ga, CORE))
+    grad_tokens = spatial_to_rows(rows_whole, rows_keep, rows_got, odd)
+    other_ga = swap(own_ga, CORE)
+    g_attn = finish_attn(place, own_ga, other_ga)
+    tab = own_ga[:, 256:272].astype(F32) + other_ga[:, 256:272].astype(F32)
     tab = jnp.concatenate(
-        [lax.dynamic_slice_in_dim(own_ga0, chip ^ m, 1, axis=0) for m in range(4)], axis=0
-    )
-    tab = tab[:, 256:272].reshape(4, 16 * D).astype(F32)
+        [lax.dynamic_slice_in_dim(tab, chip ^ m, 1, axis=0) for m in range(4)], axis=0
+    )
+    tab = tab.reshape(4, 16 * D)
     return (
         output,
         grad_tokens,

time: 1000 us -> 995 us (level)
    all_to_all x4, waiting for transfers between devices: 29.8 us -> 19 us  [exchange(): return lax.all_to_all(values, 'head', 0, 0, tiled=True)]
  transfers between devices with their start and end apart: 85 -> 85, of which waited for: 24 -> 26; matrix products, arithmetic and copies ran while one was open for 17% -> 17% of each run, Pallas kernels for 51% -> 51%
where the time goes in v7:
time: 995 us; the launch traced here: 985 us
  Pallas kernels  521 us (52%)
  other arithmetic  131 us (13%)
  waiting for transfers between devices  110 us (11%)
  local copies, waits for them, and re-layouts  98.8 us (10%)
  starting transfers between devices  92.6 us (9%)
  between operations  16.6 us (2%)
  matrix products  15.2 us (2%)
    pallas_call x2, Pallas kernels, ffn_bwd(): call(kernel, 'ffn_bwd', (NZ,), [full((rows, D)), pl.BlockSpec((rows, D),...  123 us
    pallas_call x2, Pallas kernels, attn_bwd(): call(kernel, 'attn_bwd', (NZ,), [xspec, pl.BlockSpec((parts, count, size,...  75.6 us
    pallas_call x2, Pallas kernels, ffn_fwd(): call(kernel, 'ffn_fwd', (NZ,), [full((rows, D))] + feed_specs(down_block)...  70.8 us
    ppermute x61, waiting for transfers between devices, swap(): return lax.ppermute(values, 'clip', [(i, i ^ bit) for i in range(8)])  62.1 us
    convert_element_type x13, other arithmetic, add(): return (first.astype(F32) + second.astype(F32)).astype(BF16)  53.4 us
    ppermute x61, starting transfers between devices, swap(): return lax.ppermute(values, 'clip', [(i, i ^ bit) for i in range(8)])  52.8 us
    pallas_call x2, Pallas kernels, attn_fwd(): call(kernel, 'attn_fwd', (NZ,), [pl.BlockSpec((parts, count, size, 768),...  43.4 us
    pallas_call x2, Pallas kernels, qkv_back(): call(kernel, 'qkv_back', (NZ,), [pl.BlockSpec((rows, 768), lambda z: (0,...  41.9 us
  transfers between devices with their start and end apart: 85, of which 26 were waited for; matrix products, arithmetic and copies ran while one was open for 17% of the time, Pallas kernels for 51%

profile of v7, /device:TPU:0, one launch (start us, length us, event | category | flops | bytes accessed | tf_op | source)
XLA Modules:
  0.0 985.0 jit_solution(12098976982454728612)
XLA Ops:
  71.9 10.8 %collective-permute-done.6 = bf16[3,128,1024]{2,1,0:T(8,128)(2,1)} collective-permute-done((bf16[3,128,1024]{2,1,0:T(8,128)(2,1)S(1)}, bf16[3,128,1024]{2,1,0:T(8,128)(2,1)}, u32[]{:S(2)}, u32[]{:S(2)}) %collective-permute-start.6) | collective-permute-done | bytes 786464 | tf_op jit(solution)/shard_map/ppermute | solution.py:1224
  96.0 16.0 %ln_qkv.2 = (bf16[1280,1024]{1,0:T(8,128)(2,1)}, bf16[1280,3072]{1,0:T(8,128)(2,1)}) custom-call(bf16[1280,1024]{1,0:T(8,128)(2,1)} %maximum_select_fusion.1.h_ref, f32[12,1024]{1,0:T(8,128)} %bitcast.314, bf16[2,4,128,1024]{3,2,1,0:T(8,128)(2,1)} %prep_attn.2.l_ref, bf16[4,3,128,1024]{3,2,1,0:T(8,128)(2,1)} %copy-done.2, ...), custom_call_target="tpu_custom_call" | custom-call | flops 2013265920 | bytes 5505024 | tf_op jit(solution)/shard_map/ln_qkv/pallas_call | solution.py:502
  123.6 20.6 %attn_fwd.2 = bf16[1,5,256,1024]{3,2,1,0:T(8,128)(2,1)} custom-call(bf16[1,5,256,3072]{3,2,1,0:T(8,128)(2,1)} %bitcast.334, f32[16,16,512]{2,1,0:T(8,128)} %pad.18.b_ref, s32[1]{0:T(128)} %copy.115.fc_ref), custom_call_target="tpu_custom_call" | custom-call | flops 1342177280 | bytes 2621440 | tf_op jit(solution)/shard_map/attn_fwd/pallas_call | solution.py:557
  152.3 9.3 out_proj.2
  171.4 35.7 %ffn_fwd.2 = (bf16[1280,4096]{1,0:T(8,128)(2,1)}, bf16[1280,1024]{1,0:T(8,128)(2,1)}, bf16[1280,1024]{1,0:T(8,128)(2,1)}) custom-call(bf16[1280,1024]{1,0:T(8,128)(2,1)} %get-tuple-element.287.x_ref, bf16[2,4,256,1024]{3,2,1,0:T(8,128)(2,1)} %prep_feed.2.refs_0_, bf16[4,3,128,1024]{3,2,1,0:T(8,128)(2,1)} %copy-done.6, ...), custom_call_target="tpu_custom_call" | custom-call | flops 5368709120 | bytes 10747904 | tf_op jit(solution)/shard_map/ffn_fwd/pallas_call | solution.py:747
  258.2 11.4 %collective-permute-done.25 = bf16[128,1024]{1,0:T(8,128)(2,1)} collective-permute-done((bf16[128,1024]{1,0:T(8,128)(2,1)}, bf16[128,1024]{1,0:T(8,128)(2,1)}, u32[]{:S(2)}, u32[]{:S(2)}) %collective-permute-start.25) | collective-permute-done | bytes 262176 | tf_op jit(solution)/shard_map/ppermute | solution.py:1141
  273.1 7.9 all-to-all-done
  281.0 15.9 %ln_qkv.3 = (bf16[1280,1024]{1,0:T(8,128)(2,1)}, bf16[1280,3072]{1,0:T(8,128)(2,1)}) custom-call(bf16[1280,1024]{1,0:T(8,128)(2,1)} %bitcast.40.h_ref, f32[12,1024]{1,0:T(8,128)} %bitcast.317, bf16[2,4,128,1024]{3,2,1,0:T(8,128)(2,1)} %prep_attn.3.l_ref, bf16[4,3,128,1024]{3,2,1,0:T(8,128)(2,1)} %copy-done.3, ...), custom_call_target="tpu_custom_call" | custom-call | flops 2013265920 | bytes 5505024 | tf_op jit(solution)/shard_map/ln_qkv/pallas_call | solution.py:502
  311.5 22.8 %attn_fwd.3 = bf16[5,4,64,1024]{3,2,1,0:T(8,128)(2,1)} custom-call(bf16[5,4,64,3072]{3,2,1,0:T(8,128)(2,1)} %bitcast.332, f32[16,64,640]{2,1,0:T(8,128)} %pad.19.b_ref, s32[1]{0:T(128)} %copy.115.fc_ref), custom_call_target="tpu_custom_call" | custom-call | flops 1677721600 | bytes 2621440 | tf_op jit(solution)/shard_map/attn_fwd/pallas_call | solution.py:557
  334.3 9.3 out_proj.3
  343.6 35.1 %ffn_fwd.3 = (bf16[1280,4096]{1,0:T(8,128)(2,1)}, bf16[1280,1024]{1,0:T(8,128)(2,1)}, bf16[1280,1024]{1,0:T(8,128)(2,1)}) custom-call(bf16[1280,1024]{1,0:T(8,128)(2,1)} %get-tuple-element.313.x_ref, bf16[2,4,256,1024]{3,2,1,0:T(8,128)(2,1)} %prep_feed.3.refs_0_, bf16[4,3,256,1024]{3,2,1,0:T(8,128)(2,1)} %pad_maximum_fusion.refs_1_.refs_3_, ...), custom_call_target="tpu_custom_call" | custom-call | flops 5368709120 | bytes 10747904 | tf_op jit(solution)/shard_map/ffn_fwd/pallas_call | solution.py:747
  388.2 61.2 %ffn_bwd.2 = (bf16[4,4,256,1024]{3,2,1,0:T(8,128)(2,1)}, bf16[4,4,256,1024]{3,2,1,0:T(8,128)(2,1)}, f32[1280,1024]{1,0:T(8,128)}) custom-call(bf16[1280,1024]{1,0:T(8,128)(2,1)} %get-tuple-element.603.g_ref, bf16[1280,4096]{1,0:T(8,128)(2,1)} %get-tuple-element.319.p_ref, bf16[1280,1024]{1,0:T(8,128)(2,1)} %get-tuple-element.313.x_ref, ...), custom_call_target="tpu_custom_call" | custom-call | flops 10737418240 | bytes 13631488 | tf_op jit(solution)/shard_map/ffn_bwd/pallas_call | solution.py:809
  449.5 19.1 %out_bwd.2 = (f32[1280,1024]{1,0:T(8,128)}, bf16[1280,1024]{1,0:T(8,128)(2,1)}, bf16[4,4,32,1024]{3,2,1,0:T(8,128)(2,1)}, bf16[4,4,32,1024]{3,2,1,0:T(8,128)(2,1)}, f32[8,1024]{1,0:T(8,128)}) custom-call(bf16[1280,1024]{1,0:T(8,128)(2,1)} %get-tuple-element.603.g_ref, f32[1280,1024]{1,0:T(8,128)} %get-tuple-element.324.gs_ref, ...), custom_call_target="tpu_custom_call" | custom-call | flops 1342177280 | bytes 8912896 | tf_op jit(solution)/shard_map/out_bwd/pallas_call | solution.py:873
  468.7 9.1 fusion.16
  483.2 42.7 %attn_bwd.2 = (bf16[5,4,64,3072]{3,2,1,0:T(8,128)(2,1)}, f32[16,64,640]{2,1,0:T(8,128)}) custom-call(bf16[5,4,64,3072]{3,2,1,0:T(8,128)(2,1)} %bitcast.333, bf16[5,4,64,1024]{3,2,1,0:T(8,128)(2,1)} %bitcast.392, f32[16,64,640]{2,1,0:T(8,128)} %pad.19.b_ref, s32[1]{0:T(128)} %copy.115.fc_ref), custom_call_target="tpu_custom_call" | custom-call | flops 4194304000 | bytes 5242880 | tf_op jit(solution)/shard_map/attn_bwd/pallas_call | solution.py:620
  536.9 20.4 %qkv_back.2 = (bf16[1280,1024]{1,0:T(8,128)(2,1)}, f32[8,1024]{1,0:T(8,128)}) custom-call(bf16[1280,3072]{1,0:T(8,128)(2,1)} %bitcast.296, bf16[2,4,128,1024]{3,2,1,0:T(8,128)(2,1)} %prep_attn.3.l_ref, bf16[4,3,128,1024]{3,2,1,0:T(8,128)(2,1)} %copy-done.3, bf16[4,3,128,1024]{3,2,1,0:T(8,128)(2,1)} %collective-permute-done.24.v_ref, ...), custom_call_target="tpu_custom_call" | custom-call | flops 2013265920 | bytes 8126464 | tf_op jit(solution)/shard_map/qkv_back/pallas_call | solution.py:933
  564.7 13.2 %qkv_grad.2 = (bf16[4,4,128,1024]{3,2,1,0:T(8,128)(2,1)}, bf16[1,4,128,1024]{3,2,1,0:T(8,128)(2,1)}, bf16[1,4,128,1024]{3,2,1,0:T(8,128)(2,1)}, bf16[1,4,128,102...) custom-call(bf16[1280,3072]{1,0:T(8,128)(2,1)} %bitcast.297, bf16[1280,1024]{1,0:T(8,128)(2,1)} %get-tuple-element.351.n_ref, ...), custom_call_target="tpu_custom_call" | custom-call | flops 2013265920 | bytes 4718592 | tf_op jit(solution)/shard_map/qkv_grad/pallas_call | solution.py:975
  604.3 7.1 fusion.44
  611.4 11.1 %all-to-all-done.3 = bf16[4,320,1024]{2,1,0:T(8,128)(2,1)} async-done(((bf16[4,320,1024]{2,1,0:T(8,128)(2,1)}), bf16[4,320,1024]{2,1,0:T(8,128)(2,1)}, u32[]{:S(2)}, u32[]{:S(2)}) %all-to-all-start.3) | async-done | bytes 2621472 | tf_op jit(solution)/shard_map/all_to_all | solution.py:1186
  629.9 61.7 %ffn_bwd.3 = (bf16[4,4,256,1024]{3,2,1,0:T(8,128)(2,1)}, bf16[4,4,256,1024]{3,2,1,0:T(8,128)(2,1)}, f32[1280,1024]{1,0:T(8,128)}) custom-call(bf16[1280,1024]{1,0:T(8,128)(2,1)} %bitcast.306, bf16[1280,4096]{1,0:T(8,128)(2,1)} %get-tuple-element.366.p_ref, bf16[1280,1024]{1,0:T(8,128)(2,1)} %get-tuple-element.287.x_ref, ...), custom_call_target="tpu_custom_call" | custom-call | flops 10737418240 | bytes 13631488 | tf_op jit(solution)/shard_map/ffn_bwd/pallas_call | solution.py:809
  698.5 18.6 %out_bwd.3 = (f32[1280,1024]{1,0:T(8,128)}, bf16[1280,1024]{1,0:T(8,128)(2,1)}, bf16[4,4,32,1024]{3,2,1,0:T(8,128)(2,1)}, bf16[4,4,32,1024]{3,2,1,0:T(8,128)(2,1)}, f32[8,1024]{1,0:T(8,128)}) custom-call(bf16[1280,1024]{1,0:T(8,128)(2,1)} %bitcast.307, f32[1280,1024]{1,0:T(8,128)} %get-tuple-element.375.gs_ref, ...), custom_call_target="tpu_custom_call" | custom-call | flops 1342177280 | bytes 8912896 | tf_op jit(solution)/shard_map/out_bwd/pallas_call | solution.py:873
  717.1 9.0 fusion.20
  737.0 32.9 %attn_bwd.3 = (bf16[1,5,256,3072]{3,2,1,0:T(8,128)(2,1)}, f32[16,16,512]{2,1,0:T(8,128)}) custom-call(bf16[1,5,256,3072]{3,2,1,0:T(8,128)(2,1)} %bitcast.335, bf16[1,5,256,1024]{3,2,1,0:T(8,128)(2,1)} %bitcast.391, f32[16,16,512]{2,1,0:T(8,128)} %pad.18.b_ref, s32[1]{0:T(128)} %copy.115.fc_ref), custom_call_target="tpu_custom_call" | custom-call | flops 3355443200 | bytes 5242880 | tf_op jit(solution)/shard_map/attn_bwd/pallas_call | solution.py:620
  769.9 13.1 %qkv_grad.3 = (bf16[4,4,128,1024]{3,2,1,0:T(8,128)(2,1)}, bf16[4,4,128,1024]{3,2,1,0:T(8,128)(2,1)}) custom-call(bf16[1280,3072]{1,0:T(8,128)(2,1)} %bitcast.294, bf16[1280,1024]{1,0:T(8,128)(2,1)} %get-tuple-element.386.n_ref, bf16[4,4,32,1024]{3,2,1,0:T(8,128)(2,1)} %get-tuple-element.387.ok_ref, bf16[4,4,32,1024]{3,2,1,0:T(8,128)(2,1)} %get-tuple-element.388.os_ref), custom_call_target="tpu_custom_call" | custom-call | flops 2013265920 | bytes 4718592 | tf_op jit(solution)/shard_map/qkv_grad/pallas_call | solution.py:975
  803.9 9.1 finish_feed.2
  812.9 13.7 %collective-permute-done.50 = bf16[4,128,1024]{2,1,0:T(8,128)(2,1)} collective-permute-done((bf16[4,128,1024]{2,1,0:T(8,128)(2,1)}, bf16[4,128,1024]{2,1,0:T(8,128)(2,1)}, u32[]{:S(2)}, u32[]{:S(2)}) %collective-permute-start.50) | collective-permute-done | bytes 1048608 | tf_op jit(solution)/shard_map/ppermute | solution.py:1224
  852.3 21.5 %qkv_back.3 = (f32[1280,1024]{1,0:T(8,128)}, f32[8,1024]{1,0:T(8,128)}) custom-call(bf16[1280,3072]{1,0:T(8,128)(2,1)} %bitcast.295, bf16[2,4,128,1024]{3,2,1,0:T(8,128)(2,1)} %prep_attn.2.l_ref, bf16[4,3,128,1024]{3,2,1,0:T(8,128)(2,1)} %copy-done.2, bf16[4,3,128,1024]{3,2,1,0:T(8,128)(2,1)} %collective-permute-done.10.v_ref, ...), custom_call_target="tpu_custom_call" | custom-call | flops 2013265920 | bytes 8126464 | tf_op jit(solution)/shard_map/qkv_back/pallas_call | solution.py:933
  873.8 8.2 collective-permute-done.56
  921.8 7.1 collective-permute-done.63
  928.9 8.1 collective-permute-done.64
  945.1 9.0 finish_feed.3
  968.3 9.4 finish_attn.1
  (450 shorter events, 368.5 us)
Async XLA Ops:
  7.2 78.3 %all-gather.9.cloned.1.call-start = ((), (), s32[]{:S(2)}) async-start(), calls=%async_computation.12 | async-start | bytes 1310720 | tf_op jit(solution)/shard_map/all_gather | solution.py:1360
  56.2 59.2 %all-gather.11.cloned.1.call-start = ((), (), s32[]{:S(2)}) async-start(), calls=%async_computation.13 | async-start | bytes 1310720 | tf_op jit(solution)/shard_map/all_gather | solution.py:1361
  87.7 57.3 %all-gather.13.cloned.1.call-start = ((), (), s32[]{:S(2)}) async-start(), calls=%async_computation.14 | async-start | bytes 1310720 | tf_op jit(solution)/shard_map/all_gather | solution.py:1378
  95.1 117.5 %all-gather.15.cloned.1.call-start = ((), (), s32[]{:S(2)}) async-start(), calls=%async_computation.15 | async-start | bytes 2621440 | tf_op jit(solution)/shard_map/all_gather | solution.py:1389
  167.9 44.8 %collective-permute-start.21 = (bf16[3,128,1024]{2,1,0:T(8,128)(2,1)}, bf16[3,128,1024]{2,1,0:T(8,128)(2,1)}, u32[]{:S(2)}, u32[]{:S(2)}) collective-permute-start(bf16[3,128,1024]{2,1,0:T(8,128)(2,1)} %pad_maximum_fusion.23), channel_id=1, source_target_pairs={{0,8},{4,12},{8,0},{12,4},{16,24},{20,28},{24,16},{28,20},{1,9},{5... | collective-permute-start | bytes 2359304 | tf_op jit(solution)/shard_map/ppermute | solution.py:1224
  169.0 43.7 %collective-permute-start.22 = (bf16[3,128,1024]{2,1,0:T(8,128)(2,1)}, bf16[3,128,1024]{2,1,0:T(8,128)(2,1)}, u32[]{:S(2)}, u32[]{:S(2)}) collective-permute-start(bf16[3,128,1024]{2,1,0:T(8,128)(2,1)} %pad_maximum_fusion.23), channel_id=1, source_target_pairs={{0,16},{4,20},{8,24},{12,28},{16,0},{20,4},{24,8},{28,12},{1,17},{... | collective-permute-start | bytes 2359304 | tf_op jit(solution)/shard_map/ppermute | solution.py:1224
  169.8 42.9 %collective-permute-start.23 = (bf16[3,128,1024]{2,1,0:T(8,128)(2,1)}, bf16[3,128,1024]{2,1,0:T(8,128)(2,1)}, u32[]{:S(2)}, u32[]{:S(2)}) collective-permute-start(bf16[3,128,1024]{2,1,0:T(8,128)(2,1)} %pad_maximum_fusion.23), channel_id=1, source_target_pairs={{0,24},{4,28},{8,16},{12,20},{16,8},{20,12},{24,0},{28,4},{1,25},{... | collective-permute-start | bytes 2359304 | tf_op jit(solution)/shard_map/ppermute | solution.py:1224
  216.2 64.8 %all-to-all-start = ((bf16[4,320,1024]{2,1,0:T(8,128)(2,1)}), bf16[4,320,1024]{2,1,0:T(8,128)(2,1)}, u32[]{:S(2)}, u32[]{:S(2)}) async-start(bf16[4,320,1024]{2,1,0:T(8,128)(2,1)} %bitcast.39), calls=%async_computation | async-start | bytes 5242880 | tf_op jit(solution)/shard_map/all_to_all | solution.py:1186
  223.5 49.6 %collective-permute-start.24 = (bf16[4,3,128,1024]{3,2,1,0:T(8,128)(2,1)S(1)}, bf16[4,3,128,1024]{3,2,1,0:T(8,128)(2,1)}, u32[]{:S(2)}, u32[]{:S(2)}) collective-permute-start(bf16[4,3,128,1024]{3,2,1,0:T(8,128)(2,1)S(1)} %pad_maximum_fusion.4.w_ref), channel_id=1, source_target_pairs={{0,4},{4,0},{8,12},{12,8},{16,20},{20,16},{24,28},{28,24},{1,5},{5... | collective-permute-start | bytes 9437192 | tf_op jit(solution)/shard_map/ppermute | solution.py:1224
  225.8 71.1 %collective-permute-start.26 = (bf16[3,256,1024]{2,1,0:T(8,128)(2,1)}, bf16[3,256,1024]{2,1,0:T(8,128)(2,1)}, u32[]{:S(2)}, u32[]{:S(2)}) collective-permute-start(bf16[3,256,1024]{2,1,0:T(8,128)(2,1)} %pad_maximum_fusion.11), channel_id=1, source_target_pairs={{0,8},{4,12},{8,0},{12,4},{16,24},{20,28},{24,16},{28,20},{1,9},{5... | collective-permute-start | bytes 4718600 | tf_op jit(solution)/shard_map/ppermute | solution.py:1224
  227.3 70.7 %collective-permute-start.27 = (bf16[3,256,1024]{2,1,0:T(8,128)(2,1)}, bf16[3,256,1024]{2,1,0:T(8,128)(2,1)}, u32[]{:S(2)}, u32[]{:S(2)}) collective-permute-start(bf16[3,256,1024]{2,1,0:T(8,128)(2,1)} %pad_maximum_fusion.11), channel_id=1, source_target_pairs={{0,16},{4,20},{8,24},{12,28},{16,0},{20,4},{24,8},{28,12},{1,17},{... | collective-permute-start | bytes 4718600 | tf_op jit(solution)/shard_map/ppermute | solution.py:1224
  228.7 69.2 %collective-permute-start.28 = (bf16[3,256,1024]{2,1,0:T(8,128)(2,1)}, bf16[3,256,1024]{2,1,0:T(8,128)(2,1)}, u32[]{:S(2)}, u32[]{:S(2)}) collective-permute-start(bf16[3,256,1024]{2,1,0:T(8,128)(2,1)} %pad_maximum_fusion.11), channel_id=1, source_target_pairs={{0,24},{4,28},{8,16},{12,20},{16,8},{20,12},{24,0},{28,4},{1,25},{... | collective-permute-start | bytes 4718600 | tf_op jit(solution)/shard_map/ppermute | solution.py:1224
  231.1 38.4 %collective-permute-start.25 = (bf16[128,1024]{1,0:T(8,128)(2,1)}, bf16[128,1024]{1,0:T(8,128)(2,1)}, u32[]{:S(2)}, u32[]{:S(2)}) collective-permute-start(bf16[128,1024]{1,0:T(8,128)(2,1)} %bitcast.55), channel_id=1, source_target_pairs={{0,1},{1,0},{2,3},{3,2},{4,5},{5,4},{6,7},{7,6},{8,9},{9,8},{10,11... | collective-permute-start | bytes 786440 | tf_op jit(solution)/shard_map/ppermute | solution.py:1141
  304.7 38.9 %collective-permute-start.29 = (bf16[4,3,256,1024]{3,2,1,0:T(8,128)(2,1)}, bf16[4,3,256,1024]{3,2,1,0:T(8,128)(2,1)}, u32[]{:S(2)}, u32[]{:S(2)}) collective-permute-start(bf16[4,3,256,1024]{3,2,1,0:T(8,128)(2,1)} %pad_maximum_fusion.refs_1_.refs_3_), channel_id=1, source_target_pairs={{0,4},{4,0},{8,12},{12,8},{16,20},{20,16},{24,28},{28,24},{1,5},{5... | collective-permute-start | bytes 18874376 | tf_op jit(solution)/shard_map/ppermute | solution.py:1224
  306.5 72.2 %all-to-all-start.1 = ((bf16[4,320,1024]{2,1,0:T(8,128)(2,1)}), bf16[4,320,1024]{2,1,0:T(8,128)(2,1)S(1)}, u32[]{:S(2)}, u32[]{:S(2)}) async-start(bf16[4,320,1024]{2,1,0:T(8,128)(2,1)} %bitcast.64), calls=%async_computation.1 | async-start | bytes 5242880 | tf_op jit(solution)/shard_map/all_to_all | solution.py:1186
  382.9 66.5 %all-to-all-start.2 = ((bf16[4,320,1024]{2,1,0:T(8,128)(2,1)}), bf16[4,320,1024]{2,1,0:T(8,128)(2,1)S(1)}, u32[]{:S(2)}, u32[]{:S(2)}) async-start(bf16[4,320,1024]{2,1,0:T(8,128)(2,1)} %bitcast.313), calls=%async_computation.2 | async-start | bytes 5242880 | tf_op jit(solution)/shard_map/all_to_all | solution.py:1186
  479.6 48.0 %collective-permute-start.32 = (bf16[2,4,128,1024]{3,2,1,0:T(8,128)(2,1)}, bf16[2,4,128,1024]{3,2,1,0:T(8,128)(2,1)}, u32[]{:S(2)}, u32[]{:S(2)}) collective-permute-start(bf16[2,4,128,1024]{3,2,1,0:T(8,128)(2,1)} %pad_maximum_fusion.7), channel_id=1, source_target_pairs={{0,16},{4,20},{8,24},{12,28},{16,0},{20,4},{24,8},{28,12},{1,17},{... | collective-permute-start | bytes 6291464 | tf_op jit(solution)/shard_map/ppermute | solution.py:1224
  482.6 47.7 %collective-permute-start.31 = (bf16[2,4,128,1024]{3,2,1,0:T(8,128)(2,1)}, bf16[2,4,128,1024]{3,2,1,0:T(8,128)(2,1)}, u32[]{:S(2)}, u32[]{:S(2)}) collective-permute-start(bf16[2,4,128,1024]{3,2,1,0:T(8,128)(2,1)} %pad_maximum_fusion.6), channel_id=1, source_target_pairs={{0,8},{4,12},{8,0},{12,4},{16,24},{20,28},{24,16},{28,20},{1,9},{5... | collective-permute-start | bytes 6291464 | tf_op jit(solution)/shard_map/ppermute | solution.py:1224
  559.6 62.8 %all-to-all-start.3 = ((bf16[4,320,1024]{2,1,0:T(8,128)(2,1)}), bf16[4,320,1024]{2,1,0:T(8,128)(2,1)}, u32[]{:S(2)}, u32[]{:S(2)}) async-start(bf16[4,320,1024]{2,1,0:T(8,128)(2,1)} %bitcast.355), calls=%async_computation.3 | async-start | bytes 5242880 | tf_op jit(solution)/shard_map/all_to_all | solution.py:1186
  564.7 127.0 %reduce-scatter.5.cloned.1.call-start = ((), (), s32[]{:S(2)}) async-start(), calls=%async_computation.8 | async-start | bytes 2621440 | tf_op jit(solution)/shard_map/reduce_scatter | solution.py:1312
  622.5 160.6 %reduce-scatter.7.cloned.1.call-start = ((), (), s32[]{:S(2)}) async-start(), calls=%async_computation.9 | async-start | bytes 1310720 | tf_op jit(solution)/shard_map/reduce_scatter | solution.py:1312
  622.5 69.1 %collective-permute-start.39 = (bf16[4,128,1024]{2,1,0:T(8,128)(2,1)}, bf16[4,128,1024]{2,1,0:T(8,128)(2,1)}, u32[]{:S(2)}, u32[]{:S(2)}) collective-permute-start(bf16[4,128,1024]{2,1,0:T(8,128)(2,1)} %get-tuple-element.371), channel_id=1, source_target_pairs={{0,8},{4,12},{8,0},{12,4},{16,24},{20,28},{24,16},{28,20},{1,9},{5... | collective-permute-start | bytes 3145736 | tf_op jit(solution)/shard_map/ppermute | solution.py:1224
  623.5 68.1 %collective-permute-start.40 = (bf16[4,128,1024]{2,1,0:T(8,128)(2,1)}, bf16[4,128,1024]{2,1,0:T(8,128)(2,1)}, u32[]{:S(2)}, u32[]{:S(2)}) collective-permute-start(bf16[4,128,1024]{2,1,0:T(8,128)(2,1)} %get-tuple-element.372), channel_id=1, source_target_pairs={{0,16},{4,20},{8,24},{12,28},{16,0},{20,4},{24,8},{28,12},{1,17},{... | collective-permute-start | bytes 3145736 | tf_op jit(solution)/shard_map/ppermute | solution.py:1224
  624.4 67.2 %collective-permute-start.41 = (bf16[4,128,1024]{2,1,0:T(8,128)(2,1)}, bf16[4,128,1024]{2,1,0:T(8,128)(2,1)}, u32[]{:S(2)}, u32[]{:S(2)}) collective-permute-start(bf16[4,128,1024]{2,1,0:T(8,128)(2,1)} %get-tuple-element.373), channel_id=1, source_target_pairs={{0,24},{4,28},{8,16},{12,20},{16,8},{20,12},{24,0},{28,4},{1,25},{... | collective-permute-start | bytes 3145736 | tf_op jit(solution)/shard_map/ppermute | solution.py:1224
  629.9 61.7 %collective-permute-start.42 = (bf16[128,1024]{1,0:T(8,128)(2,1)S(1)}, bf16[128,1024]{1,0:T(8,128)(2,1)S(1)}, u32[]{:S(2)}, u32[]{:S(2)}) collective-permute-start(bf16[128,1024]{1,0:T(8,128)(2,1)S(1)} %get-tuple-element.374), channel_id=1, source_target_pairs={{0,1},{1,0},{2,3},{3,2},{4,5},{5,4},{6,7},{7,6},{8,9},{9,8},{10,11... | collective-permute-start | bytes 786440 | tf_op jit(solution)/shard_map/ppermute | solution.py:1141
  698.5 204.8 %reduce-scatter.9.cloned.1.call-start = ((), (), s32[]{:S(2)}) async-start(), calls=%async_computation.10 | async-start | bytes 2621440 | tf_op jit(solution)/shard_map/reduce_scatter | solution.py:1312
  729.0 55.9 %collective-permute-start.47 = (bf16[2,4,128,1024]{3,2,1,0:T(8,128)(2,1)}, bf16[2,4,128,1024]{3,2,1,0:T(8,128)(2,1)}, u32[]{:S(2)}, u32[]{:S(2)}) collective-permute-start(bf16[2,4,128,1024]{3,2,1,0:T(8,128)(2,1)} %pad_maximum_fusion.9), channel_id=1, source_target_pairs={{0,16},{4,20},{8,24},{12,28},{16,0},{20,4},{24,8},{28,12},{1,17},{... | collective-permute-start | bytes 6291464 | tf_op jit(solution)/shard_map/ppermute | solution.py:1224
  732.1 52.8 %collective-permute-start.46 = (bf16[2,4,128,1024]{3,2,1,0:T(8,128)(2,1)}, bf16[2,4,128,1024]{3,2,1,0:T(8,128)(2,1)}, u32[]{:S(2)}, u32[]{:S(2)}) collective-permute-start(bf16[2,4,128,1024]{3,2,1,0:T(8,128)(2,1)} %pad_maximum_fusion.8), channel_id=1, source_target_pairs={{0,8},{4,12},{8,0},{12,4},{16,24},{20,28},{24,16},{28,20},{1,9},{5... | collective-permute-start | bytes 6291464 | tf_op jit(solution)/shard_map/ppermute | solution.py:1224
  733.9 49.2 %collective-permute-start.48 = (bf16[1,128,1024]{2,1,0:T(8,128)(2,1)}, bf16[1,128,1024]{2,1,0:T(8,128)(2,1)}, u32[]{:S(2)}, u32[]{:S(2)}) collective-permute-start(bf16[1,128,1024]{2,1,0:T(8,128)(2,1)} %slice.389), channel_id=1, source_target_pairs={{0,16},{4,20},{8,24},{12,28},{16,0},{20,4},{24,8},{28,12},{1,17},{... | collective-permute-start | bytes 786440 | tf_op jit(solution)/shard_map/ppermute | solution.py:1224
  736.8 48.1 %collective-permute-start.49 = (bf16[1,128,1024]{2,1,0:T(8,128)(2,1)}, bf16[1,128,1024]{2,1,0:T(8,128)(2,1)}, u32[]{:S(2)}, u32[]{:S(2)}) collective-permute-start(bf16[1,128,1024]{2,1,0:T(8,128)(2,1)} %slice.390), channel_id=1, source_target_pairs={{0,8},{4,12},{8,0},{12,4},{16,24},{20,28},{24,16},{28,20},{1,9},{5... | collective-permute-start | bytes 786440 | tf_op jit(solution)/shard_map/ppermute | solution.py:1224
  784.9 42.0 %collective-permute-start.52 = (bf16[4,4,128,1024]{3,2,1,0:T(8,128)(2,1)}, bf16[4,4,128,1024]{3,2,1,0:T(8,128)(2,1)}, u32[]{:S(2)}, u32[]{:S(2)}) collective-permute-start(bf16[4,4,128,1024]{3,2,1,0:T(8,128)(2,1)} %get-tuple-element.413), channel_id=1, source_target_pairs={{0,4},{4,0},{8,12},{12,8},{16,20},{20,16},{24,28},{28,24},{1,5},{5... | collective-permute-start | bytes 12582920 | tf_op jit(solution)/shard_map/ppermute | solution.py:1224
  843.3 95.1 %reduce-scatter.11.cloned.1.call-start = ((), (), s32[]{:S(2)}) async-start(), calls=%async_computation.11 | async-start | bytes 1474560 | tf_op jit(solution)/shard_map/reduce_scatter | solution.py:1312
  (114 other events, 1507.6 us)
Sparse Core Ops, SparseCore 0:
  56.3 29.1 all-gather.8
  87.8 27.5 all-gather.10
  117.5 27.4 all-gather.12
  168.0 44.6 all-gather.14
  622.6 46.3 reduce-scatter.4
  698.6 26.2 reduce-scatter.6
  843.4 42.9 reduce-scatter.8
  910.2 28.1 reduce-scatter.10

commit v8 on v7

--- a/solution.py
+++ b/solution.py
@@ -401,6 +401,9 @@
     return pl.BlockSpec(shape, lambda *ids: (0,) * len(shape), pipeline_mode=CONST)
 
 
+ANYWHERE = pl.BlockSpec(memory_space=pl.ANY)
+
+
 def chunk_rows(i, size):
     return pl.ds(pl.multiple_of(i * size, size), size)
 
@@ -712,8 +715,18 @@
     step = 640
 
     def kernel(x_ref, *refs):
-        parts, (mid_ref, m_ref, pre_ref, feed_ref, nx_ref, acc_ref) = refs[:5], refs[5:]
+        parts, refs = refs[:5], refs[5:]
+        mid_ref, m_ref, pre_ref, feed_ref, nx_ref, acc_ref, mid_late, sem = refs
         z = pl.program_id(0)
+        copy = pltpu.make_async_copy(mid_ref, mid_late, sem)
+
+        @pl.when(z == 0)
+        def _():
+            copy.start()
+
+        @pl.when(z == NZ - 1)
+        def _():
+            copy.wait()
 
         def work(up, down):
             def body(i, carry):
@@ -735,7 +748,7 @@
                     feed = acc_ref[sl, :] + part
                     feed_ref[sl, :] = feed.astype(BF16)
                     nx_ref[sl, :] = (
-                        mid_ref[sl, :] + m_ref[base + 5 : base + 6, :] * feed
+                        mid_late[sl, :] + m_ref[base + 5 : base + 6, :] * feed
                     ).astype(BF16)
 
                 return carry
@@ -748,14 +761,18 @@
         kernel,
         "ffn_fwd",
         (NZ,),
-        [full((rows, D))] + feed_specs(down_block) + [full((rows, D)), full((12, D))],
+        [full((rows, D))] + feed_specs(down_block) + [ANYWHERE, full((12, D))],
         [pl.BlockSpec((rows, D), lambda z: (0, z)), full((rows, D)), full((rows, D))],
         [
             jax.ShapeDtypeStruct((rows, 4 * D), BF16),
             jax.ShapeDtypeStruct((rows, D), BF16),
             jax.ShapeDtypeStruct((rows, D), BF16),
         ],
-        [pltpu.VMEM((rows, D), F32)],
+        [
+            pltpu.VMEM((rows, D), F32),
+            pltpu.VMEM((rows, D), F32),
+            pltpu.SemaphoreType.DMA,
+        ],
         16 * rows * D * D,
         rows * D * 20 + 16 * D * D,
     )(shifted, *weights, middle, mods)
@@ -767,11 +784,14 @@
 
     def kernel(g_ref, p_ref, x_ref, *refs):
         parts, refs = refs[:5], refs[5:]
-        m_ref, keep_ref, send_ref, gs_ref, gf_ref, act_ref, gp_ref = refs
+        m_ref, keep_ref, send_ref, gs_ref, gf_ref, act_ref, gp_ref, x_late, sem = refs
         z = pl.program_id(0)
+        copy = pltpu.make_async_copy(x_ref, x_late, sem)
 
         @pl.when(z == 0)
         def _():
+            copy.start()
+
             def body(i, carry):
                 sl = chunk_rows(i, step)
                 gf_ref[sl, :] = (
@@ -797,10 +817,15 @@
             lax.fori_loop(0, rows // step, body, 0)
 
         feed_by_offset(z, work, *parts)
+
+        @pl.when(z == 0)
+        def _():
+            copy.wait()
+
         for j, out_ref in enumerate((keep_ref, send_ref)):
             cols = slice(j * 512, (j + 1) * 512)
             gd = dot_tn(act_ref[:, cols], gf_ref[...]).astype(BF16)
-            gu = dot_tn(gp_ref[:, cols], x_ref[...]).astype(BF16)
+            gu = dot_tn(gp_ref[:, cols], x_late[...]).astype(BF16)
             out_ref[:, 0, 0:128] = gu.reshape(4, 128, D)
             out_ref[:, 0, 128:256] = gd.reshape(4, 128, D)
 
@@ -813,13 +838,13 @@
         [
             full((rows, D)),
             pl.BlockSpec((rows, D), lambda z: (0, z)),
-            full((rows, D)),
+            ANYWHERE,
         ]
         + feed_specs(down_block)
         + [full((12, D))],
         [gspec, gspec, full((rows, D))],
         [gshape, gshape, jax.ShapeDtypeStruct((rows, D), F32)],
-        [pltpu.VMEM((rows, D), BF16)] * 3,
+        [pltpu.VMEM((rows, D), BF16)] * 4 + [pltpu.SemaphoreType.DMA],
         32 * rows * D * D,
         rows * D * 16 + 32 * D * D,
     )(grad, pre, shifted, *weights, mods)
@@ -838,12 +863,14 @@
 
     def kernel(
         g_ref, gs_ref, mid_ref, f_ref, b_ref, a_ref, l_ref, w_ref, v_ref, m_ref, gm_ref, ga_ref,
-        keep_ref, send_ref, s_ref, gb_ref,
+        keep_ref, send_ref, s_ref, gb_ref, a_late, sem,
     ):
         i = pl.program_id(0)
+        copy = pltpu.make_async_copy(a_ref, a_late, sem)
 
         @pl.when(i == 0)
         def _():
+            copy.start()
             s_ref[...] = jnp.zeros_like(s_ref)
 
         g = g_ref[...].astype(F32)
@@ -864,8 +891,9 @@
 
         @pl.when(i == steps - 1)
         def _():
+            copy.wait()
             for d in range(NZ):
-                gw = dot_tn(a_ref[:, d * 256 : (d + 1) * 256], gb_ref[...]).astype(BF16)
+                gw = dot_tn(a_late[:, d * 256 : (d + 1) * 256], gb_ref[...]).astype(BF16)
                 split_heads(gw, keep_ref, send_ref, d, 0)
 
     tile = pl.BlockSpec((step, D), lambda i: (i, 0))
@@ -874,7 +902,7 @@
         kernel,
         "out_bwd",
         (steps,),
-        [tile, tile, tile, tile, tile, full((rows, D))] + out_specs_of(3) + [full((12, D))],
+        [tile, tile, tile, tile, tile, ANYWHERE] + out_specs_of(3) + [full((12, D))],
         [tile, tile, full(gshape.shape), full(gshape.shape), full((8, D))],
         [
             jax.ShapeDtypeStruct((rows, D), F32),
@@ -883,7 +911,11 @@
             gshape,
             jax.ShapeDtypeStruct((8, D), F32),
         ],
-        [pltpu.VMEM((rows, D), BF16)],
+        [
+            pltpu.VMEM((rows, D), BF16),
+            pltpu.VMEM((rows, D), BF16),
+            pltpu.SemaphoreType.DMA,
+        ],
         4 * rows * D * D,
         rows * D * 24 + 4 * D * D,
     )(grad, grad_shifted, middle, feed, branch, attended, *weights, mods)
@@ -896,11 +928,17 @@
     cols = D // pieces
 
     def kernel(p_ref, l_ref, w_ref, v_ref, h_ref, gm_ref, m_ref, *refs):
-        gh_refs, (s_ref, acc_ref) = refs[:pieces], refs[pieces:]
+        gh_refs, (s_ref, acc_ref, h_late, gm_late, sems) = refs[:pieces], refs[pieces:]
+        copies = [
+            pltpu.make_async_copy(h_ref, h_late, sems.at[0]),
+            pltpu.make_async_copy(gm_ref, gm_late, sems.at[1]),
+        ]
         z = pl.program_id(0)
 
         @pl.when(z == 0)
         def _():
+            for copy in copies:
+                copy.start()
             acc_ref[...] = jnp.zeros_like(acc_ref)
             s_ref[...] = jnp.zeros_like(s_ref)
 
@@ -917,11 +955,14 @@
 
         @pl.when(z == NZ - 1)
         def _():
+            for copy in copies:
+                copy.wait()
+
             def tail(n, carry):
                 sl = chunk_rows(n, 256)
                 gn = acc_ref[sl, :]
-                hat, rstd = ln_stats(h_ref[sl, :].astype(F32))
-                gh = gm_ref[sl, :] + ln_back(gn, hat, rstd, m_ref[base + 1 : base + 2, :])
+                hat, rstd = ln_stats(h_late[sl, :].astype(F32))
+                gh = gm_late[sl, :] + ln_back(gn, hat, rstd, m_ref[base + 1 : base + 2, :])
                 for i, gh_ref in enumerate(gh_refs):
                     gh_ref[sl, :] = gh[:, i * cols : (i + 1) * cols].astype(out_dtype)
                 s_ref[0:1, :] += jnp.sum(gn, axis=0, keepdims=True)
@@ -936,11 +977,16 @@
         (NZ,),
         [pl.BlockSpec((rows, 768), lambda z: (0, z))]
         + piece_specs(128, 0, 96)
-        + [full((rows, D)), full((rows, D)), full((12, D))],
+        + [ANYWHERE, ANYWHERE, full((12, D))],
         [full((rows, cols))] * pieces + [full((8, D))],
         [jax.ShapeDtypeStruct((rows, cols), out_dtype)] * pieces
         + [jax.ShapeDtypeStruct((8, D), F32)],
-        [pltpu.VMEM((rows, D), F32)],
+        [
+            pltpu.VMEM((rows, D), F32),
+            pltpu.VMEM((rows, D), hidden.dtype),
+            pltpu.VMEM((rows, D), F32),
+            pltpu.SemaphoreType.DMA((2,)),
+        ],
         6 * rows * D * D,
         rows * D * 20 + 6 * D * D,
     )(grad_proj, *weights, hidden, grad_middle, mods)
@@ -1001,7 +1047,7 @@
         compiler_params=pltpu.CompilerParams(
             dimension_semantics=("arbitrary",), vmem_limit_bytes=VMEM_LIMIT
         ),
-        cost_estimate=pl.CostEstimate(flops=0, bytes_accessed=nbytes, transcendentals=0),
+        cost_estimate=pl.CostEstimate(flops=0, bytes_accessed=nbytes // 64, transcendentals=0),
     )
 
 
@@ -1473,8 +1519,17 @@
     )
     a0_got = swap(a0_send, CORE)
     half_f0 = sum_cross(total_f0, got_f0)
-    half_f0, g_base0, sides_f1, corner_f1 = sync(half_f0, g_base0, sides_f1, corner_f1)
+    early_rows = jnp.concatenate(
+        [
+            sums_o0[2:3], sums_o0[0:2], sums_o0[3:4],
+            sums_q1[0:2], sums_o1[2:3], sums_o1[0:2], sums_o1[3:4],
+        ],
+        axis=0,
+    )
+    half_f0, early_rows = sync(half_f0, early_rows)
     got_f0 = send_corner(half_f0)
+    early_got = partner(early_rows)
+    early_got, g_base0, sides_f1, corner_f1 = sync(early_got, g_base0, sides_f1, corner_f1)
     own_gf1 = joined(sides_f1, corner_f1).reshape(4, 256, D)
     g_feed = finish_feed(place, own_gf1, swap(own_gf1, CORE), 1, ())
     gt_s = jnp.einsum(
@@ -1500,19 +1555,13 @@
     half_a0, grad0, sums_q0 = sync(half_a0, grad0, sums_q0)
     got_a0 = send_corner(half_a0)
     corner_a1 = corner_stage(sides_a1)
-    mod_rows = jnp.concatenate(
-        [
-            sums_q0[0:2], sums_o0[2:3], sums_o0[0:2], sums_o0[3:4],
-            sums_q1[0:2], sums_o1[2:3], sums_o1[0:2], sums_o1[3:4],
-        ],
-        axis=0,
-    )
+    mod_rows = sums_q0[0:2]
     mod_got = partner(mod_rows)
     got_a0, corner_a1, mine_f0, mod_got, mod_rows = sync(
         got_a0, corner_a1, mine_f0, mod_got, mod_rows
     )
     z_a0 = sum_corner(half_a0, got_a0, z)
-    mod_sum = mod_rows + mod_got
+    mod_sum = jnp.concatenate([mod_rows + mod_got, early_rows + early_got], axis=0)
     z_a0, mine_f0, mod_sum = sync(z_a0, mine_f0, mod_sum)
     mine_a0 = sum_line(z_a0)
     own_gf0 = cross_stage(mine_f0)

time: 995 us -> 988 us (level)
  Pallas kernels: 521 us -> 510 us
  transfers between devices with their start and end apart: 85 -> 86, of which waited for: 26 -> 29; matrix products, arithmetic and copies ran while one was open for 17% -> 17% of each run, Pallas kernels for 51% -> 51%
where the time goes in v8:
time: 988 us; the launch traced here: 979 us
  Pallas kernels  510 us (52%)
  other arithmetic  129 us (13%)
  waiting for transfers between devices  117 us (12%)
  local copies, waits for them, and re-layouts  99.3 us (10%)
  starting transfers between devices  91.9 us (9%)
  between operations  16.7 us (2%)
  matrix products  15.2 us (2%)
    pallas_call x2, Pallas kernels, ffn_bwd(): call(kernel, 'ffn_bwd', (NZ,), [full((rows, D)), pl.BlockSpec((rows, D),...  121 us
    pallas_call x2, Pallas kernels, attn_bwd(): call(kernel, 'attn_bwd', (NZ,), [xspec, pl.BlockSpec((parts, count, size,...  75.6 us
    pallas_call x2, Pallas kernels, ffn_fwd(): call(kernel, 'ffn_fwd', (NZ,), [full((rows, D))] + feed_specs(down_block)...  67.6 us
    ppermute x61, waiting for transfers between devices, swap(): return lax.ppermute(values, 'clip', [(i, i ^ bit) for i in range(8)])  65.7 us
    convert_element_type x13, other arithmetic, add(): return (first.astype(F32) + second.astype(F32)).astype(BF16)  53.5 us
    ppermute x61, starting transfers between devices, swap(): return lax.ppermute(values, 'clip', [(i, i ^ bit) for i in range(8)])  52.5 us
    pallas_call x2, Pallas kernels, attn_fwd(): call(kernel, 'attn_fwd', (NZ,), [pl.BlockSpec((parts, count, size, 768),...  43.4 us
    pallas_call x2, Pallas kernels, qkv_back(): call(kernel, 'qkv_back', (NZ,), [pl.BlockSpec((rows, 768), lambda z: (0,...  37 us
  transfers between devices with their start and end apart: 86, of which 29 were waited for; matrix products, arithmetic and copies ran while one was open for 17% of the time, Pallas kernels for 51%

profile of v8, /device:TPU:0, one launch (start us, length us, event | category | flops | bytes accessed | tf_op | source)
XLA Modules:
  0.0 978.8 jit_solution(9299410588163608246)
XLA Ops:
  71.9 10.8 %collective-permute-done.6 = bf16[3,128,1024]{2,1,0:T(8,128)(2,1)} collective-permute-done((bf16[3,128,1024]{2,1,0:T(8,128)(2,1)S(1)}, bf16[3,128,1024]{2,1,0:T(8,128)(2,1)}, u32[]{:S(2)}, u32[]{:S(2)}) %collective-permute-start.6) | collective-permute-done | bytes 786464 | tf_op jit(solution)/shard_map/ppermute | solution.py:1270
  96.1 16.0 %ln_qkv.2 = (bf16[1280,1024]{1,0:T(8,128)(2,1)}, bf16[1280,3072]{1,0:T(8,128)(2,1)}) custom-call(bf16[1280,1024]{1,0:T(8,128)(2,1)} %maximum_select_fusion.1.h_ref, f32[12,1024]{1,0:T(8,128)} %bitcast.314, bf16[2,4,128,1024]{3,2,1,0:T(8,128)(2,1)} %prep_attn.2.l_ref, bf16[4,3,128,1024]{3,2,1,0:T(8,128)(2,1)} %copy-done.2, ...), custom_call_target="tpu_custom_call" | custom-call | flops 2013265920 | bytes 5505024 | tf_op jit(solution)/shard_map/ln_qkv/pallas_call | solution.py:505
  123.7 20.5 %attn_fwd.2 = bf16[1,5,256,1024]{3,2,1,0:T(8,128)(2,1)} custom-call(bf16[1,5,256,3072]{3,2,1,0:T(8,128)(2,1)} %bitcast.334, f32[16,16,512]{2,1,0:T(8,128)} %pad.18.b_ref, s32[1]{0:T(128)} %copy.115.fc_ref), custom_call_target="tpu_custom_call" | custom-call | flops 1342177280 | bytes 2621440 | tf_op jit(solution)/shard_map/attn_fwd/pallas_call | solution.py:560
  152.3 9.3 out_proj.2
  171.4 34.2 %ffn_fwd.2 = (bf16[1280,4096]{1,0:T(8,128)(2,1)}, bf16[1280,1024]{1,0:T(8,128)(2,1)}, bf16[1280,1024]{1,0:T(8,128)(2,1)}) custom-call(bf16[1280,1024]{1,0:T(8,128)(2,1)} %get-tuple-element.289.x_ref, bf16[2,4,256,1024]{3,2,1,0:T(8,128)(2,1)} %prep_feed.2.refs_0_, bf16[4,3,128,1024]{3,2,1,0:T(8,128)(2,1)} %copy-done.6, ...), custom_call_target="tpu_custom_call" | custom-call | flops 5368709120 | bytes 10747904 | tf_op jit(solution)/shard_map/ffn_fwd/pallas_call | solution.py:760
  258.0 11.5 %collective-permute-done.25 = bf16[128,1024]{1,0:T(8,128)(2,1)} collective-permute-done((bf16[128,1024]{1,0:T(8,128)(2,1)}, bf16[128,1024]{1,0:T(8,128)(2,1)}, u32[]{:S(2)}, u32[]{:S(2)}) %collective-permute-start.25) | collective-permute-done | bytes 262176 | tf_op jit(solution)/shard_map/ppermute | solution.py:1187
  273.1 7.9 all-to-all-done
  281.0 15.8 %ln_qkv.3 = (bf16[1280,1024]{1,0:T(8,128)(2,1)}, bf16[1280,3072]{1,0:T(8,128)(2,1)}) custom-call(bf16[1280,1024]{1,0:T(8,128)(2,1)} %bitcast.40.h_ref, f32[12,1024]{1,0:T(8,128)} %bitcast.317, bf16[2,4,128,1024]{3,2,1,0:T(8,128)(2,1)} %prep_attn.3.l_ref, bf16[4,3,128,1024]{3,2,1,0:T(8,128)(2,1)} %copy-done.3, ...), custom_call_target="tpu_custom_call" | custom-call | flops 2013265920 | bytes 5505024 | tf_op jit(solution)/shard_map/ln_qkv/pallas_call | solution.py:505
  311.4 22.8 %attn_fwd.3 = bf16[5,4,64,1024]{3,2,1,0:T(8,128)(2,1)} custom-call(bf16[5,4,64,3072]{3,2,1,0:T(8,128)(2,1)} %bitcast.332, f32[16,64,640]{2,1,0:T(8,128)} %pad.19.b_ref, s32[1]{0:T(128)} %copy.115.fc_ref), custom_call_target="tpu_custom_call" | custom-call | flops 1677721600 | bytes 2621440 | tf_op jit(solution)/shard_map/attn_fwd/pallas_call | solution.py:560
  334.2 9.3 out_proj.3
  343.5 33.4 %ffn_fwd.3 = (bf16[1280,4096]{1,0:T(8,128)(2,1)}, bf16[1280,1024]{1,0:T(8,128)(2,1)}, bf16[1280,1024]{1,0:T(8,128)(2,1)}) custom-call(bf16[1280,1024]{1,0:T(8,128)(2,1)} %get-tuple-element.315.x_ref, bf16[2,4,256,1024]{3,2,1,0:T(8,128)(2,1)} %prep_feed.3.refs_0_, bf16[4,3,256,1024]{3,2,1,0:T(8,128)(2,1)} %pad_maximum_fusion.refs_1_.refs_3_, ...), custom_call_target="tpu_custom_call" | custom-call | flops 5368709120 | bytes 10747904 | tf_op jit(solution)/shard_map/ffn_fwd/pallas_call | solution.py:760
  386.4 60.4 %ffn_bwd.2 = (bf16[4,4,256,1024]{3,2,1,0:T(8,128)(2,1)}, bf16[4,4,256,1024]{3,2,1,0:T(8,128)(2,1)}, f32[1280,1024]{1,0:T(8,128)}) custom-call(bf16[1280,1024]{1,0:T(8,128)(2,1)} %get-tuple-element.607.g_ref, bf16[1280,4096]{1,0:T(8,128)(2,1)} %get-tuple-element.321.p_ref, bf16[1280,1024]{1,0:T(8,128)(2,1)} %get-tuple-element.315.x_ref, ...), custom_call_target="tpu_custom_call" | custom-call | flops 10737418240 | bytes 13631488 | tf_op jit(solution)/shard_map/ffn_bwd/pallas_call | solution.py:834
  446.9 18.5 %out_bwd.2 = (f32[1280,1024]{1,0:T(8,128)}, bf16[1280,1024]{1,0:T(8,128)(2,1)}, bf16[4,4,32,1024]{3,2,1,0:T(8,128)(2,1)}, bf16[4,4,32,1024]{3,2,1,0:T(8,128)(2,1)}, f32[8,1024]{1,0:T(8,128)}) custom-call(bf16[1280,1024]{1,0:T(8,128)(2,1)} %get-tuple-element.607.g_ref, f32[1280,1024]{1,0:T(8,128)} %get-tuple-element.326.gs_ref, ...), custom_call_target="tpu_custom_call" | custom-call | flops 1342177280 | bytes 8912896 | tf_op jit(solution)/shard_map/out_bwd/pallas_call | solution.py:901
  465.4 9.1 fusion.16
  480.0 42.7 %attn_bwd.2 = (bf16[5,4,64,3072]{3,2,1,0:T(8,128)(2,1)}, f32[16,64,640]{2,1,0:T(8,128)}) custom-call(bf16[5,4,64,3072]{3,2,1,0:T(8,128)(2,1)} %bitcast.333, bf16[5,4,64,1024]{3,2,1,0:T(8,128)(2,1)} %bitcast.392, f32[16,64,640]{2,1,0:T(8,128)} %pad.19.b_ref, s32[1]{0:T(128)} %copy.115.fc_ref), custom_call_target="tpu_custom_call" | custom-call | flops 4194304000 | bytes 5242880 | tf_op jit(solution)/shard_map/attn_bwd/pallas_call | solution.py:623
  533.6 17.9 %qkv_back.2 = (bf16[1280,1024]{1,0:T(8,128)(2,1)}, f32[8,1024]{1,0:T(8,128)}) custom-call(bf16[1280,3072]{1,0:T(8,128)(2,1)} %bitcast.296, bf16[2,4,128,1024]{3,2,1,0:T(8,128)(2,1)} %prep_attn.3.l_ref, bf16[4,3,128,1024]{3,2,1,0:T(8,128)(2,1)} %copy-done.3, bf16[4,3,128,1024]{3,2,1,0:T(8,128)(2,1)} %collective-permute-done.24.v_ref, ...), custom_call_target="tpu_custom_call" | custom-call | flops 2013265920 | bytes 8126464 | tf_op jit(solution)/shard_map/qkv_back/pallas_call | solution.py:974
  561.5 13.2 %qkv_grad.2 = (bf16[4,4,128,1024]{3,2,1,0:T(8,128)(2,1)}, bf16[1,4,128,1024]{3,2,1,0:T(8,128)(2,1)}, bf16[1,4,128,1024]{3,2,1,0:T(8,128)(2,1)}, bf16[1,4,128,102...) custom-call(bf16[1280,3072]{1,0:T(8,128)(2,1)} %bitcast.297, bf16[1280,1024]{1,0:T(8,128)(2,1)} %get-tuple-element.353.n_ref, ...), custom_call_target="tpu_custom_call" | custom-call | flops 2013265920 | bytes 4718592 | tf_op jit(solution)/shard_map/qkv_grad/pallas_call | solution.py:1021
  601.1 7.1 fusion.44
  608.2 11.0 %all-to-all-done.3 = bf16[4,320,1024]{2,1,0:T(8,128)(2,1)} async-done(((bf16[4,320,1024]{2,1,0:T(8,128)(2,1)}), bf16[4,320,1024]{2,1,0:T(8,128)(2,1)}, u32[]{:S(2)}, u32[]{:S(2)}) %all-to-all-start.3) | async-done | bytes 2621472 | tf_op jit(solution)/shard_map/all_to_all | solution.py:1232
  626.6 61.0 %ffn_bwd.3 = (bf16[4,4,256,1024]{3,2,1,0:T(8,128)(2,1)}, bf16[4,4,256,1024]{3,2,1,0:T(8,128)(2,1)}, f32[1280,1024]{1,0:T(8,128)}) custom-call(bf16[1280,1024]{1,0:T(8,128)(2,1)} %bitcast.306, bf16[1280,4096]{1,0:T(8,128)(2,1)} %get-tuple-element.368.p_ref, bf16[1280,1024]{1,0:T(8,128)(2,1)} %get-tuple-element.289.x_ref, ...), custom_call_target="tpu_custom_call" | custom-call | flops 10737418240 | bytes 13631488 | tf_op jit(solution)/shard_map/ffn_bwd/pallas_call | solution.py:834
  694.4 18.1 %out_bwd.3 = (f32[1280,1024]{1,0:T(8,128)}, bf16[1280,1024]{1,0:T(8,128)(2,1)}, bf16[4,4,32,1024]{3,2,1,0:T(8,128)(2,1)}, bf16[4,4,32,1024]{3,2,1,0:T(8,128)(2,1)}, f32[8,1024]{1,0:T(8,128)}) custom-call(bf16[1280,1024]{1,0:T(8,128)(2,1)} %bitcast.307, f32[1280,1024]{1,0:T(8,128)} %get-tuple-element.377.gs_ref, ...), custom_call_target="tpu_custom_call" | custom-call | flops 1342177280 | bytes 8912896 | tf_op jit(solution)/shard_map/out_bwd/pallas_call | solution.py:901
  712.5 9.0 fusion.20
  732.4 32.9 %attn_bwd.3 = (bf16[1,5,256,3072]{3,2,1,0:T(8,128)(2,1)}, f32[16,16,512]{2,1,0:T(8,128)}) custom-call(bf16[1,5,256,3072]{3,2,1,0:T(8,128)(2,1)} %bitcast.335, bf16[1,5,256,1024]{3,2,1,0:T(8,128)(2,1)} %bitcast.391, f32[16,16,512]{2,1,0:T(8,128)} %pad.18.b_ref, s32[1]{0:T(128)} %copy.115.fc_ref), custom_call_target="tpu_custom_call" | custom-call | flops 3355443200 | bytes 5242880 | tf_op jit(solution)/shard_map/attn_bwd/pallas_call | solution.py:623
  765.3 13.1 %qkv_grad.3 = (bf16[4,4,128,1024]{3,2,1,0:T(8,128)(2,1)}, bf16[4,4,128,1024]{3,2,1,0:T(8,128)(2,1)}) custom-call(bf16[1280,3072]{1,0:T(8,128)(2,1)} %bitcast.294, bf16[1280,1024]{1,0:T(8,128)(2,1)} %get-tuple-element.388.n_ref, bf16[4,4,32,1024]{3,2,1,0:T(8,128)(2,1)} %get-tuple-element.389.ok_ref, bf16[4,4,32,1024]{3,2,1,0:T(8,128)(2,1)} %get-tuple-element.390.os_ref), custom_call_target="tpu_custom_call" | custom-call | flops 2013265920 | bytes 4718592 | tf_op jit(solution)/shard_map/qkv_grad/pallas_call | solution.py:1021
  808.3 9.0 finish_feed.2
  843.8 19.1 %qkv_back.3 = (f32[1280,1024]{1,0:T(8,128)}, f32[8,1024]{1,0:T(8,128)}) custom-call(bf16[1280,3072]{1,0:T(8,128)(2,1)} %bitcast.295, bf16[2,4,128,1024]{3,2,1,0:T(8,128)(2,1)} %prep_attn.2.l_ref, bf16[4,3,128,1024]{3,2,1,0:T(8,128)(2,1)} %copy-done.2, bf16[4,3,128,1024]{3,2,1,0:T(8,128)(2,1)} %collective-permute-done.10.v_ref, ...), custom_call_target="tpu_custom_call" | custom-call | flops 2013265920 | bytes 8126464 | tf_op jit(solution)/shard_map/qkv_back/pallas_call | solution.py:974
  862.9 10.8 %collective-permute-done.57 = bf16[1,128,1024]{2,1,0:T(8,128)(2,1)S(1)} collective-permute-done((bf16[1,128,1024]{2,1,0:T(8,128)(2,1)S(1)}, bf16[1,128,1024]{2,1,0:T(8,128)(2,1)S(1)}, u32[]{:S(2)}, u32[]{:S(2)}) %collective-permute-start.57) | collective-permute-done | bytes 262176 | tf_op jit(solution)/shard_map/ppermute | solution.py:1270
  887.0 7.4 collective-permute-done.61
  914.0 7.2 collective-permute-done.64
  921.2 8.2 collective-permute-done.65
  937.8 9.0 finish_feed.3
  962.1 9.4 finish_attn.1
  (470 shorter events, 376.4 us)
Async XLA Ops:
  7.2 78.3 %all-gather.9.cloned.1.call-start = ((), (), s32[]{:S(2)}) async-start(), calls=%async_computation.12 | async-start | bytes 1310720 | tf_op jit(solution)/shard_map/all_gather | solution.py:1406
  56.2 59.2 %all-gather.11.cloned.1.call-start = ((), (), s32[]{:S(2)}) async-start(), calls=%async_computation.13 | async-start | bytes 1310720 | tf_op jit(solution)/shard_map/all_gather | solution.py:1407
  87.7 57.3 %all-gather.13.cloned.1.call-start = ((), (), s32[]{:S(2)}) async-start(), calls=%async_computation.14 | async-start | bytes 1310720 | tf_op jit(solution)/shard_map/all_gather | solution.py:1424
  95.2 117.5 %all-gather.15.cloned.1.call-start = ((), (), s32[]{:S(2)}) async-start(), calls=%async_computation.15 | async-start | bytes 2621440 | tf_op jit(solution)/shard_map/all_gather | solution.py:1435
  167.9 44.8 %collective-permute-start.21 = (bf16[3,128,1024]{2,1,0:T(8,128)(2,1)}, bf16[3,128,1024]{2,1,0:T(8,128)(2,1)}, u32[]{:S(2)}, u32[]{:S(2)}) collective-permute-start(bf16[3,128,1024]{2,1,0:T(8,128)(2,1)} %pad_maximum_fusion.23), channel_id=1, source_target_pairs={{0,8},{4,12},{8,0},{12,4},{16,24},{20,28},{24,16},{28,20},{1,9},{5... | collective-permute-start | bytes 2359304 | tf_op jit(solution)/shard_map/ppermute | solution.py:1270
  169.0 43.7 %collective-permute-start.22 = (bf16[3,128,1024]{2,1,0:T(8,128)(2,1)}, bf16[3,128,1024]{2,1,0:T(8,128)(2,1)}, u32[]{:S(2)}, u32[]{:S(2)}) collective-permute-start(bf16[3,128,1024]{2,1,0:T(8,128)(2,1)} %pad_maximum_fusion.23), channel_id=1, source_target_pairs={{0,16},{4,20},{8,24},{12,28},{16,0},{20,4},{24,8},{28,12},{1,17},{... | collective-permute-start | bytes 2359304 | tf_op jit(solution)/shard_map/ppermute | solution.py:1270
  169.8 42.9 %collective-permute-start.23 = (bf16[3,128,1024]{2,1,0:T(8,128)(2,1)}, bf16[3,128,1024]{2,1,0:T(8,128)(2,1)}, u32[]{:S(2)}, u32[]{:S(2)}) collective-permute-start(bf16[3,128,1024]{2,1,0:T(8,128)(2,1)} %pad_maximum_fusion.23), channel_id=1, source_target_pairs={{0,24},{4,28},{8,16},{12,20},{16,8},{20,12},{24,0},{28,4},{1,25},{... | collective-permute-start | bytes 2359304 | tf_op jit(solution)/shard_map/ppermute | solution.py:1270
  216.2 64.8 %all-to-all-start = ((bf16[4,320,1024]{2,1,0:T(8,128)(2,1)}), bf16[4,320,1024]{2,1,0:T(8,128)(2,1)}, u32[]{:S(2)}, u32[]{:S(2)}) async-start(bf16[4,320,1024]{2,1,0:T(8,128)(2,1)} %bitcast.39), calls=%async_computation | async-start | bytes 5242880 | tf_op jit(solution)/shard_map/all_to_all | solution.py:1232
  223.5 49.6 %collective-permute-start.24 = (bf16[4,3,128,1024]{3,2,1,0:T(8,128)(2,1)S(1)}, bf16[4,3,128,1024]{3,2,1,0:T(8,128)(2,1)}, u32[]{:S(2)}, u32[]{:S(2)}) collective-permute-start(bf16[4,3,128,1024]{3,2,1,0:T(8,128)(2,1)S(1)} %pad_maximum_fusion.4.w_ref), channel_id=1, source_target_pairs={{0,4},{4,0},{8,12},{12,8},{16,20},{20,16},{24,28},{28,24},{1,5},{5... | collective-permute-start | bytes 9437192 | tf_op jit(solution)/shard_map/ppermute | solution.py:1270
  225.7 71.2 %collective-permute-start.26 = (bf16[3,256,1024]{2,1,0:T(8,128)(2,1)}, bf16[3,256,1024]{2,1,0:T(8,128)(2,1)}, u32[]{:S(2)}, u32[]{:S(2)}) collective-permute-start(bf16[3,256,1024]{2,1,0:T(8,128)(2,1)} %pad_maximum_fusion.11), channel_id=1, source_target_pairs={{0,8},{4,12},{8,0},{12,4},{16,24},{20,28},{24,16},{28,20},{1,9},{5... | collective-permute-start | bytes 4718600 | tf_op jit(solution)/shard_map/ppermute | solution.py:1270
  227.2 70.7 %collective-permute-start.27 = (bf16[3,256,1024]{2,1,0:T(8,128)(2,1)}, bf16[3,256,1024]{2,1,0:T(8,128)(2,1)}, u32[]{:S(2)}, u32[]{:S(2)}) collective-permute-start(bf16[3,256,1024]{2,1,0:T(8,128)(2,1)} %pad_maximum_fusion.11), channel_id=1, source_target_pairs={{0,16},{4,20},{8,24},{12,28},{16,0},{20,4},{24,8},{28,12},{1,17},{... | collective-permute-start | bytes 4718600 | tf_op jit(solution)/shard_map/ppermute | solution.py:1270
  228.6 69.2 %collective-permute-start.28 = (bf16[3,256,1024]{2,1,0:T(8,128)(2,1)}, bf16[3,256,1024]{2,1,0:T(8,128)(2,1)}, u32[]{:S(2)}, u32[]{:S(2)}) collective-permute-start(bf16[3,256,1024]{2,1,0:T(8,128)(2,1)} %pad_maximum_fusion.11), channel_id=1, source_target_pairs={{0,24},{4,28},{8,16},{12,20},{16,8},{20,12},{24,0},{28,4},{1,25},{... | collective-permute-start | bytes 4718600 | tf_op jit(solution)/shard_map/ppermute | solution.py:1270
  231.0 38.5 %collective-permute-start.25 = (bf16[128,1024]{1,0:T(8,128)(2,1)}, bf16[128,1024]{1,0:T(8,128)(2,1)}, u32[]{:S(2)}, u32[]{:S(2)}) collective-permute-start(bf16[128,1024]{1,0:T(8,128)(2,1)} %bitcast.55), channel_id=1, source_target_pairs={{0,1},{1,0},{2,3},{3,2},{4,5},{5,4},{6,7},{7,6},{8,9},{9,8},{10,11... | collective-permute-start | bytes 786440 | tf_op jit(solution)/shard_map/ppermute | solution.py:1187
  304.6 38.9 %collective-permute-start.29 = (bf16[4,3,256,1024]{3,2,1,0:T(8,128)(2,1)}, bf16[4,3,256,1024]{3,2,1,0:T(8,128)(2,1)}, u32[]{:S(2)}, u32[]{:S(2)}) collective-permute-start(bf16[4,3,256,1024]{3,2,1,0:T(8,128)(2,1)} %pad_maximum_fusion.refs_1_.refs_3_), channel_id=1, source_target_pairs={{0,4},{4,0},{8,12},{12,8},{16,20},{20,16},{24,28},{28,24},{1,5},{5... | collective-permute-start | bytes 18874376 | tf_op jit(solution)/shard_map/ppermute | solution.py:1270
  306.4 70.5 %all-to-all-start.1 = ((bf16[4,320,1024]{2,1,0:T(8,128)(2,1)}), bf16[4,320,1024]{2,1,0:T(8,128)(2,1)S(1)}, u32[]{:S(2)}, u32[]{:S(2)}) async-start(bf16[4,320,1024]{2,1,0:T(8,128)(2,1)} %bitcast.64), calls=%async_computation.1 | async-start | bytes 5242880 | tf_op jit(solution)/shard_map/all_to_all | solution.py:1232
  381.1 65.8 %all-to-all-start.2 = ((bf16[4,320,1024]{2,1,0:T(8,128)(2,1)}), bf16[4,320,1024]{2,1,0:T(8,128)(2,1)S(1)}, u32[]{:S(2)}, u32[]{:S(2)}) async-start(bf16[4,320,1024]{2,1,0:T(8,128)(2,1)} %bitcast.313), calls=%async_computation.2 | async-start | bytes 5242880 | tf_op jit(solution)/shard_map/all_to_all | solution.py:1232
  476.4 48.0 %collective-permute-start.32 = (bf16[2,4,128,1024]{3,2,1,0:T(8,128)(2,1)}, bf16[2,4,128,1024]{3,2,1,0:T(8,128)(2,1)}, u32[]{:S(2)}, u32[]{:S(2)}) collective-permute-start(bf16[2,4,128,1024]{3,2,1,0:T(8,128)(2,1)} %pad_maximum_fusion.7), channel_id=1, source_target_pairs={{0,16},{4,20},{8,24},{12,28},{16,0},{20,4},{24,8},{28,12},{1,17},{... | collective-permute-start | bytes 6291464 | tf_op jit(solution)/shard_map/ppermute | solution.py:1270
  479.4 47.7 %collective-permute-start.31 = (bf16[2,4,128,1024]{3,2,1,0:T(8,128)(2,1)}, bf16[2,4,128,1024]{3,2,1,0:T(8,128)(2,1)}, u32[]{:S(2)}, u32[]{:S(2)}) collective-permute-start(bf16[2,4,128,1024]{3,2,1,0:T(8,128)(2,1)} %pad_maximum_fusion.6), channel_id=1, source_target_pairs={{0,8},{4,12},{8,0},{12,4},{16,24},{20,28},{24,16},{28,20},{1,9},{5... | collective-permute-start | bytes 6291464 | tf_op jit(solution)/shard_map/ppermute | solution.py:1270
  556.4 62.8 %all-to-all-start.3 = ((bf16[4,320,1024]{2,1,0:T(8,128)(2,1)}), bf16[4,320,1024]{2,1,0:T(8,128)(2,1)}, u32[]{:S(2)}, u32[]{:S(2)}) async-start(bf16[4,320,1024]{2,1,0:T(8,128)(2,1)} %bitcast.355), calls=%async_computation.3 | async-start | bytes 5242880 | tf_op jit(solution)/shard_map/all_to_all | solution.py:1232
  561.5 126.2 %reduce-scatter.5.cloned.1.call-start = ((), (), s32[]{:S(2)}) async-start(), calls=%async_computation.8 | async-start | bytes 2621440 | tf_op jit(solution)/shard_map/reduce_scatter | solution.py:1358
  619.2 159.2 %reduce-scatter.7.cloned.1.call-start = ((), (), s32[]{:S(2)}) async-start(), calls=%async_computation.9 | async-start | bytes 1310720 | tf_op jit(solution)/shard_map/reduce_scatter | solution.py:1358
  619.2 68.4 %collective-permute-start.39 = (bf16[4,128,1024]{2,1,0:T(8,128)(2,1)}, bf16[4,128,1024]{2,1,0:T(8,128)(2,1)}, u32[]{:S(2)}, u32[]{:S(2)}) collective-permute-start(bf16[4,128,1024]{2,1,0:T(8,128)(2,1)} %get-tuple-element.373), channel_id=1, source_target_pairs={{0,8},{4,12},{8,0},{12,4},{16,24},{20,28},{24,16},{28,20},{1,9},{5... | collective-permute-start | bytes 3145736 | tf_op jit(solution)/shard_map/ppermute | solution.py:1270
  620.3 67.3 %collective-permute-start.40 = (bf16[4,128,1024]{2,1,0:T(8,128)(2,1)}, bf16[4,128,1024]{2,1,0:T(8,128)(2,1)}, u32[]{:S(2)}, u32[]{:S(2)}) collective-permute-start(bf16[4,128,1024]{2,1,0:T(8,128)(2,1)} %get-tuple-element.374), channel_id=1, source_target_pairs={{0,16},{4,20},{8,24},{12,28},{16,0},{20,4},{24,8},{28,12},{1,17},{... | collective-permute-start | bytes 3145736 | tf_op jit(solution)/shard_map/ppermute | solution.py:1270
  621.1 66.5 %collective-permute-start.41 = (bf16[4,128,1024]{2,1,0:T(8,128)(2,1)}, bf16[4,128,1024]{2,1,0:T(8,128)(2,1)}, u32[]{:S(2)}, u32[]{:S(2)}) collective-permute-start(bf16[4,128,1024]{2,1,0:T(8,128)(2,1)} %get-tuple-element.375), channel_id=1, source_target_pairs={{0,24},{4,28},{8,16},{12,20},{16,8},{20,12},{24,0},{28,4},{1,25},{... | collective-permute-start | bytes 3145736 | tf_op jit(solution)/shard_map/ppermute | solution.py:1270
  626.6 61.0 %collective-permute-start.42 = (bf16[128,1024]{1,0:T(8,128)(2,1)S(1)}, bf16[128,1024]{1,0:T(8,128)(2,1)S(1)}, u32[]{:S(2)}, u32[]{:S(2)}) collective-permute-start(bf16[128,1024]{1,0:T(8,128)(2,1)S(1)} %get-tuple-element.376), channel_id=1, source_target_pairs={{0,1},{1,0},{2,3},{3,2},{4,5},{5,4},{6,7},{7,6},{8,9},{9,8},{10,11... | collective-permute-start | bytes 786440 | tf_op jit(solution)/shard_map/ppermute | solution.py:1187
  694.4 202.0 %reduce-scatter.9.cloned.1.call-start = ((), (), s32[]{:S(2)}) async-start(), calls=%async_computation.10 | async-start | bytes 2621440 | tf_op jit(solution)/shard_map/reduce_scatter | solution.py:1358
  724.4 56.1 %collective-permute-start.47 = (bf16[2,4,128,1024]{3,2,1,0:T(8,128)(2,1)}, bf16[2,4,128,1024]{3,2,1,0:T(8,128)(2,1)}, u32[]{:S(2)}, u32[]{:S(2)}) collective-permute-start(bf16[2,4,128,1024]{3,2,1,0:T(8,128)(2,1)} %pad_maximum_fusion.9), channel_id=1, source_target_pairs={{0,16},{4,20},{8,24},{12,28},{16,0},{20,4},{24,8},{28,12},{1,17},{... | collective-permute-start | bytes 6291464 | tf_op jit(solution)/shard_map/ppermute | solution.py:1270
  727.5 52.9 %collective-permute-start.46 = (bf16[2,4,128,1024]{3,2,1,0:T(8,128)(2,1)}, bf16[2,4,128,1024]{3,2,1,0:T(8,128)(2,1)}, u32[]{:S(2)}, u32[]{:S(2)}) collective-permute-start(bf16[2,4,128,1024]{3,2,1,0:T(8,128)(2,1)} %pad_maximum_fusion.8), channel_id=1, source_target_pairs={{0,8},{4,12},{8,0},{12,4},{16,24},{20,28},{24,16},{28,20},{1,9},{5... | collective-permute-start | bytes 6291464 | tf_op jit(solution)/shard_map/ppermute | solution.py:1270
  729.4 49.0 %collective-permute-start.48 = (bf16[1,128,1024]{2,1,0:T(8,128)(2,1)}, bf16[1,128,1024]{2,1,0:T(8,128)(2,1)}, u32[]{:S(2)}, u32[]{:S(2)}) collective-permute-start(bf16[1,128,1024]{2,1,0:T(8,128)(2,1)} %slice.389), channel_id=1, source_target_pairs={{0,16},{4,20},{8,24},{12,28},{16,0},{20,4},{24,8},{28,12},{1,17},{... | collective-permute-start | bytes 786440 | tf_op jit(solution)/shard_map/ppermute | solution.py:1270
  732.3 48.2 %collective-permute-start.49 = (bf16[1,128,1024]{2,1,0:T(8,128)(2,1)}, bf16[1,128,1024]{2,1,0:T(8,128)(2,1)}, u32[]{:S(2)}, u32[]{:S(2)}) collective-permute-start(bf16[1,128,1024]{2,1,0:T(8,128)(2,1)} %slice.390), channel_id=1, source_target_pairs={{0,8},{4,12},{8,0},{12,4},{16,24},{20,28},{24,16},{28,20},{1,9},{5... | collective-permute-start | bytes 786440 | tf_op jit(solution)/shard_map/ppermute | solution.py:1270
  780.5 38.0 %collective-permute-start.52 = (bf16[4,4,128,1024]{3,2,1,0:T(8,128)(2,1)}, bf16[4,4,128,1024]{3,2,1,0:T(8,128)(2,1)}, u32[]{:S(2)}, u32[]{:S(2)}) collective-permute-start(bf16[4,4,128,1024]{3,2,1,0:T(8,128)(2,1)} %get-tuple-element.414), channel_id=1, source_target_pairs={{0,4},{4,0},{8,12},{12,8},{16,20},{20,16},{24,28},{28,24},{1,5},{5... | collective-permute-start | bytes 12582920 | tf_op jit(solution)/shard_map/ppermute | solution.py:1270
  834.8 96.0 %reduce-scatter.11.cloned.1.call-start = ((), (), s32[]{:S(2)}) async-start(), calls=%async_computation.11 | async-start | bytes 1474560 | tf_op jit(solution)/shard_map/reduce_scatter | solution.py:1358
  (123 other events, 1538.9 us)
Sparse Core Ops, SparseCore 0:
  56.3 29.1 all-gather.8
  87.8 27.5 all-gather.10
  117.6 27.4 all-gather.12
  168.0 44.6 all-gather.14
  619.3 46.3 reduce-scatter.4
  694.5 26.2 reduce-scatter.6
  834.9 41.6 reduce-scatter.8
  902.4 28.3 reduce-scatter.10

commit v9 on v8

--- a/solution.py
+++ b/solution.py
@@ -1232,11 +1232,13 @@
     return lax.all_to_all(values, "head", 0, 0, tiled=True)
 
 
+def to_quads(wins):
+    cols = wins.shape[1]
+    return wins.reshape(5, 2, 8, 2, 8, cols).transpose(1, 3, 0, 2, 4, 5).reshape(1280, cols)
+
+
 def spatial_to_tubes(wins):
-    cols = wins.shape[1]
-    return exchange(
-        wins.reshape(5, 2, 8, 2, 8, cols).transpose(1, 3, 0, 2, 4, 5).reshape(1280, cols)
-    )
+    return exchange(to_quads(wins))
 
 
 def from_quads(quads):
@@ -1437,8 +1439,10 @@
     own_a1 = cross_stage(own_a1)
     weights_f0 = (local_f0, own_u0, other_u0, own_d0, other_d0)
     pre0, feed0, hidden1 = ffn_fwd(shifted0, weights_f0, 0, middle0, mods, 0)
-    hidden1, z_f1, own_a1, tables, d_out = sync(hidden1, z_f1, own_a1, tables, d_out)
-    tubes1 = spatial_to_tubes(hidden1)
+    quads1 = to_quads(hidden1)
+    quads1, own_a1 = sync(quads1, own_a1)
+    tubes1 = exchange(quads1)
+    quads1, z_f1, tables, d_out = sync(quads1, z_f1, tables, d_out)
     own_a1 = jnp.stack(own_a1)
     other_a1 = swap(own_a1, CORE)
     own_f1 = cross_stage(jnp.stack(others(z_f1, z)))
@@ -1549,29 +1553,29 @@
     mine_f0 = sum_line(z_f0)
     got_a0 = send_cross(total_a0)
     grad0, sums_q0 = qkv_back(g_proj0, weights_a0, hidden0, g_mid0, mods, 0, F32, 1)
-    sides_a1 = sides_stage(mine_a1[None])
-    grad0, sums_q0, got_a0, sides_a1 = sync(grad0, sums_q0, got_a0, sides_a1)
+    grad0, sums_q0, got_a0 = sync(grad0, sums_q0, got_a0)
     half_a0 = sum_cross(total_a0, got_a0)
     half_a0, grad0, sums_q0 = sync(half_a0, grad0, sums_q0)
     got_a0 = send_corner(half_a0)
-    corner_a1 = corner_stage(sides_a1)
+    sides_a1 = sides_stage(mine_a1[None])
     mod_rows = sums_q0[0:2]
     mod_got = partner(mod_rows)
-    got_a0, corner_a1, mine_f0, mod_got, mod_rows = sync(
-        got_a0, corner_a1, mine_f0, mod_got, mod_rows
+    got_a0, sides_a1, mine_f0, mod_got, mod_rows = sync(
+        got_a0, sides_a1, mine_f0, mod_got, mod_rows
     )
     z_a0 = sum_corner(half_a0, got_a0, z)
     mod_sum = jnp.concatenate([mod_rows + mod_got, early_rows + early_got], axis=0)
     z_a0, mine_f0, mod_sum = sync(z_a0, mine_f0, mod_sum)
     mine_a0 = sum_line(z_a0)
     own_gf0 = cross_stage(mine_f0)
-    own_ga1 = joined(sides_a1, corner_a1).reshape(4, 128, D)
+    corner_a1 = corner_stage(sides_a1)
     rows_whole = whole_windows(grad0, odd)
     output = spatial_to_rows(whole_windows(out_wins, odd), out_keep, out_got, odd)
     rows_keep, rows_send = last_window(grad0, odd)
-    mine_a0, own_gf0, own_ga1, rows_keep, rows_send, rows_whole, output = sync(
-        mine_a0, own_gf0, own_ga1, rows_keep, rows_send, rows_whole, output
-    )
+    mine_a0, own_gf0, corner_a1, rows_keep, rows_send, rows_whole, output = sync(
+        mine_a0, own_gf0, corner_a1, rows_keep, rows_send, rows_whole, output
+    )
+    own_ga1 = joined(sides_a1, corner_a1).reshape(4, 128, D)
     own_ga0 = cross_stage(mine_a0)
     rows_got = partner(rows_send)
     own_gf0 = jnp.stack(own_gf0)

time: 988 us -> 979 us (level)
  waiting for transfers between devices: 117 us -> 103 us
  transfers between devices with their start and end apart: 86 -> 86, of which waited for: 29 -> 25; matrix products, arithmetic and copies ran while one was open for 17% -> 18% of each run, Pallas kernels for 51% -> 51%
where the time goes in v9:
time: 979 us; the launch traced here: 970 us
  Pallas kernels  510 us (52%)
  other arithmetic  131 us (13%)
  waiting for transfers between devices  103 us (11%)
  local copies, waits for them, and re-layouts  100 us (10%)
  starting transfers between devices  94.7 us (10%)
  between operations  16.7 us (2%)
  matrix products  15.2 us (2%)
    pallas_call x2, Pallas kernels, ffn_bwd(): call(kernel, 'ffn_bwd', (NZ,), [full((rows, D)), pl.BlockSpec((rows, D),...  121 us
    pallas_call x2, Pallas kernels, attn_bwd(): call(kernel, 'attn_bwd', (NZ,), [xspec, pl.BlockSpec((parts, count, size,...  75.7 us
    pallas_call x2, Pallas kernels, ffn_fwd(): call(kernel, 'ffn_fwd', (NZ,), [full((rows, D))] + feed_specs(down_block)...  67.6 us
    ppermute x61, waiting for transfers between devices, swap(): return lax.ppermute(values, 'clip', [(i, i ^ bit) for i in range(8)])  63.3 us
    convert_element_type x13, other arithmetic, add(): return (first.astype(F32) + second.astype(F32)).astype(BF16)  53.4 us
    ppermute x61, starting transfers between devices, swap(): return lax.ppermute(values, 'clip', [(i, i ^ bit) for i in range(8)])  53.1 us
    pallas_call x2, Pallas kernels, attn_fwd(): call(kernel, 'attn_fwd', (NZ,), [pl.BlockSpec((parts, count, size, 768),...  43.4 us
    pallas_call x2, Pallas kernels, qkv_back(): call(kernel, 'qkv_back', (NZ,), [pl.BlockSpec((rows, 768), lambda z: (0,...  36.9 us
  transfers between devices with their start and end apart: 86, of which 25 were waited for; matrix products, arithmetic and copies ran while one was open for 18% of the time, Pallas kernels for 51%

profile of v9, /device:TPU:0, one launch (start us, length us, event | category | flops | bytes accessed | tf_op | source)
XLA Modules:
  0.0 969.9 jit_solution(14225969571862724714)
XLA Ops:
  23.7 7.0 prep_feed.2.refs_0_
  30.6 6.9 prep_feed.3.refs_0_
  71.9 10.8 %collective-permute-done.6 = bf16[3,128,1024]{2,1,0:T(8,128)(2,1)} collective-permute-done((bf16[3,128,1024]{2,1,0:T(8,128)(2,1)S(1)}, bf16[3,128,1024]{2,1,0:T(8,128)(2,1)}, u32[]{:S(2)}, u32[]{:S(2)}) %collective-permute-start.6) | collective-permute-done | bytes 786464 | tf_op jit(solution)/shard_map/ppermute | solution.py:1272
  96.1 15.9 %ln_qkv.2 = (bf16[1280,1024]{1,0:T(8,128)(2,1)}, bf16[1280,3072]{1,0:T(8,128)(2,1)}) custom-call(bf16[1280,1024]{1,0:T(8,128)(2,1)} %maximum_select_fusion.1.h_ref, f32[12,1024]{1,0:T(8,128)} %bitcast.315, bf16[2,4,128,1024]{3,2,1,0:T(8,128)(2,1)} %prep_attn.2.l_ref, bf16[4,3,128,1024]{3,2,1,0:T(8,128)(2,1)} %copy-done.2, ...), custom_call_target="tpu_custom_call" | custom-call | flops 2013265920 | bytes 5505024 | tf_op jit(solution)/shard_map/ln_qkv/pallas_call | solution.py:505
  123.7 20.6 %attn_fwd.2 = bf16[1,5,256,1024]{3,2,1,0:T(8,128)(2,1)} custom-call(bf16[1,5,256,3072]{3,2,1,0:T(8,128)(2,1)} %bitcast.335, f32[16,16,512]{2,1,0:T(8,128)} %pad.18.b_ref, s32[1]{0:T(128)} %copy.114.fc_ref), custom_call_target="tpu_custom_call" | custom-call | flops 1342177280 | bytes 2621440 | tf_op jit(solution)/shard_map/attn_fwd/pallas_call | solution.py:560
  152.3 9.3 out_proj.2
  171.5 34.2 %ffn_fwd.2 = (bf16[1280,4096]{1,0:T(8,128)(2,1)}, bf16[1280,1024]{1,0:T(8,128)(2,1)}, bf16[1280,1024]{1,0:T(8,128)(2,1)}) custom-call(bf16[1280,1024]{1,0:T(8,128)(2,1)} %get-tuple-element.288.x_ref, bf16[2,4,256,1024]{3,2,1,0:T(8,128)(2,1)} %prep_feed.2.refs_0_, bf16[4,3,128,1024]{3,2,1,0:T(8,128)(2,1)} %copy-done.6, ...), custom_call_target="tpu_custom_call" | custom-call | flops 5368709120 | bytes 10747904 | tf_op jit(solution)/shard_map/ffn_fwd/pallas_call | solution.py:760
  252.6 10.2 %collective-permute-done.25 = bf16[128,1024]{1,0:T(8,128)(2,1)} collective-permute-done((bf16[128,1024]{1,0:T(8,128)(2,1)}, bf16[128,1024]{1,0:T(8,128)(2,1)}, u32[]{:S(2)}, u32[]{:S(2)}) %collective-permute-start.25) | collective-permute-done | bytes 262176 | tf_op jit(solution)/shard_map/ppermute | solution.py:1187
  266.3 7.9 all-to-all-done
  274.2 16.2 %ln_qkv.3 = (bf16[1280,1024]{1,0:T(8,128)(2,1)}, bf16[1280,3072]{1,0:T(8,128)(2,1)}) custom-call(bf16[1280,1024]{1,0:T(8,128)(2,1)} %bitcast.40.h_ref, f32[12,1024]{1,0:T(8,128)} %bitcast.318, bf16[2,4,128,1024]{3,2,1,0:T(8,128)(2,1)} %prep_attn.3.l_ref, bf16[4,3,128,1024]{3,2,1,0:T(8,128)(2,1)} %copy-done.3, ...), custom_call_target="tpu_custom_call" | custom-call | flops 2013265920 | bytes 5505024 | tf_op jit(solution)/shard_map/ln_qkv/pallas_call | solution.py:505
  305.2 22.8 %attn_fwd.3 = bf16[5,4,64,1024]{3,2,1,0:T(8,128)(2,1)} custom-call(bf16[5,4,64,3072]{3,2,1,0:T(8,128)(2,1)} %bitcast.333, f32[16,64,640]{2,1,0:T(8,128)} %pad.19.b_ref, s32[1]{0:T(128)} %copy.114.fc_ref), custom_call_target="tpu_custom_call" | custom-call | flops 1677721600 | bytes 2621440 | tf_op jit(solution)/shard_map/attn_fwd/pallas_call | solution.py:560
  328.0 9.3 out_proj.3
  337.3 33.4 %ffn_fwd.3 = (bf16[1280,4096]{1,0:T(8,128)(2,1)}, bf16[1280,1024]{1,0:T(8,128)(2,1)}, bf16[1280,1024]{1,0:T(8,128)(2,1)}) custom-call(bf16[1280,1024]{1,0:T(8,128)(2,1)} %get-tuple-element.314.x_ref, bf16[2,4,256,1024]{3,2,1,0:T(8,128)(2,1)} %prep_feed.3.refs_0_, bf16[4,3,256,1024]{3,2,1,0:T(8,128)(2,1)} %pad_maximum_fusion.refs_1_.refs_3_, ...), custom_call_target="tpu_custom_call" | custom-call | flops 5368709120 | bytes 10747904 | tf_op jit(solution)/shard_map/ffn_fwd/pallas_call | solution.py:760
  380.2 60.4 %ffn_bwd.2 = (bf16[4,4,256,1024]{3,2,1,0:T(8,128)(2,1)}, bf16[4,4,256,1024]{3,2,1,0:T(8,128)(2,1)}, f32[1280,1024]{1,0:T(8,128)}) custom-call(bf16[1280,1024]{1,0:T(8,128)(2,1)} %get-tuple-element.605.g_ref, bf16[1280,4096]{1,0:T(8,128)(2,1)} %get-tuple-element.320.p_ref, bf16[1280,1024]{1,0:T(8,128)(2,1)} %get-tuple-element.314.x_ref, ...), custom_call_target="tpu_custom_call" | custom-call | flops 10737418240 | bytes 13631488 | tf_op jit(solution)/shard_map/ffn_bwd/pallas_call | solution.py:834
  440.7 18.5 %out_bwd.2 = (f32[1280,1024]{1,0:T(8,128)}, bf16[1280,1024]{1,0:T(8,128)(2,1)}, bf16[4,4,32,1024]{3,2,1,0:T(8,128)(2,1)}, bf16[4,4,32,1024]{3,2,1,0:T(8,128)(2,1)}, f32[8,1024]{1,0:T(8,128)}) custom-call(bf16[1280,1024]{1,0:T(8,128)(2,1)} %get-tuple-element.605.g_ref, f32[1280,1024]{1,0:T(8,128)} %get-tuple-element.325.gs_ref, ...), custom_call_target="tpu_custom_call" | custom-call | flops 1342177280 | bytes 8912896 | tf_op jit(solution)/shard_map/out_bwd/pallas_call | solution.py:901
  459.3 9.1 fusion.16
  473.5 42.7 %attn_bwd.2 = (bf16[5,4,64,3072]{3,2,1,0:T(8,128)(2,1)}, f32[16,64,640]{2,1,0:T(8,128)}) custom-call(bf16[5,4,64,3072]{3,2,1,0:T(8,128)(2,1)} %bitcast.334, bf16[5,4,64,1024]{3,2,1,0:T(8,128)(2,1)} %bitcast.393, f32[16,64,640]{2,1,0:T(8,128)} %pad.19.b_ref, s32[1]{0:T(128)} %copy.114.fc_ref), custom_call_target="tpu_custom_call" | custom-call | flops 4194304000 | bytes 5242880 | tf_op jit(solution)/shard_map/attn_bwd/pallas_call | solution.py:623
  527.4 17.9 %qkv_back.2 = (bf16[1280,1024]{1,0:T(8,128)(2,1)}, f32[8,1024]{1,0:T(8,128)}) custom-call(bf16[1280,3072]{1,0:T(8,128)(2,1)} %bitcast.297, bf16[2,4,128,1024]{3,2,1,0:T(8,128)(2,1)} %prep_attn.3.l_ref, bf16[4,3,128,1024]{3,2,1,0:T(8,128)(2,1)} %copy-done.3, bf16[4,3,128,1024]{3,2,1,0:T(8,128)(2,1)} %collective-permute-done.24.v_ref, ...), custom_call_target="tpu_custom_call" | custom-call | flops 2013265920 | bytes 8126464 | tf_op jit(solution)/shard_map/qkv_back/pallas_call | solution.py:974
  555.3 13.2 %qkv_grad.2 = (bf16[4,4,128,1024]{3,2,1,0:T(8,128)(2,1)}, bf16[1,4,128,1024]{3,2,1,0:T(8,128)(2,1)}, bf16[1,4,128,1024]{3,2,1,0:T(8,128)(2,1)}, bf16[1,4,128,102...) custom-call(bf16[1280,3072]{1,0:T(8,128)(2,1)} %bitcast.298, bf16[1280,1024]{1,0:T(8,128)(2,1)} %get-tuple-element.352.n_ref, ...), custom_call_target="tpu_custom_call" | custom-call | flops 2013265920 | bytes 4718592 | tf_op jit(solution)/shard_map/qkv_grad/pallas_call | solution.py:1021
  594.9 7.1 fusion.44
  602.0 10.9 %all-to-all-done.3 = bf16[4,320,1024]{2,1,0:T(8,128)(2,1)} async-done(((bf16[4,320,1024]{2,1,0:T(8,128)(2,1)}), bf16[4,320,1024]{2,1,0:T(8,128)(2,1)}, u32[]{:S(2)}, u32[]{:S(2)}) %all-to-all-start.3) | async-done | bytes 2621472 | tf_op jit(solution)/shard_map/all_to_all | solution.py:1232
  620.3 60.9 %ffn_bwd.3 = (bf16[4,4,256,1024]{3,2,1,0:T(8,128)(2,1)}, bf16[4,4,256,1024]{3,2,1,0:T(8,128)(2,1)}, f32[1280,1024]{1,0:T(8,128)}) custom-call(bf16[1280,1024]{1,0:T(8,128)(2,1)} %bitcast.307, bf16[1280,4096]{1,0:T(8,128)(2,1)} %get-tuple-element.367.p_ref, bf16[1280,1024]{1,0:T(8,128)(2,1)} %get-tuple-element.288.x_ref, ...), custom_call_target="tpu_custom_call" | custom-call | flops 10737418240 | bytes 13631488 | tf_op jit(solution)/shard_map/ffn_bwd/pallas_call | solution.py:834
  688.2 18.1 %out_bwd.3 = (f32[1280,1024]{1,0:T(8,128)}, bf16[1280,1024]{1,0:T(8,128)(2,1)}, bf16[4,4,32,1024]{3,2,1,0:T(8,128)(2,1)}, bf16[4,4,32,1024]{3,2,1,0:T(8,128)(2,1)}, f32[8,1024]{1,0:T(8,128)}) custom-call(bf16[1280,1024]{1,0:T(8,128)(2,1)} %bitcast.308, f32[1280,1024]{1,0:T(8,128)} %get-tuple-element.376.gs_ref, ...), custom_call_target="tpu_custom_call" | custom-call | flops 1342177280 | bytes 8912896 | tf_op jit(solution)/shard_map/out_bwd/pallas_call | solution.py:901
  706.3 9.0 fusion.20
  726.1 32.9 %attn_bwd.3 = (bf16[1,5,256,3072]{3,2,1,0:T(8,128)(2,1)}, f32[16,16,512]{2,1,0:T(8,128)}) custom-call(bf16[1,5,256,3072]{3,2,1,0:T(8,128)(2,1)} %bitcast.336, bf16[1,5,256,1024]{3,2,1,0:T(8,128)(2,1)} %bitcast.392, f32[16,16,512]{2,1,0:T(8,128)} %pad.18.b_ref, s32[1]{0:T(128)} %copy.114.fc_ref), custom_call_target="tpu_custom_call" | custom-call | flops 3355443200 | bytes 5242880 | tf_op jit(solution)/shard_map/attn_bwd/pallas_call | solution.py:623
  759.1 13.1 %qkv_grad.3 = (bf16[4,4,128,1024]{3,2,1,0:T(8,128)(2,1)}, bf16[4,4,128,1024]{3,2,1,0:T(8,128)(2,1)}) custom-call(bf16[1280,3072]{1,0:T(8,128)(2,1)} %bitcast.295, bf16[1280,1024]{1,0:T(8,128)(2,1)} %get-tuple-element.387.n_ref, bf16[4,4,32,1024]{3,2,1,0:T(8,128)(2,1)} %get-tuple-element.388.ok_ref, bf16[4,4,32,1024]{3,2,1,0:T(8,128)(2,1)} %get-tuple-element.389.os_ref), custom_call_target="tpu_custom_call" | custom-call | flops 2013265920 | bytes 4718592 | tf_op jit(solution)/shard_map/qkv_grad/pallas_call | solution.py:1021
  802.0 9.0 finish_feed.2
  836.0 19.0 %qkv_back.3 = (f32[1280,1024]{1,0:T(8,128)}, f32[8,1024]{1,0:T(8,128)}) custom-call(bf16[1280,3072]{1,0:T(8,128)(2,1)} %bitcast.296, bf16[2,4,128,1024]{3,2,1,0:T(8,128)(2,1)} %prep_attn.2.l_ref, bf16[4,3,128,1024]{3,2,1,0:T(8,128)(2,1)} %copy-done.2, bf16[4,3,128,1024]{3,2,1,0:T(8,128)(2,1)} %collective-permute-done.10.v_ref, ...), custom_call_target="tpu_custom_call" | custom-call | flops 2013265920 | bytes 8126464 | tf_op jit(solution)/shard_map/qkv_back/pallas_call | solution.py:974
  872.0 13.0 %collective-permute-done.59 = bf16[1,128,1024]{2,1,0:T(8,128)(2,1)S(1)} collective-permute-done((bf16[1,128,1024]{2,1,0:T(8,128)(2,1)S(1)}, bf16[1,128,1024]{2,1,0:T(8,128)(2,1)S(1)}, u32[]{:S(2)}, u32[]{:S(2)}) %collective-permute-start.59) | collective-permute-done | bytes 262176 | tf_op jit(solution)/shard_map/ppermute | solution.py:1272
  907.4 13.1 %collective-permute-done.65 = bf16[1,64,1024]{2,1,0:T(8,128)(2,1)S(1)} collective-permute-done((bf16[1,64,1024]{2,1,0:T(8,128)(2,1)S(1)}, bf16[1,64,1024]{2,1,0:T(8,128)(2,1)S(1)}, u32[]{:S(2)}, u32[]{:S(2)}) %collective-permute-start.65) | collective-permute-done | bytes 131104 | tf_op jit(solution)/shard_map/ppermute | solution.py:1272
  930.1 9.0 finish_feed.3
  953.2 9.4 finish_attn.1
  (456 shorter events, 362.5 us)
Async XLA Ops:
  7.2 78.3 %all-gather.9.cloned.1.call-start = ((), (), s32[]{:S(2)}) async-start(), calls=%async_computation.12 | async-start | bytes 1310720 | tf_op jit(solution)/shard_map/all_gather | solution.py:1408
  56.2 59.2 %all-gather.11.cloned.1.call-start = ((), (), s32[]{:S(2)}) async-start(), calls=%async_computation.13 | async-start | bytes 1310720 | tf_op jit(solution)/shard_map/all_gather | solution.py:1409
  87.7 57.3 %all-gather.13.cloned.1.call-start = ((), (), s32[]{:S(2)}) async-start(), calls=%async_computation.14 | async-start | bytes 1310720 | tf_op jit(solution)/shard_map/all_gather | solution.py:1426
  95.2 122.0 %all-gather.15.cloned.1.call-start = ((), (), s32[]{:S(2)}) async-start(), calls=%async_computation.15 | async-start | bytes 2621440 | tf_op jit(solution)/shard_map/all_gather | solution.py:1437
  167.9 41.3 %collective-permute-start.21 = (bf16[3,128,1024]{2,1,0:T(8,128)(2,1)}, bf16[3,128,1024]{2,1,0:T(8,128)(2,1)}, u32[]{:S(2)}, u32[]{:S(2)}) collective-permute-start(bf16[3,128,1024]{2,1,0:T(8,128)(2,1)} %pad_maximum_fusion.23), channel_id=1, source_target_pairs={{0,8},{4,12},{8,0},{12,4},{16,24},{20,28},{24,16},{28,20},{1,9},{5... | collective-permute-start | bytes 2359304 | tf_op jit(solution)/shard_map/ppermute | solution.py:1272
  169.0 40.2 %collective-permute-start.22 = (bf16[3,128,1024]{2,1,0:T(8,128)(2,1)}, bf16[3,128,1024]{2,1,0:T(8,128)(2,1)}, u32[]{:S(2)}, u32[]{:S(2)}) collective-permute-start(bf16[3,128,1024]{2,1,0:T(8,128)(2,1)} %pad_maximum_fusion.23), channel_id=1, source_target_pairs={{0,16},{4,20},{8,24},{12,28},{16,0},{20,4},{24,8},{28,12},{1,17},{... | collective-permute-start | bytes 2359304 | tf_op jit(solution)/shard_map/ppermute | solution.py:1272
  169.8 39.4 %collective-permute-start.23 = (bf16[3,128,1024]{2,1,0:T(8,128)(2,1)}, bf16[3,128,1024]{2,1,0:T(8,128)(2,1)}, u32[]{:S(2)}, u32[]{:S(2)}) collective-permute-start(bf16[3,128,1024]{2,1,0:T(8,128)(2,1)} %pad_maximum_fusion.23), channel_id=1, source_target_pairs={{0,24},{4,28},{8,16},{12,20},{16,8},{20,12},{24,0},{28,4},{1,25},{... | collective-permute-start | bytes 2359304 | tf_op jit(solution)/shard_map/ppermute | solution.py:1272
  209.2 65.0 %all-to-all-start = ((bf16[4,320,1024]{2,1,0:T(8,128)(2,1)}), bf16[4,320,1024]{2,1,0:T(8,128)(2,1)}, u32[]{:S(2)}, u32[]{:S(2)}) async-start(bf16[4,320,1024]{2,1,0:T(8,128)(2,1)} %bitcast.39), calls=%async_computation | async-start | bytes 5242880 | tf_op jit(solution)/shard_map/all_to_all | solution.py:1232
  216.4 49.9 %collective-permute-start.24 = (bf16[4,3,128,1024]{3,2,1,0:T(8,128)(2,1)S(1)}, bf16[4,3,128,1024]{3,2,1,0:T(8,128)(2,1)}, u32[]{:S(2)}, u32[]{:S(2)}) collective-permute-start(bf16[4,3,128,1024]{3,2,1,0:T(8,128)(2,1)S(1)} %pad_maximum_fusion.4.w_ref), channel_id=1, source_target_pairs={{0,4},{4,0},{8,12},{12,8},{16,20},{20,16},{24,28},{28,24},{1,5},{5... | collective-permute-start | bytes 9437192 | tf_op jit(solution)/shard_map/ppermute | solution.py:1272
  220.3 70.2 %collective-permute-start.26 = (bf16[3,256,1024]{2,1,0:T(8,128)(2,1)}, bf16[3,256,1024]{2,1,0:T(8,128)(2,1)}, u32[]{:S(2)}, u32[]{:S(2)}) collective-permute-start(bf16[3,256,1024]{2,1,0:T(8,128)(2,1)} %pad_maximum_fusion.11), channel_id=1, source_target_pairs={{0,8},{4,12},{8,0},{12,4},{16,24},{20,28},{24,16},{28,20},{1,9},{5... | collective-permute-start | bytes 4718600 | tf_op jit(solution)/shard_map/ppermute | solution.py:1272
  221.1 70.5 %collective-permute-start.27 = (bf16[3,256,1024]{2,1,0:T(8,128)(2,1)}, bf16[3,256,1024]{2,1,0:T(8,128)(2,1)}, u32[]{:S(2)}, u32[]{:S(2)}) collective-permute-start(bf16[3,256,1024]{2,1,0:T(8,128)(2,1)} %pad_maximum_fusion.11), channel_id=1, source_target_pairs={{0,16},{4,20},{8,24},{12,28},{16,0},{20,4},{24,8},{28,12},{1,17},{... | collective-permute-start | bytes 4718600 | tf_op jit(solution)/shard_map/ppermute | solution.py:1272
  221.9 69.8 %collective-permute-start.28 = (bf16[3,256,1024]{2,1,0:T(8,128)(2,1)}, bf16[3,256,1024]{2,1,0:T(8,128)(2,1)}, u32[]{:S(2)}, u32[]{:S(2)}) collective-permute-start(bf16[3,256,1024]{2,1,0:T(8,128)(2,1)} %pad_maximum_fusion.11), channel_id=1, source_target_pairs={{0,24},{4,28},{8,16},{12,20},{16,8},{20,12},{24,0},{28,4},{1,25},{... | collective-permute-start | bytes 4718600 | tf_op jit(solution)/shard_map/ppermute | solution.py:1272
  225.6 37.2 %collective-permute-start.25 = (bf16[128,1024]{1,0:T(8,128)(2,1)}, bf16[128,1024]{1,0:T(8,128)(2,1)}, u32[]{:S(2)}, u32[]{:S(2)}) collective-permute-start(bf16[128,1024]{1,0:T(8,128)(2,1)} %bitcast.56), channel_id=1, source_target_pairs={{0,1},{1,0},{2,3},{3,2},{4,5},{5,4},{6,7},{7,6},{8,9},{9,8},{10,11... | collective-permute-start | bytes 786440 | tf_op jit(solution)/shard_map/ppermute | solution.py:1187
  298.4 39.0 %collective-permute-start.29 = (bf16[4,3,256,1024]{3,2,1,0:T(8,128)(2,1)}, bf16[4,3,256,1024]{3,2,1,0:T(8,128)(2,1)}, u32[]{:S(2)}, u32[]{:S(2)}) collective-permute-start(bf16[4,3,256,1024]{3,2,1,0:T(8,128)(2,1)} %pad_maximum_fusion.refs_1_.refs_3_), channel_id=1, source_target_pairs={{0,4},{4,0},{8,12},{12,8},{16,20},{20,16},{24,28},{28,24},{1,5},{5... | collective-permute-start | bytes 18874376 | tf_op jit(solution)/shard_map/ppermute | solution.py:1272
  300.1 70.6 %all-to-all-start.1 = ((bf16[4,320,1024]{2,1,0:T(8,128)(2,1)}), bf16[4,320,1024]{2,1,0:T(8,128)(2,1)S(1)}, u32[]{:S(2)}, u32[]{:S(2)}) async-start(bf16[4,320,1024]{2,1,0:T(8,128)(2,1)} %bitcast.65), calls=%async_computation.1 | async-start | bytes 5242880 | tf_op jit(solution)/shard_map/all_to_all | solution.py:1232
  374.9 65.7 %all-to-all-start.2 = ((bf16[4,320,1024]{2,1,0:T(8,128)(2,1)}), bf16[4,320,1024]{2,1,0:T(8,128)(2,1)S(1)}, u32[]{:S(2)}, u32[]{:S(2)}) async-start(bf16[4,320,1024]{2,1,0:T(8,128)(2,1)} %bitcast.314), calls=%async_computation.2 | async-start | bytes 5242880 | tf_op jit(solution)/shard_map/all_to_all | solution.py:1232
  470.2 48.0 %collective-permute-start.32 = (bf16[2,4,128,1024]{3,2,1,0:T(8,128)(2,1)}, bf16[2,4,128,1024]{3,2,1,0:T(8,128)(2,1)}, u32[]{:S(2)}, u32[]{:S(2)}) collective-permute-start(bf16[2,4,128,1024]{3,2,1,0:T(8,128)(2,1)} %pad_maximum_fusion.7), channel_id=1, source_target_pairs={{0,16},{4,20},{8,24},{12,28},{16,0},{20,4},{24,8},{28,12},{1,17},{... | collective-permute-start | bytes 6291464 | tf_op jit(solution)/shard_map/ppermute | solution.py:1272
  472.6 47.7 %collective-permute-start.31 = (bf16[2,4,128,1024]{3,2,1,0:T(8,128)(2,1)}, bf16[2,4,128,1024]{3,2,1,0:T(8,128)(2,1)}, u32[]{:S(2)}, u32[]{:S(2)}) collective-permute-start(bf16[2,4,128,1024]{3,2,1,0:T(8,128)(2,1)} %pad_maximum_fusion.6), channel_id=1, source_target_pairs={{0,8},{4,12},{8,0},{12,4},{16,24},{20,28},{24,16},{28,20},{1,9},{5... | collective-permute-start | bytes 6291464 | tf_op jit(solution)/shard_map/ppermute | solution.py:1272
  550.2 62.6 %all-to-all-start.3 = ((bf16[4,320,1024]{2,1,0:T(8,128)(2,1)}), bf16[4,320,1024]{2,1,0:T(8,128)(2,1)}, u32[]{:S(2)}, u32[]{:S(2)}) async-start(bf16[4,320,1024]{2,1,0:T(8,128)(2,1)} %bitcast.356), calls=%async_computation.3 | async-start | bytes 5242880 | tf_op jit(solution)/shard_map/all_to_all | solution.py:1232
  555.3 126.0 %reduce-scatter.5.cloned.1.call-start = ((), (), s32[]{:S(2)}) async-start(), calls=%async_computation.8 | async-start | bytes 2621440 | tf_op jit(solution)/shard_map/reduce_scatter | solution.py:1360
  612.9 159.3 %reduce-scatter.7.cloned.1.call-start = ((), (), s32[]{:S(2)}) async-start(), calls=%async_computation.9 | async-start | bytes 1310720 | tf_op jit(solution)/shard_map/reduce_scatter | solution.py:1360
  612.9 68.4 %collective-permute-start.39 = (bf16[4,128,1024]{2,1,0:T(8,128)(2,1)}, bf16[4,128,1024]{2,1,0:T(8,128)(2,1)}, u32[]{:S(2)}, u32[]{:S(2)}) collective-permute-start(bf16[4,128,1024]{2,1,0:T(8,128)(2,1)} %get-tuple-element.372), channel_id=1, source_target_pairs={{0,8},{4,12},{8,0},{12,4},{16,24},{20,28},{24,16},{28,20},{1,9},{5... | collective-permute-start | bytes 3145736 | tf_op jit(solution)/shard_map/ppermute | solution.py:1272
  614.1 67.2 %collective-permute-start.40 = (bf16[4,128,1024]{2,1,0:T(8,128)(2,1)}, bf16[4,128,1024]{2,1,0:T(8,128)(2,1)}, u32[]{:S(2)}, u32[]{:S(2)}) collective-permute-start(bf16[4,128,1024]{2,1,0:T(8,128)(2,1)} %get-tuple-element.373), channel_id=1, source_target_pairs={{0,16},{4,20},{8,24},{12,28},{16,0},{20,4},{24,8},{28,12},{1,17},{... | collective-permute-start | bytes 3145736 | tf_op jit(solution)/shard_map/ppermute | solution.py:1272
  614.9 66.4 %collective-permute-start.41 = (bf16[4,128,1024]{2,1,0:T(8,128)(2,1)}, bf16[4,128,1024]{2,1,0:T(8,128)(2,1)}, u32[]{:S(2)}, u32[]{:S(2)}) collective-permute-start(bf16[4,128,1024]{2,1,0:T(8,128)(2,1)} %get-tuple-element.374), channel_id=1, source_target_pairs={{0,24},{4,28},{8,16},{12,20},{16,8},{20,12},{24,0},{28,4},{1,25},{... | collective-permute-start | bytes 3145736 | tf_op jit(solution)/shard_map/ppermute | solution.py:1272
  620.3 61.0 %collective-permute-start.42 = (bf16[128,1024]{1,0:T(8,128)(2,1)S(1)}, bf16[128,1024]{1,0:T(8,128)(2,1)S(1)}, u32[]{:S(2)}, u32[]{:S(2)}) collective-permute-start(bf16[128,1024]{1,0:T(8,128)(2,1)S(1)} %get-tuple-element.375), channel_id=1, source_target_pairs={{0,1},{1,0},{2,3},{3,2},{4,5},{5,4},{6,7},{7,6},{8,9},{9,8},{10,11... | collective-permute-start | bytes 786440 | tf_op jit(solution)/shard_map/ppermute | solution.py:1187
  688.1 198.5 %reduce-scatter.9.cloned.1.call-start = ((), (), s32[]{:S(2)}) async-start(), calls=%async_computation.10 | async-start | bytes 2621440 | tf_op jit(solution)/shard_map/reduce_scatter | solution.py:1360
  718.1 56.2 %collective-permute-start.47 = (bf16[2,4,128,1024]{3,2,1,0:T(8,128)(2,1)}, bf16[2,4,128,1024]{3,2,1,0:T(8,128)(2,1)}, u32[]{:S(2)}, u32[]{:S(2)}) collective-permute-start(bf16[2,4,128,1024]{3,2,1,0:T(8,128)(2,1)} %pad_maximum_fusion.9), channel_id=1, source_target_pairs={{0,16},{4,20},{8,24},{12,28},{16,0},{20,4},{24,8},{28,12},{1,17},{... | collective-permute-start | bytes 6291464 | tf_op jit(solution)/shard_map/ppermute | solution.py:1272
  721.5 52.9 %collective-permute-start.46 = (bf16[2,4,128,1024]{3,2,1,0:T(8,128)(2,1)}, bf16[2,4,128,1024]{3,2,1,0:T(8,128)(2,1)}, u32[]{:S(2)}, u32[]{:S(2)}) collective-permute-start(bf16[2,4,128,1024]{3,2,1,0:T(8,128)(2,1)} %pad_maximum_fusion.8), channel_id=1, source_target_pairs={{0,8},{4,12},{8,0},{12,4},{16,24},{20,28},{24,16},{28,20},{1,9},{5... | collective-permute-start | bytes 6291464 | tf_op jit(solution)/shard_map/ppermute | solution.py:1272
  723.2 49.0 %collective-permute-start.48 = (bf16[1,128,1024]{2,1,0:T(8,128)(2,1)}, bf16[1,128,1024]{2,1,0:T(8,128)(2,1)}, u32[]{:S(2)}, u32[]{:S(2)}) collective-permute-start(bf16[1,128,1024]{2,1,0:T(8,128)(2,1)} %slice.389), channel_id=1, source_target_pairs={{0,16},{4,20},{8,24},{12,28},{16,0},{20,4},{24,8},{28,12},{1,17},{... | collective-permute-start | bytes 786440 | tf_op jit(solution)/shard_map/ppermute | solution.py:1272
  725.6 48.8 %collective-permute-start.49 = (bf16[1,128,1024]{2,1,0:T(8,128)(2,1)}, bf16[1,128,1024]{2,1,0:T(8,128)(2,1)}, u32[]{:S(2)}, u32[]{:S(2)}) collective-permute-start(bf16[1,128,1024]{2,1,0:T(8,128)(2,1)} %slice.390), channel_id=1, source_target_pairs={{0,8},{4,12},{8,0},{12,4},{16,24},{20,28},{24,16},{28,20},{1,9},{5... | collective-permute-start | bytes 786440 | tf_op jit(solution)/shard_map/ppermute | solution.py:1272
  774.4 37.8 %collective-permute-start.52 = (bf16[4,4,128,1024]{3,2,1,0:T(8,128)(2,1)}, bf16[4,4,128,1024]{3,2,1,0:T(8,128)(2,1)}, u32[]{:S(2)}, u32[]{:S(2)}) collective-permute-start(bf16[4,4,128,1024]{3,2,1,0:T(8,128)(2,1)} %get-tuple-element.413), channel_id=1, source_target_pairs={{0,4},{4,0},{8,12},{12,8},{16,20},{20,16},{24,28},{28,24},{1,5},{5... | collective-permute-start | bytes 12582920 | tf_op jit(solution)/shard_map/ppermute | solution.py:1272
  828.5 92.7 %reduce-scatter.11.cloned.1.call-start = ((), (), s32[]{:S(2)}) async-start(), calls=%async_computation.11 | async-start | bytes 1474560 | tf_op jit(solution)/shard_map/reduce_scatter | solution.py:1360
  (116 other events, 1522.2 us)
Sparse Core Ops, SparseCore 0:
  56.3 29.1 all-gather.8
  87.8 27.5 all-gather.10
  117.6 27.4 all-gather.12
  168.0 44.6 all-gather.14
  613.0 46.3 reduce-scatter.4
  688.3 26.2 reduce-scatter.6
  828.6 41.6 reduce-scatter.8
  892.9 27.9 reduce-scatter.10
